TPU v7x, 32 devices: a whole 2x2x4 slice. The times are simulated.
32 devices in a mesh: sample: 2 (over x), axial: 16 (over z, y, core).
Axes of the slice: x: 2, y: 2, z: 4, core: 2. Of those that a mesh axis runs over, the one named last changes fastest.
Arguments:
- initial_state: float32 [10, 512, 1024], P('sample', 'axial'), parts along dimension 0, may hold values from -6 to 6
- forcing: float32 [10, 512, 1024], P('sample', 'axial'), parts along dimension 0, may hold values from -6 to 6
- coefficients: float32 [50, 64], P('sample', 'axial'), parts along dimension 0, may hold values from -0.5 to 0.5, as said below
- region_ids: int32 [512, 8], P('axial'), may hold values from 0 to 63
Outputs:
- updated_state: float32 [10, 512, 1024], P('sample', 'axial'), parts along dimension 0
There are 2 independent parts, one for each index of `sample`. A program takes and returns all parts, laid end to end along the dimension named above; an argument that names none is the same for every part. Nothing has to cross between parts.
Inputs may be any that keep to these rules, and one draw needn't show every extreme that they name: `coefficients`: entry 5 f + g holds row f, column g of a region's block; every diagonal entry is positive and exceeds the sum of magnitudes of the other entries of its row.
All inputs are finite; a program needn't handle non-finite values.
Results may differ from a plain program's by a relative error of at most 0.0001.
Values sent between devices are 32-bit elements; how exact they have to be, the bound alone decides.
No kernel may reach another device: no remote copies, remote signals or barrier semaphores. Data moves between devices by JAX's collectives and lax.ppermute only.
A program may use at most 128 MiB of HBM per device.

v0:
```python
import jax
import jax.numpy as jnp
from jax import lax
from jax.sharding import PartitionSpec as P

SWEEPS_PRE = 2
SWEEPS_POST = 2
SWEEPS_COARSE = 4
CYCLES = 2


DIFFUSION = 1.0
RELAXATION = 0.8
SOURCE_GAIN = 0.05


def padded_2(array, sides, width):
    for axis, dim in sides:
        size, length = (lax.axis_size(axis), array.shape[dim])
        up = [(i, (i + 1) % size) for i in range(size - 1)]
        down = [(j, i) for i, j in up]
        last = lax.slice_in_dim(array, length - width, length, axis=dim)
        initial = lax.slice_in_dim(array, 0, width, axis=dim)
        before = lax.ppermute(last, axis, up)
        after = lax.ppermute(initial, axis, down)
        array = jnp.concatenate([before, array, after], axis=dim)
    return array


def matvec_block(matrix, vector):
    block_order = vector.shape[0]
    blocks = matrix.reshape((block_order, block_order) + vector.shape[1:])
    return jnp.sum(blocks * vector[None], axis=1)


def invert_blocks(matrix):
    block_order = 5
    ones_block = jnp.ones_like(matrix[0])
    nothing = jnp.zeros_like(matrix[0])
    augmented = [
        [matrix[block_order * row_at + col_at] for col_at in range(block_order)]
        + [ones_block if row_at == col_at else nothing for col_at in range(block_order)]
        for row_at in range(block_order)
    ]
    for column in range(block_order):
        leading = 1.0 / augmented[column][column]
        augmented[column] = [element * leading for element in augmented[column]]
        for row_at in range(block_order):
            if row_at != column:
                factor = augmented[row_at][column]
                augmented[row_at] = [
                    element - factor * source
                    for element, source in zip(augmented[row_at], augmented[column])
                ]
    return jnp.stack(
        [
            augmented[row_at][block_order + col_at]
            for row_at in range(block_order)
            for col_at in range(block_order)
        ]
    )


def diagonal_block(matrix, weight):
    identity = jnp.eye(5, dtype=matrix.dtype).reshape(25, 1, 1)
    return matrix + 4.0 * weight * identity


def operate(padded, matrix, weight):
    centre = padded[:, 1:-1]
    radial = jnp.pad(centre, ((0, 0), (0, 0), (1, 1)))
    beside = padded[:, 2:] + padded[:, :-2] + radial[:, :, 2:] + radial[:, :, :-2]
    return (
        matvec_block(matrix, centre)
        + weight * (4.0 * centre - beside)
        + SOURCE_GAIN * jnp.tanh(centre)
    )


def relax_sweep(padded, forcing, matrix, inverse, weight):
    centre = padded[:, 1:-1]
    return centre + RELAXATION * matvec_block(inverse, forcing - operate(padded, matrix, weight))


def spread_table(coarse_count, factor, scale):
    fine_index = lax.broadcasted_iota(jnp.int32, (coarse_count, coarse_count * factor), 1)
    coarse_index = lax.broadcasted_iota(jnp.int32, (coarse_count, coarse_count * factor), 0)
    return jnp.where(fine_index // factor == coarse_index, scale, 0.0).astype(jnp.float32)


def radial_apply(values, table):
    return jnp.einsum(
        "far,rs->fas",
        values,
        table,
        precision=lax.Precision.HIGHEST,
        preferred_element_type=jnp.float32,
    )


def restrict(values):
    leading = values.shape[0]
    rows = values.shape[1]
    radial_cells = values.shape[2]
    paired = values.reshape(leading, rows // 2, 2, radial_cells)
    axial_half = 0.5 * (paired[:, :, 0] + paired[:, :, 1])
    averaging = jnp.transpose(spread_table(radial_cells // 2, 2, 0.5))
    return radial_apply(axial_half, averaging)


def prolong(values):
    leading = values.shape[0]
    rows = values.shape[1]
    radial_cells = values.shape[2]
    widened = radial_apply(values, spread_table(radial_cells, 2, 1.0))
    doubled = jnp.broadcast_to(widened[:, :, None, :], (leading, rows, 2, 2 * radial_cells))
    return doubled.reshape(leading, 2 * rows, 2 * radial_cells)


def with_rim(values):
    return padded_2(values, (("axial", 1),), 1)


def smooth(values, source, matrix, inverse, weight, count):
    for sweep_at in range(count):
        values = relax_sweep(with_rim(values), source, matrix, inverse, weight)
    return values


def per_device(initial_state, forcing, coefficients, region_ids):
    gathered = lax.all_gather(coefficients, "axial", axis=1, tiled=True)
    regions = gathered.shape[1]
    flat_ids = region_ids.reshape(-1)
    selector = (
        lax.broadcasted_iota(jnp.int32, (regions, flat_ids.shape[0]), 0) == flat_ids[None, :]
    ).astype(jnp.float32)
    picked = jnp.dot(
        gathered, selector, precision=lax.Precision.HIGHEST, preferred_element_type=jnp.float32
    )
    picked = picked.reshape((gathered.shape[0],) + region_ids.shape)
    block_span = initial_state.shape[2] // region_ids.shape[1]
    matrices = [radial_apply(picked, spread_table(region_ids.shape[1], block_span, 1.0))]
    for level_at in range(3):
        matrices.append(restrict(matrices[-1]))
    weights = [DIFFUSION / 4.0**level_at for level_at in range(4)]
    inverses = [
        invert_blocks(diagonal_block(matrices[level_at], weights[level_at]))
        for level_at in range(3)
    ]
    inverses.append(invert_blocks(diagonal_block(matrices[3], weights[3])))

    def relax_level(level_at, values, source, count):
        return smooth(
            values, source, matrices[level_at], inverses[level_at], weights[level_at], count
        )

    def vcycle_level(level_at, values, source):
        if level_at == 3:
            return relax_level(3, values, source, SWEEPS_COARSE)
        values = relax_level(level_at, values, source, SWEEPS_PRE)
        coarse = restrict(values)
        rimmed = padded_2(values, (("axial", 1),), 1)
        residual = source - operate(rimmed, matrices[level_at], weights[level_at])
        coarse_padded = padded_2(coarse, (("axial", 1),), 1)
        coarse_source = operate(
            coarse_padded, matrices[level_at + 1], weights[level_at + 1]
        ) + restrict(residual)
        corrected = vcycle_level(level_at + 1, coarse, coarse_source)
        values = values + prolong(corrected - coarse)
        return relax_level(level_at, values, source, SWEEPS_POST)

    values = initial_state
    for cycle_at in range(CYCLES):
        values = vcycle_level(0, values, forcing)
    return values


def solution(mesh):
    placed = (
        P("sample", "axial", None),
        P("sample", "axial", None),
        P("sample", "axial"),
        P("axial", None),
    )
    return jax.shard_map(
        per_device,
        mesh=mesh,
        in_specs=placed,
        out_specs=P("sample", "axial", None),
        check_vma=False,
    )
```

profile of v0, /device:TPU:10, one launch (start us, length us, event | category | flops | bytes accessed | tf_op | source)
XLA Modules:
  0.0 582.8 jit_solution(17887865604170375036)
XLA Ops:
  7.0 19.4 %all-gather = f32[16,4,25]{2,1,0:T(4,128)S(1)} all-gather(f32[1,4,25]{2,1,0:T(4,128)} %bitcast.191), channel_id=1, replica_groups=mesh['sample'=2,'axial'=16] {'axial'}, dimensions={0}, use_global_device_ids=true | all-gather | bytes 6800 | tf_op jit(solution)/shard_map/all_gather | solution.py:131
  49.3 3.4 reshape.347
  55.3 5.3 fusion.784
  60.7 6.2 %broadcast_add_fusion.1 = (f32[25,16,512]{2,1,0:T(8,128)S(1)}, f32[25,16,512]{2,1,0:T(8,128)}) fusion(f32[25]{0:T(128)S(1)} %reshape.373, s32[1024]{0:T(1024)S(1)} %get-tuple-element.345, s32[1024]{0:T(1024)S(1)} %get-tuple-element.346, pred[1024]{0:T(1024)(128)(4,1)S(1)} %fusion.644, f32[25,16,1,1024]{3,2,1,0:T(1,128)} %get-tuple-element.208, ...), kind=kOutput, calls=%fused_computation.248 | convolution fusion | flops 2519179264 | bytes 4924516 | tf_op jit(solution)/shard_map/far,rs->fas/dot_general | solution.py:92
  158.6 4.5 collective-permute-start.4
  170.8 3.7 fusion.837
  175.9 4.5 collective-permute-start.8
  182.5 3.8 collective-permute-done.9
  199.8 4.0 collective-permute-start.10
  214.2 4.5 collective-permute-start.14
  220.9 3.7 collective-permute-done.15
  236.1 4.1 collective-permute-start.16
  248.7 4.5 collective-permute-start.20
  255.2 3.9 collective-permute-done.21
  264.4 3.4 collective-permute-done.23
  273.1 3.4 collective-permute-done.25
  285.5 3.4 collective-permute-done.27
  295.1 3.4 collective-permute-done.29
  389.1 4.0 collective-permute-start.42
  400.8 3.7 fusion.840
  405.9 4.5 collective-permute-start.46
  412.5 3.8 collective-permute-done.47
  429.7 4.0 collective-permute-start.48
  444.2 4.5 collective-permute-start.52
  450.7 3.9 collective-permute-done.53
  466.9 4.0 collective-permute-start.54
  479.0 4.4 collective-permute-start.58
  485.4 3.9 collective-permute-done.59
  494.6 3.4 collective-permute-done.61
  503.3 3.4 collective-permute-done.63
  514.3 3.4 collective-permute-done.65
  524.0 3.4 collective-permute-done.67
  (603 shorter events, 436.2 us)
Async XLA Ops:
  1.6 123.8 %collective-permute-start = (f32[5,1,1024]{2,1,0:T(1,128)}, f32[5,1,1024]{2,1,0:T(1,128)}, u32[]{:S(2)}, u32[]{:S(2)}) collective-permute-start(f32[5,1,1024]{2,1,0:T(1,128)} %get-tuple-element.243), channel_id=1, source_target_pairs={{1,0},{2,1},{3,2},{4,3},{5,4},{6,5},{7,6},{8,7},{9,8},{10,9},{11,1... | collective-permute-start | bytes 61448 | tf_op jit(solution)/shard_map/ppermute | solution.py:25
  4.4 121.1 %collective-permute-start.1 = (f32[5,1,1024]{2,1,0:T(1,128)S(1)}, f32[5,1,1024]{2,1,0:T(1,128)}, u32[]{:S(2)}, u32[]{:S(2)}) collective-permute-start(f32[5,1,1024]{2,1,0:T(1,128)S(1)} %get-tuple-element.244), channel_id=1, source_target_pairs={{0,1},{1,2},{2,3},{3,4},{4,5},{5,6},{6,7},{7,8},{8,9},{9,10},{10,1... | collective-permute-start | bytes 61448 | tf_op jit(solution)/shard_map/ppermute | solution.py:24
  146.9 18.1 %collective-permute-start.6 = (f32[5,1,1024]{2,1,0:T(1,128)}, f32[5,1,1024]{2,1,0:T(1,128)S(1)}, u32[]{:S(2)}, u32[]{:S(2)}) collective-permute-start(f32[5,1,1024]{2,1,0:T(1,128)} %get-tuple-element.237), channel_id=1, source_target_pairs={{1,0},{2,1},{3,2},{4,3},{5,4},{6,5},{7,6},{8,7},{9,8},{10,9},{11,1... | collective-permute-start | bytes 61448 | tf_op jit(solution)/shard_map/ppermute | solution.py:25
  150.3 14.8 %collective-permute-start.7 = (f32[5,1,1024]{2,1,0:T(1,128)S(1)}, f32[5,1,1024]{2,1,0:T(1,128)S(1)}, u32[]{:S(2)}, u32[]{:S(2)}) collective-permute-start(f32[5,1,1024]{2,1,0:T(1,128)S(1)} %get-tuple-element.238), channel_id=1, source_target_pairs={{0,1},{1,2},{2,3},{3,4},{4,5},{5,6},{6,7},{7,8},{8,9},{9,10},{10,1... | collective-permute-start | bytes 61448 | tf_op jit(solution)/shard_map/ppermute | solution.py:24
  158.6 12.2 %collective-permute-start.4 = (f32[5,1,512]{2,1,0:T(1,128)}, f32[5,1,512]{2,1,0:T(1,128)}, u32[]{:S(2)}, u32[]{:S(2)}) collective-permute-start(f32[5,1,512]{2,1,0:T(1,128)} %get-tuple-element.276), channel_id=1, source_target_pairs={{1,0},{2,1},{3,2},{4,3},{5,4},{6,5},{7,6},{8,7},{9,8},{10,9},{11,1... | collective-permute-start | bytes 30728 | tf_op jit(solution)/shard_map/ppermute | solution.py:25
  163.1 7.6 %collective-permute-start.5 = (f32[5,1,512]{2,1,0:T(1,128)}, f32[5,1,512]{2,1,0:T(1,128)}, u32[]{:S(2)}, u32[]{:S(2)}) collective-permute-start(f32[5,1,512]{2,1,0:T(1,128)} %get-tuple-element.277), channel_id=1, source_target_pairs={{0,1},{1,2},{2,3},{3,4},{4,5},{5,6},{6,7},{7,8},{8,9},{9,10},{10,1... | collective-permute-start | bytes 30728 | tf_op jit(solution)/shard_map/ppermute | solution.py:24
  175.9 6.6 %collective-permute-start.8 = (f32[5,1,512]{2,1,0:T(1,128)S(1)}, f32[5,1,512]{2,1,0:T(1,128)S(1)}, u32[]{:S(2)}, u32[]{:S(2)}) collective-permute-start(f32[5,1,512]{2,1,0:T(1,128)S(1)} %get-tuple-element.274), channel_id=1, source_target_pairs={{1,0},{2,1},{3,2},{4,3},{5,4},{6,5},{7,6},{8,7},{9,8},{10,9},{11,1... | collective-permute-start | bytes 30728 | tf_op jit(solution)/shard_map/ppermute | solution.py:25
  193.6 12.2 %collective-permute-start.12 = (f32[5,1,512]{2,1,0:T(1,128)S(1)}, f32[5,1,512]{2,1,0:T(1,128)S(1)}, u32[]{:S(2)}, u32[]{:S(2)}) collective-permute-start(f32[5,1,512]{2,1,0:T(1,128)S(1)} %get-tuple-element.270), channel_id=1, source_target_pairs={{1,0},{2,1},{3,2},{4,3},{5,4},{6,5},{7,6},{8,7},{9,8},{10,9},{11,1... | collective-permute-start | bytes 30728 | tf_op jit(solution)/shard_map/ppermute | solution.py:25
  195.5 10.3 %collective-permute-start.13 = (f32[5,1,512]{2,1,0:T(1,128)S(1)}, f32[5,1,512]{2,1,0:T(1,128)S(1)}, u32[]{:S(2)}, u32[]{:S(2)}) collective-permute-start(f32[5,1,512]{2,1,0:T(1,128)S(1)} %get-tuple-element.271), channel_id=1, source_target_pairs={{0,1},{1,2},{2,3},{3,4},{4,5},{5,6},{6,7},{7,8},{8,9},{9,10},{10,1... | collective-permute-start | bytes 30728 | tf_op jit(solution)/shard_map/ppermute | solution.py:24
  199.8 11.0 %collective-permute-start.10 = (f32[5,1,256]{2,1,0:T(1,128)}, f32[5,1,256]{2,1,0:T(1,128)}, u32[]{:S(2)}, u32[]{:S(2)}) collective-permute-start(f32[5,1,256]{2,1,0:T(1,128)} %get-tuple-element.307), channel_id=1, source_target_pairs={{1,0},{2,1},{3,2},{4,3},{5,4},{6,5},{7,6},{8,7},{9,8},{10,9},{11,1... | collective-permute-start | bytes 15368 | tf_op jit(solution)/shard_map/ppermute | solution.py:25
  203.8 7.0 %collective-permute-start.11 = (f32[5,1,256]{2,1,0:T(1,128)S(1)}, f32[5,1,256]{2,1,0:T(1,128)}, u32[]{:S(2)}, u32[]{:S(2)}) collective-permute-start(f32[5,1,256]{2,1,0:T(1,128)S(1)} %get-tuple-element.308), channel_id=1, source_target_pairs={{0,1},{1,2},{2,3},{3,4},{4,5},{5,6},{6,7},{7,8},{8,9},{9,10},{10,1... | collective-permute-start | bytes 15368 | tf_op jit(solution)/shard_map/ppermute | solution.py:24
  214.2 6.7 %collective-permute-start.14 = (f32[5,1,256]{2,1,0:T(1,128)S(1)}, f32[5,1,256]{2,1,0:T(1,128)S(1)}, u32[]{:S(2)}, u32[]{:S(2)}) collective-permute-start(f32[5,1,256]{2,1,0:T(1,128)S(1)} %get-tuple-element.305), channel_id=1, source_target_pairs={{1,0},{2,1},{3,2},{4,3},{5,4},{6,5},{7,6},{8,7},{9,8},{10,9},{11,1... | collective-permute-start | bytes 15368 | tf_op jit(solution)/shard_map/ppermute | solution.py:25
  231.8 10.9 %collective-permute-start.18 = (f32[5,1,256]{2,1,0:T(1,128)S(1)}, f32[5,1,256]{2,1,0:T(1,128)S(1)}, u32[]{:S(2)}, u32[]{:S(2)}) collective-permute-start(f32[5,1,256]{2,1,0:T(1,128)S(1)} %get-tuple-element.301), channel_id=1, source_target_pairs={{1,0},{2,1},{3,2},{4,3},{5,4},{6,5},{7,6},{8,7},{9,8},{10,9},{11,1... | collective-permute-start | bytes 15368 | tf_op jit(solution)/shard_map/ppermute | solution.py:25
  233.7 9.0 %collective-permute-start.19 = (f32[5,1,256]{2,1,0:T(1,128)S(1)}, f32[5,1,256]{2,1,0:T(1,128)S(1)}, u32[]{:S(2)}, u32[]{:S(2)}) collective-permute-start(f32[5,1,256]{2,1,0:T(1,128)S(1)} %get-tuple-element.302), channel_id=1, source_target_pairs={{0,1},{1,2},{2,3},{3,4},{4,5},{5,6},{6,7},{7,8},{8,9},{9,10},{10,1... | collective-permute-start | bytes 15368 | tf_op jit(solution)/shard_map/ppermute | solution.py:24
  236.1 10.7 %collective-permute-start.16 = (f32[5,1,128]{2,0,1:T(8,128)}, f32[5,1,128]{2,0,1:T(8,128)}, u32[]{:S(2)}, u32[]{:S(2)}) collective-permute-start(f32[5,1,128]{2,0,1:T(8,128)} %get-tuple-element.323), channel_id=1, source_target_pairs={{1,0},{2,1},{3,2},{4,3},{5,4},{6,5},{7,6},{8,7},{9,8},{10,9},{11,1... | collective-permute-start | bytes 7688 | tf_op jit(solution)/shard_map/ppermute | solution.py:25
  240.2 6.6 %collective-permute-start.17 = (f32[5,1,128]{2,0,1:T(8,128)}, f32[5,1,128]{2,0,1:T(8,128)}, u32[]{:S(2)}, u32[]{:S(2)}) collective-permute-start(f32[5,1,128]{2,0,1:T(8,128)} %get-tuple-element.324), channel_id=1, source_target_pairs={{0,1},{1,2},{2,3},{3,4},{4,5},{5,6},{6,7},{7,8},{8,9},{9,10},{10,1... | collective-permute-start | bytes 7688 | tf_op jit(solution)/shard_map/ppermute | solution.py:24
  248.7 6.5 %collective-permute-start.20 = (f32[5,1,128]{2,0,1:T(8,128)S(1)}, f32[5,1,128]{2,0,1:T(8,128)S(1)}, u32[]{:S(2)}, u32[]{:S(2)}) collective-permute-start(f32[5,1,128]{2,0,1:T(8,128)S(1)} %get-tuple-element.321), channel_id=1, source_target_pairs={{1,0},{2,1},{3,2},{4,3},{5,4},{6,5},{7,6},{8,7},{9,8},{10,9},{11,1... | collective-permute-start | bytes 7688 | tf_op jit(solution)/shard_map/ppermute | solution.py:25
  381.0 14.1 %collective-permute-start.44 = (f32[5,1,1024]{2,1,0:T(1,128)S(1)}, f32[5,1,1024]{2,1,0:T(1,128)S(1)}, u32[]{:S(2)}, u32[]{:S(2)}) collective-permute-start(f32[5,1,1024]{2,1,0:T(1,128)S(1)} %get-tuple-element.223), channel_id=1, source_target_pairs={{1,0},{2,1},{3,2},{4,3},{5,4},{6,5},{7,6},{8,7},{9,8},{10,9},{11,1... | collective-permute-start | bytes 61448 | tf_op jit(solution)/shard_map/ppermute | solution.py:25
  382.9 12.2 %collective-permute-start.45 = (f32[5,1,1024]{2,1,0:T(1,128)S(1)}, f32[5,1,1024]{2,1,0:T(1,128)S(1)}, u32[]{:S(2)}, u32[]{:S(2)}) collective-permute-start(f32[5,1,1024]{2,1,0:T(1,128)S(1)} %get-tuple-element.224), channel_id=1, source_target_pairs={{0,1},{1,2},{2,3},{3,4},{4,5},{5,6},{6,7},{7,8},{8,9},{9,10},{10,1... | collective-permute-start | bytes 61448 | tf_op jit(solution)/shard_map/ppermute | solution.py:24
  389.1 11.7 %collective-permute-start.42 = (f32[5,1,512]{2,1,0:T(1,128)}, f32[5,1,512]{2,1,0:T(1,128)}, u32[]{:S(2)}, u32[]{:S(2)}) collective-permute-start(f32[5,1,512]{2,1,0:T(1,128)} %get-tuple-element.262), channel_id=1, source_target_pairs={{1,0},{2,1},{3,2},{4,3},{5,4},{6,5},{7,6},{8,7},{9,8},{10,9},{11,1... | collective-permute-start | bytes 30728 | tf_op jit(solution)/shard_map/ppermute | solution.py:25
  393.1 7.7 %collective-permute-start.43 = (f32[5,1,512]{2,1,0:T(1,128)S(1)}, f32[5,1,512]{2,1,0:T(1,128)}, u32[]{:S(2)}, u32[]{:S(2)}) collective-permute-start(f32[5,1,512]{2,1,0:T(1,128)S(1)} %get-tuple-element.263), channel_id=1, source_target_pairs={{0,1},{1,2},{2,3},{3,4},{4,5},{5,6},{6,7},{7,8},{8,9},{9,10},{10,1... | collective-permute-start | bytes 30728 | tf_op jit(solution)/shard_map/ppermute | solution.py:24
  405.9 6.6 %collective-permute-start.46 = (f32[5,1,512]{2,1,0:T(1,128)S(1)}, f32[5,1,512]{2,1,0:T(1,128)S(1)}, u32[]{:S(2)}, u32[]{:S(2)}) collective-permute-start(f32[5,1,512]{2,1,0:T(1,128)S(1)} %get-tuple-element.260), channel_id=1, source_target_pairs={{1,0},{2,1},{3,2},{4,3},{5,4},{6,5},{7,6},{8,7},{9,8},{10,9},{11,1... | collective-permute-start | bytes 30728 | tf_op jit(solution)/shard_map/ppermute | solution.py:25
  423.5 12.2 %collective-permute-start.50 = (f32[5,1,512]{2,1,0:T(1,128)S(1)}, f32[5,1,512]{2,1,0:T(1,128)S(1)}, u32[]{:S(2)}, u32[]{:S(2)}) collective-permute-start(f32[5,1,512]{2,1,0:T(1,128)S(1)} %get-tuple-element.256), channel_id=1, source_target_pairs={{1,0},{2,1},{3,2},{4,3},{5,4},{6,5},{7,6},{8,7},{9,8},{10,9},{11,1... | collective-permute-start | bytes 30728 | tf_op jit(solution)/shard_map/ppermute | solution.py:25
  425.4 10.3 %collective-permute-start.51 = (f32[5,1,512]{2,1,0:T(1,128)S(1)}, f32[5,1,512]{2,1,0:T(1,128)S(1)}, u32[]{:S(2)}, u32[]{:S(2)}) collective-permute-start(f32[5,1,512]{2,1,0:T(1,128)S(1)} %get-tuple-element.257), channel_id=1, source_target_pairs={{0,1},{1,2},{2,3},{3,4},{4,5},{5,6},{6,7},{7,8},{8,9},{9,10},{10,1... | collective-permute-start | bytes 30728 | tf_op jit(solution)/shard_map/ppermute | solution.py:24
  429.7 11.0 %collective-permute-start.48 = (f32[5,1,256]{2,1,0:T(1,128)}, f32[5,1,256]{2,1,0:T(1,128)}, u32[]{:S(2)}, u32[]{:S(2)}) collective-permute-start(f32[5,1,256]{2,1,0:T(1,128)} %get-tuple-element.293), channel_id=1, source_target_pairs={{1,0},{2,1},{3,2},{4,3},{5,4},{6,5},{7,6},{8,7},{9,8},{10,9},{11,1... | collective-permute-start | bytes 15368 | tf_op jit(solution)/shard_map/ppermute | solution.py:25
  433.8 7.0 %collective-permute-start.49 = (f32[5,1,256]{2,1,0:T(1,128)S(1)}, f32[5,1,256]{2,1,0:T(1,128)}, u32[]{:S(2)}, u32[]{:S(2)}) collective-permute-start(f32[5,1,256]{2,1,0:T(1,128)S(1)} %get-tuple-element.294), channel_id=1, source_target_pairs={{0,1},{1,2},{2,3},{3,4},{4,5},{5,6},{6,7},{7,8},{8,9},{9,10},{10,1... | collective-permute-start | bytes 15368 | tf_op jit(solution)/shard_map/ppermute | solution.py:24
  444.2 6.5 %collective-permute-start.52 = (f32[5,1,256]{2,1,0:T(1,128)S(1)}, f32[5,1,256]{2,1,0:T(1,128)S(1)}, u32[]{:S(2)}, u32[]{:S(2)}) collective-permute-start(f32[5,1,256]{2,1,0:T(1,128)S(1)} %get-tuple-element.291), channel_id=1, source_target_pairs={{1,0},{2,1},{3,2},{4,3},{5,4},{6,5},{7,6},{8,7},{9,8},{10,9},{11,1... | collective-permute-start | bytes 15368 | tf_op jit(solution)/shard_map/ppermute | solution.py:25
  461.7 11.2 %collective-permute-start.56 = (f32[5,1,256]{2,1,0:T(1,128)S(1)}, f32[5,1,256]{2,1,0:T(1,128)S(1)}, u32[]{:S(2)}, u32[]{:S(2)}) collective-permute-start(f32[5,1,256]{2,1,0:T(1,128)S(1)} %get-tuple-element.287), channel_id=1, source_target_pairs={{1,0},{2,1},{3,2},{4,3},{5,4},{6,5},{7,6},{8,7},{9,8},{10,9},{11,1... | collective-permute-start | bytes 15368 | tf_op jit(solution)/shard_map/ppermute | solution.py:25
  463.9 9.0 %collective-permute-start.57 = (f32[5,1,256]{2,1,0:T(1,128)S(1)}, f32[5,1,256]{2,1,0:T(1,128)S(1)}, u32[]{:S(2)}, u32[]{:S(2)}) collective-permute-start(f32[5,1,256]{2,1,0:T(1,128)S(1)} %get-tuple-element.288), channel_id=1, source_target_pairs={{0,1},{1,2},{2,3},{3,4},{4,5},{5,6},{6,7},{7,8},{8,9},{9,10},{10,1... | collective-permute-start | bytes 15368 | tf_op jit(solution)/shard_map/ppermute | solution.py:24
  466.9 10.1 %collective-permute-start.54 = (f32[5,1,128]{2,0,1:T(8,128)}, f32[5,1,128]{2,0,1:T(8,128)}, u32[]{:S(2)}, u32[]{:S(2)}) collective-permute-start(f32[5,1,128]{2,0,1:T(8,128)} %get-tuple-element.315), channel_id=1, source_target_pairs={{1,0},{2,1},{3,2},{4,3},{5,4},{6,5},{7,6},{8,7},{9,8},{10,9},{11,1... | collective-permute-start | bytes 7688 | tf_op jit(solution)/shard_map/ppermute | solution.py:25
  471.0 6.1 %collective-permute-start.55 = (f32[5,1,128]{2,0,1:T(8,128)}, f32[5,1,128]{2,0,1:T(8,128)}, u32[]{:S(2)}, u32[]{:S(2)}) collective-permute-start(f32[5,1,128]{2,0,1:T(8,128)} %get-tuple-element.316), channel_id=1, source_target_pairs={{0,1},{1,2},{2,3},{3,4},{4,5},{5,6},{6,7},{7,8},{8,9},{9,10},{10,1... | collective-permute-start | bytes 7688 | tf_op jit(solution)/shard_map/ppermute | solution.py:24
  479.0 6.4 %collective-permute-start.58 = (f32[5,1,128]{2,0,1:T(8,128)S(1)}, f32[5,1,128]{2,0,1:T(8,128)S(1)}, u32[]{:S(2)}, u32[]{:S(2)}) collective-permute-start(f32[5,1,128]{2,0,1:T(8,128)S(1)} %get-tuple-element.313), channel_id=1, source_target_pairs={{1,0},{2,1},{3,2},{4,3},{5,4},{6,5},{7,6},{8,7},{9,8},{10,9},{11,1... | collective-permute-start | bytes 7688 | tf_op jit(solution)/shard_map/ppermute | solution.py:25
  (95 other events, 1423.8 us)
where the time goes:
time: 594 us; the launch traced here: 583 us
  starting transfers between devices  190 us (32%)
  other arithmetic  157 us (26%)
  local copies, waits for them, and re-layouts  90.5 us (15%)
  waiting for transfers between devices  82.5 us (14%)
  matrix products  40.4 us (7%)
  blocking collectives  19.4 us (3%)
    ppermute x38, starting transfers between devices, padded_2(): after = lax.ppermute(initial, axis, down)  105 us
    ppermute x38, starting transfers between devices, padded_2(): before = lax.ppermute(last, axis, up)  85.3 us
    ppermute x38, waiting for transfers between devices, padded_2(): before = lax.ppermute(last, axis, up)  82.4 us
    reduce_sum x70, other arithmetic, matvec_block(): return jnp.sum(blocks * vector[None], axis=1)  64.2 us
    unnamed x80, other arithmetic  52.1 us
    dot_general x22, matrix products, radial_apply(): jnp.einsum('far,rs->fas', values, table, precision=lax.Precision.HIGHEST,...  40.2 us
    reshape x15, local copies, waits for them, and re-layouts, restrict(): paired = values.reshape(leading, rows // 2, 2, radial_cells)  28.3 us
    slice x15, local copies, waits for them, and re-layouts, restrict(): axial_half = 0.5 * (paired[:, :, 0] + paired[:, :, 1])  24.9 us
  transfers between devices with their start and end apart: 76, of which 26 were waited for; matrix products, arithmetic and copies ran while one was open for 26% of the time, Pallas kernels for 0%

commit v1 on v0

v1 whole, which is shorter than its diff:
```python
import functools

import jax
import jax.numpy as jnp
from jax import lax
from jax.experimental import pallas as pl
from jax.experimental.pallas import tpu as pltpu
from jax.sharding import PartitionSpec as P

DIFFUSION = 1.0
RELAXATION = 0.8
SOURCE_GAIN = 0.05
CYCLES = 2

FIELDS = 5
ENTRIES = FIELDS * FIELDS
SUB, LANES = 8, 128

OWN = 32
FINE_HALO = 11
PAD = 9
HEAD = 8
T0, O0 = 64, 16
T1, O1 = 32, 8
T2, O2 = 40, 16
T3, O3 = 20, 8
GROUP = 4


def padded_rows(rows):
    return HEAD + PAD * rows + 16


def at(row):
    return HEAD + PAD * row


def lane_iota():
    return lax.broadcasted_iota(jnp.int32, (SUB, LANES), 1)


def tile(ref, field, row):
    return ref[field, pl.ds(at(row), SUB), :]


def put(ref, field, row, value):
    ref[field, pl.ds(at(row), SUB), :] = value


def rows_loop(first, last, body):
    def step(row, carry):
        body(row)
        return carry

    lax.fori_loop(first, last, step, 0)


def neighbours(ref, row, level):
    width = 2**level
    lane = lane_iota()
    sums, centres = [], []
    for field in range(FIELDS):
        start = at(row)
        centre = ref[field, pl.ds(start, SUB), :]
        lower = ref[field, pl.ds(start - 1, SUB), :]
        upper = ref[field, pl.ds(start + 1, SUB), :]
        left = pltpu.roll(jnp.where(lane >= LANES - width, lower, centre), width, 1)
        right = pltpu.roll(jnp.where(lane < width, upper, centre), LANES - width, 1)
        axial = ref[field, pl.ds(start - PAD, SUB), :] + ref[field, pl.ds(start + PAD, SUB), :]
        sums.append((left + right) + axial)
        centres.append(centre)
    return sums, centres


def table_tile(table, row):
    return table[pl.ds(pl.multiple_of(row * SUB, SUB), SUB), :]


def block_times(entries, first, vectors):
    out = []
    for row in range(FIELDS):
        total = None
        for column in range(FIELDS):
            lane = first + FIELDS * row + column
            term = jnp.broadcast_to(entries[:, lane : lane + 1], (SUB, LANES)) * vectors[column]
            total = term if total is None else total + term
        out.append(total)
    return out


MATRIX_LANE = 32


def gain_of(level):
    return SOURCE_GAIN * 4.0**level / DIFFUSION


def sweep(source_of, old, new, table, level, first, last):
    gain = gain_of(level)

    def body(row):
        sums, centres = neighbours(old, row, level)
        rest = [
            (source_of(field, row) + sums[field]) - gain * jnp.tanh(centres[field])
            for field in range(FIELDS)
        ]
        moved = block_times(table_tile(table, row), 0, rest)
        for field in range(FIELDS):
            put(new, field, row, (1.0 - RELAXATION) * centres[field] + moved[field])

    rows_loop(first, last, body)


def residual(source_of, values, table, level, row):
    gain = gain_of(level)
    sums, centres = neighbours(values, row, level)
    applied = block_times(table_tile(table, row), MATRIX_LANE, centres)
    left = [
        ((source_of(field, row) + sums[field]) - gain * jnp.tanh(centres[field])) - applied[field]
        for field in range(FIELDS)
    ]
    return left, centres


def pair_sum(value, level):
    width = 2**level
    lane = lane_iota()
    other = jnp.where(
        (lane & width) == 0, pltpu.roll(value, LANES - width, 1), pltpu.roll(value, width, 1)
    )
    return value + other


def coarsen(source_of, values, table, level, row):
    upper_r, upper_v = residual(source_of, values, table, level, 2 * row)
    lower_r, lower_v = residual(source_of, values, table, level, 2 * row + 1)
    coarse = [0.25 * pair_sum(upper_v[f] + lower_v[f], level) for f in range(FIELDS)]
    rest = [pair_sum(upper_r[f] + lower_r[f], level) for f in range(FIELDS)]
    return coarse, rest


def first_sweep(coarse, rest, table, row):
    moved = block_times(table_tile(table, row), 0, rest)
    return [coarse[f] + moved[f] for f in range(FIELDS)]


def make_source(coarse, rest, source, table, level, first, last):
    gain = gain_of(level)

    def body(row):
        sums, centres = neighbours(coarse, row, level)
        applied = block_times(table_tile(table, row), MATRIX_LANE, centres)
        for field in range(FIELDS):
            source[field, row] = (applied[field] - sums[field]) + (
                gain * jnp.tanh(centres[field]) + rest[field, row]
            )

    rows_loop(first, last, body)


def correct(fine, after, before, offset, first, last):
    def body(row):
        coarse_row = row // 2 + offset
        for field in range(FIELDS):
            change = tile(after, field, coarse_row) - tile(before, field, coarse_row)
            put(fine, field, row, tile(fine, field, row) + change)

    rows_loop(first, last, body)


def clear(ref):
    ref[...] = jnp.zeros_like(ref)


def tables_kernel(where_ref, coeff_ref, ids_ref, tab0, tab1, tab2, tab3, mats, full):
    device, devices = where_ref[0], where_ref[1]
    regions = coeff_ref.shape[1]
    wide = 5 * 256
    exact = lax.Precision.HIGHEST
    region = lax.broadcasted_iota(jnp.int32, (regions, LANES), 0)
    coeff = coeff_ref[...]
    for chunk in range(10):
        ids = jnp.broadcast_to(ids_ref[chunk : chunk + 1, :], (regions, LANES)).astype(jnp.int32)
        chosen = (region == ids).astype(jnp.float32)
        mats[:, chunk * LANES : (chunk + 1) * LANES] = jnp.dot(
            coeff, chosen, precision=exact, preferred_element_type=jnp.float32
        )

    def averaged(lanes_in, lanes_out, span, source):
        into = lax.broadcasted_iota(jnp.int32, (lanes_in, lanes_out), 0)
        out = lax.broadcasted_iota(jnp.int32, (lanes_in, lanes_out), 1)
        same = (into // (SUB * span) == out // SUB) & ((into % SUB) == (out % SUB))
        average = jnp.where(same, 1.0 / span, 0.0).astype(jnp.float32)
        return jnp.dot(source, average, precision=exact, preferred_element_type=jnp.float32)

    def build(matrix, level, rows, own_first, out):
        lanes = rows * SUB
        weight = DIFFUSION / 4.0**level
        row = lax.broadcasted_iota(jnp.int32, (SUB, lanes), 1) // SUB
        own = OWN >> level
        whole = (row - own_first) + device * own
        inside = (whole >= 0) & (whole < devices * own)
        full[:, :lanes] = jnp.zeros((LANES, lanes), jnp.float32)
        full[0:32, :lanes] = matrix
        entry = lambda e: jnp.broadcast_to(full[e : e + 1, :lanes], (SUB, lanes))
        block = [[entry(FIELDS * i + j) for j in range(FIELDS)] for i in range(FIELDS)]
        for i in range(FIELDS):
            block[i][i] = block[i][i] + 4.0 * weight
        for i in range(FIELDS):
            for j in range(FIELDS):
                e = MATRIX_LANE + FIELDS * i + j
                full[e : e + 1, :lanes] = (block[i][j] * (1.0 / weight))[0:1]
        right = [[None] * FIELDS for _ in range(FIELDS)]
        for i in range(FIELDS):
            right[i][i] = jnp.ones((SUB, lanes), jnp.float32)
        for c in range(FIELDS):
            lead = 1.0 / block[c][c]
            for j in range(c + 1, FIELDS):
                block[c][j] = block[c][j] * lead
            for j in range(FIELDS):
                if right[c][j] is not None:
                    right[c][j] = right[c][j] * lead
            for i in range(FIELDS):
                if i == c:
                    continue
                factor = block[i][c]
                for j in range(c + 1, FIELDS):
                    block[i][j] = block[i][j] - factor * block[c][j]
                for j in range(FIELDS):
                    if right[c][j] is not None:
                        term = factor * right[c][j]
                        right[i][j] = -term if right[i][j] is None else right[i][j] - term
        for i in range(FIELDS):
            for j in range(FIELDS):
                e = FIELDS * i + j
                scaled = jnp.where(inside, right[i][j] * (RELAXATION * weight), 0.0)
                full[e : e + 1, :lanes] = scaled[0:1]
        padded_lanes = -(-lanes // LANES) * LANES
        for start in range(0, padded_lanes, LANES):
            count = min(LANES, lanes - start)
            turned = jnp.transpose(full[:, start : start + LANES])
            out[start : start + count, :] = turned[:count]

    fine = mats[:, 6 * SUB * 8 : (6 * 8 + T0) * SUB]
    build(fine, 0, T0, O0, tab0)
    build(averaged(T0 * SUB, T1 * SUB, 2, fine), 1, T1, O1, tab1)
    second = averaged(wide, 3 * LANES, 4, mats[...])
    build(second[:, : T2 * SUB], 2, T2, O2, tab2)
    build(averaged(3 * LANES, 2 * LANES, 2, second)[:, : T3 * SUB], 3, T3, O3, tab3)


def split_kernel(where_ref, state_ref, forcing_ref, state_rows, forcing_rows, send_a, send_b):
    odd = where_ref[0] % 2
    for which, (source, target) in enumerate(
        ((state_ref, state_rows), (forcing_ref, forcing_rows))
    ):
        for field in range(FIELDS):
            for block in range(SUB):
                for start in range(0, OWN, SUB):
                    target[field, pl.ds(start * SUB + block, SUB, stride=SUB), :] = source[
                        field, start : start + SUB, block * LANES : (block + 1) * LANES
                    ]
    low, high = 0, (OWN - FINE_HALO) * SUB
    size = FINE_HALO * SUB
    for which, rows in enumerate((state_rows, forcing_rows)):
        for field in range(FIELDS):
            first = rows[field, low : low + size, :]
            last = rows[field, high : high + size, :]
            send_a[which * FIELDS + field] = jnp.where(odd == 1, first, last)
            send_b[which * FIELDS + field] = jnp.where(odd == 1, last, first)


def place_halo(where_ref, buffer, own_rows, got_a, got_b, first, padded):
    odd = where_ref[0] % 2
    row_a = jnp.where(odd == 1, O0 - FINE_HALO, O0 + OWN)
    row_b = jnp.where(odd == 1, O0 + OWN, O0 - FINE_HALO)

    def put_row(field, row, value):
        if padded:
            put(buffer, field, row, value)
        else:
            buffer[field, row] = value

    def own(row):
        start = pl.multiple_of(row * SUB, SUB)
        for field in range(FIELDS):
            put_row(field, O0 + row, own_rows[field, pl.ds(start, SUB), :])

    def halo(row):
        start = pl.multiple_of(row * SUB, SUB)
        for field in range(FIELDS):
            put_row(field, row_a + row, got_a[first + field, pl.ds(start, SUB), :])
            put_row(field, row_b + row, got_b[first + field, pl.ds(start, SUB), :])

    rows_loop(0, OWN, own)
    rows_loop(0, FINE_HALO, halo)


def down_kernel(fresh, *refs):
    if fresh:
        where_ref, state, force, got_a, got_b, tab0, tab1, v0, v1, s1, c1, send, f0, tmp0, tmp1, q1 = refs
    else:
        where_ref, state, got_a, got_b, f0, tab0, tab1, v0, v1, s1, c1, send, tmp0, tmp1, q1 = refs
    for ref in (v0, v1, c1, tmp0, tmp1):
        clear(ref)
    place_halo(where_ref, v0, state, got_a, got_b, 0, True)
    if fresh:
        place_halo(where_ref, f0, force, got_a, got_b, FIELDS, False)
    fine_source = lambda field, row: f0[field, row]
    low, high = O0 - FINE_HALO, O0 + OWN + FINE_HALO
    sweep(fine_source, v0, tmp0, tab0, 0, low + 1, high - 1)
    sweep(fine_source, tmp0, v0, tab0, 0, low + 2, high - 2)

    def to_first(row):
        coarse, rest = coarsen(fine_source, v0, tab0, 0, row)
        start = first_sweep(coarse, rest, tab1, row)
        for field in range(FIELDS):
            put(c1, field, row, coarse[field])
            q1[field, row] = rest[field]
            put(tmp1, field, row, start[field])

    half = OWN // 2
    rows_loop(O1 - 4, O1 + half + 4, to_first)
    make_source(c1, q1, s1, tab1, 1, O1 - 3, O1 + half + 3)
    first_source = lambda field, row: s1[field, row]
    sweep(first_source, tmp1, v1, tab1, 1, O1 - 3, O1 + half + 3)

    lane = lane_iota()

    def to_second(index):
        coarse, rest = coarsen(first_source, v1, tab1, 1, index + O1 // 2)
        group, place = index // GROUP, index % GROUP
        mine = (lane & (GROUP - 1)) == place
        for field in range(FIELDS):
            for which, value in ((field, coarse[field]), (FIELDS + field, rest[field])):
                send[group, which] = jnp.where(mine, value, send[group, which])

    clear(send)
    rows_loop(0, OWN // 4, to_second)


def spread(packed, place):
    lane = lane_iota()
    value = jnp.where((lane & (GROUP - 1)) == place, packed, 0.0)
    near = 1 if place % 2 == 0 else LANES - 1
    far = 2 if place < 2 else LANES - 2
    value = value + pltpu.roll(value, near, 1)
    return value + pltpu.roll(value, far, 1)


def up_kernel(last, *refs):
    if last:
        (where_ref, own, got_a, got_b, got_a2, v0, f0, v1, s1, c1, tab0, tab1, tab2, tab3, out,
         tmp0, work0, tmp1, work1, c2, q2, s2, v2, tmp2, c3, q3, s3, v3, tmp3) = refs
    else:
        (where_ref, own, got_a, got_b, got_a2, v0, f0, v1, s1, c1, tab0, tab1, tab2, tab3, out,
         send_a, send_b, tmp0, work0, tmp1, work1, c2, q2, s2, v2, tmp2, c3, q3, s3, v3, tmp3) = refs
    odd = where_ref[0] % 2
    for ref in (c2, v2, tmp2, c3, v3, tmp3, tmp0, tmp1):
        clear(ref)

    def unpack(source, index, group):
        for place in range(GROUP):
            row = group * GROUP + place
            coarse = [spread(source[index, f], place) for f in range(FIELDS)]
            rest = [spread(source[index, FIELDS + f], place) for f in range(FIELDS)]
            start = first_sweep(coarse, rest, tab2, row)
            for field in range(FIELDS):
                put(c2, field, row, coarse[field])
                q2[field, row] = rest[field]
                put(tmp2, field, row, start[field])

    pick = lambda a, b: jnp.where(odd == 1, b, a)
    rows_loop(0, 2, lambda i: unpack(own, i, 4 + i))
    rows_loop(0, 2, lambda i: unpack(got_a, i, pick(6, 2) + i))
    rows_loop(0, 3, lambda i: unpack(got_b, i, pick(1, 6) + i))
    rows_loop(0, 1, lambda i: unpack(got_a2, i, pick(8, 1) + i))

    quarter, eighth = OWN // 4, OWN // 8
    make_source(c2, q2, s2, tab2, 2, O2 - 11, O2 + quarter + 11)
    second_source = lambda field, row: s2[field, row]
    sweep(second_source, tmp2, v2, tab2, 2, O2 - 11, O2 + quarter + 11)

    def to_third(row):
        coarse, rest = coarsen(second_source, v2, tab2, 2, row)
        start = first_sweep(coarse, rest, tab3, row)
        for field in range(FIELDS):
            put(c3, field, row, coarse[field])
            q3[field, row] = rest[field]
            put(tmp3, field, row, start[field])

    rows_loop(O3 - 5, O3 + eighth + 5, to_third)
    make_source(c3, q3, s3, tab3, 3, O3 - 4, O3 + eighth + 4)
    third_source = lambda field, row: s3[field, row]
    sweep(third_source, tmp3, v3, tab3, 3, O3 - 4, O3 + eighth + 4)
    sweep(third_source, v3, tmp3, tab3, 3, O3 - 3, O3 + eighth + 3)
    sweep(third_source, tmp3, v3, tab3, 3, O3 - 2, O3 + eighth + 2)
    correct(v2, v3, c3, 0, O2 - 4, O2 + quarter + 4)
    sweep(second_source, v2, tmp2, tab2, 2, O2 - 3, O2 + quarter + 3)
    sweep(second_source, tmp2, v2, tab2, 2, O2 - 2, O2 + quarter + 2)

    half = OWN // 2
    work1[...] = v1[...]
    first_source = lambda field, row: s1[field, row]
    correct(work1, v2, c2, O2 - O1 // 2, O1 - 3, O1 + half + 3)
    sweep(first_source, work1, tmp1, tab1, 1, O1 - 2, O1 + half + 2)
    sweep(first_source, tmp1, work1, tab1, 1, O1 - 1, O1 + half + 1)

    work0[...] = v0[...]
    fine_source = lambda field, row: f0[field, row]
    correct(work0, work1, c1, 0, O0 - 2, O0 + OWN + 2)
    sweep(fine_source, work0, tmp0, tab0, 0, O0 - 1, O0 + OWN + 1)
    sweep(fine_source, tmp0, work0, tab0, 0, O0, O0 + OWN)

    if last:
        for field in range(FIELDS):
            for block in range(SUB):
                for start in range(0, OWN, SUB):
                    out[field, start : start + SUB, block * LANES : (block + 1) * LANES] = work0[
                        field, pl.ds(at(O0 + start) + block, SUB, stride=PAD), :
                    ]
        return

    def leave(row):
        start = pl.multiple_of(row * SUB, SUB)
        for field in range(FIELDS):
            out[field, pl.ds(start, SUB), :] = tile(work0, field, O0 + row)

    rows_loop(0, OWN, leave)
    from_a, from_b = pick(OWN - FINE_HALO, 0), pick(0, OWN - FINE_HALO)

    def edge(row):
        start = pl.multiple_of(row * SUB, SUB)
        for field in range(FIELDS):
            send_a[field, pl.ds(start, SUB), :] = tile(work0, field, O0 + from_a + row)
            send_b[field, pl.ds(start, SUB), :] = tile(work0, field, O0 + from_b + row)

    rows_loop(0, FINE_HALO, edge)


VMEM = pl.BlockSpec(memory_space=pltpu.VMEM)
SMEM = pl.BlockSpec(memory_space=pltpu.SMEM)


def f32(*shape):
    return jax.ShapeDtypeStruct(shape, jnp.float32)


def scratch(*shape):
    return pltpu.VMEM(shape, jnp.float32)


def padded(rows):
    return (FIELDS, padded_rows(rows), LANES)


def plain(rows):
    return (FIELDS, rows, SUB, LANES)


def call(kernel, name, outs, operands, scratches=()):
    return pl.pallas_call(
        kernel,
        out_shape=outs,
        in_specs=[SMEM] + [VMEM] * (len(operands) - 1),
        out_specs=[VMEM] * len(outs),
        scratch_shapes=list(scratches),
        name=name,
        compiler_params=pltpu.CompilerParams(vmem_limit_bytes=48 * 1024 * 1024),
    )(*operands)


def per_device(initial_state, forcing, coefficients, region_ids):
    size = lax.axis_size("axial")
    device = lax.axis_index("axial")
    assert initial_state.shape == (FIELDS, OWN, SUB * LANES)
    assert region_ids.shape == (OWN, SUB)
    where_ref = jnp.stack([device, jnp.int32(size)]).astype(jnp.int32)
    odd = device % 2
    pair_a = [(i, i ^ 1) for i in range(size)]
    pair_b = [(i, i + 1 if i % 2 else i - 1) for i in range(1, size - 1)]
    swap_a = lambda x: lax.ppermute(x, "axial", pair_a)
    swap_b = lambda x: lax.ppermute(x, "axial", pair_b)

    share = coefficients.shape[1]
    regions = share * size
    lanes = -(-regions // LANES) * LANES
    table = lax.dynamic_update_slice(
        jnp.zeros((32, lanes), jnp.float32),
        jnp.pad(coefficients, ((0, 32 - ENTRIES), (0, 0))),
        (0, device * share),
    )
    table = jnp.concatenate([table[:, i : i + LANES] for i in range(0, lanes, LANES)], axis=0)
    ids = lax.dynamic_update_slice(
        jnp.zeros((2 * size + 8, LANES), jnp.float32),
        region_ids.reshape(2, LANES).astype(jnp.float32),
        (2 * device + 4, 0),
    )
    gathered = jnp.concatenate([table, ids], axis=0)
    step = 1
    while step < size:
        swap = [(i, i ^ step) for i in range(size)]
        gathered = gathered + lax.ppermute(gathered, "axial", swap)
        step *= 2
    count = 32 * (lanes // LANES)
    table = jnp.concatenate([gathered[i : i + 32] for i in range(0, count, 32)], axis=1)
    near_ids = lax.dynamic_slice(gathered, (count + 2 * device, 0), (10, LANES))
    near_ids = jnp.pad(near_ids, ((0, 6), (0, 0)))

    state, force, send_a, send_b = call(
        split_kernel,
        "split",
        [f32(FIELDS, OWN * SUB, LANES)] * 2 + [f32(2 * FIELDS, FINE_HALO * SUB, LANES)] * 2,
        [where_ref, initial_state, forcing],
    )
    got_b, got_a = swap_b(send_b), swap_a(send_a)
    tables = call(
        tables_kernel,
        "tables",
        [f32(rows * SUB, LANES) for rows in (T0, T1, T2, T3)],
        [where_ref, table, near_ids],
        [scratch(32, 5 * 256), scratch(LANES, T0 * SUB)],
    )

    f0 = None
    for cycle in range(CYCLES):
        outs = [f32(*padded(T0)), f32(*padded(T1)), f32(*plain(T1)), f32(*padded(T1)),
                f32(2, 2 * FIELDS, SUB, LANES)]
        temps = [scratch(*padded(T0)), scratch(*padded(T1)), scratch(*plain(T1))]
        if cycle == 0:
            v0, v1, s1, c1, own, f0 = call(
                functools.partial(down_kernel, True), "down_fresh", outs + [f32(*plain(T0))],
                [where_ref, state, force, got_a, got_b, tables[0], tables[1]], temps,
            )
        else:
            v0, v1, s1, c1, own = call(
                functools.partial(down_kernel, False), "down", outs,
                [where_ref, state, got_a, got_b, f0, tables[0], tables[1]], temps,
            )
        beside = swap_a(own)
        row = jnp.concatenate([beside[1:], own, beside[:1]], axis=0)
        far = swap_b(lax.dynamic_slice_in_dim(row, 1 - odd, 3, axis=0))
        last_one = swap_a(lax.dynamic_slice_in_dim(far, 2 - 2 * odd, 1, axis=0))
        operands = [where_ref, own, beside, far, last_one, v0, f0, v1, s1, c1, *tables]
        temps = [scratch(*padded(T0))] * 2 + [scratch(*padded(T1))] * 2
        temps += [scratch(*padded(T2)), scratch(*plain(T2)), scratch(*plain(T2)), scratch(*padded(T2)), scratch(*padded(T2))]
        temps += [scratch(*padded(T3)), scratch(*plain(T3)), scratch(*plain(T3)), scratch(*padded(T3)), scratch(*padded(T3))]
        if cycle == CYCLES - 1:
            return call(
                functools.partial(up_kernel, True), "up_last",
                [f32(FIELDS, OWN, SUB * LANES)], operands, temps,
            )[0]
        state, send_a, send_b = call(
            functools.partial(up_kernel, False), "up",
            [f32(FIELDS, OWN * SUB, LANES)] + [f32(FIELDS, FINE_HALO * SUB, LANES)] * 2,
            operands, temps,
        )
        got_b, got_a = swap_b(send_b), swap_a(send_a)


def solution(mesh):
    placed = (
        P("sample", "axial", None),
        P("sample", "axial", None),
        P("sample", "axial"),
        P("axial", None),
    )
    return jax.shard_map(
        per_device,
        mesh=mesh,
        in_specs=placed,
        out_specs=P("sample", "axial", None),
        check_vma=False,
    )
```

time: 594 us -> 217 us (0.37)
  the two profiles are of different devices: /device:TPU:10 before, /device:TPU:17 now
where the time goes in v1:
time: 217 us; the launch traced here: 216 us
  Pallas kernels  147 us (68%)
  waiting for transfers between devices  39.2 us (18%)
  starting transfers between devices  15.7 us (7%)
  local copies, waits for them, and re-layouts  13.2 us (6%)
    pallas_call x6, Pallas kernels, call(): pl.pallas_call(kernel, out_shape=outs, in_specs=[SMEM] + [VMEM] * (len(op...  147 us
    ppermute x4, waiting for transfers between devices, per_device(): swap_b = lambda x: lax.ppermute(x, 'axial', pair_b)  18.5 us
    ppermute x4, waiting for transfers between devices, per_device(): gathered = gathered + lax.ppermute(gathered, 'axial', swap)  16.1 us
    unnamed x27, local copies, waits for them, and re-layouts  12.7 us
    ppermute x4, starting transfers between devices, per_device(): swap_b = lambda x: lax.ppermute(x, 'axial', pair_b)  9.46 us
    ppermute x6, waiting for transfers between devices, per_device(): swap_a = lambda x: lax.ppermute(x, 'axial', pair_a)  4.6 us
  transfers between devices with their start and end apart: 14, of which 10 were waited for; matrix products, arithmetic and copies ran while one was open for 0% of the time, Pallas kernels for 2%

profile of v1, /device:TPU:17, one launch (start us, length us, event | category | flops | bytes accessed | tf_op | source)
XLA Modules:
  0.0 215.8 jit_solution(16054445216487869909)
XLA Ops:
  0.9 0.8 copy.7
  2.9 1.1 copy-done.3
  4.0 1.1 copy-done.4
  5.0 1.6 split.1
  6.6 3.5 %collective-permute-start.1 = (f32[10,88,128]{2,1,0:T(8,128)S(1)}, f32[10,88,128]{2,1,0:T(8,128)S(1)}, u32[]{:S(2)}, u32[]{:S(2)}) collective-permute-start(f32[10,88,128]{2,1,0:T(8,128)S(1)} %get-tuple-element.30), channel_id=1, source_target_pairs={{1,2},{2,1},{3,4},{4,3},{5,6},{6,5},{7,8},{8,7},{9,10},{10,9},{11,... | collective-permute-start | bytes 1351688 | tf_op jit(solution)/shard_map/ppermute | solution.py:483
  10.2 1.3 collective-permute-start.3
  11.5 9.6 %collective-permute-done.3 = f32[72,128]{1,0:T(8,128)S(1)} collective-permute-done((f32[72,128]{1,0:T(8,128)S(1)}, f32[72,128]{1,0:T(8,128)S(1)}, u32[]{:S(2)}, u32[]{:S(2)}) %collective-permute-start.3) | collective-permute-done | bytes 36896 | tf_op jit(solution)/shard_map/ppermute | solution.py:503
  21.1 2.8 %collective-permute-done.4 = f32[72,128]{1,0:T(8,128)S(1)} collective-permute-done((f32[72,128]{1,0:T(8,128)S(1)}, f32[72,128]{1,0:T(8,128)S(1)}, u32[]{:S(2)}, u32[]{:S(2)}) %collective-permute-start.4) | collective-permute-done | bytes 36896 | tf_op jit(solution)/shard_map/ppermute | solution.py:503
  24.0 3.7 %collective-permute-done.5 = f32[72,128]{1,0:T(8,128)S(1)} collective-permute-done((f32[72,128]{1,0:T(8,128)S(1)}, f32[72,128]{1,0:T(8,128)S(1)}, u32[]{:S(2)}, u32[]{:S(2)}) %collective-permute-start.5) | collective-permute-done | bytes 36896 | tf_op jit(solution)/shard_map/ppermute | solution.py:503
  27.7 3.2 %tables.1 = (f32[512,128]{1,0:T(8,128)S(1)}, f32[256,128]{1,0:T(8,128)S(1)}, f32[320,128]{1,0:T(8,128)S(1)}, f32[160,128]{1,0:T(8,128)S(1)}) custom-call(s32[2]{0:T(128)S(1)} %pad_add_fusion.where_ref.refs_0_, f32[32,128]{1,0:T(8,128)S(1)} %slice.20.coeff_ref, f32[16,128]{1,0:T(8,128)S(1)} %pad.9.ids_ref), custom_call_target="tpu_custom_call" | custom-call | tf_op jit(solution)/shard_map/tables/pallas_call | solution.py:462
  33.0 1.0 copy-done.8
  34.1 1.0 copy-done.10
  35.1 30.4 %down_fresh.1 = (f32[5,600,128]{2,1,0:T(8,128)}, f32[5,312,128]{2,1,0:T(8,128)S(1)}, f32[5,32,8,128]{3,2,1,0:T(8,128)S(1)}, f32[5,312,128]{2,1,0:T(8,128)S(1)}, ...) custom-call(s32[2]{0:T(128)S(1)} %pad_add_fusion.where_ref.refs_0_, ...), custom_call_target="tpu_custom_call" | custom-call | tf_op jit(solution)/shard_map/down_fresh/pallas_call | solution.py:462
  65.5 0.8 copy-done.5
  66.3 3.9 %collective-permute-start.6 = (f32[2,10,8,128]{3,2,1,0:T(8,128)S(1)}, f32[2,10,8,128]{3,2,1,0:T(8,128)S(1)}, u32[]{:S(2)}, u32[]{:S(2)}) collective-permute-start(f32[2,10,8,128]{3,2,1,0:T(8,128)S(1)} %get-tuple-element.33.refs_1_), channel_id=1, source_target_pairs={{0,1},{1,0},{2,3},{3,2},{4,5},{5,4},{6,7},{7,6},{8,9},{9,8},{10,11... | collective-permute-start | bytes 245768 | tf_op jit(solution)/shard_map/ppermute | solution.py:482
  70.2 0.9 collective-permute-done.6.refs_2_
  71.2 1.9 collective-permute-start.7
  73.1 5.6 %collective-permute-done.7.refs_3_ = f32[3,10,8,128]{3,2,1,0:T(8,128)S(1)} collective-permute-done((f32[3,10,8,128]{3,2,1,0:T(8,128)S(1)}, f32[3,10,8,128]{3,2,1,0:T(8,128)S(1)}, u32[]{:S(2)}, u32[]{:S(2)}) %collective-permute-start.7) | collective-permute-done | bytes 122912 | tf_op jit(solution)/shard_map/ppermute | solution.py:483
  78.7 1.2 collective-permute-done.8.refs_4_
  79.9 1.3 copy-done
  81.2 1.1 copy-done.6
  82.3 0.9 copy-done.12
  83.2 41.0 %up.1 = (f32[5,256,128]{2,1,0:T(8,128)S(1)}, f32[5,88,128]{2,1,0:T(8,128)S(1)}, f32[5,88,128]{2,1,0:T(8,128)S(1)}) custom-call(s32[2]{0:T(128)S(1)} %pad_add_fusion.where_ref.refs_0_, f32[2,10,8,128]{3,2,1,0:T(8,128)S(1)} %get-tuple-element.33.refs_1_, f32[2,10,8,128]{3,2,1,0:T(8,128)S(1)} %collective-permute-done.6.refs_2_, ...), custom_call_target="tpu_custom_call" | custom-call | tf_op jit(solution)/shard_map/up/pallas_call | solution.py:462
  124.2 1.9 collective-permute-start.10
  126.3 7.6 %collective-permute-done.10.refs_3_ = f32[5,88,128]{2,1,0:T(8,128)S(1)} collective-permute-done((f32[5,88,128]{2,1,0:T(8,128)S(1)}, f32[5,88,128]{2,1,0:T(8,128)S(1)}, u32[]{:S(2)}, u32[]{:S(2)}) %collective-permute-start.10) | collective-permute-done | bytes 225312 | tf_op jit(solution)/shard_map/ppermute | solution.py:483
  133.9 29.8 %down.1 = (f32[5,600,128]{2,1,0:T(8,128)}, f32[5,312,128]{2,1,0:T(8,128)S(1)}, f32[5,32,8,128]{3,2,1,0:T(8,128)S(1)}, f32[5,312,128]{2,1,0:T(8,128)S(1)}, f32[2,10,8,128]{3,2,1,0:T(8,128)S(1)}) custom-call(s32[2]{0:T(128)S(1)} %pad_add_fusion.where_ref.refs_0_, f32[5,256,128]{2,1,0:T(8,128)S(1)} %get-tuple-element.41.refs_1_, ...), custom_call_target="tpu_custom_call" | custom-call | tf_op jit(solution)/shard_map/down/pallas_call | solution.py:462
  163.7 1.3 collective-permute-done.11.refs_2_
  165.0 2.1 collective-permute-start.12
  167.1 5.4 %collective-permute-done.12.refs_3_ = f32[3,10,8,128]{3,2,1,0:T(8,128)S(1)} collective-permute-done((f32[3,10,8,128]{3,2,1,0:T(8,128)S(1)}, f32[3,10,8,128]{3,2,1,0:T(8,128)S(1)}, u32[]{:S(2)}, u32[]{:S(2)}) %collective-permute-start.12) | collective-permute-done | bytes 122912 | tf_op jit(solution)/shard_map/ppermute | solution.py:483
  172.6 1.2 collective-permute-done.13.refs_4_
  173.8 1.4 copy-done.2
  175.2 40.6 %up_last.1 = f32[5,32,1024]{2,1,0:T(8,128)} custom-call(s32[2]{0:T(128)S(1)} %pad_add_fusion.where_ref.refs_0_, f32[2,10,8,128]{3,2,1,0:T(8,128)S(1)} %get-tuple-element.44.refs_1_, f32[2,10,8,128]{3,2,1,0:T(8,128)S(1)} %collective-permute-done.11.refs_2_, f32[3,10,8,128]{3,2,1,0:T(8,128)S(1)} %collective-permute-done.12.refs_3_, ...), custom_call_target="tpu_custom_call" | custom-call | tf_op jit(solution)/shard_map/up_last/pallas_call | solution.py:462
  (52 shorter events, 4.7 us)
Async XLA Ops:
  2.0 8.1 %collective-permute-start.2 = (f32[72,128]{1,0:T(8,128)S(1)}, f32[72,128]{1,0:T(8,128)S(1)}, u32[]{:S(2)}, u32[]{:S(2)}) collective-permute-start(f32[72,128]{1,0:T(8,128)S(1)} %pad_maximum_fusion), channel_id=1, source_target_pairs={{0,1},{1,0},{2,3},{3,2},{4,5},{5,4},{6,7},{7,6},{8,9},{9,8},{10,11... | collective-permute-start | bytes 110600 | tf_op jit(solution)/shard_map/ppermute | solution.py:503
  2.9 1.1 copy-start.3
  4.0 1.1 copy-start.4
  6.6 24.9 %collective-permute-start = (f32[10,88,128]{2,1,0:T(8,128)}, f32[10,88,128]{2,1,0:T(8,128)S(1)}, u32[]{:S(2)}, u32[]{:S(2)}) collective-permute-start(f32[10,88,128]{2,1,0:T(8,128)} %get-tuple-element.29), channel_id=1, source_target_pairs={{0,1},{1,0},{2,3},{3,2},{4,5},{5,4},{6,7},{7,6},{8,9},{9,8},{10,11... | collective-permute-start | bytes 1351688 | tf_op jit(solution)/shard_map/ppermute | solution.py:482
  6.6 25.6 %collective-permute-start.1 = (f32[10,88,128]{2,1,0:T(8,128)S(1)}, f32[10,88,128]{2,1,0:T(8,128)S(1)}, u32[]{:S(2)}, u32[]{:S(2)}) collective-permute-start(f32[10,88,128]{2,1,0:T(8,128)S(1)} %get-tuple-element.30), channel_id=1, source_target_pairs={{1,2},{2,1},{3,4},{4,3},{5,6},{6,5},{7,8},{8,7},{9,10},{10,9},{11,... | collective-permute-start | bytes 1351688 | tf_op jit(solution)/shard_map/ppermute | solution.py:483
  10.2 10.9 %collective-permute-start.3 = (f32[72,128]{1,0:T(8,128)S(1)}, f32[72,128]{1,0:T(8,128)S(1)}, u32[]{:S(2)}, u32[]{:S(2)}) collective-permute-start(f32[72,128]{1,0:T(8,128)S(1)} %fusion.4), channel_id=1, source_target_pairs={{0,2},{1,3},{2,0},{3,1},{4,6},{5,7},{6,4},{7,5},{8,10},{9,11},{10,... | collective-permute-start | bytes 110600 | tf_op jit(solution)/shard_map/ppermute | solution.py:503
  21.1 2.8 %collective-permute-start.4 = (f32[72,128]{1,0:T(8,128)S(1)}, f32[72,128]{1,0:T(8,128)S(1)}, u32[]{:S(2)}, u32[]{:S(2)}) collective-permute-start(f32[72,128]{1,0:T(8,128)S(1)} %add.50), channel_id=1, source_target_pairs={{0,4},{1,5},{2,6},{3,7},{4,0},{5,1},{6,2},{7,3},{8,12},{9,13},{10,... | collective-permute-start | bytes 110600 | tf_op jit(solution)/shard_map/ppermute | solution.py:503
  23.9 3.7 %collective-permute-start.5 = (f32[72,128]{1,0:T(8,128)S(1)}, f32[72,128]{1,0:T(8,128)S(1)}, u32[]{:S(2)}, u32[]{:S(2)}) collective-permute-start(f32[72,128]{1,0:T(8,128)S(1)} %add.51), channel_id=1, source_target_pairs={{0,8},{1,9},{2,10},{3,11},{4,12},{5,13},{6,14},{7,15},{8,0},{9,1},... | collective-permute-start | bytes 110600 | tf_op jit(solution)/shard_map/ppermute | solution.py:503
  30.9 0.6 copy-start.11
  31.5 0.8 copy-start.7
  32.3 0.8 copy-start.9
  33.0 1.0 copy-start.8
  34.1 1.0 copy-start.10
  65.5 0.8 copy-start.5
  66.3 4.8 %collective-permute-start.6 = (f32[2,10,8,128]{3,2,1,0:T(8,128)S(1)}, f32[2,10,8,128]{3,2,1,0:T(8,128)S(1)}, u32[]{:S(2)}, u32[]{:S(2)}) collective-permute-start(f32[2,10,8,128]{3,2,1,0:T(8,128)S(1)} %get-tuple-element.33.refs_1_), channel_id=1, source_target_pairs={{0,1},{1,0},{2,3},{3,2},{4,5},{5,4},{6,7},{7,6},{8,9},{9,8},{10,11... | collective-permute-start | bytes 245768 | tf_op jit(solution)/shard_map/ppermute | solution.py:482
  71.2 7.5 %collective-permute-start.7 = (f32[3,10,8,128]{3,2,1,0:T(8,128)S(1)}, f32[3,10,8,128]{3,2,1,0:T(8,128)S(1)}, u32[]{:S(2)}, u32[]{:S(2)}) collective-permute-start(f32[3,10,8,128]{3,2,1,0:T(8,128)S(1)} %fusion.3), channel_id=1, source_target_pairs={{1,2},{2,1},{3,4},{4,3},{5,6},{6,5},{7,8},{8,7},{9,10},{10,9},{11,... | collective-permute-start | bytes 368648 | tf_op jit(solution)/shard_map/ppermute | solution.py:483
  78.7 1.2 collective-permute-start.8
  79.9 1.3 copy-start
  81.2 1.1 copy-start.6
  82.3 0.9 copy-start.12
  83.2 50.7 %copy-start.1 = (f32[5,64,8,128]{3,2,1,0:T(8,128)S(1)}, f32[5,64,8,128]{3,2,1,0:T(8,128)}, u32[]{:S(2)}) copy-start(f32[5,64,8,128]{3,2,1,0:T(8,128)} %get-tuple-element.35.refs_6_.refs_4_) | copy-start | bytes 3932164
  124.2 9.7 %collective-permute-start.10 = (f32[5,88,128]{2,1,0:T(8,128)S(1)}, f32[5,88,128]{2,1,0:T(8,128)S(1)}, u32[]{:S(2)}, u32[]{:S(2)}) collective-permute-start(f32[5,88,128]{2,1,0:T(8,128)S(1)} %get-tuple-element.43), channel_id=1, source_target_pairs={{1,2},{2,1},{3,4},{4,3},{5,6},{6,5},{7,8},{8,7},{9,10},{10,9},{11,... | collective-permute-start | bytes 675848 | tf_op jit(solution)/shard_map/ppermute | solution.py:483
  126.1 7.8 %collective-permute-start.9 = (f32[5,88,128]{2,1,0:T(8,128)S(1)}, f32[5,88,128]{2,1,0:T(8,128)S(1)}, u32[]{:S(2)}, u32[]{:S(2)}) collective-permute-start(f32[5,88,128]{2,1,0:T(8,128)S(1)} %get-tuple-element.42), channel_id=1, source_target_pairs={{0,1},{1,0},{2,3},{3,2},{4,5},{5,4},{6,7},{7,6},{8,9},{9,8},{10,11... | collective-permute-start | bytes 675848 | tf_op jit(solution)/shard_map/ppermute | solution.py:482
  163.7 1.3 collective-permute-start.11
  165.0 7.5 %collective-permute-start.12 = (f32[3,10,8,128]{3,2,1,0:T(8,128)S(1)}, f32[3,10,8,128]{3,2,1,0:T(8,128)S(1)}, u32[]{:S(2)}, u32[]{:S(2)}) collective-permute-start(f32[3,10,8,128]{3,2,1,0:T(8,128)S(1)} %fusion.1), channel_id=1, source_target_pairs={{1,2},{2,1},{3,4},{4,3},{5,6},{6,5},{7,8},{8,7},{9,10},{10,9},{11,... | collective-permute-start | bytes 368648 | tf_op jit(solution)/shard_map/ppermute | solution.py:483
  172.6 1.2 collective-permute-start.13
  173.8 1.4 copy-start.2

commit v2 on v1

--- a/solution.py
+++ b/solution.py
@@ -18,33 +18,45 @@
 
 OWN = 32
 FINE_HALO = 11
-PAD = 9
-HEAD = 8
 T0, O0 = 64, 16
 T1, O1 = 32, 8
 T2, O2 = 40, 16
 T3, O3 = 20, 8
 GROUP = 4
-
-
-def padded_rows(rows):
-    return HEAD + PAD * rows + 16
-
-
-def at(row):
-    return HEAD + PAD * row
+SPREAD = 16
+
+
+def stride_of(level):
+    return SUB + 2 * 2**level
+
+
+def padded_rows(rows, level):
+    return -(-stride_of(level) * rows // SUB) * SUB
+
+
+def at(row, level):
+    return stride_of(level) * row + 2**level
 
 
 def lane_iota():
     return lax.broadcasted_iota(jnp.int32, (SUB, LANES), 1)
 
 
-def tile(ref, field, row):
-    return ref[field, pl.ds(at(row), SUB), :]
-
-
-def put(ref, field, row, value):
-    ref[field, pl.ds(at(row), SUB), :] = value
+def sub_iota():
+    return lax.broadcasted_iota(jnp.int32, (SUB, LANES), 0)
+
+
+def tile(ref, field, row, level):
+    return ref[field, pl.ds(at(row, level), SUB), :]
+
+
+def put(ref, field, row, level, value):
+    start, width, lane = at(row, level), 2**level, lane_iota()
+    before = jnp.where(lane == 0, 0.0, pltpu.roll(value, 1, 1))
+    after = jnp.where(lane == LANES - 1, 0.0, pltpu.roll(value, LANES - 1, 1))
+    ref[field, pl.ds(start, SUB), :] = value
+    ref[field, pl.ds(start - width, width), :] = before[SUB - width :]
+    ref[field, pl.ds(start + SUB, width), :] = after[:width]
 
 
 def rows_loop(first, last, body):
@@ -55,40 +67,41 @@
     lax.fori_loop(first, last, step, 0)
 
 
+def batches(first, last, batch, compute, store):
+    def body(index):
+        rows = [first + index * batch + i for i in range(batch)]
+        results = [compute(row) for row in rows]
+        for row, result in zip(rows, results):
+            store(row, result)
+
+    rows_loop(0, -(-(last - first) // batch), body)
+
+
 def neighbours(ref, row, level):
-    width = 2**level
-    lane = lane_iota()
+    start, width, stride = at(row, level), 2**level, stride_of(level)
     sums, centres = [], []
     for field in range(FIELDS):
-        start = at(row)
-        centre = ref[field, pl.ds(start, SUB), :]
-        lower = ref[field, pl.ds(start - 1, SUB), :]
-        upper = ref[field, pl.ds(start + 1, SUB), :]
-        left = pltpu.roll(jnp.where(lane >= LANES - width, lower, centre), width, 1)
-        right = pltpu.roll(jnp.where(lane < width, upper, centre), LANES - width, 1)
-        axial = ref[field, pl.ds(start - PAD, SUB), :] + ref[field, pl.ds(start + PAD, SUB), :]
-        sums.append((left + right) + axial)
-        centres.append(centre)
+        load = lambda first: ref[field, pl.ds(first, SUB), :]
+        radial = load(start - width) + load(start + width)
+        sums.append(radial + (load(start - stride) + load(start + stride)))
+        centres.append(load(start))
     return sums, centres
 
 
-def table_tile(table, row):
-    return table[pl.ds(pl.multiple_of(row * SUB, SUB), SUB), :]
-
-
-def block_times(entries, first, vectors):
+def block_times(table, row, first, vectors):
     out = []
-    for row in range(FIELDS):
+    for i in range(FIELDS):
         total = None
-        for column in range(FIELDS):
-            lane = first + FIELDS * row + column
-            term = jnp.broadcast_to(entries[:, lane : lane + 1], (SUB, LANES)) * vectors[column]
+        for j in range(FIELDS):
+            entry = first + FIELDS * i + j
+            term = jnp.broadcast_to(table[row, entry : entry + 1, :], (SUB, LANES)) * vectors[j]
             total = term if total is None else total + term
         out.append(total)
     return out
 
 
-MATRIX_LANE = 32
+MATRIX_AT = 32
+ENTRY_ROWS = 64
 
 
 def gain_of(level):
@@ -98,23 +111,26 @@
 def sweep(source_of, old, new, table, level, first, last):
     gain = gain_of(level)
 
-    def body(row):
+    def compute(row):
         sums, centres = neighbours(old, row, level)
         rest = [
             (source_of(field, row) + sums[field]) - gain * jnp.tanh(centres[field])
             for field in range(FIELDS)
         ]
-        moved = block_times(table_tile(table, row), 0, rest)
-        for field in range(FIELDS):
-            put(new, field, row, (1.0 - RELAXATION) * centres[field] + moved[field])
-
-    rows_loop(first, last, body)
+        moved = block_times(table, row, 0, rest)
+        return [(1.0 - RELAXATION) * centres[f] + moved[f] for f in range(FIELDS)]
+
+    def store(row, values):
+        for field in range(FIELDS):
+            put(new, field, row, level, values[field])
+
+    batches(first, last, SWEEP_BATCH, compute, store)
 
 
 def residual(source_of, values, table, level, row):
     gain = gain_of(level)
     sums, centres = neighbours(values, row, level)
-    applied = block_times(table_tile(table, row), MATRIX_LANE, centres)
+    applied = block_times(table, row, MATRIX_AT, centres)
     left = [
         ((source_of(field, row) + sums[field]) - gain * jnp.tanh(centres[field])) - applied[field]
         for field in range(FIELDS)
@@ -124,10 +140,9 @@
 
 def pair_sum(value, level):
     width = 2**level
-    lane = lane_iota()
-    other = jnp.where(
-        (lane & width) == 0, pltpu.roll(value, LANES - width, 1), pltpu.roll(value, width, 1)
-    )
+    other = pltpu.roll(value, SUB - width, 0)
+    if 2 * width != SUB:
+        other = jnp.where((sub_iota() & width) == 0, other, pltpu.roll(value, width, 0))
     return value + other
 
 
@@ -140,36 +155,56 @@
 
 
 def first_sweep(coarse, rest, table, row):
-    moved = block_times(table_tile(table, row), 0, rest)
+    moved = block_times(table, row, 0, rest)
     return [coarse[f] + moved[f] for f in range(FIELDS)]
+
+
+def descend(source_of, values, table, level, c, q, first_values, coarse_table, first, last):
+    def compute(row):
+        coarse, rest = coarsen(source_of, values, table, level, row)
+        return coarse, rest, first_sweep(coarse, rest, coarse_table, row)
+
+    def store(row, results):
+        for field in range(FIELDS):
+            put(c, field, row, level + 1, results[0][field])
+            q[field, row] = results[1][field]
+            put(first_values, field, row, level + 1, results[2][field])
+
+    batches(first, last, COARSEN_BATCH, compute, store)
 
 
 def make_source(coarse, rest, source, table, level, first, last):
     gain = gain_of(level)
 
-    def body(row):
+    def compute(row):
         sums, centres = neighbours(coarse, row, level)
-        applied = block_times(table_tile(table, row), MATRIX_LANE, centres)
-        for field in range(FIELDS):
-            source[field, row] = (applied[field] - sums[field]) + (
-                gain * jnp.tanh(centres[field]) + rest[field, row]
-            )
-
-    rows_loop(first, last, body)
-
-
-def correct(fine, after, before, offset, first, last):
-    def body(row):
-        coarse_row = row // 2 + offset
-        for field in range(FIELDS):
-            change = tile(after, field, coarse_row) - tile(before, field, coarse_row)
-            put(fine, field, row, tile(fine, field, row) + change)
-
-    rows_loop(first, last, body)
-
-
-def clear(ref):
-    ref[...] = jnp.zeros_like(ref)
+        applied = block_times(table, row, MATRIX_AT, centres)
+        return [
+            (applied[f] - sums[f]) + (gain * jnp.tanh(centres[f]) + rest[f, row])
+            for f in range(FIELDS)
+        ]
+
+    def store(row, values):
+        for field in range(FIELDS):
+            source[field, row] = values[field]
+
+    batches(first, last, SWEEP_BATCH, compute, store)
+
+
+def correct(new, fine, after, before, level, offset, first, last):
+    def body(index):
+        coarse_row = first // 2 + index + offset
+        row = first // 2 * 2 + 2 * index
+        for field in range(FIELDS):
+            change = tile(after, field, coarse_row, level + 1) - tile(before, field, coarse_row, level + 1)
+            put(new, field, row, level, tile(fine, field, row, level) + change)
+            put(new, field, row + 1, level, tile(fine, field, row + 1, level) + change)
+
+    rows_loop(0, (last + 1) // 2 - first // 2, body)
+
+
+SWEEP_BATCH = 4
+COARSEN_BATCH = 2
 
 
 def tables_kernel(where_ref, coeff_ref, ids_ref, tab0, tab1, tab2, tab3, mats, full):
@@ -200,7 +235,7 @@
         own = OWN >> level
         whole = (row - own_first) + device * own
         inside = (whole >= 0) & (whole < devices * own)
-        full[:, :lanes] = jnp.zeros((LANES, lanes), jnp.float32)
+        full[:, :lanes] = jnp.zeros((ENTRY_ROWS, lanes), jnp.float32)
         full[0:32, :lanes] = matrix
         entry = lambda e: jnp.broadcast_to(full[e : e + 1, :lanes], (SUB, lanes))
         block = [[entry(FIELDS * i + j) for j in range(FIELDS)] for i in range(FIELDS)]
@@ -208,7 +243,7 @@
             block[i][i] = block[i][i] + 4.0 * weight
         for i in range(FIELDS):
             for j in range(FIELDS):
-                e = MATRIX_LANE + FIELDS * i + j
+                e = MATRIX_AT + FIELDS * i + j
                 full[e : e + 1, :lanes] = (block[i][j] * (1.0 / weight))[0:1]
         right = [[None] * FIELDS for _ in range(FIELDS)]
         for i in range(FIELDS):
@@ -235,11 +270,25 @@
                 e = FIELDS * i + j
                 scaled = jnp.where(inside, right[i][j] * (RELAXATION * weight), 0.0)
                 full[e : e + 1, :lanes] = scaled[0:1]
-        padded_lanes = -(-lanes // LANES) * LANES
-        for start in range(0, padded_lanes, LANES):
-            count = min(LANES, lanes - start)
-            turned = jnp.transpose(full[:, start : start + LANES])
-            out[start : start + count, :] = turned[:count]
+        block_of = lax.broadcasted_iota(jnp.int32, (SUB, LANES), 1) // SPREAD
+
+        def widen(place):
+            lane_of = place * SUB + block_of
+            for start in range(0, rows, LANES // SUB):
+
+                def one():
+                    chunk = start * SUB
+                    for entry in range(0, ENTRY_ROWS, SUB):
+                        out[start + place, entry : entry + SUB, :] = jnp.take_along_axis(
+                            full[entry : entry + SUB, chunk : chunk + LANES], lane_of, axis=1
+                        )
+
+                if start + LANES // SUB <= rows:
+                    one()
+                else:
+                    pl.when(start + place < rows)(one)
+
+        rows_loop(0, LANES // SUB, widen)
 
     fine = mats[:, 6 * SUB * 8 : (6 * 8 + T0) * SUB]
     build(fine, 0, T0, O0, tab0)
@@ -249,17 +298,41 @@
     build(averaged(3 * LANES, 2 * LANES, 2, second)[:, : T3 * SUB], 3, T3, O3, tab3)
 
 
+def turn(inward):
+    into = lax.broadcasted_iota(jnp.int32, (LANES, LANES), 0 if inward else 1)
+    out = lax.broadcasted_iota(jnp.int32, (LANES, LANES), 1 if inward else 0)
+    return ((into % SUB) * SPREAD + into // SUB == out).astype(jnp.float32)
+
+
+def swap_chunks(tiles):
+    chunk = lax.broadcasted_iota(jnp.int32, tiles[0].shape, 1) // SPREAD
+    tiles = list(tiles)
+    for bit in (1, 2, 4):
+        shift = bit * SPREAD
+        for i in range(SUB):
+            if i & bit:
+                continue
+            low, high = tiles[i], tiles[i | bit]
+            keep = (chunk & bit) == 0
+            tiles[i] = jnp.where(keep, low, pltpu.roll(high, shift, 1))
+            tiles[i | bit] = jnp.where(keep, pltpu.roll(low, LANES - shift, 1), high)
+    return tiles
+
+
+def reordered(value, matrix):
+    return jnp.dot(value, matrix, precision=lax.Precision.HIGHEST, preferred_element_type=jnp.float32)
+
+
 def split_kernel(where_ref, state_ref, forcing_ref, state_rows, forcing_rows, send_a, send_b):
     odd = where_ref[0] % 2
-    for which, (source, target) in enumerate(
-        ((state_ref, state_rows), (forcing_ref, forcing_rows))
-    ):
-        for field in range(FIELDS):
-            for block in range(SUB):
-                for start in range(0, OWN, SUB):
-                    target[field, pl.ds(start * SUB + block, SUB, stride=SUB), :] = source[
-                        field, start : start + SUB, block * LANES : (block + 1) * LANES
-                    ]
+    matrix = turn(True)
+    for source, target in ((state_ref, state_rows), (forcing_ref, forcing_rows)):
+        for field in range(FIELDS):
+            blocks = [
+                reordered(source[field, :, b * LANES : (b + 1) * LANES], matrix) for b in range(SUB)
+            ]
+            for sub, value in enumerate(swap_chunks(blocks)):
+                target[field, pl.ds(sub, OWN, stride=SUB), :] = value
     low, high = 0, (OWN - FINE_HALO) * SUB
     size = FINE_HALO * SUB
     for which, rows in enumerate((state_rows, forcing_rows)):
@@ -277,7 +350,7 @@
 
     def put_row(field, row, value):
         if padded:
-            put(buffer, field, row, value)
+            put(buffer, field, row, 0, value)
         else:
             buffer[field, row] = value
 
@@ -301,8 +374,6 @@
         where_ref, state, force, got_a, got_b, tab0, tab1, v0, v1, s1, c1, send, f0, tmp0, tmp1, q1 = refs
     else:
         where_ref, state, got_a, got_b, f0, tab0, tab1, v0, v1, s1, c1, send, tmp0, tmp1, q1 = refs
-    for ref in (v0, v1, c1, tmp0, tmp1):
-        clear(ref)
     place_halo(where_ref, v0, state, got_a, got_b, 0, True)
     if fresh:
         place_halo(where_ref, f0, force, got_a, got_b, FIELDS, False)
@@ -311,41 +382,31 @@
     sweep(fine_source, v0, tmp0, tab0, 0, low + 1, high - 1)
     sweep(fine_source, tmp0, v0, tab0, 0, low + 2, high - 2)
 
-    def to_first(row):
-        coarse, rest = coarsen(fine_source, v0, tab0, 0, row)
-        start = first_sweep(coarse, rest, tab1, row)
-        for field in range(FIELDS):
-            put(c1, field, row, coarse[field])
-            q1[field, row] = rest[field]
-            put(tmp1, field, row, start[field])
-
     half = OWN // 2
-    rows_loop(O1 - 4, O1 + half + 4, to_first)
+    descend(fine_source, v0, tab0, 0, c1, q1, tmp1, tab1, O1 - 4, O1 + half + 4)
     make_source(c1, q1, s1, tab1, 1, O1 - 3, O1 + half + 3)
     first_source = lambda field, row: s1[field, row]
     sweep(first_source, tmp1, v1, tab1, 1, O1 - 3, O1 + half + 3)
 
-    lane = lane_iota()
+    sub = sub_iota()
 
     def to_second(index):
         coarse, rest = coarsen(first_source, v1, tab1, 1, index + O1 // 2)
+        return coarse + rest
+
+    def pack(index, values):
         group, place = index // GROUP, index % GROUP
-        mine = (lane & (GROUP - 1)) == place
-        for field in range(FIELDS):
-            for which, value in ((field, coarse[field]), (FIELDS + field, rest[field])):
-                send[group, which] = jnp.where(mine, value, send[group, which])
-
-    clear(send)
-    rows_loop(0, OWN // 4, to_second)
-
-
-def spread(packed, place):
-    lane = lane_iota()
-    value = jnp.where((lane & (GROUP - 1)) == place, packed, 0.0)
-    near = 1 if place % 2 == 0 else LANES - 1
-    far = 2 if place < 2 else LANES - 2
-    value = value + pltpu.roll(value, near, 1)
-    return value + pltpu.roll(value, far, 1)
+        mine = (sub & (GROUP - 1)) == place
+        for which in range(2 * FIELDS):
+            send[group, which] = jnp.where(mine, values[which], send[group, which])
+
+    send[...] = jnp.zeros_like(send)
+    batches(0, OWN // 4, COARSEN_BATCH, to_second, pack)
+
+
+def spread(source, index, which, place):
+    take = lambda sub: jnp.broadcast_to(source[index, which, sub : sub + 1, :], (SUB, LANES))
+    return jnp.where(sub_iota() < GROUP, take(place), take(GROUP + place))
 
 
 def up_kernel(last, *refs):
@@ -356,19 +417,17 @@
         (where_ref, own, got_a, got_b, got_a2, v0, f0, v1, s1, c1, tab0, tab1, tab2, tab3, out,
          send_a, send_b, tmp0, work0, tmp1, work1, c2, q2, s2, v2, tmp2, c3, q3, s3, v3, tmp3) = refs
     odd = where_ref[0] % 2
-    for ref in (c2, v2, tmp2, c3, v3, tmp3, tmp0, tmp1):
-        clear(ref)
 
     def unpack(source, index, group):
         for place in range(GROUP):
             row = group * GROUP + place
-            coarse = [spread(source[index, f], place) for f in range(FIELDS)]
-            rest = [spread(source[index, FIELDS + f], place) for f in range(FIELDS)]
+            coarse = [spread(source, index, f, place) for f in range(FIELDS)]
+            rest = [spread(source, index, FIELDS + f, place) for f in range(FIELDS)]
             start = first_sweep(coarse, rest, tab2, row)
             for field in range(FIELDS):
-                put(c2, field, row, coarse[field])
+                put(c2, field, row, 2, coarse[field])
                 q2[field, row] = rest[field]
-                put(tmp2, field, row, start[field])
+                put(tmp2, field, row, 2, start[field])
 
     pick = lambda a, b: jnp.where(odd == 1, b, a)
     rows_loop(0, 2, lambda i: unpack(own, i, 4 + i))
@@ -381,50 +440,41 @@
     second_source = lambda field, row: s2[field, row]
     sweep(second_source, tmp2, v2, tab2, 2, O2 - 11, O2 + quarter + 11)
 
-    def to_third(row):
-        coarse, rest = coarsen(second_source, v2, tab2, 2, row)
-        start = first_sweep(coarse, rest, tab3, row)
-        for field in range(FIELDS):
-            put(c3, field, row, coarse[field])
-            q3[field, row] = rest[field]
-            put(tmp3, field, row, start[field])
-
-    rows_loop(O3 - 5, O3 + eighth + 5, to_third)
+    descend(second_source, v2, tab2, 2, c3, q3, tmp3, tab3, O3 - 5, O3 + eighth + 5)
     make_source(c3, q3, s3, tab3, 3, O3 - 4, O3 + eighth + 4)
     third_source = lambda field, row: s3[field, row]
     sweep(third_source, tmp3, v3, tab3, 3, O3 - 4, O3 + eighth + 4)
     sweep(third_source, v3, tmp3, tab3, 3, O3 - 3, O3 + eighth + 3)
     sweep(third_source, tmp3, v3, tab3, 3, O3 - 2, O3 + eighth + 2)
-    correct(v2, v3, c3, 0, O2 - 4, O2 + quarter + 4)
+    correct(v2, v2, v3, c3, 2, 0, O2 - 4, O2 + quarter + 4)
     sweep(second_source, v2, tmp2, tab2, 2, O2 - 3, O2 + quarter + 3)
     sweep(second_source, tmp2, v2, tab2, 2, O2 - 2, O2 + quarter + 2)
 
     half = OWN // 2
-    work1[...] = v1[...]
     first_source = lambda field, row: s1[field, row]
-    correct(work1, v2, c2, O2 - O1 // 2, O1 - 3, O1 + half + 3)
+    correct(work1, v1, v2, c2, 1, O2 - O1 // 2, O1 - 3, O1 + half + 3)
     sweep(first_source, work1, tmp1, tab1, 1, O1 - 2, O1 + half + 2)
     sweep(first_source, tmp1, work1, tab1, 1, O1 - 1, O1 + half + 1)
 
-    work0[...] = v0[...]
     fine_source = lambda field, row: f0[field, row]
-    correct(work0, work1, c1, 0, O0 - 2, O0 + OWN + 2)
+    correct(work0, v0, work1, c1, 0, 0, O0 - 2, O0 + OWN + 2)
     sweep(fine_source, work0, tmp0, tab0, 0, O0 - 1, O0 + OWN + 1)
     sweep(fine_source, tmp0, work0, tab0, 0, O0, O0 + OWN)
 
     if last:
-        for field in range(FIELDS):
-            for block in range(SUB):
-                for start in range(0, OWN, SUB):
-                    out[field, start : start + SUB, block * LANES : (block + 1) * LANES] = work0[
-                        field, pl.ds(at(O0 + start) + block, SUB, stride=PAD), :
-                    ]
+        matrix = turn(False)
+        for field in range(FIELDS):
+            tiles = [
+                work0[field, pl.ds(at(O0, 0) + sub, OWN, stride=stride_of(0)), :] for sub in range(SUB)
+            ]
+            for block, value in enumerate(swap_chunks(tiles)):
+                out[field, :, block * LANES : (block + 1) * LANES] = reordered(value, matrix)
         return
 
     def leave(row):
         start = pl.multiple_of(row * SUB, SUB)
         for field in range(FIELDS):
-            out[field, pl.ds(start, SUB), :] = tile(work0, field, O0 + row)
+            out[field, pl.ds(start, SUB), :] = tile(work0, field, O0 + row, 0)
 
     rows_loop(0, OWN, leave)
     from_a, from_b = pick(OWN - FINE_HALO, 0), pick(0, OWN - FINE_HALO)
@@ -432,8 +482,8 @@
     def edge(row):
         start = pl.multiple_of(row * SUB, SUB)
         for field in range(FIELDS):
-            send_a[field, pl.ds(start, SUB), :] = tile(work0, field, O0 + from_a + row)
-            send_b[field, pl.ds(start, SUB), :] = tile(work0, field, O0 + from_b + row)
+            send_a[field, pl.ds(start, SUB), :] = tile(work0, field, O0 + from_a + row, 0)
+            send_b[field, pl.ds(start, SUB), :] = tile(work0, field, O0 + from_b + row, 0)
 
     rows_loop(0, FINE_HALO, edge)
 
@@ -450,8 +500,8 @@
     return pltpu.VMEM(shape, jnp.float32)
 
 
-def padded(rows):
-    return (FIELDS, padded_rows(rows), LANES)
+def padded(rows, level):
+    return (FIELDS, padded_rows(rows, level), LANES)
 
 
 def plain(rows):
@@ -517,16 +567,16 @@
     tables = call(
         tables_kernel,
         "tables",
-        [f32(rows * SUB, LANES) for rows in (T0, T1, T2, T3)],
+        [f32(rows, ENTRY_ROWS, LANES) for rows in (T0, T1, T2, T3)],
         [where_ref, table, near_ids],
-        [scratch(32, 5 * 256), scratch(LANES, T0 * SUB)],
+        [scratch(32, 5 * 256), scratch(ENTRY_ROWS, T0 * SUB)],
     )
 
     f0 = None
     for cycle in range(CYCLES):
-        outs = [f32(*padded(T0)), f32(*padded(T1)), f32(*plain(T1)), f32(*padded(T1)),
+        outs = [f32(*padded(T0, 0)), f32(*padded(T1, 1)), f32(*plain(T1)), f32(*padded(T1, 1)),
                 f32(2, 2 * FIELDS, SUB, LANES)]
-        temps = [scratch(*padded(T0)), scratch(*padded(T1)), scratch(*plain(T1))]
+        temps = [scratch(*padded(T0, 0)), scratch(*padded(T1, 1)), scratch(*plain(T1))]
         if cycle == 0:
             v0, v1, s1, c1, own, f0 = call(
                 functools.partial(down_kernel, True), "down_fresh", outs + [f32(*plain(T0))],
@@ -542,9 +592,9 @@
         far = swap_b(lax.dynamic_slice_in_dim(row, 1 - odd, 3, axis=0))
         last_one = swap_a(lax.dynamic_slice_in_dim(far, 2 - 2 * odd, 1, axis=0))
         operands = [where_ref, own, beside, far, last_one, v0, f0, v1, s1, c1, *tables]
-        temps = [scratch(*padded(T0))] * 2 + [scratch(*padded(T1))] * 2
-        temps += [scratch(*padded(T2)), scratch(*plain(T2)), scratch(*plain(T2)), scratch(*padded(T2)), scratch(*padded(T2))]
-        temps += [scratch(*padded(T3)), scratch(*plain(T3)), scratch(*plain(T3)), scratch(*padded(T3)), scratch(*padded(T3))]
+        temps = [scratch(*padded(T0, 0))] * 2 + [scratch(*padded(T1, 1))] * 2
+        temps += [scratch(*padded(T2, 2)), scratch(*plain(T2)), scratch(*plain(T2)), scratch(*padded(T2, 2)), scratch(*padded(T2, 2))]
+        temps += [scratch(*padded(T3, 3)), scratch(*plain(T3)), scratch(*plain(T3)), scratch(*padded(T3, 3)), scratch(*padded(T3, 3))]
         if cycle == CYCLES - 1:
             return call(
                 functools.partial(up_kernel, True), "up_last",

time: 217 us -> 151 us (0.70)
  Pallas kernels: 147 us -> 77.2 us
  local copies, waits for them, and re-layouts: 13.2 us -> 16.3 us
    pallas_call x6, Pallas kernels: 147 us -> 77.2 us  [call(): pl.pallas_call(kernel, out_shape=outs, in_specs=[SMEM] + [VMEM] * (len(op...]
    unnamed x27 -> x31, local copies, waits for them, and re-layouts: 12.7 us -> 14.9 us
  transfers between devices with their start and end apart: 14 -> 14, of which waited for: 10 -> 10; matrix products, arithmetic and copies ran while one was open for 0% -> 0% of each run, Pallas kernels for 2% -> 10%
where the time goes in v2:
time: 151 us; the launch traced here: 150 us
  Pallas kernels  77.2 us (51%)
  waiting for transfers between devices  39.5 us (26%)
  local copies, waits for them, and re-layouts  16.3 us (11%)
  starting transfers between devices  15.7 us (10%)
    pallas_call x6, Pallas kernels, call(): pl.pallas_call(kernel, out_shape=outs, in_specs=[SMEM] + [VMEM] * (len(op...  77.2 us
    ppermute x4, waiting for transfers between devices, per_device(): swap_b = lambda x: lax.ppermute(x, 'axial', pair_b)  18.9 us
    ppermute x4, waiting for transfers between devices, per_device(): gathered = gathered + lax.ppermute(gathered, 'axial', swap)  16.1 us
    unnamed x31, local copies, waits for them, and re-layouts  14.9 us
    ppermute x4, starting transfers between devices, per_device(): swap_b = lambda x: lax.ppermute(x, 'axial', pair_b)  9.45 us
    ppermute x6, waiting for transfers between devices, per_device(): swap_a = lambda x: lax.ppermute(x, 'axial', pair_a)  4.6 us
    ppermute x6, starting transfers between devices, per_device(): swap_a = lambda x: lax.ppermute(x, 'axial', pair_a)  4.16 us
  transfers between devices with their start and end apart: 14, of which 10 were waited for; matrix products, arithmetic and copies ran while one was open for 0% of the time, Pallas kernels for 10%

profile of v2, /device:TPU:17, one launch (start us, length us, event | category | flops | bytes accessed | tf_op | source)
XLA Modules:
  0.0 150.4 jit_solution(3852317466110541521)
XLA Ops:
  2.9 1.1 copy-done.5
  4.0 1.1 copy-done.6
  5.0 5.0 %split.1 = (f32[5,256,128]{2,1,0:T(8,128)S(1)}, f32[5,256,128]{2,1,0:T(8,128)S(1)}, f32[10,88,128]{2,1,0:T(8,128)S(1)}, f32[10,88,128]{2,1,0:T(8,128)S(1)}) custom-call(s32[2]{0:T(128)S(1)} %pad_add_fusion.where_ref.refs_0_, f32[5,32,1024]{2,1,0:T(8,128)S(1)} %copy-done.5, f32[5,32,1024]{2,1,0:T(8,128)S(1)} %copy-done.6), custom_call_target="tpu_custom_call" | custom-call | tf_op jit(solution)/shard_map/split/pallas_call | solution.py:512
  11.7 3.5 %collective-permute-start.1 = (f32[10,88,128]{2,1,0:T(8,128)S(1)}, f32[10,88,128]{2,1,0:T(8,128)S(1)}, u32[]{:S(2)}, u32[]{:S(2)}) collective-permute-start(f32[10,88,128]{2,1,0:T(8,128)S(1)} %get-tuple-element.30), channel_id=1, source_target_pairs={{1,2},{2,1},{3,4},{4,3},{5,6},{6,5},{7,8},{8,7},{9,10},{10,9},{11,... | collective-permute-start | bytes 1351688 | tf_op jit(solution)/shard_map/ppermute | solution.py:533
  15.3 1.3 collective-permute-start.3
  16.6 9.6 %collective-permute-done.3 = f32[72,128]{1,0:T(8,128)S(1)} collective-permute-done((f32[72,128]{1,0:T(8,128)S(1)}, f32[72,128]{1,0:T(8,128)S(1)}, u32[]{:S(2)}, u32[]{:S(2)}) %collective-permute-start.3) | collective-permute-done | bytes 36896 | tf_op jit(solution)/shard_map/ppermute | solution.py:553
  26.2 2.8 %collective-permute-done.4 = f32[72,128]{1,0:T(8,128)S(1)} collective-permute-done((f32[72,128]{1,0:T(8,128)S(1)}, f32[72,128]{1,0:T(8,128)S(1)}, u32[]{:S(2)}, u32[]{:S(2)}) %collective-permute-start.4) | collective-permute-done | bytes 36896 | tf_op jit(solution)/shard_map/ppermute | solution.py:553
  29.0 3.7 %collective-permute-done.5 = f32[72,128]{1,0:T(8,128)S(1)} collective-permute-done((f32[72,128]{1,0:T(8,128)S(1)}, f32[72,128]{1,0:T(8,128)S(1)}, u32[]{:S(2)}, u32[]{:S(2)}) %collective-permute-start.5) | collective-permute-done | bytes 36896 | tf_op jit(solution)/shard_map/ppermute | solution.py:553
  32.7 9.5 %tables.1 = (f32[64,64,128]{2,1,0:T(8,128)S(1)}, f32[32,64,128]{2,1,0:T(8,128)S(1)}, f32[40,64,128]{2,1,0:T(8,128)S(1)}, f32[20,64,128]{2,1,0:T(8,128)S(1)}) custom-call(s32[2]{0:T(128)S(1)} %pad_add_fusion.where_ref.refs_0_, f32[32,128]{1,0:T(8,128)S(1)} %slice.20.coeff_ref, f32[16,128]{1,0:T(8,128)S(1)} %pad.9.ids_ref), custom_call_target="tpu_custom_call" | custom-call | tf_op jit(solution)/shard_map/tables/pallas_call | solution.py:512
  42.2 1.4 copy-done
  43.6 1.1 copy-done.2
  46.2 1.1 copy-done.8
  47.3 1.1 copy-done.10
  48.3 1.0 copy-done.12
  49.4 1.0 copy-done.14
  50.4 14.1 %down_fresh.1 = (f32[5,640,128]{2,1,0:T(8,128)}, f32[5,384,128]{2,1,0:T(8,128)S(1)}, f32[5,32,8,128]{3,2,1,0:T(8,128)S(1)}, f32[5,384,128]{2,1,0:T(8,128)S(1)}, ...) custom-call(s32[2]{0:T(128)S(1)} %pad_add_fusion.where_ref.refs_0_, f32[5,256,128]{2,1,0:T(8,128)S(1)} %copy-done.8, ...), custom_call_target="tpu_custom_call" | custom-call | tf_op jit(solution)/shard_map/down_fresh/pallas_call | solution.py:512
  64.4 0.9 copy-done.3
  65.4 3.9 %collective-permute-start.6 = (f32[2,10,8,128]{3,2,1,0:T(8,128)S(1)}, f32[2,10,8,128]{3,2,1,0:T(8,128)S(1)}, u32[]{:S(2)}, u32[]{:S(2)}) collective-permute-start(f32[2,10,8,128]{3,2,1,0:T(8,128)S(1)} %get-tuple-element.33.refs_1_), channel_id=1, source_target_pairs={{0,1},{1,0},{2,3},{3,2},{4,5},{5,4},{6,7},{7,6},{8,9},{9,8},{10,11... | collective-permute-start | bytes 245768 | tf_op jit(solution)/shard_map/ppermute | solution.py:532
  69.2 0.9 collective-permute-done.6.refs_2_
  70.8 1.9 %collective-permute-start.7 = (f32[3,10,8,128]{3,2,1,0:T(8,128)}, f32[3,10,8,128]{3,2,1,0:T(8,128)}, u32[]{:S(2)}, u32[]{:S(2)}) collective-permute-start(f32[3,10,8,128]{3,2,1,0:T(8,128)} %fusion.3), channel_id=1, source_target_pairs={{1,2},{2,1},{3,4},{4,3},{5,6},{6,5},{7,8},{8,7},{9,10},{10,9},{11,... | collective-permute-start | bytes 368648 | tf_op jit(solution)/shard_map/ppermute | solution.py:533
  72.8 5.9 %collective-permute-done.7.refs_3_ = f32[3,10,8,128]{3,2,1,0:T(8,128)} collective-permute-done((f32[3,10,8,128]{3,2,1,0:T(8,128)}, f32[3,10,8,128]{3,2,1,0:T(8,128)}, u32[]{:S(2)}, u32[]{:S(2)}) %collective-permute-start.7) | collective-permute-done | bytes 122912 | tf_op jit(solution)/shard_map/ppermute | solution.py:533
  79.5 1.2 collective-permute-done.8.refs_4_
  80.7 1.2 copy-done.4
  81.9 16.5 %up.1 = (f32[5,256,128]{2,1,0:T(8,128)S(1)}, f32[5,88,128]{2,1,0:T(8,128)S(1)}, f32[5,88,128]{2,1,0:T(8,128)S(1)}) custom-call(s32[2]{0:T(128)S(1)} %pad_add_fusion.where_ref.refs_0_, f32[2,10,8,128]{3,2,1,0:T(8,128)S(1)} %get-tuple-element.33.refs_1_, f32[2,10,8,128]{3,2,1,0:T(8,128)S(1)} %collective-permute-done.6.refs_2_, ...), custom_call_target="tpu_custom_call" | custom-call | tf_op jit(solution)/shard_map/up/pallas_call | solution.py:512
  98.4 2.1 %collective-permute-start.10 = (f32[5,88,128]{2,1,0:T(8,128)S(1)}, f32[5,88,128]{2,1,0:T(8,128)S(1)}, u32[]{:S(2)}, u32[]{:S(2)}) collective-permute-start(f32[5,88,128]{2,1,0:T(8,128)S(1)} %get-tuple-element.43), channel_id=1, source_target_pairs={{1,2},{2,1},{3,4},{4,3},{5,6},{6,5},{7,8},{8,7},{9,10},{10,9},{11,... | collective-permute-start | bytes 675848 | tf_op jit(solution)/shard_map/ppermute | solution.py:533
  100.7 7.4 %collective-permute-done.10.refs_3_ = f32[5,88,128]{2,1,0:T(8,128)S(1)} collective-permute-done((f32[5,88,128]{2,1,0:T(8,128)S(1)}, f32[5,88,128]{2,1,0:T(8,128)S(1)}, u32[]{:S(2)}, u32[]{:S(2)}) %collective-permute-start.10) | collective-permute-done | bytes 225312 | tf_op jit(solution)/shard_map/ppermute | solution.py:533
  108.1 13.4 %down.1 = (f32[5,640,128]{2,1,0:T(8,128)}, f32[5,384,128]{2,1,0:T(8,128)S(1)}, f32[5,32,8,128]{3,2,1,0:T(8,128)S(1)}, f32[5,384,128]{2,1,0:T(8,128)S(1)}, f32[2,10,8,128]{3,2,1,0:T(8,128)S(1)}) custom-call(s32[2]{0:T(128)S(1)} %pad_add_fusion.where_ref.refs_0_, f32[5,256,128]{2,1,0:T(8,128)S(1)} %get-tuple-element.41.refs_1_, ...), custom_call_target="tpu_custom_call" | custom-call | tf_op jit(solution)/shard_map/down/pallas_call | solution.py:512
  121.6 1.3 collective-permute-done.11.refs_2_
  122.9 1.9 %collective-permute-start.12 = (f32[3,10,8,128]{3,2,1,0:T(8,128)S(1)}, f32[3,10,8,128]{3,2,1,0:T(8,128)S(1)}, u32[]{:S(2)}, u32[]{:S(2)}) collective-permute-start(f32[3,10,8,128]{3,2,1,0:T(8,128)S(1)} %fusion.1), channel_id=1, source_target_pairs={{1,2},{2,1},{3,4},{4,3},{5,6},{6,5},{7,8},{8,7},{9,10},{10,9},{11,... | collective-permute-start | bytes 368648 | tf_op jit(solution)/shard_map/ppermute | solution.py:533
  124.8 5.6 %collective-permute-done.12.refs_3_ = f32[3,10,8,128]{3,2,1,0:T(8,128)S(1)} collective-permute-done((f32[3,10,8,128]{3,2,1,0:T(8,128)S(1)}, f32[3,10,8,128]{3,2,1,0:T(8,128)S(1)}, u32[]{:S(2)}, u32[]{:S(2)}) %collective-permute-start.12) | collective-permute-done | bytes 122912 | tf_op jit(solution)/shard_map/ppermute | solution.py:533
  130.4 1.2 collective-permute-done.13.refs_4_
  131.6 18.8 %up_last.1 = f32[5,32,1024]{2,1,0:T(8,128)} custom-call(s32[2]{0:T(128)S(1)} %pad_add_fusion.where_ref.refs_0_, f32[2,10,8,128]{3,2,1,0:T(8,128)S(1)} %get-tuple-element.44.refs_1_, f32[2,10,8,128]{3,2,1,0:T(8,128)S(1)} %collective-permute-done.11.refs_2_, f32[3,10,8,128]{3,2,1,0:T(8,128)S(1)} %collective-permute-done.12.refs_3_, ...), custom_call_target="tpu_custom_call" | custom-call | tf_op jit(solution)/shard_map/up_last/pallas_call | solution.py:512
  (56 shorter events, 8.0 us)
Async XLA Ops:
  2.0 13.2 %collective-permute-start.2 = (f32[72,128]{1,0:T(8,128)S(1)}, f32[72,128]{1,0:T(8,128)S(1)}, u32[]{:S(2)}, u32[]{:S(2)}) collective-permute-start(f32[72,128]{1,0:T(8,128)S(1)} %pad_maximum_fusion), channel_id=1, source_target_pairs={{0,1},{1,0},{2,3},{3,2},{4,5},{5,4},{6,7},{7,6},{8,9},{9,8},{10,11... | collective-permute-start | bytes 110600 | tf_op jit(solution)/shard_map/ppermute | solution.py:553
  2.9 1.1 copy-start.5
  4.0 1.1 copy-start.6
  10.0 0.8 copy-start.7
  10.8 0.8 copy-start.9
  11.7 32.9 %collective-permute-start = (f32[10,88,128]{2,1,0:T(8,128)S(1)}, f32[10,88,128]{2,1,0:T(8,128)S(1)}, u32[]{:S(2)}, u32[]{:S(2)}) collective-permute-start(f32[10,88,128]{2,1,0:T(8,128)S(1)} %get-tuple-element.29), channel_id=1, source_target_pairs={{0,1},{1,0},{2,3},{3,2},{4,5},{5,4},{6,7},{7,6},{8,9},{9,8},{10,11... | collective-permute-start | bytes 1351688 | tf_op jit(solution)/shard_map/ppermute | solution.py:532
  11.7 33.7 %collective-permute-start.1 = (f32[10,88,128]{2,1,0:T(8,128)S(1)}, f32[10,88,128]{2,1,0:T(8,128)S(1)}, u32[]{:S(2)}, u32[]{:S(2)}) collective-permute-start(f32[10,88,128]{2,1,0:T(8,128)S(1)} %get-tuple-element.30), channel_id=1, source_target_pairs={{1,2},{2,1},{3,4},{4,3},{5,6},{6,5},{7,8},{8,7},{9,10},{10,9},{11,... | collective-permute-start | bytes 1351688 | tf_op jit(solution)/shard_map/ppermute | solution.py:533
  15.3 10.9 %collective-permute-start.3 = (f32[72,128]{1,0:T(8,128)S(1)}, f32[72,128]{1,0:T(8,128)S(1)}, u32[]{:S(2)}, u32[]{:S(2)}) collective-permute-start(f32[72,128]{1,0:T(8,128)S(1)} %fusion.4), channel_id=1, source_target_pairs={{0,2},{1,3},{2,0},{3,1},{4,6},{5,7},{6,4},{7,5},{8,10},{9,11},{10,... | collective-permute-start | bytes 110600 | tf_op jit(solution)/shard_map/ppermute | solution.py:553
  26.2 2.8 %collective-permute-start.4 = (f32[72,128]{1,0:T(8,128)S(1)}, f32[72,128]{1,0:T(8,128)S(1)}, u32[]{:S(2)}, u32[]{:S(2)}) collective-permute-start(f32[72,128]{1,0:T(8,128)S(1)} %add.50), channel_id=1, source_target_pairs={{0,4},{1,5},{2,6},{3,7},{4,0},{5,1},{6,2},{7,3},{8,12},{9,13},{10,... | collective-permute-start | bytes 110600 | tf_op jit(solution)/shard_map/ppermute | solution.py:553
  29.0 3.7 %collective-permute-start.5 = (f32[72,128]{1,0:T(8,128)S(1)}, f32[72,128]{1,0:T(8,128)S(1)}, u32[]{:S(2)}, u32[]{:S(2)}) collective-permute-start(f32[72,128]{1,0:T(8,128)S(1)} %add.51), channel_id=1, source_target_pairs={{0,8},{1,9},{2,10},{3,11},{4,12},{5,13},{6,14},{7,15},{8,0},{9,1},... | collective-permute-start | bytes 110600 | tf_op jit(solution)/shard_map/ppermute | solution.py:553
  42.2 1.4 copy-start
  43.6 1.1 copy-start.2
  44.6 0.8 copy-start.11
  45.4 0.8 copy-start.13
  46.2 1.1 copy-start.8
  47.3 1.1 copy-start.10
  48.3 1.0 copy-start.12
  49.4 1.0 copy-start.14
  64.4 0.9 copy-start.3
  65.4 4.8 %collective-permute-start.6 = (f32[2,10,8,128]{3,2,1,0:T(8,128)S(1)}, f32[2,10,8,128]{3,2,1,0:T(8,128)S(1)}, u32[]{:S(2)}, u32[]{:S(2)}) collective-permute-start(f32[2,10,8,128]{3,2,1,0:T(8,128)S(1)} %get-tuple-element.33.refs_1_), channel_id=1, source_target_pairs={{0,1},{1,0},{2,3},{3,2},{4,5},{5,4},{6,7},{7,6},{8,9},{9,8},{10,11... | collective-permute-start | bytes 245768 | tf_op jit(solution)/shard_map/ppermute | solution.py:532
  70.8 7.8 %collective-permute-start.7 = (f32[3,10,8,128]{3,2,1,0:T(8,128)}, f32[3,10,8,128]{3,2,1,0:T(8,128)}, u32[]{:S(2)}, u32[]{:S(2)}) collective-permute-start(f32[3,10,8,128]{3,2,1,0:T(8,128)} %fusion.3), channel_id=1, source_target_pairs={{1,2},{2,1},{3,4},{4,3},{5,6},{6,5},{7,8},{8,7},{9,10},{10,9},{11,... | collective-permute-start | bytes 368648 | tf_op jit(solution)/shard_map/ppermute | solution.py:533
  79.4 1.2 collective-permute-start.8
  80.7 1.2 copy-start.4
  81.9 26.3 %copy-start.1 = (f32[5,64,8,128]{3,2,1,0:T(8,128)S(1)}, f32[5,64,8,128]{3,2,1,0:T(8,128)}, u32[]{:S(2)}) copy-start(f32[5,64,8,128]{3,2,1,0:T(8,128)} %get-tuple-element.35.refs_6_.refs_4_) | copy-start | bytes 3932164
  98.4 9.7 %collective-permute-start.10 = (f32[5,88,128]{2,1,0:T(8,128)S(1)}, f32[5,88,128]{2,1,0:T(8,128)S(1)}, u32[]{:S(2)}, u32[]{:S(2)}) collective-permute-start(f32[5,88,128]{2,1,0:T(8,128)S(1)} %get-tuple-element.43), channel_id=1, source_target_pairs={{1,2},{2,1},{3,4},{4,3},{5,6},{6,5},{7,8},{8,7},{9,10},{10,9},{11,... | collective-permute-start | bytes 675848 | tf_op jit(solution)/shard_map/ppermute | solution.py:533
  100.5 7.6 %collective-permute-start.9 = (f32[5,88,128]{2,1,0:T(8,128)S(1)}, f32[5,88,128]{2,1,0:T(8,128)S(1)}, u32[]{:S(2)}, u32[]{:S(2)}) collective-permute-start(f32[5,88,128]{2,1,0:T(8,128)S(1)} %get-tuple-element.42), channel_id=1, source_target_pairs={{0,1},{1,0},{2,3},{3,2},{4,5},{5,4},{6,7},{7,6},{8,9},{9,8},{10,11... | collective-permute-start | bytes 675848 | tf_op jit(solution)/shard_map/ppermute | solution.py:532
  121.6 1.3 collective-permute-start.11
  122.9 7.5 %collective-permute-start.12 = (f32[3,10,8,128]{3,2,1,0:T(8,128)S(1)}, f32[3,10,8,128]{3,2,1,0:T(8,128)S(1)}, u32[]{:S(2)}, u32[]{:S(2)}) collective-permute-start(f32[3,10,8,128]{3,2,1,0:T(8,128)S(1)} %fusion.1), channel_id=1, source_target_pairs={{1,2},{2,1},{3,4},{4,3},{5,6},{6,5},{7,8},{8,7},{9,10},{10,9},{11,... | collective-permute-start | bytes 368648 | tf_op jit(solution)/shard_map/ppermute | solution.py:533
  130.4 1.2 collective-permute-start.13

commit v3 on v2

v3 whole, which is shorter than its diff:
```python
import functools

import jax
import jax.numpy as jnp
from jax import lax
from jax.experimental import pallas as pl
from jax.experimental.pallas import tpu as pltpu
from jax.sharding import PartitionSpec as P

DIFFUSION = 1.0
RELAXATION = 0.8
SOURCE_GAIN = 0.05
CYCLES = 2

FIELDS = 5
ENTRIES = FIELDS * FIELDS
SUB, LANES = 8, 128

OWN = 32
FINE_HALO = 11
T0, O0 = 64, 16
T1, O1 = 32, 8
T2, O2 = 40, 16
T3, O3 = 20, 8
GROUP = 4
SPREAD = 16


def stride_of(level):
    return SUB + 2 * 2**level


def padded_rows(rows, level):
    return stride_of(level) * (rows + SUB)


def at(row, level):
    return stride_of(level) * row + 2**level


def lane_iota():
    return lax.broadcasted_iota(jnp.int32, (SUB, LANES), 1)


def sub_iota():
    return lax.broadcasted_iota(jnp.int32, (SUB, LANES), 0)


def tile(ref, field, row, level):
    return ref[field, pl.ds(at(row, level), SUB), :]


def put(ref, field, row, level, value):
    ref[field, pl.ds(at(row, level), SUB), :] = value


def edges(ref, level, first, last):
    width, stride, lane = 2**level, stride_of(level), lane_iota()
    for row in range(first, last, SUB):
        start = at(row, level)
        for field in range(FIELDS):
            rows = lambda sub: (field, pl.ds(start + sub, SUB, stride=stride), slice(None))
            before = jnp.where(lane == 0, 0.0, pltpu.roll(ref[rows(SUB - 1)], 1, 1))
            after = jnp.where(lane == LANES - 1, 0.0, pltpu.roll(ref[rows(0)], LANES - 1, 1))
            for i in range(width):
                ref[rows(i - width)] = before
                ref[rows(SUB + i)] = after


def rows_loop(first, last, body):
    def step(row, carry):
        body(row)
        return carry

    lax.fori_loop(first, last, step, 0)


def batches(first, last, batch, compute, store):
    def body(index):
        rows = [first + index * batch + i for i in range(batch)]
        results = [compute(row) for row in rows]
        for row, result in zip(rows, results):
            store(row, result)

    rows_loop(0, -(-(last - first) // batch), body)


def neighbours(ref, row, level):
    start, width, stride = at(row, level), 2**level, stride_of(level)
    sums, centres = [], []
    for field in range(FIELDS):
        load = lambda first: ref[field, pl.ds(first, SUB), :]
        radial = load(start - width) + load(start + width)
        sums.append(radial + (load(start - stride) + load(start + stride)))
        centres.append(load(start))
    return sums, centres


def block_times(table, level, row, first, vectors):
    row = TABLE_AT[level] + row
    out = []
    for i in range(FIELDS):
        total = None
        for j in range(FIELDS):
            entry = first + FIELDS * i + j
            term = jnp.broadcast_to(table[entry, pl.ds(row, 1), :], (SUB, LANES)) * vectors[j]
            total = term if total is None else total + term
        out.append(total)
    return out


MATRIX_AT = ENTRIES
TABLE_AT = (0, T0, T0 + T1, T0 + T1 + T2)
TABLE_ROWS = 160
NEAR = 5


def gain_of(level):
    return SOURCE_GAIN * 4.0**level / DIFFUSION


def sweep(source_of, old, new, table, level, first, last, more=True):
    gain = gain_of(level)

    def compute(row):
        sums, centres = neighbours(old, row, level)
        rest = [
            (source_of(field, row) + sums[field]) - gain * jnp.tanh(centres[field])
            for field in range(FIELDS)
        ]
        moved = block_times(table, level, row, 0, rest)
        return [(1.0 - RELAXATION) * centres[f] + moved[f] for f in range(FIELDS)]

    def store(row, values):
        for field in range(FIELDS):
            put(new, field, row, level, values[field])

    batches(first, last, SWEEP_BATCH, compute, store)
    if more:
        edges(new, level, first, last)


def residual(source_of, values, table, level, row):
    gain = gain_of(level)
    sums, centres = neighbours(values, row, level)
    applied = block_times(table, level, row, MATRIX_AT, centres)
    left = [
        ((source_of(field, row) + sums[field]) - gain * jnp.tanh(centres[field])) - applied[field]
        for field in range(FIELDS)
    ]
    return left, centres


def pair_sum(value, level):
    width = 2**level
    other = pltpu.roll(value, SUB - width, 0)
    if 2 * width != SUB:
        other = jnp.where((sub_iota() & width) == 0, other, pltpu.roll(value, width, 0))
    return value + other


def coarsen(source_of, values, table, level, row):
    upper_r, upper_v = residual(source_of, values, table, level, 2 * row)
    lower_r, lower_v = residual(source_of, values, table, level, 2 * row + 1)
    coarse = [0.25 * pair_sum(upper_v[f] + lower_v[f], level) for f in range(FIELDS)]
    rest = [pair_sum(upper_r[f] + lower_r[f], level) for f in range(FIELDS)]
    return coarse, rest


def first_sweep(coarse, rest, table, level, row):
    moved = block_times(table, level, row, 0, rest)
    return [coarse[f] + moved[f] for f in range(FIELDS)]


def descend(source_of, values, table, level, c, q, first_values, first, last):
    def compute(row):
        coarse, rest = coarsen(source_of, values, table, level, row)
        return coarse, rest, first_sweep(coarse, rest, table, level + 1, row)

    def store(row, results):
        for field in range(FIELDS):
            put(c, field, row, level + 1, results[0][field])
            q[field, row] = results[1][field]
            put(first_values, field, row, level + 1, results[2][field])

    batches(first, last, COARSEN_BATCH, compute, store)
    edges(c, level + 1, first, last)
    edges(first_values, level + 1, first, last)


def make_source(coarse, rest, source, table, level, first, last):
    gain = gain_of(level)

    def compute(row):
        sums, centres = neighbours(coarse, row, level)
        applied = block_times(table, level, row, MATRIX_AT, centres)
        return [
            (applied[f] - sums[f]) + (gain * jnp.tanh(centres[f]) + rest[f, row])
            for f in range(FIELDS)
        ]

    def store(row, values):
        for field in range(FIELDS):
            source[field, row] = values[field]

    batches(first, last, SWEEP_BATCH, compute, store)


def correct(new, fine, after, before, level, offset, first, last):
    def body(index):
        coarse_row = first // 2 + index + offset
        row = first // 2 * 2 + 2 * index
        for field in range(FIELDS):
            change = tile(after, field, coarse_row, level + 1) - tile(before, field, coarse_row, level + 1)
            put(new, field, row, level, tile(fine, field, row, level) + change)
            put(new, field, row + 1, level, tile(fine, field, row + 1, level) + change)

    rows_loop(0, (last + 1) // 2 - first // 2, body)
    edges(new, level, first, last)


SWEEP_BATCH = 4
COARSEN_BATCH = 2


def three_parts(value):
    high = value.astype(jnp.bfloat16)
    rest = value - high.astype(jnp.float32)
    middle = rest.astype(jnp.bfloat16)
    low = (rest - middle.astype(jnp.float32)).astype(jnp.bfloat16)
    return high, middle, low


def dot(left, right):
    return jnp.dot(left, right, preferred_element_type=jnp.float32)


def tables_kernel(regions, where_ref, regions_ref, table, mats, parts):
    device, devices = where_ref[0], where_ref[1]
    wide = 2 * LANES
    lane = lane_iota()
    ids = [jnp.full((SUB, LANES), -1.0, jnp.float32)] * 2
    per_tile = LANES // OWN
    for i in range(NEAR):
        owner = jnp.clip(device + (i - NEAR // 2), 0, devices - 1)
        start = pl.multiple_of(regions + owner // per_tile * SUB, SUB)
        held = regions_ref[pl.ds(start, SUB), :]
        turned = pltpu.roll(held, ((i % per_tile) - owner % per_tile + per_tile) % per_tile * OWN, 1)
        place = i // per_tile
        ids[place] = jnp.where(lane // OWN == i % per_tile, turned, ids[place])
    ids = jnp.concatenate(ids, axis=1).astype(jnp.int32)

    coefficients = jnp.transpose(regions_ref[0:regions, :])[0:32]
    coefficients = jnp.concatenate(three_parts(coefficients), axis=0)
    region = lax.broadcasted_iota(jnp.int32, (regions, wide), 0)
    for block in range(SUB):
        chosen = region == jnp.broadcast_to(ids[block : block + 1], (regions, wide))
        found = dot(coefficients, chosen.astype(jnp.float32).astype(jnp.bfloat16))
        found = (found[0:32] + found[32:64]) + found[64:96]
        for half in range(2):
            mats[half, pl.ds(block, 32, stride=SUB), :] = found[:, half * LANES : (half + 1) * LANES]

    fine = lax.broadcasted_iota(jnp.int32, (wide, wide), 0)
    out = lax.broadcasted_iota(jnp.int32, (wide, wide), 1)
    average = jnp.zeros((wide, wide), jnp.float32)
    own_at = NEAR // 2 * OWN
    for level, (first_own, rows) in enumerate(((O0, T0), (O1, T1), (O2, T2), (O3, T3))):
        span = 2**level
        row = out - TABLE_AT[level]
        same = (row >= 0) & (row < rows) & (fine // span == row + (own_at // span - first_own))
        average = jnp.where(same, 1.0 / span, average)
    average = average.astype(jnp.bfloat16)
    used = SUB * ENTRIES
    high, middle, low = three_parts(jnp.concatenate([mats[0, 0:used], mats[1, 0:used]], axis=1))
    levels = (dot(high, average) + dot(middle, average)) + dot(low, average)

    row = lax.broadcasted_iota(jnp.int32, (SUB, wide), 1)
    weight = jnp.zeros((SUB, wide), jnp.float32) + DIFFUSION
    whole = jnp.zeros((SUB, wide), jnp.int32)
    limit = jnp.zeros((SUB, wide), jnp.int32)
    for level, first_own in enumerate((O0, O1, O2, O3)):
        here = row >= TABLE_AT[level]
        weight = jnp.where(here, DIFFUSION / 4.0**level, weight)
        whole = jnp.where(here, row - TABLE_AT[level] - first_own + device * (OWN >> level), whole)
        limit = jnp.where(here, devices * (OWN >> level), limit)
    inside = (whole >= 0) & (whole < limit)
    scale = jnp.where(inside, RELAXATION * weight, 0.0)
    unscale = 1.0 / weight

    n = FIELDS
    block = [[levels[SUB * (n * i + j) : SUB * (n * i + j + 1)] for j in range(n)] for i in range(n)]
    for i in range(n):
        block[i][i] = block[i][i] + 4.0 * weight
    entries = [block[i][j] * unscale for i in range(n) for j in range(n)]
    right = [[None] * n for _ in range(n)]
    for i in range(n):
        right[i][i] = jnp.ones((SUB, wide), jnp.float32)
    for c in range(n):
        lead = 1.0 / block[c][c]
        for j in range(c + 1, n):
            block[c][j] = block[c][j] * lead
        for j in range(n):
            if right[c][j] is not None:
                right[c][j] = right[c][j] * lead
        for i in range(n):
            if i == c:
                continue
            factor = block[i][c]
            for j in range(c + 1, n):
                block[i][j] = block[i][j] - factor * block[c][j]
            for j in range(n):
                if right[c][j] is not None:
                    term = factor * right[c][j]
                    right[i][j] = -term if right[i][j] is None else right[i][j] - term
    entries = [right[i][j] * scale for i in range(n) for j in range(n)] + entries

    group = FIELDS
    into = lax.broadcasted_iota(jnp.int32, (LANES, group * LANES), 0)
    out = lax.broadcasted_iota(jnp.int32, (LANES, group * LANES), 1)
    same = (into // (3 * SUB) == out // LANES) & (into % SUB == out % LANES // SPREAD)
    widen = same.astype(jnp.float32).astype(jnp.bfloat16)
    parts[...] = jnp.zeros_like(parts)
    for first in range(0, len(entries), group):
        for i in range(group):
            for p, part in enumerate(three_parts(entries[first + i])):
                start = (3 * i + p) * SUB
                parts[start : start + SUB, :] = part.astype(jnp.float32)
        turned = jnp.transpose(parts[...])[0:TABLE_ROWS].astype(jnp.bfloat16)
        wide_rows = dot(turned, widen)
        for i in range(group):
            table[first + i] = wide_rows[:, i * LANES : (i + 1) * LANES]


def turn(first_sub, inward):
    shape = (SUB * LANES, 2 * LANES)
    into = lax.broadcasted_iota(jnp.int32, shape, 0)
    out = lax.broadcasted_iota(jnp.int32, shape, 1)
    if inward:
        wanted = (out % LANES) * SUB + first_sub + out // LANES
    else:
        cell = out + first_sub * LANES
        wanted = (cell % SUB) * LANES + cell // SUB
    return (into == wanted).astype(jnp.float32).astype(jnp.bfloat16)


def split_kernel(where_ref, state_ref, forcing_ref, state_rows, forcing_rows, send_a, send_b, parts):
    odd = where_ref[0] % 2
    held = 2 * FIELDS * OWN
    for which, source in enumerate((state_ref, forcing_ref)):
        for field in range(FIELDS):
            for p, part in enumerate(three_parts(source[field])):
                start = p * held + (which * FIELDS + field) * OWN
                parts[start : start + OWN, :] = part

    def two_subs(index):
        values = dot(parts[...], turn(2 * index, True))
        values = (values[:held] + values[held : 2 * held]) + values[2 * held :]
        for which, target in enumerate((state_rows, forcing_rows)):
            for field in range(FIELDS):
                start = (which * FIELDS + field) * OWN
                for half in range(2):
                    target[field, pl.ds(2 * index + half, OWN, stride=SUB), :] = values[
                        start : start + OWN, half * LANES : (half + 1) * LANES
                    ]

    rows_loop(0, SUB // 2, two_subs)
    low, high = 0, (OWN - FINE_HALO) * SUB
    size = FINE_HALO * SUB
    for which, rows in enumerate((state_rows, forcing_rows)):
        for field in range(FIELDS):
            first = rows[field, low : low + size, :]
            last = rows[field, high : high + size, :]
            send_a[which * FIELDS + field] = jnp.where(odd == 1, first, last)
            send_b[which * FIELDS + field] = jnp.where(odd == 1, last, first)


def place_halo(where_ref, buffer, own_rows, got_a, got_b, first, padded):
    odd = where_ref[0] % 2
    row_a = jnp.where(odd == 1, O0 - FINE_HALO, O0 + OWN)
    row_b = jnp.where(odd == 1, O0 + OWN, O0 - FINE_HALO)

    def put_row(field, row, value):
        if padded:
            put(buffer, field, row, 0, value)
        else:
            buffer[field, row] = value

    def own(row):
        start = pl.multiple_of(row * SUB, SUB)
        for field in range(FIELDS):
            put_row(field, O0 + row, own_rows[field, pl.ds(start, SUB), :])

    def halo(row):
        start = pl.multiple_of(row * SUB, SUB)
        for field in range(FIELDS):
            put_row(field, row_a + row, got_a[first + field, pl.ds(start, SUB), :])
            put_row(field, row_b + row, got_b[first + field, pl.ds(start, SUB), :])

    rows_loop(0, OWN, own)
    rows_loop(0, FINE_HALO, halo)


def down_kernel(fresh, *refs):
    if fresh:
        where_ref, state, force, got_a, got_b, table, v0, v1, s1, c1, send, f0, tmp0, tmp1, q1 = refs
    else:
        where_ref, state, got_a, got_b, f0, table, v0, v1, s1, c1, send, tmp0, tmp1, q1 = refs
    place_halo(where_ref, v0, state, got_a, got_b, 0, True)
    edges(v0, 0, O0 - FINE_HALO, O0 + OWN + FINE_HALO)
    if fresh:
        place_halo(where_ref, f0, force, got_a, got_b, FIELDS, False)
    fine_source = lambda field, row: f0[field, row]
    low, high = O0 - FINE_HALO, O0 + OWN + FINE_HALO
    sweep(fine_source, v0, tmp0, table, 0, low + 1, high - 1)
    sweep(fine_source, tmp0, v0, table, 0, low + 2, high - 2)

    half = OWN // 2
    descend(fine_source, v0, table, 0, c1, q1, tmp1, O1 - 4, O1 + half + 4)
    make_source(c1, q1, s1, table, 1, O1 - 3, O1 + half + 3)
    first_source = lambda field, row: s1[field, row]
    sweep(first_source, tmp1, v1, table, 1, O1 - 3, O1 + half + 3)

    sub = sub_iota()

    def to_second(index):
        coarse, rest = coarsen(first_source, v1, table, 1, index + O1 // 2)
        return coarse + rest

    def pack(index, values):
        group, place = index // GROUP, index % GROUP
        mine = (sub & (GROUP - 1)) == place
        for which in range(2 * FIELDS):
            send[group, which] = jnp.where(mine, values[which], send[group, which])

    send[...] = jnp.zeros_like(send)
    batches(0, OWN // 4, COARSEN_BATCH, to_second, pack)


def spread(source, index, which, place):
    take = lambda sub: jnp.broadcast_to(source[index, which, sub : sub + 1, :], (SUB, LANES))
    return jnp.where(sub_iota() < GROUP, take(place), take(GROUP + place))


def up_kernel(last, *refs):
    if last:
        (where_ref, own, got_a, got_b, got_a2, v0, f0, v1, s1, c1, table, out,
         parts, tmp0, work0, tmp1, work1, c2, q2, s2, v2, tmp2, c3, q3, s3, v3, tmp3) = refs
    else:
        (where_ref, own, got_a, got_b, got_a2, v0, f0, v1, s1, c1, table, out,
         send_a, send_b, tmp0, work0, tmp1, work1, c2, q2, s2, v2, tmp2, c3, q3, s3, v3, tmp3) = refs
    odd = where_ref[0] % 2

    def unpack(source, index, group):
        for place in range(GROUP):
            row = group * GROUP + place
            coarse = [spread(source, index, f, place) for f in range(FIELDS)]
            rest = [spread(source, index, FIELDS + f, place) for f in range(FIELDS)]
            start = first_sweep(coarse, rest, table, 2, row)
            for field in range(FIELDS):
                put(c2, field, row, 2, coarse[field])
                q2[field, row] = rest[field]
                put(tmp2, field, row, 2, start[field])

    pick = lambda a, b: jnp.where(odd == 1, b, a)
    rows_loop(0, 2, lambda i: unpack(own, i, 4 + i))
    rows_loop(0, 2, lambda i: unpack(got_a, i, pick(6, 2) + i))
    rows_loop(0, 3, lambda i: unpack(got_b, i, pick(1, 6) + i))
    rows_loop(0, 1, lambda i: unpack(got_a2, pick(0, 2) + i, pick(8, 1) + i))

    quarter, eighth = OWN // 4, OWN // 8
    for ref in (c2, tmp2):
        edges(ref, 2, O2 - 12, O2 + quarter + 12)
    make_source(c2, q2, s2, table, 2, O2 - 11, O2 + quarter + 11)
    second_source = lambda field, row: s2[field, row]
    sweep(second_source, tmp2, v2, table, 2, O2 - 11, O2 + quarter + 11)

    descend(second_source, v2, table, 2, c3, q3, tmp3, O3 - 5, O3 + eighth + 5)
    make_source(c3, q3, s3, table, 3, O3 - 4, O3 + eighth + 4)
    third_source = lambda field, row: s3[field, row]
    sweep(third_source, tmp3, v3, table, 3, O3 - 4, O3 + eighth + 4)
    sweep(third_source, v3, tmp3, table, 3, O3 - 3, O3 + eighth + 3)
    sweep(third_source, tmp3, v3, table, 3, O3 - 2, O3 + eighth + 2, False)
    correct(v2, v2, v3, c3, 2, 0, O2 - 4, O2 + quarter + 4)
    sweep(second_source, v2, tmp2, table, 2, O2 - 3, O2 + quarter + 3)
    sweep(second_source, tmp2, v2, table, 2, O2 - 2, O2 + quarter + 2, False)

    half = OWN // 2
    first_source = lambda field, row: s1[field, row]
    correct(work1, v1, v2, c2, 1, O2 - O1 // 2, O1 - 3, O1 + half + 3)
    sweep(first_source, work1, tmp1, table, 1, O1 - 2, O1 + half + 2)
    sweep(first_source, tmp1, work1, table, 1, O1 - 1, O1 + half + 1, False)

    fine_source = lambda field, row: f0[field, row]
    correct(work0, v0, work1, c1, 0, 0, O0 - 2, O0 + OWN + 2)
    sweep(fine_source, work0, tmp0, table, 0, O0 - 1, O0 + OWN + 1)
    sweep(fine_source, tmp0, work0, table, 0, O0, O0 + OWN, False)

    if last:
        held = FIELDS * OWN
        for field in range(FIELDS):
            for sub in range(SUB):
                value = work0[field, pl.ds(at(O0, 0) + sub, OWN, stride=stride_of(0)), :]
                for p, part in enumerate(three_parts(value)):
                    start = p * held + field * OWN
                    parts[start : start + OWN, sub * LANES : (sub + 1) * LANES] = part

        def columns_out(index):
            values = dot(parts[...], turn(2 * index, False))
            values = (values[:held] + values[held : 2 * held]) + values[2 * held :]
            cells = pl.ds(pl.multiple_of(index * 2 * LANES, 2 * LANES), 2 * LANES)
            for field in range(FIELDS):
                out[field, :, cells] = values[field * OWN : (field + 1) * OWN]

        rows_loop(0, SUB // 2, columns_out)
        return

    def leave(row):
        start = pl.multiple_of(row * SUB, SUB)
        for field in range(FIELDS):
            out[field, pl.ds(start, SUB), :] = tile(work0, field, O0 + row, 0)

    rows_loop(0, OWN, leave)
    from_a, from_b = pick(OWN - FINE_HALO, 0), pick(0, OWN - FINE_HALO)

    def edge(row):
        start = pl.multiple_of(row * SUB, SUB)
        for field in range(FIELDS):
            send_a[field, pl.ds(start, SUB), :] = tile(work0, field, O0 + from_a + row, 0)
            send_b[field, pl.ds(start, SUB), :] = tile(work0, field, O0 + from_b + row, 0)

    rows_loop(0, FINE_HALO, edge)


VMEM = pl.BlockSpec(memory_space=pltpu.VMEM)
SMEM = pl.BlockSpec(memory_space=pltpu.SMEM)


def f32(*shape):
    return jax.ShapeDtypeStruct(shape, jnp.float32)


def scratch(*shape):
    return pltpu.VMEM(shape, jnp.float32)


def padded(rows, level):
    return (FIELDS, padded_rows(rows, level), LANES)


def plain(rows):
    return (FIELDS, rows, SUB, LANES)


def call(kernel, name, outs, operands, scratches=()):
    return pl.pallas_call(
        kernel,
        out_shape=outs,
        in_specs=[SMEM] + [VMEM] * (len(operands) - 1),
        out_specs=[VMEM] * len(outs),
        scratch_shapes=list(scratches),
        name=name,
        compiler_params=pltpu.CompilerParams(vmem_limit_bytes=28 * 1024 * 1024),
    )(*operands)


def per_device(initial_state, forcing, coefficients, region_ids):
    size = lax.axis_size("axial")
    device = lax.axis_index("axial")
    assert initial_state.shape == (FIELDS, OWN, SUB * LANES)
    assert region_ids.shape == (OWN, SUB)
    where_ref = jnp.stack([device, jnp.int32(size)]).astype(jnp.int32)
    odd = device % 2
    pair_a = [(i, i ^ 1) for i in range(size)]
    pair_b = [(i, i + 1 if i % 2 else i - 1) for i in range(1, size - 1)]
    swap_a = lambda x: lax.ppermute(x, "axial", pair_a)
    swap_b = lambda x: lax.ppermute(x, "axial", pair_b)

    share = coefficients.shape[1]
    regions = share * size
    per_tile = LANES // OWN
    gathered = jnp.zeros((regions + SUB * -(-size // per_tile), LANES), jnp.float32)
    gathered = lax.dynamic_update_slice(gathered, coefficients.T, (device * share, 0))
    gathered = lax.dynamic_update_slice(
        gathered,
        region_ids.T.astype(jnp.float32),
        (regions + device // per_tile * SUB, device % per_tile * OWN),
    )
    step = 1
    while step < size:
        swap = [(i, i ^ step) for i in range(size)]
        gathered = gathered + lax.ppermute(gathered, "axial", swap)
        step *= 2

    state, force, send_a, send_b = call(
        split_kernel,
        "split",
        [f32(FIELDS, OWN * SUB, LANES)] * 2 + [f32(2 * FIELDS, FINE_HALO * SUB, LANES)] * 2,
        [where_ref, initial_state, forcing],
        [pltpu.VMEM((3 * 2 * FIELDS * OWN, SUB * LANES), jnp.bfloat16)],
    )
    send_a, send_b, gathered = lax.optimization_barrier((send_a, send_b, gathered))
    got_b, got_a = swap_b(send_b), swap_a(send_a)
    (table,) = call(
        functools.partial(tables_kernel, regions),
        "tables",
        [f32(2 * ENTRIES, TABLE_ROWS, LANES)],
        [where_ref, gathered],
        [scratch(2, 32 * SUB, LANES), scratch(LANES, 2 * LANES)],
    )

    f0 = None
    for cycle in range(CYCLES):
        outs = [f32(*padded(T0, 0)), f32(*padded(T1, 1)), f32(*plain(T1)), f32(*padded(T1, 1)),
                f32(2, 2 * FIELDS, SUB, LANES)]
        temps = [scratch(*padded(T0, 0)), scratch(*padded(T1, 1)), scratch(*plain(T1))]
        if cycle == 0:
            v0, v1, s1, c1, own, f0 = call(
                functools.partial(down_kernel, True), "down_fresh", outs + [f32(*plain(T0))],
                [where_ref, state, force, got_a, got_b, table], temps,
            )
        else:
            v0, v1, s1, c1, own = call(
                functools.partial(down_kernel, False), "down", outs,
                [where_ref, state, got_a, got_b, f0, table], temps,
            )
        beside = swap_a(own)
        row = jnp.concatenate([beside[1:], own, beside[:1]], axis=0)
        far = swap_b(lax.dynamic_slice_in_dim(row, 1 - odd, 3, axis=0))
        beyond = swap_a(far)
        operands = [where_ref, own, beside, far, beyond, v0, f0, v1, s1, c1, table]
        temps = [scratch(*padded(T0, 0))] * 2 + [scratch(*padded(T1, 1))] * 2
        temps += [scratch(*padded(T2, 2)), scratch(*plain(T2)), scratch(*plain(T2)), scratch(*padded(T2, 2)), scratch(*padded(T2, 2))]
        temps += [scratch(*padded(T3, 3)), scratch(*plain(T3)), scratch(*plain(T3)), scratch(*padded(T3, 3)), scratch(*padded(T3, 3))]
        if cycle == CYCLES - 1:
            return call(
                functools.partial(up_kernel, True), "up_last",
                [f32(FIELDS, OWN, SUB * LANES)], operands,
                [pltpu.VMEM((3 * FIELDS * OWN, SUB * LANES), jnp.bfloat16)] + temps,
            )[0]
        state, send_a, send_b = call(
            functools.partial(up_kernel, False), "up",
            [f32(FIELDS, OWN * SUB, LANES)] + [f32(FIELDS, FINE_HALO * SUB, LANES)] * 2,
            operands, temps,
        )
        got_b, got_a = swap_b(send_b), swap_a(send_a)


def solution(mesh):
    placed = (
        P("sample", "axial", None),
        P("sample", "axial", None),
        P("sample", "axial"),
        P("axial", None),
    )
    return jax.shard_map(
        per_device,
        mesh=mesh,
        in_specs=placed,
        out_specs=P("sample", "axial", None),
        check_vma=False,
    )
```

time: 151 us -> 108 us (0.72)
  the two profiles are of different devices: /device:TPU:17 before, /device:TPU:11 now
where the time goes in v3:
time: 108 us; the launch traced here: 107 us
  Pallas kernels  37.6 us (35%)
  waiting for transfers between devices  35.6 us (33%)
  starting transfers between devices  19.9 us (18%)
  local copies, waits for them, and re-layouts  13 us (12%)
    pallas_call x6, Pallas kernels, call(): pl.pallas_call(kernel, out_shape=outs, in_specs=[SMEM] + [VMEM] * (len(op...  37.6 us
    ppermute x4, waiting for transfers between devices, per_device(): swap_b = lambda x: lax.ppermute(x, 'axial', pair_b)  25.1 us
    ppermute x4, starting transfers between devices, per_device(): swap_b = lambda x: lax.ppermute(x, 'axial', pair_b)  12 us
    unnamed x20, local copies, waits for them, and re-layouts  11 us
    ppermute x4, waiting for transfers between devices, per_device(): gathered = gathered + lax.ppermute(gathered, 'axial', swap)  5.24 us
    ppermute x6, waiting for transfers between devices, per_device(): swap_a = lambda x: lax.ppermute(x, 'axial', pair_a)  5.21 us
    ppermute x4, starting transfers between devices, per_device(): gathered = gathered + lax.ppermute(gathered, 'axial', swap)  4.53 us
    ppermute x6, starting transfers between devices, per_device(): swap_a = lambda x: lax.ppermute(x, 'axial', pair_a)  3.35 us
  transfers between devices with their start and end apart: 14, of which 11 were waited for; matrix products, arithmetic and copies ran while one was open for 0% of the time, Pallas kernels for 5%

profile of v3, /device:TPU:11, one launch (start us, length us, event | category | flops | bytes accessed | tf_op | source)
XLA Modules:
  0.0 107.1 jit_solution(3837524111221672980)
XLA Ops:
  0.7 1.5 %dynamic_update_slice.6 = f32[96,128]{1,0:T(8,128)S(1)} dynamic-update-slice(f32[96,128]{1,0:T(8,128)S(1)} %broadcast_in_dim.3, f32[4,25]{1,0:T(4,128)} %bitcast.4, s32[]{:T(128)S(6)} %select_n.28, s32[]{:T(128)} %constant.46.clone.1) | dynamic-update-slice | bytes 804 | tf_op jit(solution)/shard_map/dynamic_update_slice | solution.py:582
  4.3 1.4 %collective-permute-start.1 = (f32[96,128]{1,0:T(8,128)S(1)}, f32[96,128]{1,0:T(8,128)S(1)}, u32[]{:S(2)}, u32[]{:S(2)}) collective-permute-start(f32[96,128]{1,0:T(8,128)S(1)} %add.40), channel_id=1, source_target_pairs={{0,2},{1,3},{2,0},{3,1},{4,6},{5,7},{6,4},{7,5},{8,10},{9,11},{10,... | collective-permute-start | bytes 147464 | tf_op jit(solution)/shard_map/ppermute | solution.py:591
  5.6 1.6 %collective-permute-done.1 = f32[96,128]{1,0:T(8,128)S(1)} collective-permute-done((f32[96,128]{1,0:T(8,128)S(1)}, f32[96,128]{1,0:T(8,128)S(1)}, u32[]{:S(2)}, u32[]{:S(2)}) %collective-permute-start.1) | collective-permute-done | bytes 49184 | tf_op jit(solution)/shard_map/ppermute | solution.py:591
  7.4 2.8 %collective-permute-done.2 = f32[96,128]{1,0:T(8,128)S(1)} collective-permute-done((f32[96,128]{1,0:T(8,128)S(1)}, f32[96,128]{1,0:T(8,128)S(1)}, u32[]{:S(2)}, u32[]{:S(2)}) %collective-permute-start.2) | collective-permute-done | bytes 49184 | tf_op jit(solution)/shard_map/ppermute | solution.py:591
  10.2 2.3 %collective-permute-start.3 = (f32[96,128]{1,0:T(8,128)S(1)}, f32[96,128]{1,0:T(8,128)S(1)}, u32[]{:S(2)}, u32[]{:S(2)}) collective-permute-start(f32[96,128]{1,0:T(8,128)S(1)} %add.42), channel_id=1, source_target_pairs={{0,8},{1,9},{2,10},{3,11},{4,12},{5,13},{6,14},{7,15},{8,0},{9,1},... | collective-permute-start | bytes 147464 | tf_op jit(solution)/shard_map/ppermute | solution.py:591
  12.6 1.1 %copy-done.8 = f32[5,32,1024]{2,1,0:T(8,128)S(1)} copy-done((f32[5,32,1024]{2,1,0:T(8,128)S(1)}, f32[5,32,1024]{2,1,0:T(8,128)}, u32[]{:S(2)}) %copy-start.8) | copy-done | bytes 655384
  13.7 1.1 %copy-done.9 = f32[5,32,1024]{2,1,0:T(8,128)S(1)} copy-done((f32[5,32,1024]{2,1,0:T(8,128)S(1)}, f32[5,32,1024]{2,1,0:T(8,128)}, u32[]{:S(2)}) %copy-start.9) | copy-done | bytes 655384
  14.8 3.6 %split.1 = (f32[5,256,128]{2,1,0:T(8,128)S(1)}, f32[5,256,128]{2,1,0:T(8,128)S(1)}, f32[10,88,128]{2,1,0:T(8,128)S(1)}, f32[10,88,128]{2,1,0:T(8,128)S(1)}) custom-call(s32[2]{0:T(128)S(1)} %pad_add_fusion.where_ref.refs_0_, f32[5,32,1024]{2,1,0:T(8,128)S(1)} %copy-done.8, f32[5,32,1024]{2,1,0:T(8,128)S(1)} %copy-done.9), custom_call_target="tpu_custom_call" | custom-call | tf_op jit(solution)/shard_map/split/pallas_call | solution.py:555
  18.4 3.1 %collective-permute-start.4 = (f32[10,88,128]{2,1,0:T(8,128)S(1)}, f32[10,88,128]{2,1,0:T(8,128)S(1)}, u32[]{:S(2)}, u32[]{:S(2)}) collective-permute-start(f32[10,88,128]{2,1,0:T(8,128)S(1)} %get-tuple-element.30), channel_id=1, source_target_pairs={{0,1},{1,0},{2,3},{3,2},{4,5},{5,4},{6,7},{7,6},{8,9},{9,8},{10,11... | collective-permute-start | bytes 1351688 | tf_op jit(solution)/shard_map/ppermute | solution.py:575
  21.5 3.2 %collective-permute-start.5 = (f32[10,88,128]{2,1,0:T(8,128)S(1)}, f32[10,88,128]{2,1,0:T(8,128)S(1)}, u32[]{:S(2)}, u32[]{:S(2)}) collective-permute-start(f32[10,88,128]{2,1,0:T(8,128)S(1)} %get-tuple-element.31), channel_id=1, source_target_pairs={{1,2},{2,1},{3,4},{4,3},{5,6},{6,5},{7,8},{8,7},{9,10},{10,9},{11,... | collective-permute-start | bytes 1351688 | tf_op jit(solution)/shard_map/ppermute | solution.py:576
  24.7 2.0 %tables.1.refs_5_.refs_10_ = f32[50,160,128]{2,1,0:T(8,128)S(1)} custom-call(s32[2]{0:T(128)S(1)} %pad_add_fusion.where_ref.refs_0_, f32[96,128]{1,0:T(8,128)S(1)} %add.43.regions_ref), custom_call_target="tpu_custom_call" | custom-call | tf_op jit(solution)/shard_map/tables/pallas_call | solution.py:555
  26.7 9.3 %collective-permute-done.5.refs_4_ = f32[10,88,128]{2,1,0:T(8,128)S(1)} collective-permute-done((f32[10,88,128]{2,1,0:T(8,128)S(1)}, f32[10,88,128]{2,1,0:T(8,128)S(1)}, u32[]{:S(2)}, u32[]{:S(2)}) %collective-permute-start.5) | collective-permute-done | bytes 450592 | tf_op jit(solution)/shard_map/ppermute | solution.py:576
  36.0 6.0 %down_fresh.1 = (f32[5,720,128]{2,1,0:T(8,128)S(1)}, f32[5,480,128]{2,1,0:T(8,128)S(1)}, f32[5,32,8,128]{3,2,1,0:T(8,128)S(1)}, f32[5,480,128]{2,1,0:T(8,128)S(1...) custom-call(s32[2]{0:T(128)S(1)} %pad_add_fusion.where_ref.refs_0_, ...), custom_call_target="tpu_custom_call" | custom-call | tf_op jit(solution)/shard_map/down_fresh/pallas_call | solution.py:555
  42.1 1.1 %copy-done.2 = f32[5,480,128]{2,1,0:T(8,128)} copy-done((f32[5,480,128]{2,1,0:T(8,128)}, f32[5,480,128]{2,1,0:T(8,128)S(1)}, u32[]{:S(2)}) %copy-start.2) | copy-done | bytes 1228824
  43.2 1.0 copy-done.4
  45.1 1.3 %collective-permute-done.6.refs_2_ = f32[2,10,8,128]{3,2,1,0:T(8,128)S(1)} collective-permute-done((f32[2,10,8,128]{3,2,1,0:T(8,128)S(1)}, f32[2,10,8,128]{3,2,1,0:T(8,128)S(1)}, u32[]{:S(2)}, u32[]{:S(2)}) %collective-permute-start.6) | collective-permute-done | bytes 81952 | tf_op jit(solution)/shard_map/ppermute | solution.py:575
  46.4 3.2 %collective-permute-start.7 = (f32[3,10,8,128]{3,2,1,0:T(8,128)S(1)}, f32[3,10,8,128]{3,2,1,0:T(8,128)S(1)}, u32[]{:S(2)}, u32[]{:S(2)}) collective-permute-start(f32[3,10,8,128]{3,2,1,0:T(8,128)S(1)} %fusion.3), channel_id=1, source_target_pairs={{1,2},{2,1},{3,4},{4,3},{5,6},{6,5},{7,8},{8,7},{9,10},{10,9},{11,... | collective-permute-start | bytes 368648 | tf_op jit(solution)/shard_map/ppermute | solution.py:576
  49.6 4.3 %collective-permute-done.7.refs_3_ = f32[3,10,8,128]{3,2,1,0:T(8,128)S(1)} collective-permute-done((f32[3,10,8,128]{3,2,1,0:T(8,128)S(1)}, f32[3,10,8,128]{3,2,1,0:T(8,128)S(1)}, u32[]{:S(2)}, u32[]{:S(2)}) %collective-permute-start.7) | collective-permute-done | bytes 122912 | tf_op jit(solution)/shard_map/ppermute | solution.py:576
  53.9 1.3 %collective-permute-done.8.refs_4_ = f32[3,10,8,128]{3,2,1,0:T(8,128)S(1)} collective-permute-done((f32[3,10,8,128]{3,2,1,0:T(8,128)S(1)}, f32[3,10,8,128]{3,2,1,0:T(8,128)S(1)}, u32[]{:S(2)}, u32[]{:S(2)}) %collective-permute-start.8) | collective-permute-done | bytes 122912 | tf_op jit(solution)/shard_map/ppermute | solution.py:575
  55.2 2.2 %copy-done.1 = f32[50,160,128]{2,1,0:T(8,128)S(1)} copy-done((f32[50,160,128]{2,1,0:T(8,128)S(1)}, f32[50,160,128]{2,1,0:T(8,128)}, u32[]{:S(2)}) %copy-start.1) | copy-done | bytes 4096024
  57.4 1.3 %copy-done.3 = f32[5,480,128]{2,1,0:T(8,128)S(1)} copy-done((f32[5,480,128]{2,1,0:T(8,128)S(1)}, f32[5,480,128]{2,1,0:T(8,128)}, u32[]{:S(2)}) %copy-start.3) | copy-done | bytes 1228824
  58.7 1.3 %copy-done.5 = f32[5,480,128]{2,1,0:T(8,128)S(1)} copy-done((f32[5,480,128]{2,1,0:T(8,128)S(1)}, f32[5,480,128]{2,1,0:T(8,128)}, u32[]{:S(2)}) %copy-start.5) | copy-done | bytes 1228824
  60.0 1.1 %copy-done.7 = f32[5,32,8,128]{3,2,1,0:T(8,128)S(1)} copy-done((f32[5,32,8,128]{3,2,1,0:T(8,128)S(1)}, f32[5,32,8,128]{3,2,1,0:T(8,128)}, u32[]{:S(2)}) %copy-start.7) | copy-done | bytes 655384
  61.1 8.8 %up.1 = (f32[5,256,128]{2,1,0:T(8,128)S(1)}, f32[5,88,128]{2,1,0:T(8,128)S(1)}, f32[5,88,128]{2,1,0:T(8,128)S(1)}) custom-call(s32[2]{0:T(128)S(1)} %pad_add_fusion.where_ref.refs_0_, f32[2,10,8,128]{3,2,1,0:T(8,128)S(1)} %get-tuple-element.33.refs_1_, f32[2,10,8,128]{3,2,1,0:T(8,128)S(1)} %collective-permute-done.6.refs_2_, ...), custom_call_target="tpu_custom_call" | custom-call | tf_op jit(solution)/shard_map/up/pallas_call | solution.py:555
  70.1 2.8 %collective-permute-start.10 = (f32[5,88,128]{2,1,0:T(8,128)S(1)}, f32[5,88,128]{2,1,0:T(8,128)S(1)}, u32[]{:S(2)}, u32[]{:S(2)}) collective-permute-start(f32[5,88,128]{2,1,0:T(8,128)S(1)} %get-tuple-element.41), channel_id=1, source_target_pairs={{1,2},{2,1},{3,4},{4,3},{5,6},{6,5},{7,8},{8,7},{9,10},{10,9},{11,... | collective-permute-start | bytes 675848 | tf_op jit(solution)/shard_map/ppermute | solution.py:576
  72.9 6.8 %collective-permute-done.10.refs_3_ = f32[5,88,128]{2,1,0:T(8,128)S(1)} collective-permute-done((f32[5,88,128]{2,1,0:T(8,128)S(1)}, f32[5,88,128]{2,1,0:T(8,128)S(1)}, u32[]{:S(2)}, u32[]{:S(2)}) %collective-permute-start.10) | collective-permute-done | bytes 225312 | tf_op jit(solution)/shard_map/ppermute | solution.py:576
  79.8 5.8 %down.1 = (f32[5,720,128]{2,1,0:T(8,128)S(1)}, f32[5,480,128]{2,1,0:T(8,128)S(1)}, f32[5,32,8,128]{3,2,1,0:T(8,128)S(1)}, f32[5,480,128]{2,1,0:T(8,128)S(1)}, f32[2,10,8,128]{3,2,1,0:T(8,128)S(1)}) custom-call(s32[2]{0:T(128)S(1)} %pad_add_fusion.where_ref.refs_0_, f32[5,256,128]{2,1,0:T(8,128)S(1)} %get-tuple-element.39.refs_1_, ...), custom_call_target="tpu_custom_call" | custom-call | tf_op jit(solution)/shard_map/down/pallas_call | solution.py:555
  85.7 1.3 %collective-permute-done.11.refs_2_ = f32[2,10,8,128]{3,2,1,0:T(8,128)S(1)} collective-permute-done((f32[2,10,8,128]{3,2,1,0:T(8,128)S(1)}, f32[2,10,8,128]{3,2,1,0:T(8,128)S(1)}, u32[]{:S(2)}, u32[]{:S(2)}) %collective-permute-start.11) | collective-permute-done | bytes 81952 | tf_op jit(solution)/shard_map/ppermute | solution.py:575
  86.9 2.8 %collective-permute-start.12 = (f32[3,10,8,128]{3,2,1,0:T(8,128)S(1)}, f32[3,10,8,128]{3,2,1,0:T(8,128)S(1)}, u32[]{:S(2)}, u32[]{:S(2)}) collective-permute-start(f32[3,10,8,128]{3,2,1,0:T(8,128)S(1)} %fusion.1), channel_id=1, source_target_pairs={{1,2},{2,1},{3,4},{4,3},{5,6},{6,5},{7,8},{8,7},{9,10},{10,9},{11,... | collective-permute-start | bytes 368648 | tf_op jit(solution)/shard_map/ppermute | solution.py:576
  89.8 4.7 %collective-permute-done.12.refs_3_ = f32[3,10,8,128]{3,2,1,0:T(8,128)S(1)} collective-permute-done((f32[3,10,8,128]{3,2,1,0:T(8,128)S(1)}, f32[3,10,8,128]{3,2,1,0:T(8,128)S(1)}, u32[]{:S(2)}, u32[]{:S(2)}) %collective-permute-start.12) | collective-permute-done | bytes 122912 | tf_op jit(solution)/shard_map/ppermute | solution.py:576
  94.5 1.3 %collective-permute-done.13.refs_4_ = f32[3,10,8,128]{3,2,1,0:T(8,128)S(1)} collective-permute-done((f32[3,10,8,128]{3,2,1,0:T(8,128)S(1)}, f32[3,10,8,128]{3,2,1,0:T(8,128)S(1)}, u32[]{:S(2)}, u32[]{:S(2)}) %collective-permute-start.13) | collective-permute-done | bytes 122912 | tf_op jit(solution)/shard_map/ppermute | solution.py:575
  95.8 11.3 %up_last.1 = f32[5,32,1024]{2,1,0:T(8,128)} custom-call(s32[2]{0:T(128)S(1)} %pad_add_fusion.where_ref.refs_0_, f32[2,10,8,128]{3,2,1,0:T(8,128)S(1)} %get-tuple-element.42.refs_1_, f32[2,10,8,128]{3,2,1,0:T(8,128)S(1)} %collective-permute-done.11.refs_2_, f32[3,10,8,128]{3,2,1,0:T(8,128)S(1)} %collective-permute-done.12.refs_3_, ...), custom_call_target="tpu_custom_call" | custom-call | tf_op jit(solution)/shard_map/up_last/pallas_call | solution.py:555
  (35 shorter events, 4.3 us)
Async XLA Ops:
  2.8 1.5 %collective-permute-start = (f32[96,128]{1,0:T(8,128)S(1)}, f32[96,128]{1,0:T(8,128)S(1)}, u32[]{:S(2)}, u32[]{:S(2)}) collective-permute-start(f32[96,128]{1,0:T(8,128)S(1)} %dynamic_update_slice.7), channel_id=1, source_target_pairs={{0,1},{1,0},{2,3},{3,2},{4,5},{5,4},{6,7},{7,6},{8,9},{9,8},{10,11... | collective-permute-start | bytes 147464 | tf_op jit(solution)/shard_map/ppermute | solution.py:591
  4.3 2.9 %collective-permute-start.1 = (f32[96,128]{1,0:T(8,128)S(1)}, f32[96,128]{1,0:T(8,128)S(1)}, u32[]{:S(2)}, u32[]{:S(2)}) collective-permute-start(f32[96,128]{1,0:T(8,128)S(1)} %add.40), channel_id=1, source_target_pairs={{0,2},{1,3},{2,0},{3,1},{4,6},{5,7},{6,4},{7,5},{8,10},{9,11},{10,... | collective-permute-start | bytes 147464 | tf_op jit(solution)/shard_map/ppermute | solution.py:591
  7.2 3.0 %collective-permute-start.2 = (f32[96,128]{1,0:T(8,128)S(1)}, f32[96,128]{1,0:T(8,128)S(1)}, u32[]{:S(2)}, u32[]{:S(2)}) collective-permute-start(f32[96,128]{1,0:T(8,128)S(1)} %add.41), channel_id=1, source_target_pairs={{0,4},{1,5},{2,6},{3,7},{4,0},{5,1},{6,2},{7,3},{8,12},{9,13},{10,... | collective-permute-start | bytes 147464 | tf_op jit(solution)/shard_map/ppermute | solution.py:591
  10.2 8.2 %collective-permute-start.3 = (f32[96,128]{1,0:T(8,128)S(1)}, f32[96,128]{1,0:T(8,128)S(1)}, u32[]{:S(2)}, u32[]{:S(2)}) collective-permute-start(f32[96,128]{1,0:T(8,128)S(1)} %add.42), channel_id=1, source_target_pairs={{0,8},{1,9},{2,10},{3,11},{4,12},{5,13},{6,14},{7,15},{8,0},{9,1},... | collective-permute-start | bytes 147464 | tf_op jit(solution)/shard_map/ppermute | solution.py:591
  12.6 1.1 %copy-start.8 = (f32[5,32,1024]{2,1,0:T(8,128)S(1)}, f32[5,32,1024]{2,1,0:T(8,128)}, u32[]{:S(2)}) copy-start(f32[5,32,1024]{2,1,0:T(8,128)} %state_ref.1) | copy-start | bytes 1966084
  13.7 1.1 %copy-start.9 = (f32[5,32,1024]{2,1,0:T(8,128)S(1)}, f32[5,32,1024]{2,1,0:T(8,128)}, u32[]{:S(2)}) copy-start(f32[5,32,1024]{2,1,0:T(8,128)} %forcing_ref.1) | copy-start | bytes 1966084
  18.4 8.3 %collective-permute-start.4 = (f32[10,88,128]{2,1,0:T(8,128)S(1)}, f32[10,88,128]{2,1,0:T(8,128)S(1)}, u32[]{:S(2)}, u32[]{:S(2)}) collective-permute-start(f32[10,88,128]{2,1,0:T(8,128)S(1)} %get-tuple-element.30), channel_id=1, source_target_pairs={{0,1},{1,0},{2,3},{3,2},{4,5},{5,4},{6,7},{7,6},{8,9},{9,8},{10,11... | collective-permute-start | bytes 1351688 | tf_op jit(solution)/shard_map/ppermute | solution.py:575
  21.5 14.5 %collective-permute-start.5 = (f32[10,88,128]{2,1,0:T(8,128)S(1)}, f32[10,88,128]{2,1,0:T(8,128)S(1)}, u32[]{:S(2)}, u32[]{:S(2)}) collective-permute-start(f32[10,88,128]{2,1,0:T(8,128)S(1)} %get-tuple-element.31), channel_id=1, source_target_pairs={{1,2},{2,1},{3,4},{4,3},{5,6},{6,5},{7,8},{8,7},{9,10},{10,9},{11,... | collective-permute-start | bytes 1351688 | tf_op jit(solution)/shard_map/ppermute | solution.py:576
  26.7 15.4 %copy-start = (f32[50,160,128]{2,1,0:T(8,128)}, f32[50,160,128]{2,1,0:T(8,128)S(1)}, u32[]{:S(2)}) copy-start(f32[50,160,128]{2,1,0:T(8,128)S(1)} %tables.1.refs_5_.refs_10_) | copy-start | bytes 12288004
  42.1 1.1 %copy-start.2 = (f32[5,480,128]{2,1,0:T(8,128)}, f32[5,480,128]{2,1,0:T(8,128)S(1)}, u32[]{:S(2)}) copy-start(f32[5,480,128]{2,1,0:T(8,128)S(1)} %get-tuple-element.36.refs_7_) | copy-start | bytes 3686404
  43.2 1.0 copy-start.4
  44.2 0.8 copy-start.6
  45.1 1.3 %collective-permute-start.6 = (f32[2,10,8,128]{3,2,1,0:T(8,128)S(1)}, f32[2,10,8,128]{3,2,1,0:T(8,128)S(1)}, u32[]{:S(2)}, u32[]{:S(2)}) collective-permute-start(f32[2,10,8,128]{3,2,1,0:T(8,128)S(1)} %get-tuple-element.33.refs_1_), channel_id=1, source_target_pairs={{0,1},{1,0},{2,3},{3,2},{4,5},{5,4},{6,7},{7,6},{8,9},{9,8},{10,11... | collective-permute-start | bytes 245768 | tf_op jit(solution)/shard_map/ppermute | solution.py:575
  46.4 7.5 %collective-permute-start.7 = (f32[3,10,8,128]{3,2,1,0:T(8,128)S(1)}, f32[3,10,8,128]{3,2,1,0:T(8,128)S(1)}, u32[]{:S(2)}, u32[]{:S(2)}) collective-permute-start(f32[3,10,8,128]{3,2,1,0:T(8,128)S(1)} %fusion.3), channel_id=1, source_target_pairs={{1,2},{2,1},{3,4},{4,3},{5,6},{6,5},{7,8},{8,7},{9,10},{10,9},{11,... | collective-permute-start | bytes 368648 | tf_op jit(solution)/shard_map/ppermute | solution.py:576
  53.9 1.3 %collective-permute-start.8 = (f32[3,10,8,128]{3,2,1,0:T(8,128)S(1)}, f32[3,10,8,128]{3,2,1,0:T(8,128)S(1)}, u32[]{:S(2)}, u32[]{:S(2)}) collective-permute-start(f32[3,10,8,128]{3,2,1,0:T(8,128)S(1)} %collective-permute-done.7.refs_3_), channel_id=1, source_target_pairs={{0,1},{1,0},{2,3},{3,2},{4,5},{5,4},{6,7},{7,6},{8,9},{9,8},{10,11... | collective-permute-start | bytes 368648 | tf_op jit(solution)/shard_map/ppermute | solution.py:575
  55.2 2.2 %copy-start.1 = (f32[50,160,128]{2,1,0:T(8,128)S(1)}, f32[50,160,128]{2,1,0:T(8,128)}, u32[]{:S(2)}) copy-start(f32[50,160,128]{2,1,0:T(8,128)} %copy-done) | copy-start | bytes 12288004
  57.4 1.3 %copy-start.3 = (f32[5,480,128]{2,1,0:T(8,128)S(1)}, f32[5,480,128]{2,1,0:T(8,128)}, u32[]{:S(2)}) copy-start(f32[5,480,128]{2,1,0:T(8,128)} %copy-done.2) | copy-start | bytes 3686404
  58.7 1.3 %copy-start.5 = (f32[5,480,128]{2,1,0:T(8,128)S(1)}, f32[5,480,128]{2,1,0:T(8,128)}, u32[]{:S(2)}) copy-start(f32[5,480,128]{2,1,0:T(8,128)} %copy-done.4) | copy-start | bytes 3686404
  60.0 1.1 %copy-start.7 = (f32[5,32,8,128]{3,2,1,0:T(8,128)S(1)}, f32[5,32,8,128]{3,2,1,0:T(8,128)}, u32[]{:S(2)}) copy-start(f32[5,32,8,128]{3,2,1,0:T(8,128)} %copy-done.6) | copy-start | bytes 1966084
  69.9 3.1 %collective-permute-start.9 = (f32[5,88,128]{2,1,0:T(8,128)S(1)}, f32[5,88,128]{2,1,0:T(8,128)S(1)}, u32[]{:S(2)}, u32[]{:S(2)}) collective-permute-start(f32[5,88,128]{2,1,0:T(8,128)S(1)} %get-tuple-element.40), channel_id=1, source_target_pairs={{0,1},{1,0},{2,3},{3,2},{4,5},{5,4},{6,7},{7,6},{8,9},{9,8},{10,11... | collective-permute-start | bytes 675848 | tf_op jit(solution)/shard_map/ppermute | solution.py:575
  70.1 9.7 %collective-permute-start.10 = (f32[5,88,128]{2,1,0:T(8,128)S(1)}, f32[5,88,128]{2,1,0:T(8,128)S(1)}, u32[]{:S(2)}, u32[]{:S(2)}) collective-permute-start(f32[5,88,128]{2,1,0:T(8,128)S(1)} %get-tuple-element.41), channel_id=1, source_target_pairs={{1,2},{2,1},{3,4},{4,3},{5,6},{6,5},{7,8},{8,7},{9,10},{10,9},{11,... | collective-permute-start | bytes 675848 | tf_op jit(solution)/shard_map/ppermute | solution.py:576
  85.6 1.3 %collective-permute-start.11 = (f32[2,10,8,128]{3,2,1,0:T(8,128)S(1)}, f32[2,10,8,128]{3,2,1,0:T(8,128)S(1)}, u32[]{:S(2)}, u32[]{:S(2)}) collective-permute-start(f32[2,10,8,128]{3,2,1,0:T(8,128)S(1)} %get-tuple-element.42.refs_1_), channel_id=1, source_target_pairs={{0,1},{1,0},{2,3},{3,2},{4,5},{5,4},{6,7},{7,6},{8,9},{9,8},{10,11... | collective-permute-start | bytes 245768 | tf_op jit(solution)/shard_map/ppermute | solution.py:575
  86.9 7.5 %collective-permute-start.12 = (f32[3,10,8,128]{3,2,1,0:T(8,128)S(1)}, f32[3,10,8,128]{3,2,1,0:T(8,128)S(1)}, u32[]{:S(2)}, u32[]{:S(2)}) collective-permute-start(f32[3,10,8,128]{3,2,1,0:T(8,128)S(1)} %fusion.1), channel_id=1, source_target_pairs={{1,2},{2,1},{3,4},{4,3},{5,6},{6,5},{7,8},{8,7},{9,10},{10,9},{11,... | collective-permute-start | bytes 368648 | tf_op jit(solution)/shard_map/ppermute | solution.py:576
  94.5 1.3 %collective-permute-start.13 = (f32[3,10,8,128]{3,2,1,0:T(8,128)S(1)}, f32[3,10,8,128]{3,2,1,0:T(8,128)S(1)}, u32[]{:S(2)}, u32[]{:S(2)}) collective-permute-start(f32[3,10,8,128]{3,2,1,0:T(8,128)S(1)} %collective-permute-done.12.refs_3_), channel_id=1, source_target_pairs={{0,1},{1,0},{2,3},{3,2},{4,5},{5,4},{6,7},{7,6},{8,9},{9,8},{10,11... | collective-permute-start | bytes 368648 | tf_op jit(solution)/shard_map/ppermute | solution.py:575

commit v4 on v3

--- a/solution.py
+++ b/solution.py
@@ -233,6 +233,29 @@
 
 def dot(left, right):
     return jnp.dot(left, right, preferred_element_type=jnp.float32)
+
+
+def prep_kernel(share, where_ref, coefficients_ref, ids_ref, out, own_coefficients, own_ids, sems):
+    device, devices = where_ref[0], where_ref[1]
+    copies = [
+        pltpu.make_async_copy(coefficients_ref, own_coefficients, sems.at[0]),
+        pltpu.make_async_copy(ids_ref, own_ids, sems.at[1]),
+    ]
+    for copy in copies:
+        copy.start()
+    out[...] = jnp.zeros_like(out)
+    for copy in copies:
+        copy.wait()
+    for i in range(share):
+        out[pl.ds(device * share + i, 1), 0:ENTRIES] = own_coefficients[i : i + 1, :]
+    ids = own_ids[...].astype(jnp.float32)
+    per_tile = LANES // OWN
+    start = pl.multiple_of(devices * share + device // per_tile * SUB, SUB)
+    for place in range(per_tile):
+
+        @pl.when(device % per_tile == place)
+        def _():
+            out[pl.ds(start, SUB), place * OWN : (place + 1) * OWN] = ids
 
 
 def tables_kernel(regions, where_ref, regions_ref, table, mats, parts):
@@ -343,12 +366,19 @@
     return (into == wanted).astype(jnp.float32).astype(jnp.bfloat16)
 
 
-def split_kernel(where_ref, state_ref, forcing_ref, state_rows, forcing_rows, send_a, send_b, parts):
+def split_kernel(where_ref, state_ref, forcing_ref, state_rows, forcing_rows, send_a, send_b, parts, held_in, sems):
+    copies = [
+        pltpu.make_async_copy(source, held_in.at[i], sems.at[i])
+        for i, source in enumerate((state_ref, forcing_ref))
+    ]
+    for copy in copies:
+        copy.start()
     odd = where_ref[0] % 2
     held = 2 * FIELDS * OWN
-    for which, source in enumerate((state_ref, forcing_ref)):
-        for field in range(FIELDS):
-            for p, part in enumerate(three_parts(source[field])):
+    for which, copy in enumerate(copies):
+        copy.wait()
+        for field in range(FIELDS):
+            for p, part in enumerate(three_parts(held_in[which, field])):
                 start = p * held + (which * FIELDS + field) * OWN
                 parts[start : start + OWN, :] = part
 
@@ -531,8 +561,16 @@
     rows_loop(0, FINE_HALO, edge)
 
 
+def relay_kernel(where_ref, own, beside, row):
+    odd = where_ref[0] % 2
+    row[odd] = own[0]
+    row[odd + 1] = own[1]
+    row[2 - 2 * odd] = beside[odd]
+
+
 VMEM = pl.BlockSpec(memory_space=pltpu.VMEM)
 SMEM = pl.BlockSpec(memory_space=pltpu.SMEM)
+ANY = pl.BlockSpec(memory_space=pltpu.HBM)
 
 
 def f32(*shape):
@@ -551,15 +589,15 @@
     return (FIELDS, rows, SUB, LANES)
 
 
-def call(kernel, name, outs, operands, scratches=()):
+def call(kernel, name, grant, outs, operands, scratches=(), raw=False):
     return pl.pallas_call(
         kernel,
         out_shape=outs,
-        in_specs=[SMEM] + [VMEM] * (len(operands) - 1),
+        in_specs=[SMEM] + [ANY if raw else VMEM] * (len(operands) - 1),
         out_specs=[VMEM] * len(outs),
         scratch_shapes=list(scratches),
         name=name,
-        compiler_params=pltpu.CompilerParams(vmem_limit_bytes=28 * 1024 * 1024),
+        compiler_params=pltpu.CompilerParams(vmem_limit_bytes=grant * 1024 * 1024),
     )(*operands)
 
 
@@ -578,31 +616,47 @@
     share = coefficients.shape[1]
     regions = share * size
     per_tile = LANES // OWN
-    gathered = jnp.zeros((regions + SUB * -(-size // per_tile), LANES), jnp.float32)
-    gathered = lax.dynamic_update_slice(gathered, coefficients.T, (device * share, 0))
-    gathered = lax.dynamic_update_slice(
-        gathered,
-        region_ids.T.astype(jnp.float32),
-        (regions + device // per_tile * SUB, device % per_tile * OWN),
+    (gathered,) = call(
+        functools.partial(prep_kernel, share),
+        "prep",
+        4,
+        [f32(regions + SUB * -(-size // per_tile), LANES)],
+        [where_ref, coefficients.T, region_ids.T],
+        [
+            scratch(share, ENTRIES),
+            pltpu.VMEM((SUB, OWN), jnp.int32),
+            pltpu.SemaphoreType.DMA((2,)),
+        ],
+        True,
+    )
+
+    def doubled(held, step):
+        return held + lax.ppermute(held, "axial", [(i, i ^ step) for i in range(size)])
+
+    state, force, send_a, send_b = call(
+        split_kernel,
+        "split", 12,
+        [f32(FIELDS, OWN * SUB, LANES)] * 2 + [f32(2 * FIELDS, FINE_HALO * SUB, LANES)] * 2,
+        [where_ref, initial_state, forcing],
+        [
+            pltpu.VMEM((3 * 2 * FIELDS * OWN, SUB * LANES), jnp.bfloat16),
+            scratch(2, FIELDS, OWN, SUB * LANES),
+            pltpu.SemaphoreType.DMA((2,)),
+        ],
+        True,
     )
     step = 1
+    while step < min(size, 4):
+        gathered = doubled(gathered, step)
+        step *= 2
+    gathered, send_a, send_b = lax.optimization_barrier((gathered, send_a, send_b))
+    got_b, got_a = swap_b(send_b), swap_a(send_a)
     while step < size:
-        swap = [(i, i ^ step) for i in range(size)]
-        gathered = gathered + lax.ppermute(gathered, "axial", swap)
+        gathered = doubled(gathered, step)
         step *= 2
-
-    state, force, send_a, send_b = call(
-        split_kernel,
-        "split",
-        [f32(FIELDS, OWN * SUB, LANES)] * 2 + [f32(2 * FIELDS, FINE_HALO * SUB, LANES)] * 2,
-        [where_ref, initial_state, forcing],
-        [pltpu.VMEM((3 * 2 * FIELDS * OWN, SUB * LANES), jnp.bfloat16)],
-    )
-    send_a, send_b, gathered = lax.optimization_barrier((send_a, send_b, gathered))
-    got_b, got_a = swap_b(send_b), swap_a(send_a)
     (table,) = call(
         functools.partial(tables_kernel, regions),
-        "tables",
+        "tables", 12,
         [f32(2 * ENTRIES, TABLE_ROWS, LANES)],
         [where_ref, gathered],
         [scratch(2, 32 * SUB, LANES), scratch(LANES, 2 * LANES)],
@@ -615,17 +669,19 @@
         temps = [scratch(*padded(T0, 0)), scratch(*padded(T1, 1)), scratch(*plain(T1))]
         if cycle == 0:
             v0, v1, s1, c1, own, f0 = call(
-                functools.partial(down_kernel, True), "down_fresh", outs + [f32(*plain(T0))],
+                functools.partial(down_kernel, True), "down_fresh", 14, outs + [f32(*plain(T0))],
                 [where_ref, state, force, got_a, got_b, table], temps,
             )
         else:
             v0, v1, s1, c1, own = call(
-                functools.partial(down_kernel, False), "down", outs,
+                functools.partial(down_kernel, False), "down", 14, outs,
                 [where_ref, state, got_a, got_b, f0, table], temps,
             )
         beside = swap_a(own)
-        row = jnp.concatenate([beside[1:], own, beside[:1]], axis=0)
-        far = swap_b(lax.dynamic_slice_in_dim(row, 1 - odd, 3, axis=0))
+        (row,) = call(
+            relay_kernel, "relay", 2, [f32(3, 2 * FIELDS, SUB, LANES)], [where_ref, own, beside]
+        )
+        far = swap_b(row)
         beyond = swap_a(far)
         operands = [where_ref, own, beside, far, beyond, v0, f0, v1, s1, c1, table]
         temps = [scratch(*padded(T0, 0))] * 2 + [scratch(*padded(T1, 1))] * 2
@@ -633,12 +689,12 @@
         temps += [scratch(*padded(T3, 3)), scratch(*plain(T3)), scratch(*plain(T3)), scratch(*padded(T3, 3)), scratch(*padded(T3, 3))]
         if cycle == CYCLES - 1:
             return call(
-                functools.partial(up_kernel, True), "up_last",
+                functools.partial(up_kernel, True), "up_last", 26,
                 [f32(FIELDS, OWN, SUB * LANES)], operands,
                 [pltpu.VMEM((3 * FIELDS * OWN, SUB * LANES), jnp.bfloat16)] + temps,
             )[0]
         state, send_a, send_b = call(
-            functools.partial(up_kernel, False), "up",
+            functools.partial(up_kernel, False), "up", 26,
             [f32(FIELDS, OWN * SUB, LANES)] + [f32(FIELDS, FINE_HALO * SUB, LANES)] * 2,
             operands, temps,
         )

time: 108 us -> 94.1 us (0.87)
  the two profiles are of different devices: /device:TPU:11 before, /device:TPU:17 now
where the time goes in v4:
time: 94.1 us; the launch traced here: 93.7 us
  Pallas kernels  39.8 us (42%)
  waiting for transfers between devices  33.7 us (36%)
  starting transfers between devices  16.5 us (18%)
  local copies, waits for them, and re-layouts  3.54 us (4%)
    pallas_call x9, Pallas kernels, call(): pl.pallas_call(kernel, out_shape=outs, in_specs=[SMEM] + [ANY if raw else...  39.8 us
    ppermute x4, waiting for transfers between devices, per_device(): swap_b = lambda x: lax.ppermute(x, 'axial', pair_b)  21.7 us
    ppermute x4, starting transfers between devices, per_device(): swap_b = lambda x: lax.ppermute(x, 'axial', pair_b)  7.73 us
    ppermute x4, waiting for transfers between devices, doubled(): lax.ppermute(held, 'axial', [(i, i ^ step) for i in range(size)])  7.17 us
    ppermute x6, starting transfers between devices, per_device(): swap_a = lambda x: lax.ppermute(x, 'axial', pair_a)  5.34 us
    ppermute x6, waiting for transfers between devices, per_device(): swap_a = lambda x: lax.ppermute(x, 'axial', pair_a)  4.83 us
    unnamed x8, local copies, waits for them, and re-layouts  3.54 us
    ppermute x4, starting transfers between devices, doubled(): lax.ppermute(held, 'axial', [(i, i ^ step) for i in range(size)])  3.41 us
  transfers between devices with their start and end apart: 14, of which 11 were waited for; matrix products, arithmetic and copies ran while one was open for 0% of the time, Pallas kernels for 6%

profile of v4, /device:TPU:17, one launch (start us, length us, event | category | flops | bytes accessed | tf_op | source)
XLA Modules:
  0.0 93.7 jit_solution(7907326382892984853)
XLA Ops:
  0.1 0.7 copy-done.2
  0.8 0.7 copy-done.3
  1.4 0.6 prep.1
  2.1 0.7 collective-permute-start
  2.8 0.9 collective-permute-done
  3.7 1.3 %collective-permute-start.1 = (f32[96,128]{1,0:T(8,128)S(1)}, f32[96,128]{1,0:T(8,128)S(1)}, u32[]{:S(2)}, u32[]{:S(2)}) collective-permute-start(f32[96,128]{1,0:T(8,128)S(1)} %add.12), channel_id=1, source_target_pairs={{0,2},{1,3},{2,0},{3,1},{4,6},{5,7},{6,4},{7,5},{8,10},{9,11},{10,... | collective-permute-start | bytes 147464 | tf_op jit(solution)/shard_map/ppermute | solution.py:634
  5.0 1.1 %copy-done = f32[5,32,1024]{2,1,0:T(8,128)S(1)} copy-done((f32[5,32,1024]{2,1,0:T(8,128)S(1)}, f32[5,32,1024]{2,1,0:T(8,128)}, u32[]{:S(2)}) %copy-start) | copy-done | bytes 655384
  6.1 1.1 %copy-done.1 = f32[5,32,1024]{2,1,0:T(8,128)S(1)} copy-done((f32[5,32,1024]{2,1,0:T(8,128)S(1)}, f32[5,32,1024]{2,1,0:T(8,128)}, u32[]{:S(2)}) %copy-start.1) | copy-done | bytes 655384
  7.2 4.0 %split.1 = (f32[5,256,128]{2,1,0:T(8,128)S(1)}, f32[5,256,128]{2,1,0:T(8,128)S(1)}, f32[10,88,128]{2,1,0:T(8,128)S(1)}, f32[10,88,128]{2,1,0:T(8,128)S(1)}) custom-call(s32[2]{0:T(128)S(1)} %pad_add_fusion.where_ref.refs_0_, f32[5,32,1024]{2,1,0:T(8,128)S(1)} %copy-done, f32[5,32,1024]{2,1,0:T(8,128)S(1)} %copy-done.1), custom_call_target="tpu_custom_call" | custom-call | tf_op jit(solution)/shard_map/split/pallas_call | solution.py:593
  11.2 0.7 collective-permute-start.2
  12.0 2.0 %collective-permute-start.3 = (f32[10,88,128]{2,1,0:T(8,128)S(1)}, f32[10,88,128]{2,1,0:T(8,128)S(1)}, u32[]{:S(2)}, u32[]{:S(2)}) collective-permute-start(f32[10,88,128]{2,1,0:T(8,128)S(1)} %get-tuple-element.31), channel_id=1, source_target_pairs={{1,2},{2,1},{3,4},{4,3},{5,6},{6,5},{7,8},{8,7},{9,10},{10,9},{11,... | collective-permute-start | bytes 1351688 | tf_op jit(solution)/shard_map/ppermute | solution.py:614
  14.0 1.4 %collective-permute-start.4 = (f32[96,128]{1,0:T(8,128)S(1)}, f32[96,128]{1,0:T(8,128)S(1)}, u32[]{:S(2)}, u32[]{:S(2)}) collective-permute-start(f32[96,128]{1,0:T(8,128)S(1)} %add.13), channel_id=1, source_target_pairs={{0,4},{1,5},{2,6},{3,7},{4,0},{5,1},{6,2},{7,3},{8,12},{9,13},{10,... | collective-permute-start | bytes 147464 | tf_op jit(solution)/shard_map/ppermute | solution.py:634
  15.3 2.2 %collective-permute-done.4 = f32[96,128]{1,0:T(8,128)S(1)} collective-permute-done((f32[96,128]{1,0:T(8,128)S(1)}, f32[96,128]{1,0:T(8,128)S(1)}, u32[]{:S(2)}, u32[]{:S(2)}) %collective-permute-start.4) | collective-permute-done | bytes 49184 | tf_op jit(solution)/shard_map/ppermute | solution.py:634
  17.6 4.1 %collective-permute-done.5 = f32[96,128]{1,0:T(8,128)S(1)} collective-permute-done((f32[96,128]{1,0:T(8,128)S(1)}, f32[96,128]{1,0:T(8,128)S(1)}, u32[]{:S(2)}, u32[]{:S(2)}) %collective-permute-start.5) | collective-permute-done | bytes 49184 | tf_op jit(solution)/shard_map/ppermute | solution.py:634
  21.7 2.0 %tables.1.refs_5_.refs_10_ = f32[50,160,128]{2,1,0:T(8,128)S(1)} custom-call(s32[2]{0:T(128)S(1)} %pad_add_fusion.where_ref.refs_0_, f32[96,128]{1,0:T(8,128)S(1)} %add.15.regions_ref), custom_call_target="tpu_custom_call" | custom-call | tf_op jit(solution)/shard_map/tables/pallas_call | solution.py:593
  23.8 2.8 %collective-permute-done.3.refs_4_ = f32[10,88,128]{2,1,0:T(8,128)S(1)} collective-permute-done((f32[10,88,128]{2,1,0:T(8,128)S(1)}, f32[10,88,128]{2,1,0:T(8,128)S(1)}, u32[]{:S(2)}, u32[]{:S(2)}) %collective-permute-start.3) | collective-permute-done | bytes 450592 | tf_op jit(solution)/shard_map/ppermute | solution.py:614
  26.5 6.0 %down_fresh.1 = (f32[5,720,128]{2,1,0:T(8,128)S(1)}, f32[5,480,128]{2,1,0:T(8,128)S(1)}, f32[5,32,8,128]{3,2,1,0:T(8,128)S(1)}, f32[5,480,128]{2,1,0:T(8,128)S(1...) custom-call(s32[2]{0:T(128)S(1)} %pad_add_fusion.where_ref.refs_0_, ...), custom_call_target="tpu_custom_call" | custom-call | tf_op jit(solution)/shard_map/down_fresh/pallas_call | solution.py:593
  32.6 4.3 %collective-permute-start.6 = (f32[2,10,8,128]{3,2,1,0:T(8,128)S(1)}, f32[2,10,8,128]{3,2,1,0:T(8,128)S(1)}, u32[]{:S(2)}, u32[]{:S(2)}) collective-permute-start(f32[2,10,8,128]{3,2,1,0:T(8,128)S(1)} %get-tuple-element.33.own.refs_1_), channel_id=1, source_target_pairs={{0,1},{1,0},{2,3},{3,2},{4,5},{5,4},{6,7},{7,6},{8,9},{9,8},{10,11... | collective-permute-start | bytes 245768 | tf_op jit(solution)/shard_map/ppermute | solution.py:613
  36.8 0.9 collective-permute-done.6.beside.refs_2_
  38.3 1.9 %collective-permute-start.7 = (f32[3,10,8,128]{3,2,1,0:T(8,128)S(1)}, f32[3,10,8,128]{3,2,1,0:T(8,128)S(1)}, u32[]{:S(2)}, u32[]{:S(2)}) collective-permute-start(f32[3,10,8,128]{3,2,1,0:T(8,128)S(1)} %relay.2), channel_id=1, source_target_pairs={{1,2},{2,1},{3,4},{4,3},{5,6},{6,5},{7,8},{8,7},{9,10},{10,9},{11,... | collective-permute-start | bytes 368648 | tf_op jit(solution)/shard_map/ppermute | solution.py:614
  40.2 5.6 %collective-permute-done.7.refs_3_ = f32[3,10,8,128]{3,2,1,0:T(8,128)S(1)} collective-permute-done((f32[3,10,8,128]{3,2,1,0:T(8,128)S(1)}, f32[3,10,8,128]{3,2,1,0:T(8,128)S(1)}, u32[]{:S(2)}, u32[]{:S(2)}) %collective-permute-start.7) | collective-permute-done | bytes 122912 | tf_op jit(solution)/shard_map/ppermute | solution.py:614
  45.9 1.3 %collective-permute-done.8.refs_4_ = f32[3,10,8,128]{3,2,1,0:T(8,128)S(1)} collective-permute-done((f32[3,10,8,128]{3,2,1,0:T(8,128)S(1)}, f32[3,10,8,128]{3,2,1,0:T(8,128)S(1)}, u32[]{:S(2)}, u32[]{:S(2)}) %collective-permute-start.8) | collective-permute-done | bytes 122912 | tf_op jit(solution)/shard_map/ppermute | solution.py:613
  47.2 8.8 %up.1 = (f32[5,256,128]{2,1,0:T(8,128)S(1)}, f32[5,88,128]{2,1,0:T(8,128)S(1)}, f32[5,88,128]{2,1,0:T(8,128)S(1)}) custom-call(s32[2]{0:T(128)S(1)} %pad_add_fusion.where_ref.refs_0_, f32[2,10,8,128]{3,2,1,0:T(8,128)S(1)} %get-tuple-element.33.own.refs_1_, f32[2,10,8,128]{3,2,1,0:T(8,128)S(1)} %collective-permute-done.6.beside.refs_2_, ...), custom_call_target="tpu_custom_call" | custom-call | tf_op jit(solution)/shard_map/up/pallas_call | solution.py:593
  56.2 1.9 %collective-permute-start.10 = (f32[5,88,128]{2,1,0:T(8,128)S(1)}, f32[5,88,128]{2,1,0:T(8,128)S(1)}, u32[]{:S(2)}, u32[]{:S(2)}) collective-permute-start(f32[5,88,128]{2,1,0:T(8,128)S(1)} %get-tuple-element.41), channel_id=1, source_target_pairs={{1,2},{2,1},{3,4},{4,3},{5,6},{6,5},{7,8},{8,7},{9,10},{10,9},{11,... | collective-permute-start | bytes 675848 | tf_op jit(solution)/shard_map/ppermute | solution.py:614
  58.1 7.8 %collective-permute-done.10.refs_3_ = f32[5,88,128]{2,1,0:T(8,128)S(1)} collective-permute-done((f32[5,88,128]{2,1,0:T(8,128)S(1)}, f32[5,88,128]{2,1,0:T(8,128)S(1)}, u32[]{:S(2)}, u32[]{:S(2)}) %collective-permute-start.10) | collective-permute-done | bytes 225312 | tf_op jit(solution)/shard_map/ppermute | solution.py:614
  65.9 5.8 %down.1 = (f32[5,720,128]{2,1,0:T(8,128)S(1)}, f32[5,480,128]{2,1,0:T(8,128)S(1)}, f32[5,32,8,128]{3,2,1,0:T(8,128)S(1)}, f32[5,480,128]{2,1,0:T(8,128)S(1)}, f32[2,10,8,128]{3,2,1,0:T(8,128)S(1)}) custom-call(s32[2]{0:T(128)S(1)} %pad_add_fusion.where_ref.refs_0_, f32[5,256,128]{2,1,0:T(8,128)S(1)} %get-tuple-element.39.refs_1_, ...), custom_call_target="tpu_custom_call" | custom-call | tf_op jit(solution)/shard_map/down/pallas_call | solution.py:593
  71.8 1.3 %collective-permute-done.11.beside.refs_2_ = f32[2,10,8,128]{3,2,1,0:T(8,128)S(1)} collective-permute-done((f32[2,10,8,128]{3,2,1,0:T(8,128)S(1)}, f32[2,10,8,128]{3,2,1,0:T(8,128)S(1)}, u32[]{:S(2)}, u32[]{:S(2)}) %collective-permute-start.11) | collective-permute-done | bytes 81952 | tf_op jit(solution)/shard_map/ppermute | solution.py:613
  73.0 0.6 relay.3
  73.6 1.9 %collective-permute-start.12 = (f32[3,10,8,128]{3,2,1,0:T(8,128)S(1)}, f32[3,10,8,128]{3,2,1,0:T(8,128)S(1)}, u32[]{:S(2)}, u32[]{:S(2)}) collective-permute-start(f32[3,10,8,128]{3,2,1,0:T(8,128)S(1)} %relay.3), channel_id=1, source_target_pairs={{1,2},{2,1},{3,4},{4,3},{5,6},{6,5},{7,8},{8,7},{9,10},{10,9},{11,... | collective-permute-start | bytes 368648 | tf_op jit(solution)/shard_map/ppermute | solution.py:614
  75.5 5.6 %collective-permute-done.12.refs_3_ = f32[3,10,8,128]{3,2,1,0:T(8,128)S(1)} collective-permute-done((f32[3,10,8,128]{3,2,1,0:T(8,128)S(1)}, f32[3,10,8,128]{3,2,1,0:T(8,128)S(1)}, u32[]{:S(2)}, u32[]{:S(2)}) %collective-permute-start.12) | collective-permute-done | bytes 122912 | tf_op jit(solution)/shard_map/ppermute | solution.py:614
  81.1 1.3 %collective-permute-done.13.refs_4_ = f32[3,10,8,128]{3,2,1,0:T(8,128)S(1)} collective-permute-done((f32[3,10,8,128]{3,2,1,0:T(8,128)S(1)}, f32[3,10,8,128]{3,2,1,0:T(8,128)S(1)}, u32[]{:S(2)}, u32[]{:S(2)}) %collective-permute-start.13) | collective-permute-done | bytes 122912 | tf_op jit(solution)/shard_map/ppermute | solution.py:613
  82.4 11.3 %up_last.1 = f32[5,32,1024]{2,1,0:T(8,128)} custom-call(s32[2]{0:T(128)S(1)} %pad_add_fusion.where_ref.refs_0_, f32[2,10,8,128]{3,2,1,0:T(8,128)S(1)} %get-tuple-element.42.own.refs_1_, f32[2,10,8,128]{3,2,1,0:T(8,128)S(1)} %collective-permute-done.11.beside.refs_2_, f32[3,10,8,128]{3,2,1,0:T(8,128)S(1)} %collective-permute-done.12.refs_3_, ...), custom_call_target="tpu_custom_call" | custom-call | tf_op jit(solution)/shard_map/up_last/pallas_call | solution.py:593
  (18 shorter events, 1.1 us)
Async XLA Ops:
  0.1 0.7 copy-start.2
  0.8 0.7 copy-start.3
  2.1 1.6 %collective-permute-start = (f32[96,128]{1,0:T(8,128)S(1)}, f32[96,128]{1,0:T(8,128)S(1)}, u32[]{:S(2)}, u32[]{:S(2)}) collective-permute-start(f32[96,128]{1,0:T(8,128)S(1)} %prep.1), channel_id=1, source_target_pairs={{0,1},{1,0},{2,3},{3,2},{4,5},{5,4},{6,7},{7,6},{8,9},{9,8},{10,11... | collective-permute-start | bytes 147464 | tf_op jit(solution)/shard_map/ppermute | solution.py:634
  3.7 7.5 %collective-permute-start.1 = (f32[96,128]{1,0:T(8,128)S(1)}, f32[96,128]{1,0:T(8,128)S(1)}, u32[]{:S(2)}, u32[]{:S(2)}) collective-permute-start(f32[96,128]{1,0:T(8,128)S(1)} %add.12), channel_id=1, source_target_pairs={{0,2},{1,3},{2,0},{3,1},{4,6},{5,7},{6,4},{7,5},{8,10},{9,11},{10,... | collective-permute-start | bytes 147464 | tf_op jit(solution)/shard_map/ppermute | solution.py:634
  5.0 1.1 %copy-start = (f32[5,32,1024]{2,1,0:T(8,128)S(1)}, f32[5,32,1024]{2,1,0:T(8,128)}, u32[]{:S(2)}) copy-start(f32[5,32,1024]{2,1,0:T(8,128)} %state_ref.1) | copy-start | bytes 1966084
  6.1 1.1 %copy-start.1 = (f32[5,32,1024]{2,1,0:T(8,128)S(1)}, f32[5,32,1024]{2,1,0:T(8,128)}, u32[]{:S(2)}) copy-start(f32[5,32,1024]{2,1,0:T(8,128)} %forcing_ref.1) | copy-start | bytes 1966084
  11.2 12.5 %collective-permute-start.2 = (f32[10,88,128]{2,1,0:T(8,128)S(1)}, f32[10,88,128]{2,1,0:T(8,128)S(1)}, u32[]{:S(2)}, u32[]{:S(2)}) collective-permute-start(f32[10,88,128]{2,1,0:T(8,128)S(1)} %get-tuple-element.30), channel_id=1, source_target_pairs={{0,1},{1,0},{2,3},{3,2},{4,5},{5,4},{6,7},{7,6},{8,9},{9,8},{10,11... | collective-permute-start | bytes 1351688 | tf_op jit(solution)/shard_map/ppermute | solution.py:613
  12.0 14.5 %collective-permute-start.3 = (f32[10,88,128]{2,1,0:T(8,128)S(1)}, f32[10,88,128]{2,1,0:T(8,128)S(1)}, u32[]{:S(2)}, u32[]{:S(2)}) collective-permute-start(f32[10,88,128]{2,1,0:T(8,128)S(1)} %get-tuple-element.31), channel_id=1, source_target_pairs={{1,2},{2,1},{3,4},{4,3},{5,6},{6,5},{7,8},{8,7},{9,10},{10,9},{11,... | collective-permute-start | bytes 1351688 | tf_op jit(solution)/shard_map/ppermute | solution.py:614
  14.0 3.5 %collective-permute-start.4 = (f32[96,128]{1,0:T(8,128)S(1)}, f32[96,128]{1,0:T(8,128)S(1)}, u32[]{:S(2)}, u32[]{:S(2)}) collective-permute-start(f32[96,128]{1,0:T(8,128)S(1)} %add.13), channel_id=1, source_target_pairs={{0,4},{1,5},{2,6},{3,7},{4,0},{5,1},{6,2},{7,3},{8,12},{9,13},{10,... | collective-permute-start | bytes 147464 | tf_op jit(solution)/shard_map/ppermute | solution.py:634
  17.5 4.2 %collective-permute-start.5 = (f32[96,128]{1,0:T(8,128)S(1)}, f32[96,128]{1,0:T(8,128)S(1)}, u32[]{:S(2)}, u32[]{:S(2)}) collective-permute-start(f32[96,128]{1,0:T(8,128)S(1)} %add.14), channel_id=1, source_target_pairs={{0,8},{1,9},{2,10},{3,11},{4,12},{5,13},{6,14},{7,15},{8,0},{9,1},... | collective-permute-start | bytes 147464 | tf_op jit(solution)/shard_map/ppermute | solution.py:634
  32.6 5.2 %collective-permute-start.6 = (f32[2,10,8,128]{3,2,1,0:T(8,128)S(1)}, f32[2,10,8,128]{3,2,1,0:T(8,128)S(1)}, u32[]{:S(2)}, u32[]{:S(2)}) collective-permute-start(f32[2,10,8,128]{3,2,1,0:T(8,128)S(1)} %get-tuple-element.33.own.refs_1_), channel_id=1, source_target_pairs={{0,1},{1,0},{2,3},{3,2},{4,5},{5,4},{6,7},{7,6},{8,9},{9,8},{10,11... | collective-permute-start | bytes 245768 | tf_op jit(solution)/shard_map/ppermute | solution.py:613
  38.3 7.5 %collective-permute-start.7 = (f32[3,10,8,128]{3,2,1,0:T(8,128)S(1)}, f32[3,10,8,128]{3,2,1,0:T(8,128)S(1)}, u32[]{:S(2)}, u32[]{:S(2)}) collective-permute-start(f32[3,10,8,128]{3,2,1,0:T(8,128)S(1)} %relay.2), channel_id=1, source_target_pairs={{1,2},{2,1},{3,4},{4,3},{5,6},{6,5},{7,8},{8,7},{9,10},{10,9},{11,... | collective-permute-start | bytes 368648 | tf_op jit(solution)/shard_map/ppermute | solution.py:614
  45.8 1.3 %collective-permute-start.8 = (f32[3,10,8,128]{3,2,1,0:T(8,128)S(1)}, f32[3,10,8,128]{3,2,1,0:T(8,128)S(1)}, u32[]{:S(2)}, u32[]{:S(2)}) collective-permute-start(f32[3,10,8,128]{3,2,1,0:T(8,128)S(1)} %collective-permute-done.7.refs_3_), channel_id=1, source_target_pairs={{0,1},{1,0},{2,3},{3,2},{4,5},{5,4},{6,7},{7,6},{8,9},{9,8},{10,11... | collective-permute-start | bytes 368648 | tf_op jit(solution)/shard_map/ppermute | solution.py:613
  56.0 2.1 %collective-permute-start.9 = (f32[5,88,128]{2,1,0:T(8,128)S(1)}, f32[5,88,128]{2,1,0:T(8,128)S(1)}, u32[]{:S(2)}, u32[]{:S(2)}) collective-permute-start(f32[5,88,128]{2,1,0:T(8,128)S(1)} %get-tuple-element.40), channel_id=1, source_target_pairs={{0,1},{1,0},{2,3},{3,2},{4,5},{5,4},{6,7},{7,6},{8,9},{9,8},{10,11... | collective-permute-start | bytes 675848 | tf_op jit(solution)/shard_map/ppermute | solution.py:613
  56.2 9.7 %collective-permute-start.10 = (f32[5,88,128]{2,1,0:T(8,128)S(1)}, f32[5,88,128]{2,1,0:T(8,128)S(1)}, u32[]{:S(2)}, u32[]{:S(2)}) collective-permute-start(f32[5,88,128]{2,1,0:T(8,128)S(1)} %get-tuple-element.41), channel_id=1, source_target_pairs={{1,2},{2,1},{3,4},{4,3},{5,6},{6,5},{7,8},{8,7},{9,10},{10,9},{11,... | collective-permute-start | bytes 675848 | tf_op jit(solution)/shard_map/ppermute | solution.py:614
  71.7 1.3 %collective-permute-start.11 = (f32[2,10,8,128]{3,2,1,0:T(8,128)S(1)}, f32[2,10,8,128]{3,2,1,0:T(8,128)S(1)}, u32[]{:S(2)}, u32[]{:S(2)}) collective-permute-start(f32[2,10,8,128]{3,2,1,0:T(8,128)S(1)} %get-tuple-element.42.own.refs_1_), channel_id=1, source_target_pairs={{0,1},{1,0},{2,3},{3,2},{4,5},{5,4},{6,7},{7,6},{8,9},{9,8},{10,11... | collective-permute-start | bytes 245768 | tf_op jit(solution)/shard_map/ppermute | solution.py:613
  73.6 7.5 %collective-permute-start.12 = (f32[3,10,8,128]{3,2,1,0:T(8,128)S(1)}, f32[3,10,8,128]{3,2,1,0:T(8,128)S(1)}, u32[]{:S(2)}, u32[]{:S(2)}) collective-permute-start(f32[3,10,8,128]{3,2,1,0:T(8,128)S(1)} %relay.3), channel_id=1, source_target_pairs={{1,2},{2,1},{3,4},{4,3},{5,6},{6,5},{7,8},{8,7},{9,10},{10,9},{11,... | collective-permute-start | bytes 368648 | tf_op jit(solution)/shard_map/ppermute | solution.py:614
  81.1 1.3 %collective-permute-start.13 = (f32[3,10,8,128]{3,2,1,0:T(8,128)S(1)}, f32[3,10,8,128]{3,2,1,0:T(8,128)S(1)}, u32[]{:S(2)}, u32[]{:S(2)}) collective-permute-start(f32[3,10,8,128]{3,2,1,0:T(8,128)S(1)} %collective-permute-done.12.refs_3_), channel_id=1, source_target_pairs={{0,1},{1,0},{2,3},{3,2},{4,5},{5,4},{6,7},{7,6},{8,9},{9,8},{10,11... | collective-permute-start | bytes 368648 | tf_op jit(solution)/shard_map/ppermute | solution.py:613

commit v5 on v4

--- a/solution.py
+++ b/solution.py
@@ -119,7 +119,7 @@
     return SOURCE_GAIN * 4.0**level / DIFFUSION
 
 
-def sweep(source_of, old, new, table, level, first, last, more=True):
+def sweep(source_of, old, new, table, level, first, last, more=True, batch=None):
     gain = gain_of(level)
 
     def compute(row):
@@ -135,7 +135,7 @@
         for field in range(FIELDS):
             put(new, field, row, level, values[field])
 
-    batches(first, last, SWEEP_BATCH, compute, store)
+    batches(first, last, batch or SWEEP_BATCH, compute, store)
     if more:
         edges(new, level, first, last)
 
@@ -220,6 +220,7 @@
 
 
 SWEEP_BATCH = 4
+INNER = 2
 COARSEN_BATCH = 2
 
 
@@ -355,9 +356,8 @@
 
 
 def turn(first_sub, inward):
-    shape = (SUB * LANES, 2 * LANES)
-    into = lax.broadcasted_iota(jnp.int32, shape, 0)
-    out = lax.broadcasted_iota(jnp.int32, shape, 1)
+    into = lax.broadcasted_iota(jnp.int32, (SUB * LANES, 2 * LANES), 0)
+    out = lax.broadcasted_iota(jnp.int32, (1, 2 * LANES), 1)
     if inward:
         wanted = (out % LANES) * SUB + first_sub + out // LANES
     else:
@@ -426,26 +426,60 @@
             put_row(field, row_a + row, got_a[first + field, pl.ds(start, SUB), :])
             put_row(field, row_b + row, got_b[first + field, pl.ds(start, SUB), :])
 
+    if own_rows is not None:
+        rows_loop(0, OWN, own)
+    rows_loop(0, FINE_HALO, halo)
+
+
+def interior_kernel(fresh, where_ref, state, force, table, v0, tmp0, c1, q1, tmp1):
+    def own(row):
+        start = pl.multiple_of(row * SUB, SUB)
+        for field in range(FIELDS):
+            put(v0, field, O0 + row, 0, state[field, pl.ds(start, SUB), :])
+
     rows_loop(0, OWN, own)
-    rows_loop(0, FINE_HALO, halo)
+    edges(v0, 0, O0, O0 + OWN)
+    if fresh:
+        source = lambda field, row: force[field, pl.ds(pl.multiple_of((row - O0) * SUB, SUB), SUB), :]
+    else:
+        source = lambda field, row: force[field, row]
+    sweep(source, v0, tmp0, table, 0, O0 + 1, O0 + OWN - 1, batch=5)
+    sweep(source, tmp0, v0, table, 0, O0 + 2, O0 + OWN - 2, batch=4)
+    descend(source, v0, table, 0, c1, q1, tmp1, O1 + INNER, O1 + OWN // 2 - INNER)
 
 
 def down_kernel(fresh, *refs):
     if fresh:
-        where_ref, state, force, got_a, got_b, table, v0, v1, s1, c1, send, f0, tmp0, tmp1, q1 = refs
+        (where_ref, v0_in, tmp0_in, c1_in, q1_in, tmp1_in, force, got_a, got_b, table,
+         v0, v1, s1, c1, send, f0, tmp0, tmp1, q1) = refs
     else:
-        where_ref, state, got_a, got_b, f0, table, v0, v1, s1, c1, send, tmp0, tmp1, q1 = refs
-    place_halo(where_ref, v0, state, got_a, got_b, 0, True)
-    edges(v0, 0, O0 - FINE_HALO, O0 + OWN + FINE_HALO)
+        (where_ref, v0_in, tmp0_in, c1_in, q1_in, tmp1_in, got_a, got_b, f0, table,
+         v0, v1, s1, c1, send, tmp0, tmp1, q1) = refs
+    half = OWN // 2
+
+    def take(target, source, level, first, last):
+        rows = slice(at(first, level) - 2**level, at(last, level) - 2**level)
+        target[:, rows, :] = source[:, rows, :]
+
+    take(v0, v0_in, 0, O0, O0 + OWN)
+    take(tmp0, tmp0_in, 0, O0 + 1, O0 + 3)
+    take(tmp0, tmp0_in, 0, O0 + OWN - 3, O0 + OWN - 1)
+    inner = slice(O1 + INNER, O1 + half - INNER)
+    take(c1, c1_in, 1, inner.start, inner.stop)
+    take(tmp1, tmp1_in, 1, inner.start, inner.stop)
+    q1[:, inner] = q1_in[:, inner]
+
+    place_halo(where_ref, v0, None, got_a, got_b, 0, True)
+    edges(v0, 0, O0 - FINE_HALO, O0)
+    edges(v0, 0, O0 + OWN, O0 + OWN + FINE_HALO)
     if fresh:
         place_halo(where_ref, f0, force, got_a, got_b, FIELDS, False)
     fine_source = lambda field, row: f0[field, row]
-    low, high = O0 - FINE_HALO, O0 + OWN + FINE_HALO
-    sweep(fine_source, v0, tmp0, table, 0, low + 1, high - 1)
-    sweep(fine_source, tmp0, v0, table, 0, low + 2, high - 2)
-
-    half = OWN // 2
-    descend(fine_source, v0, table, 0, c1, q1, tmp1, O1 - 4, O1 + half + 4)
+    for swept, (old, new) in enumerate(((v0, tmp0), (tmp0, v0))):
+        for first in (O0 - FINE_HALO + swept, O0 + OWN - 1 - swept):
+            sweep(fine_source, old, new, table, 0, first, first + FINE_HALO + 1)
+    for first in (O1 - 4, O1 + half - INNER):
+        descend(fine_source, v0, table, 0, c1, q1, tmp1, first, first + 4 + INNER)
     make_source(c1, q1, s1, table, 1, O1 - 3, O1 + half + 3)
     first_source = lambda field, row: s1[field, row]
     sweep(first_source, tmp1, v1, table, 1, O1 - 3, O1 + half + 3)
@@ -599,6 +633,10 @@
         name=name,
         compiler_params=pltpu.CompilerParams(vmem_limit_bytes=grant * 1024 * 1024),
     )(*operands)
+
+
+def in_hbm(array):
+    return pltpu.with_memory_space_constraint(array, pltpu.HBM)
 
 
 def per_device(initial_state, forcing, coefficients, region_ids):
@@ -621,7 +659,7 @@
         "prep",
         4,
         [f32(regions + SUB * -(-size // per_tile), LANES)],
-        [where_ref, coefficients.T, region_ids.T],
+        [where_ref, in_hbm(coefficients.T), in_hbm(region_ids.T)],
         [
             scratch(share, ENTRIES),
             pltpu.VMEM((SUB, OWN), jnp.int32),
@@ -637,7 +675,7 @@
         split_kernel,
         "split", 12,
         [f32(FIELDS, OWN * SUB, LANES)] * 2 + [f32(2 * FIELDS, FINE_HALO * SUB, LANES)] * 2,
-        [where_ref, initial_state, forcing],
+        [where_ref, in_hbm(initial_state), in_hbm(forcing)],
         [
             pltpu.VMEM((3 * 2 * FIELDS * OWN, SUB * LANES), jnp.bfloat16),
             scratch(2, FIELDS, OWN, SUB * LANES),
@@ -646,7 +684,7 @@
         True,
     )
     step = 1
-    while step < min(size, 4):
+    while step < min(size, 8):
         gathered = doubled(gathered, step)
         step *= 2
     gathered, send_a, send_b = lax.optimization_barrier((gathered, send_a, send_b))
@@ -664,18 +702,24 @@
 
     f0 = None
     for cycle in range(CYCLES):
+        fresh = cycle == 0
+        inner = call(
+            functools.partial(interior_kernel, fresh), "interior", 4,
+            [f32(*padded(T0, 0))] * 2 + [f32(*padded(T1, 1)), f32(*plain(T1)), f32(*padded(T1, 1))],
+            [where_ref, state, force if fresh else f0, table],
+        )
         outs = [f32(*padded(T0, 0)), f32(*padded(T1, 1)), f32(*plain(T1)), f32(*padded(T1, 1)),
                 f32(2, 2 * FIELDS, SUB, LANES)]
         temps = [scratch(*padded(T0, 0)), scratch(*padded(T1, 1)), scratch(*plain(T1))]
-        if cycle == 0:
+        if fresh:
             v0, v1, s1, c1, own, f0 = call(
                 functools.partial(down_kernel, True), "down_fresh", 14, outs + [f32(*plain(T0))],
-                [where_ref, state, force, got_a, got_b, table], temps,
+                [where_ref, *inner, force, got_a, got_b, table], temps,
             )
         else:
             v0, v1, s1, c1, own = call(
                 functools.partial(down_kernel, False), "down", 14, outs,
-                [where_ref, state, got_a, got_b, f0, table], temps,
+                [where_ref, *inner, got_a, got_b, f0, table], temps,
             )
         beside = swap_a(own)
         (row,) = call(

time: 94.1 us -> 91.9 us (0.977)
  the two profiles are of different devices: /device:TPU:17 before, /device:TPU:9 now
where the time goes in v5:
time: 91.9 us; the launch traced here: 91.7 us
  Pallas kernels  43.6 us (47%)
  waiting for transfers between devices  27 us (29%)
  starting transfers between devices  20.9 us (23%)
    pallas_call x11, Pallas kernels, call(): pl.pallas_call(kernel, out_shape=outs, in_specs=[SMEM] + [ANY if raw else...  43.6 us
    ppermute x4, waiting for transfers between devices, per_device(): swap_b = lambda x: lax.ppermute(x, 'axial', pair_b)  17.8 us
    ppermute x4, starting transfers between devices, per_device(): swap_b = lambda x: lax.ppermute(x, 'axial', pair_b)  9.49 us
    ppermute x6, starting transfers between devices, per_device(): swap_a = lambda x: lax.ppermute(x, 'axial', pair_a)  6.95 us
    ppermute x6, waiting for transfers between devices, per_device(): swap_a = lambda x: lax.ppermute(x, 'axial', pair_a)  4.83 us
    ppermute x4, starting transfers between devices, doubled(): lax.ppermute(held, 'axial', [(i, i ^ step) for i in range(size)])  4.43 us
    ppermute x4, waiting for transfers between devices, doubled(): lax.ppermute(held, 'axial', [(i, i ^ step) for i in range(size)])  4.34 us
  transfers between devices with their start and end apart: 14, of which 11 were waited for; matrix products, arithmetic and copies ran while one was open for 0% of the time, Pallas kernels for 14%

profile of v5, /device:TPU:9, one launch (start us, length us, event | category | flops | bytes accessed | tf_op | source)
XLA Modules:
  0.0 91.7 jit_solution(10259208133332028294)
XLA Ops:
  0.1 1.3 %prep.1 = f32[96,128]{1,0:T(8,128)S(1)} custom-call(s32[2]{0:T(128)S(1)} %pad_add_fusion.where_ref.refs_0_, f32[4,25]{1,0:T(4,128)} %bitcast.4, s32[8,32]{1,0:T(8,128)} %bitcast.3), custom_call_target="tpu_custom_call" | custom-call | tf_op jit(solution)/shard_map/prep/pallas_call | solution.py:627
  1.4 0.7 collective-permute-start
  2.1 0.9 collective-permute-done
  3.0 1.3 %collective-permute-start.1 = (f32[96,128]{1,0:T(8,128)S(1)}, f32[96,128]{1,0:T(8,128)S(1)}, u32[]{:S(2)}, u32[]{:S(2)}) collective-permute-start(f32[96,128]{1,0:T(8,128)S(1)} %add.12), channel_id=1, source_target_pairs={{0,2},{1,3},{2,0},{3,1},{4,6},{5,7},{6,4},{7,5},{8,10},{9,11},{10,... | collective-permute-start | bytes 147464 | tf_op jit(solution)/shard_map/ppermute | solution.py:672
  4.3 1.6 %collective-permute-done.1 = f32[96,128]{1,0:T(8,128)S(1)} collective-permute-done((f32[96,128]{1,0:T(8,128)S(1)}, f32[96,128]{1,0:T(8,128)S(1)}, u32[]{:S(2)}, u32[]{:S(2)}) %collective-permute-start.1) | collective-permute-done | bytes 49184 | tf_op jit(solution)/shard_map/ppermute | solution.py:672
  6.0 4.8 %split.1 = (f32[5,256,128]{2,1,0:T(8,128)S(1)}, f32[5,256,128]{2,1,0:T(8,128)S(1)}, f32[10,88,128]{2,1,0:T(8,128)S(1)}, f32[10,88,128]{2,1,0:T(8,128)S(1)}) custom-call(s32[2]{0:T(128)S(1)} %pad_add_fusion.where_ref.refs_0_, f32[5,32,1024]{2,1,0:T(8,128)} %state_ref.1, f32[5,32,1024]{2,1,0:T(8,128)} %forcing_ref.1), custom_call_target="tpu_custom_call" | custom-call | tf_op jit(solution)/shard_map/split/pallas_call | solution.py:627
  10.8 1.6 %collective-permute-start.4 = (f32[10,88,128]{2,1,0:T(8,128)S(1)}, f32[10,88,128]{2,1,0:T(8,128)S(1)}, u32[]{:S(2)}, u32[]{:S(2)}) collective-permute-start(f32[10,88,128]{2,1,0:T(8,128)S(1)} %get-tuple-element.46), channel_id=1, source_target_pairs={{0,1},{1,0},{2,3},{3,2},{4,5},{5,4},{6,7},{7,6},{8,9},{9,8},{10,11... | collective-permute-start | bytes 1351688 | tf_op jit(solution)/shard_map/ppermute | solution.py:651
  12.4 3.5 %collective-permute-start.5 = (f32[10,88,128]{2,1,0:T(8,128)S(1)}, f32[10,88,128]{2,1,0:T(8,128)S(1)}, u32[]{:S(2)}, u32[]{:S(2)}) collective-permute-start(f32[10,88,128]{2,1,0:T(8,128)S(1)} %get-tuple-element.47), channel_id=1, source_target_pairs={{1,2},{2,1},{3,4},{4,3},{5,6},{6,5},{7,8},{8,7},{9,10},{10,9},{11,... | collective-permute-start | bytes 1351688 | tf_op jit(solution)/shard_map/ppermute | solution.py:652
  16.0 2.4 %collective-permute-start.3 = (f32[96,128]{1,0:T(8,128)S(1)}, f32[96,128]{1,0:T(8,128)S(1)}, u32[]{:S(2)}, u32[]{:S(2)}) collective-permute-start(f32[96,128]{1,0:T(8,128)S(1)} %add.14), channel_id=1, source_target_pairs={{0,8},{1,9},{2,10},{3,11},{4,12},{5,13},{6,14},{7,15},{8,0},{9,1},... | collective-permute-start | bytes 147464 | tf_op jit(solution)/shard_map/ppermute | solution.py:672
  18.4 1.8 %collective-permute-done.3 = f32[96,128]{1,0:T(8,128)S(1)} collective-permute-done((f32[96,128]{1,0:T(8,128)S(1)}, f32[96,128]{1,0:T(8,128)S(1)}, u32[]{:S(2)}, u32[]{:S(2)}) %collective-permute-start.3) | collective-permute-done | bytes 49184 | tf_op jit(solution)/shard_map/ppermute | solution.py:672
  20.2 2.0 %tables.1.table.refs_9_.refs_10_ = f32[50,160,128]{2,1,0:T(8,128)S(1)} custom-call(s32[2]{0:T(128)S(1)} %pad_add_fusion.where_ref.refs_0_, f32[96,128]{1,0:T(8,128)S(1)} %add.15.regions_ref), custom_call_target="tpu_custom_call" | custom-call | tf_op jit(solution)/shard_map/tables/pallas_call | solution.py:627
  22.2 2.8 %interior.2 = (f32[5,720,128]{2,1,0:T(8,128)S(1)}, f32[5,720,128]{2,1,0:T(8,128)S(1)}, f32[5,480,128]{2,1,0:T(8,128)S(1)}, f32[5,32,8,128]{3,2,1,0:T(8,128)S(1)}, f32[5,480,128]{2,1,0:T(8,128)S(1)}) custom-call(s32[2]{0:T(128)S(1)} %pad_add_fusion.where_ref.refs_0_, f32[5,256,128]{2,1,0:T(8,128)S(1)} %get-tuple-element.36.state, ...), custom_call_target="tpu_custom_call" | custom-call | tf_op jit(solution)/shard_map/interior/pallas_call | solution.py:627
  25.1 1.9 %collective-permute-done.5.refs_8_ = f32[10,88,128]{2,1,0:T(8,128)S(1)} collective-permute-done((f32[10,88,128]{2,1,0:T(8,128)S(1)}, f32[10,88,128]{2,1,0:T(8,128)S(1)}, u32[]{:S(2)}, u32[]{:S(2)}) %collective-permute-start.5) | collective-permute-done | bytes 450592 | tf_op jit(solution)/shard_map/ppermute | solution.py:652
  27.0 4.4 %down_fresh.1 = (f32[5,720,128]{2,1,0:T(8,128)S(1)}, f32[5,480,128]{2,1,0:T(8,128)S(1)}, f32[5,32,8,128]{3,2,1,0:T(8,128)S(1)}, f32[5,480,128]{2,1,0:T(8,128)S(1...) custom-call(s32[2]{0:T(128)S(1)} %pad_add_fusion.where_ref.refs_0_, ...), custom_call_target="tpu_custom_call" | custom-call | tf_op jit(solution)/shard_map/down_fresh/pallas_call | solution.py:627
  31.4 5.0 %collective-permute-start.6 = (f32[2,10,8,128]{3,2,1,0:T(8,128)S(1)}, f32[2,10,8,128]{3,2,1,0:T(8,128)S(1)}, u32[]{:S(2)}, u32[]{:S(2)}) collective-permute-start(f32[2,10,8,128]{3,2,1,0:T(8,128)S(1)} %get-tuple-element.48.own.refs_1_), channel_id=1, source_target_pairs={{0,1},{1,0},{2,3},{3,2},{4,5},{5,4},{6,7},{7,6},{8,9},{9,8},{10,11... | collective-permute-start | bytes 245768 | tf_op jit(solution)/shard_map/ppermute | solution.py:651
  36.4 0.9 %collective-permute-done.6.beside.refs_2_ = f32[2,10,8,128]{3,2,1,0:T(8,128)S(1)} collective-permute-done((f32[2,10,8,128]{3,2,1,0:T(8,128)S(1)}, f32[2,10,8,128]{3,2,1,0:T(8,128)S(1)}, u32[]{:S(2)}, u32[]{:S(2)}) %collective-permute-start.6) | collective-permute-done | bytes 81952 | tf_op jit(solution)/shard_map/ppermute | solution.py:651
  37.3 0.6 relay.2
  37.9 1.9 %collective-permute-start.7 = (f32[3,10,8,128]{3,2,1,0:T(8,128)S(1)}, f32[3,10,8,128]{3,2,1,0:T(8,128)S(1)}, u32[]{:S(2)}, u32[]{:S(2)}) collective-permute-start(f32[3,10,8,128]{3,2,1,0:T(8,128)S(1)} %relay.2), channel_id=1, source_target_pairs={{1,2},{2,1},{3,4},{4,3},{5,6},{6,5},{7,8},{8,7},{9,10},{10,9},{11,... | collective-permute-start | bytes 368648 | tf_op jit(solution)/shard_map/ppermute | solution.py:652
  39.8 5.6 %collective-permute-done.7.refs_3_ = f32[3,10,8,128]{3,2,1,0:T(8,128)S(1)} collective-permute-done((f32[3,10,8,128]{3,2,1,0:T(8,128)S(1)}, f32[3,10,8,128]{3,2,1,0:T(8,128)S(1)}, u32[]{:S(2)}, u32[]{:S(2)}) %collective-permute-start.7) | collective-permute-done | bytes 122912 | tf_op jit(solution)/shard_map/ppermute | solution.py:652
  45.4 1.3 %collective-permute-done.8.refs_4_ = f32[3,10,8,128]{3,2,1,0:T(8,128)S(1)} collective-permute-done((f32[3,10,8,128]{3,2,1,0:T(8,128)S(1)}, f32[3,10,8,128]{3,2,1,0:T(8,128)S(1)}, u32[]{:S(2)}, u32[]{:S(2)}) %collective-permute-start.8) | collective-permute-done | bytes 122912 | tf_op jit(solution)/shard_map/ppermute | solution.py:651
  46.7 8.8 %up.1 = (f32[5,256,128]{2,1,0:T(8,128)S(1)}, f32[5,88,128]{2,1,0:T(8,128)S(1)}, f32[5,88,128]{2,1,0:T(8,128)S(1)}) custom-call(s32[2]{0:T(128)S(1)} %pad_add_fusion.where_ref.refs_0_, f32[2,10,8,128]{3,2,1,0:T(8,128)S(1)} %get-tuple-element.48.own.refs_1_, f32[2,10,8,128]{3,2,1,0:T(8,128)S(1)} %collective-permute-done.6.beside.refs_2_, ...), custom_call_target="tpu_custom_call" | custom-call | tf_op jit(solution)/shard_map/up/pallas_call | solution.py:627
  55.6 0.2 collective-permute-start.9
  55.8 1.9 %collective-permute-start.10 = (f32[5,88,128]{2,1,0:T(8,128)S(1)}, f32[5,88,128]{2,1,0:T(8,128)S(1)}, u32[]{:S(2)}, u32[]{:S(2)}) collective-permute-start(f32[5,88,128]{2,1,0:T(8,128)S(1)} %get-tuple-element.61), channel_id=1, source_target_pairs={{1,2},{2,1},{3,4},{4,3},{5,6},{6,5},{7,8},{8,7},{9,10},{10,9},{11,... | collective-permute-start | bytes 675848 | tf_op jit(solution)/shard_map/ppermute | solution.py:652
  57.7 2.8 %interior.3 = (f32[5,720,128]{2,1,0:T(8,128)S(1)}, f32[5,720,128]{2,1,0:T(8,128)S(1)}, f32[5,480,128]{2,1,0:T(8,128)S(1)}, f32[5,32,8,128]{3,2,1,0:T(8,128)S(1)}, f32[5,480,128]{2,1,0:T(8,128)S(1)}) custom-call(s32[2]{0:T(128)S(1)} %pad_add_fusion.where_ref.refs_0_, f32[5,256,128]{2,1,0:T(8,128)S(1)} %get-tuple-element.54.state, ...), custom_call_target="tpu_custom_call" | custom-call | tf_op jit(solution)/shard_map/interior/pallas_call | solution.py:627
  60.5 4.9 %collective-permute-done.10.refs_7_ = f32[5,88,128]{2,1,0:T(8,128)S(1)} collective-permute-done((f32[5,88,128]{2,1,0:T(8,128)S(1)}, f32[5,88,128]{2,1,0:T(8,128)S(1)}, u32[]{:S(2)}, u32[]{:S(2)}) %collective-permute-start.10) | collective-permute-done | bytes 225312 | tf_op jit(solution)/shard_map/ppermute | solution.py:652
  65.5 4.2 %down.1 = (f32[5,720,128]{2,1,0:T(8,128)S(1)}, f32[5,480,128]{2,1,0:T(8,128)S(1)}, f32[5,32,8,128]{3,2,1,0:T(8,128)S(1)}, f32[5,480,128]{2,1,0:T(8,128)S(1)}, f32[2,10,8,128]{3,2,1,0:T(8,128)S(1)}) custom-call(s32[2]{0:T(128)S(1)} %pad_add_fusion.where_ref.refs_0_, f32[5,720,128]{2,1,0:T(8,128)S(1)} %get-tuple-element.55.refs_1_, ...), custom_call_target="tpu_custom_call" | custom-call | tf_op jit(solution)/shard_map/down/pallas_call | solution.py:627
  69.7 1.3 %collective-permute-done.11.beside.refs_2_ = f32[2,10,8,128]{3,2,1,0:T(8,128)S(1)} collective-permute-done((f32[2,10,8,128]{3,2,1,0:T(8,128)S(1)}, f32[2,10,8,128]{3,2,1,0:T(8,128)S(1)}, u32[]{:S(2)}, u32[]{:S(2)}) %collective-permute-start.11) | collective-permute-done | bytes 81952 | tf_op jit(solution)/shard_map/ppermute | solution.py:651
  71.0 0.6 relay.3
  71.6 2.1 %collective-permute-start.12 = (f32[3,10,8,128]{3,2,1,0:T(8,128)S(1)}, f32[3,10,8,128]{3,2,1,0:T(8,128)S(1)}, u32[]{:S(2)}, u32[]{:S(2)}) collective-permute-start(f32[3,10,8,128]{3,2,1,0:T(8,128)S(1)} %relay.3), channel_id=1, source_target_pairs={{1,2},{2,1},{3,4},{4,3},{5,6},{6,5},{7,8},{8,7},{9,10},{10,9},{11,... | collective-permute-start | bytes 368648 | tf_op jit(solution)/shard_map/ppermute | solution.py:652
  73.7 5.4 %collective-permute-done.12.refs_3_ = f32[3,10,8,128]{3,2,1,0:T(8,128)S(1)} collective-permute-done((f32[3,10,8,128]{3,2,1,0:T(8,128)S(1)}, f32[3,10,8,128]{3,2,1,0:T(8,128)S(1)}, u32[]{:S(2)}, u32[]{:S(2)}) %collective-permute-start.12) | collective-permute-done | bytes 122912 | tf_op jit(solution)/shard_map/ppermute | solution.py:652
  79.1 1.3 %collective-permute-done.13.refs_4_ = f32[3,10,8,128]{3,2,1,0:T(8,128)S(1)} collective-permute-done((f32[3,10,8,128]{3,2,1,0:T(8,128)S(1)}, f32[3,10,8,128]{3,2,1,0:T(8,128)S(1)}, u32[]{:S(2)}, u32[]{:S(2)}) %collective-permute-start.13) | collective-permute-done | bytes 122912 | tf_op jit(solution)/shard_map/ppermute | solution.py:651
  80.4 11.3 %up_last.1 = f32[5,32,1024]{2,1,0:T(8,128)} custom-call(s32[2]{0:T(128)S(1)} %pad_add_fusion.where_ref.refs_0_, f32[2,10,8,128]{3,2,1,0:T(8,128)S(1)} %get-tuple-element.62.own.refs_1_, f32[2,10,8,128]{3,2,1,0:T(8,128)S(1)} %collective-permute-done.11.beside.refs_2_, f32[3,10,8,128]{3,2,1,0:T(8,128)S(1)} %collective-permute-done.12.refs_3_, ...), custom_call_target="tpu_custom_call" | custom-call | tf_op jit(solution)/shard_map/up_last/pallas_call | solution.py:627
  (12 shorter events, 0.3 us)
Async XLA Ops:
  1.4 1.6 %collective-permute-start = (f32[96,128]{1,0:T(8,128)S(1)}, f32[96,128]{1,0:T(8,128)S(1)}, u32[]{:S(2)}, u32[]{:S(2)}) collective-permute-start(f32[96,128]{1,0:T(8,128)S(1)} %prep.1), channel_id=1, source_target_pairs={{0,1},{1,0},{2,3},{3,2},{4,5},{5,4},{6,7},{7,6},{8,9},{9,8},{10,11... | collective-permute-start | bytes 147464 | tf_op jit(solution)/shard_map/ppermute | solution.py:672
  3.0 2.9 %collective-permute-start.1 = (f32[96,128]{1,0:T(8,128)S(1)}, f32[96,128]{1,0:T(8,128)S(1)}, u32[]{:S(2)}, u32[]{:S(2)}) collective-permute-start(f32[96,128]{1,0:T(8,128)S(1)} %add.12), channel_id=1, source_target_pairs={{0,2},{1,3},{2,0},{3,1},{4,6},{5,7},{6,4},{7,5},{8,10},{9,11},{10,... | collective-permute-start | bytes 147464 | tf_op jit(solution)/shard_map/ppermute | solution.py:672
  5.9 4.9 %collective-permute-start.2 = (f32[96,128]{1,0:T(8,128)S(1)}, f32[96,128]{1,0:T(8,128)S(1)}, u32[]{:S(2)}, u32[]{:S(2)}) collective-permute-start(f32[96,128]{1,0:T(8,128)S(1)} %add.13), channel_id=1, source_target_pairs={{0,4},{1,5},{2,6},{3,7},{4,0},{5,1},{6,2},{7,3},{8,12},{9,13},{10,... | collective-permute-start | bytes 147464 | tf_op jit(solution)/shard_map/ppermute | solution.py:672
  10.8 14.3 %collective-permute-start.4 = (f32[10,88,128]{2,1,0:T(8,128)S(1)}, f32[10,88,128]{2,1,0:T(8,128)S(1)}, u32[]{:S(2)}, u32[]{:S(2)}) collective-permute-start(f32[10,88,128]{2,1,0:T(8,128)S(1)} %get-tuple-element.46), channel_id=1, source_target_pairs={{0,1},{1,0},{2,3},{3,2},{4,5},{5,4},{6,7},{7,6},{8,9},{9,8},{10,11... | collective-permute-start | bytes 1351688 | tf_op jit(solution)/shard_map/ppermute | solution.py:651
  12.4 14.5 %collective-permute-start.5 = (f32[10,88,128]{2,1,0:T(8,128)S(1)}, f32[10,88,128]{2,1,0:T(8,128)S(1)}, u32[]{:S(2)}, u32[]{:S(2)}) collective-permute-start(f32[10,88,128]{2,1,0:T(8,128)S(1)} %get-tuple-element.47), channel_id=1, source_target_pairs={{1,2},{2,1},{3,4},{4,3},{5,6},{6,5},{7,8},{8,7},{9,10},{10,9},{11,... | collective-permute-start | bytes 1351688 | tf_op jit(solution)/shard_map/ppermute | solution.py:652
  16.0 4.2 %collective-permute-start.3 = (f32[96,128]{1,0:T(8,128)S(1)}, f32[96,128]{1,0:T(8,128)S(1)}, u32[]{:S(2)}, u32[]{:S(2)}) collective-permute-start(f32[96,128]{1,0:T(8,128)S(1)} %add.14), channel_id=1, source_target_pairs={{0,8},{1,9},{2,10},{3,11},{4,12},{5,13},{6,14},{7,15},{8,0},{9,1},... | collective-permute-start | bytes 147464 | tf_op jit(solution)/shard_map/ppermute | solution.py:672
  31.4 5.9 %collective-permute-start.6 = (f32[2,10,8,128]{3,2,1,0:T(8,128)S(1)}, f32[2,10,8,128]{3,2,1,0:T(8,128)S(1)}, u32[]{:S(2)}, u32[]{:S(2)}) collective-permute-start(f32[2,10,8,128]{3,2,1,0:T(8,128)S(1)} %get-tuple-element.48.own.refs_1_), channel_id=1, source_target_pairs={{0,1},{1,0},{2,3},{3,2},{4,5},{5,4},{6,7},{7,6},{8,9},{9,8},{10,11... | collective-permute-start | bytes 245768 | tf_op jit(solution)/shard_map/ppermute | solution.py:651
  37.9 7.5 %collective-permute-start.7 = (f32[3,10,8,128]{3,2,1,0:T(8,128)S(1)}, f32[3,10,8,128]{3,2,1,0:T(8,128)S(1)}, u32[]{:S(2)}, u32[]{:S(2)}) collective-permute-start(f32[3,10,8,128]{3,2,1,0:T(8,128)S(1)} %relay.2), channel_id=1, source_target_pairs={{1,2},{2,1},{3,4},{4,3},{5,6},{6,5},{7,8},{8,7},{9,10},{10,9},{11,... | collective-permute-start | bytes 368648 | tf_op jit(solution)/shard_map/ppermute | solution.py:652
  45.4 1.3 %collective-permute-start.8 = (f32[3,10,8,128]{3,2,1,0:T(8,128)S(1)}, f32[3,10,8,128]{3,2,1,0:T(8,128)S(1)}, u32[]{:S(2)}, u32[]{:S(2)}) collective-permute-start(f32[3,10,8,128]{3,2,1,0:T(8,128)S(1)} %collective-permute-done.7.refs_3_), channel_id=1, source_target_pairs={{0,1},{1,0},{2,3},{3,2},{4,5},{5,4},{6,7},{7,6},{8,9},{9,8},{10,11... | collective-permute-start | bytes 368648 | tf_op jit(solution)/shard_map/ppermute | solution.py:651
  55.6 5.0 %collective-permute-start.9 = (f32[5,88,128]{2,1,0:T(8,128)S(1)}, f32[5,88,128]{2,1,0:T(8,128)S(1)}, u32[]{:S(2)}, u32[]{:S(2)}) collective-permute-start(f32[5,88,128]{2,1,0:T(8,128)S(1)} %get-tuple-element.60), channel_id=1, source_target_pairs={{0,1},{1,0},{2,3},{3,2},{4,5},{5,4},{6,7},{7,6},{8,9},{9,8},{10,11... | collective-permute-start | bytes 675848 | tf_op jit(solution)/shard_map/ppermute | solution.py:651
  55.8 9.7 %collective-permute-start.10 = (f32[5,88,128]{2,1,0:T(8,128)S(1)}, f32[5,88,128]{2,1,0:T(8,128)S(1)}, u32[]{:S(2)}, u32[]{:S(2)}) collective-permute-start(f32[5,88,128]{2,1,0:T(8,128)S(1)} %get-tuple-element.61), channel_id=1, source_target_pairs={{1,2},{2,1},{3,4},{4,3},{5,6},{6,5},{7,8},{8,7},{9,10},{10,9},{11,... | collective-permute-start | bytes 675848 | tf_op jit(solution)/shard_map/ppermute | solution.py:652
  69.7 1.3 %collective-permute-start.11 = (f32[2,10,8,128]{3,2,1,0:T(8,128)S(1)}, f32[2,10,8,128]{3,2,1,0:T(8,128)S(1)}, u32[]{:S(2)}, u32[]{:S(2)}) collective-permute-start(f32[2,10,8,128]{3,2,1,0:T(8,128)S(1)} %get-tuple-element.62.own.refs_1_), channel_id=1, source_target_pairs={{0,1},{1,0},{2,3},{3,2},{4,5},{5,4},{6,7},{7,6},{8,9},{9,8},{10,11... | collective-permute-start | bytes 245768 | tf_op jit(solution)/shard_map/ppermute | solution.py:651
  71.6 7.5 %collective-permute-start.12 = (f32[3,10,8,128]{3,2,1,0:T(8,128)S(1)}, f32[3,10,8,128]{3,2,1,0:T(8,128)S(1)}, u32[]{:S(2)}, u32[]{:S(2)}) collective-permute-start(f32[3,10,8,128]{3,2,1,0:T(8,128)S(1)} %relay.3), channel_id=1, source_target_pairs={{1,2},{2,1},{3,4},{4,3},{5,6},{6,5},{7,8},{8,7},{9,10},{10,9},{11,... | collective-permute-start | bytes 368648 | tf_op jit(solution)/shard_map/ppermute | solution.py:652
  79.1 1.3 %collective-permute-start.13 = (f32[3,10,8,128]{3,2,1,0:T(8,128)S(1)}, f32[3,10,8,128]{3,2,1,0:T(8,128)S(1)}, u32[]{:S(2)}, u32[]{:S(2)}) collective-permute-start(f32[3,10,8,128]{3,2,1,0:T(8,128)S(1)} %collective-permute-done.12.refs_3_), channel_id=1, source_target_pairs={{0,1},{1,0},{2,3},{3,2},{4,5},{5,4},{6,7},{7,6},{8,9},{9,8},{10,11... | collective-permute-start | bytes 368648 | tf_op jit(solution)/shard_map/ppermute | solution.py:651

commit v6 on v5

--- a/solution.py
+++ b/solution.py
@@ -22,12 +22,14 @@
 T1, O1 = 32, 8
 T2, O2 = 40, 16
 T3, O3 = 20, 8
+COARSEST = 3
+EDGE_BATCH = 10
 GROUP = 4
 SPREAD = 16
 
 
 def stride_of(level):
-    return SUB + 2 * 2**level
+    return SUB + (0 if level == COARSEST else 2 * 2**level)
 
 
 def padded_rows(rows, level):
@@ -35,7 +37,7 @@
 
 
 def at(row, level):
-    return stride_of(level) * row + 2**level
+    return stride_of(level) * row + (0 if level == COARSEST else 2**level)
 
 
 def lane_iota():
@@ -55,13 +57,20 @@
 
 
 def edges(ref, level, first, last):
+    if level == COARSEST:
+        return
     width, stride, lane = 2**level, stride_of(level), lane_iota()
-    for row in range(first, last, SUB):
-        start = at(row, level)
-        for field in range(FIELDS):
-            rows = lambda sub: (field, pl.ds(start + sub, SUB, stride=stride), slice(None))
+    places = [(row, field) for row in range(first, last, SUB) for field in range(FIELDS)]
+    for part in range(0, len(places), EDGE_BATCH):
+        written = []
+        for row, field in places[part : part + EDGE_BATCH]:
+            rows = lambda sub, row=row, field=field: (
+                field, pl.ds(at(row, level) + sub, SUB, stride=stride), slice(None)
+            )
             before = jnp.where(lane == 0, 0.0, pltpu.roll(ref[rows(SUB - 1)], 1, 1))
             after = jnp.where(lane == LANES - 1, 0.0, pltpu.roll(ref[rows(0)], LANES - 1, 1))
+            written.append((rows, before, after))
+        for rows, before, after in written:
             for i in range(width):
                 ref[rows(i - width)] = before
                 ref[rows(SUB + i)] = after
@@ -87,12 +96,19 @@
 
 def neighbours(ref, row, level):
     start, width, stride = at(row, level), 2**level, stride_of(level)
+    lane = lane_iota()
     sums, centres = [], []
     for field in range(FIELDS):
-        load = lambda first: ref[field, pl.ds(first, SUB), :]
-        radial = load(start - width) + load(start + width)
+        load = lambda first, field=field: ref[field, pl.ds(first, SUB), :]
+        centre = load(start)
+        if level == COARSEST:
+            radial = jnp.where(lane == 0, 0.0, pltpu.roll(centre, 1, 1)) + jnp.where(
+                lane == LANES - 1, 0.0, pltpu.roll(centre, LANES - 1, 1)
+            )
+        else:
+            radial = load(start - width) + load(start + width)
         sums.append(radial + (load(start - stride) + load(start + stride)))
-        centres.append(load(start))
+        centres.append(centre)
     return sums, centres
 
 
@@ -366,34 +382,35 @@
     return (into == wanted).astype(jnp.float32).astype(jnp.bfloat16)
 
 
-def split_kernel(where_ref, state_ref, forcing_ref, state_rows, forcing_rows, send_a, send_b, parts, held_in, sems):
-    copies = [
-        pltpu.make_async_copy(source, held_in.at[i], sems.at[i])
-        for i, source in enumerate((state_ref, forcing_ref))
-    ]
-    for copy in copies:
-        copy.start()
-    odd = where_ref[0] % 2
-    held = 2 * FIELDS * OWN
-    for which, copy in enumerate(copies):
-        copy.wait()
-        for field in range(FIELDS):
-            for p, part in enumerate(three_parts(held_in[which, field])):
-                start = p * held + (which * FIELDS + field) * OWN
-                parts[start : start + OWN, :] = part
+def split_kernel(source_ref, target, parts, held_in, sem):
+    copy = pltpu.make_async_copy(source_ref, held_in, sem)
+    copy.start()
+    held = FIELDS * OWN
+    copy.wait()
+    for field in range(FIELDS):
+        for p, part in enumerate(three_parts(held_in[field])):
+            start = p * held + field * OWN
+            parts[start : start + OWN, :] = part
 
     def two_subs(index):
         values = dot(parts[...], turn(2 * index, True))
         values = (values[:held] + values[held : 2 * held]) + values[2 * held :]
-        for which, target in enumerate((state_rows, forcing_rows)):
-            for field in range(FIELDS):
-                start = (which * FIELDS + field) * OWN
-                for half in range(2):
-                    target[field, pl.ds(2 * index + half, OWN, stride=SUB), :] = values[
-                        start : start + OWN, half * LANES : (half + 1) * LANES
-                    ]
+        for field in range(FIELDS):
+            for half in range(2):
+                target[field, pl.ds(2 * index + half, OWN, stride=SUB), :] = values[
+                    field * OWN : (field + 1) * OWN, half * LANES : (half + 1) * LANES
+                ]
 
     rows_loop(0, SUB // 2, two_subs)
+
+
+def split_state_kernel(where_ref, state_ref, state_rows, *scratches):
+    split_kernel(state_ref, state_rows, *scratches)
+
+
+def split_forcing_kernel(where_ref, forcing_ref, state_rows, forcing_rows, send_a, send_b, *scratches):
+    split_kernel(forcing_ref, forcing_rows, *scratches)
+    odd = where_ref[0] % 2
     low, high = 0, (OWN - FINE_HALO) * SUB
     size = FINE_HALO * SUB
     for which, rows in enumerate((state_rows, forcing_rows)):
@@ -604,7 +621,7 @@
 
 VMEM = pl.BlockSpec(memory_space=pltpu.VMEM)
 SMEM = pl.BlockSpec(memory_space=pltpu.SMEM)
-ANY = pl.BlockSpec(memory_space=pltpu.HBM)
+HBM = pl.BlockSpec(memory_space=pltpu.HBM)
 
 
 def f32(*shape):
@@ -623,11 +640,11 @@
     return (FIELDS, rows, SUB, LANES)
 
 
-def call(kernel, name, grant, outs, operands, scratches=(), raw=False):
+def call(kernel, name, grant, outs, operands, scratches=(), raw=()):
     return pl.pallas_call(
         kernel,
         out_shape=outs,
-        in_specs=[SMEM] + [ANY if raw else VMEM] * (len(operands) - 1),
+        in_specs=[SMEM] + [HBM if i in raw else VMEM for i in range(1, len(operands))],
         out_specs=[VMEM] * len(outs),
         scratch_shapes=list(scratches),
         name=name,
@@ -665,33 +682,36 @@
             pltpu.VMEM((SUB, OWN), jnp.int32),
             pltpu.SemaphoreType.DMA((2,)),
         ],
-        True,
+        (1, 2),
     )
 
     def doubled(held, step):
         return held + lax.ppermute(held, "axial", [(i, i ^ step) for i in range(size)])
 
-    state, force, send_a, send_b = call(
-        split_kernel,
-        "split", 12,
-        [f32(FIELDS, OWN * SUB, LANES)] * 2 + [f32(2 * FIELDS, FINE_HALO * SUB, LANES)] * 2,
-        [where_ref, in_hbm(initial_state), in_hbm(forcing)],
-        [
-            pltpu.VMEM((3 * 2 * FIELDS * OWN, SUB * LANES), jnp.bfloat16),
-            scratch(2, FIELDS, OWN, SUB * LANES),
-            pltpu.SemaphoreType.DMA((2,)),
-        ],
-        True,
+    temps = [
+        pltpu.VMEM((3 * FIELDS * OWN, SUB * LANES), jnp.bfloat16),
+        scratch(FIELDS, OWN, SUB * LANES),
+        pltpu.SemaphoreType.DMA,
+    ]
+    rows = f32(FIELDS, OWN * SUB, LANES)
+    (state,) = call(
+        split_state_kernel, "split_state", 8, [rows], [where_ref, in_hbm(initial_state)], temps, (1,)
+    )
+    force, send_a, send_b = call(
+        split_forcing_kernel, "split_forcing", 10,
+        [rows] + [f32(2 * FIELDS, FINE_HALO * SUB, LANES)] * 2,
+        [where_ref, in_hbm(forcing), state], temps, (1,),
     )
     step = 1
-    while step < min(size, 8):
-        gathered = doubled(gathered, step)
-        step *= 2
-    gathered, send_a, send_b = lax.optimization_barrier((gathered, send_a, send_b))
-    got_b, got_a = swap_b(send_b), swap_a(send_a)
     while step < size:
         gathered = doubled(gathered, step)
         step *= 2
+        if step == 4:
+            gathered, state = lax.optimization_barrier((gathered, state))
+        elif step == 8:
+            gathered, force = lax.optimization_barrier((gathered, force))
+    gathered, send_a, send_b = lax.optimization_barrier((gathered, send_a, send_b))
+    got_b, got_a = swap_b(send_b), swap_a(send_a)
     (table,) = call(
         functools.partial(tables_kernel, regions),
         "tables", 12,

time: 91.9 us -> 93.9 us (1.022)
  the two profiles are of different devices: /device:TPU:9 before, /device:TPU:17 now
where the time goes in v6:
time: 93.9 us; the launch traced here: 93.6 us
  Pallas kernels  45.9 us (49%)
  waiting for transfers between devices  33.2 us (35%)
  starting transfers between devices  14.2 us (15%)
    pallas_call x12, Pallas kernels, call(): pl.pallas_call(kernel, out_shape=outs, in_specs=[SMEM] + [HBM if i in raw...  45.9 us
    ppermute x4, waiting for transfers between devices, per_device(): swap_b = lambda x: lax.ppermute(x, 'axial', pair_b)  23.3 us
    ppermute x4, starting transfers between devices, per_device(): swap_b = lambda x: lax.ppermute(x, 'axial', pair_b)  8.19 us
    ppermute x6, waiting for transfers between devices, per_device(): swap_a = lambda x: lax.ppermute(x, 'axial', pair_a)  5.2 us
    ppermute x4, waiting for transfers between devices, doubled(): lax.ppermute(held, 'axial', [(i, i ^ step) for i in range(size)])  4.67 us
    ppermute x4, starting transfers between devices, doubled(): lax.ppermute(held, 'axial', [(i, i ^ step) for i in range(size)])  3.46 us
    ppermute x6, starting transfers between devices, per_device(): swap_a = lambda x: lax.ppermute(x, 'axial', pair_a)  2.54 us
  transfers between devices with their start and end apart: 14, of which 10 were waited for; matrix products, arithmetic and copies ran while one was open for 0% of the time, Pallas kernels for 16%

profile of v6, /device:TPU:17, one launch (start us, length us, event | category | flops | bytes accessed | tf_op | source)
XLA Modules:
  0.0 93.6 jit_solution(5995726350138421653)
XLA Ops:
  0.1 1.3 %prep.1 = f32[96,128]{1,0:T(8,128)S(1)} custom-call(s32[2]{0:T(128)S(1)} %pad_add_fusion.where_ref.refs_0_, f32[4,25]{1,0:T(4,128)} %bitcast.4, s32[8,32]{1,0:T(8,128)} %bitcast.3), custom_call_target="tpu_custom_call" | custom-call | tf_op jit(solution)/shard_map/prep/pallas_call | solution.py:644
  1.4 0.7 collective-permute-start
  2.1 0.9 collective-permute-done
  3.0 1.3 %collective-permute-start.1 = (f32[96,128]{1,0:T(8,128)S(1)}, f32[96,128]{1,0:T(8,128)S(1)}, u32[]{:S(2)}, u32[]{:S(2)}) collective-permute-start(f32[96,128]{1,0:T(8,128)S(1)} %add.12), channel_id=1, source_target_pairs={{0,2},{1,3},{2,0},{3,1},{4,6},{5,7},{6,4},{7,5},{8,10},{9,11},{10,... | collective-permute-start | bytes 147464 | tf_op jit(solution)/shard_map/ppermute | solution.py:689
  4.3 3.5 %split_state.1.state_rows.state = f32[5,256,128]{2,1,0:T(8,128)S(1)} custom-call(s32[2]{0:T(128)S(1)} %pad_add_fusion.where_ref.refs_0_, f32[5,32,1024]{2,1,0:T(8,128)} %state_ref.1), custom_call_target="tpu_custom_call" | custom-call | tf_op jit(solution)/shard_map/split_state/pallas_call | solution.py:644
  7.8 1.4 %collective-permute-start.2 = (f32[96,128]{1,0:T(8,128)S(1)}, f32[96,128]{1,0:T(8,128)S(1)}, u32[]{:S(2)}, u32[]{:S(2)}) collective-permute-start(f32[96,128]{1,0:T(8,128)S(1)} %add.13), channel_id=1, source_target_pairs={{0,4},{1,5},{2,6},{3,7},{4,0},{5,1},{6,2},{7,3},{8,12},{9,13},{10,... | collective-permute-start | bytes 147464 | tf_op jit(solution)/shard_map/ppermute | solution.py:689
  9.2 3.6 %split_forcing.1 = (f32[5,256,128]{2,1,0:T(8,128)S(1)}, f32[10,88,128]{2,1,0:T(8,128)S(1)}, f32[10,88,128]{2,1,0:T(8,128)S(1)}) custom-call(s32[2]{0:T(128)S(1)} %pad_add_fusion.where_ref.refs_0_, f32[5,32,1024]{2,1,0:T(8,128)} %forcing_ref.1, f32[5,256,128]{2,1,0:T(8,128)S(1)} %split_state.1.state_rows.state), custom_call_target="tpu_custom_call" | custom-call | tf_op jit(solution)/shard_map/split_forcing/pallas_call | solution.py:644
  12.8 0.1 collective-permute-start.3
  12.9 3.8 %collective-permute-done.3 = f32[96,128]{1,0:T(8,128)S(1)} collective-permute-done((f32[96,128]{1,0:T(8,128)S(1)}, f32[96,128]{1,0:T(8,128)S(1)}, u32[]{:S(2)}, u32[]{:S(2)}) %collective-permute-start.3) | collective-permute-done | bytes 49184 | tf_op jit(solution)/shard_map/ppermute | solution.py:689
  16.7 2.2 %collective-permute-start.4 = (f32[10,88,128]{2,1,0:T(8,128)S(1)}, f32[10,88,128]{2,1,0:T(8,128)S(1)}, u32[]{:S(2)}, u32[]{:S(2)}) collective-permute-start(f32[10,88,128]{2,1,0:T(8,128)S(1)} %get-tuple-element.52), channel_id=1, source_target_pairs={{0,1},{1,0},{2,3},{3,2},{4,5},{5,4},{6,7},{7,6},{8,9},{9,8},{10,11... | collective-permute-start | bytes 1351688 | tf_op jit(solution)/shard_map/ppermute | solution.py:668
  18.9 2.1 %collective-permute-start.5 = (f32[10,88,128]{2,1,0:T(8,128)S(1)}, f32[10,88,128]{2,1,0:T(8,128)S(1)}, u32[]{:S(2)}, u32[]{:S(2)}) collective-permute-start(f32[10,88,128]{2,1,0:T(8,128)S(1)} %get-tuple-element.53), channel_id=1, source_target_pairs={{1,2},{2,1},{3,4},{4,3},{5,6},{6,5},{7,8},{8,7},{9,10},{10,9},{11,... | collective-permute-start | bytes 1351688 | tf_op jit(solution)/shard_map/ppermute | solution.py:669
  21.0 2.0 %tables.1.table.refs_9_.refs_10_ = f32[50,160,128]{2,1,0:T(8,128)S(1)} custom-call(s32[2]{0:T(128)S(1)} %pad_add_fusion.where_ref.refs_0_, f32[96,128]{1,0:T(8,128)S(1)} %add.15.regions_ref), custom_call_target="tpu_custom_call" | custom-call | tf_op jit(solution)/shard_map/tables/pallas_call | solution.py:644
  23.0 2.8 %interior.2 = (f32[5,720,128]{2,1,0:T(8,128)S(1)}, f32[5,720,128]{2,1,0:T(8,128)S(1)}, f32[5,480,128]{2,1,0:T(8,128)S(1)}, f32[5,32,8,128]{3,2,1,0:T(8,128)S(1)}, f32[5,480,128]{2,1,0:T(8,128)S(1)}) custom-call(s32[2]{0:T(128)S(1)} %pad_add_fusion.where_ref.refs_0_, f32[5,256,128]{2,1,0:T(8,128)S(1)} %split_state.1.state_rows.state, ...), custom_call_target="tpu_custom_call" | custom-call | tf_op jit(solution)/shard_map/interior/pallas_call | solution.py:644
  25.8 7.6 %collective-permute-done.5.refs_8_ = f32[10,88,128]{2,1,0:T(8,128)S(1)} collective-permute-done((f32[10,88,128]{2,1,0:T(8,128)S(1)}, f32[10,88,128]{2,1,0:T(8,128)S(1)}, u32[]{:S(2)}, u32[]{:S(2)}) %collective-permute-start.5) | collective-permute-done | bytes 450592 | tf_op jit(solution)/shard_map/ppermute | solution.py:669
  33.4 4.4 %down_fresh.1 = (f32[5,720,128]{2,1,0:T(8,128)S(1)}, f32[5,480,128]{2,1,0:T(8,128)S(1)}, f32[5,32,8,128]{3,2,1,0:T(8,128)S(1)}, f32[5,480,128]{2,1,0:T(8,128)S(1...) custom-call(s32[2]{0:T(128)S(1)} %pad_add_fusion.where_ref.refs_0_, ...), custom_call_target="tpu_custom_call" | custom-call | tf_op jit(solution)/shard_map/down_fresh/pallas_call | solution.py:644
  37.9 1.3 %collective-permute-done.6.beside.refs_2_ = f32[2,10,8,128]{3,2,1,0:T(8,128)S(1)} collective-permute-done((f32[2,10,8,128]{3,2,1,0:T(8,128)S(1)}, f32[2,10,8,128]{3,2,1,0:T(8,128)S(1)}, u32[]{:S(2)}, u32[]{:S(2)}) %collective-permute-start.6) | collective-permute-done | bytes 81952 | tf_op jit(solution)/shard_map/ppermute | solution.py:668
  39.2 0.6 relay.2
  39.7 2.1 %collective-permute-start.7 = (f32[3,10,8,128]{3,2,1,0:T(8,128)S(1)}, f32[3,10,8,128]{3,2,1,0:T(8,128)S(1)}, u32[]{:S(2)}, u32[]{:S(2)}) collective-permute-start(f32[3,10,8,128]{3,2,1,0:T(8,128)S(1)} %relay.2), channel_id=1, source_target_pairs={{1,2},{2,1},{3,4},{4,3},{5,6},{6,5},{7,8},{8,7},{9,10},{10,9},{11,... | collective-permute-start | bytes 368648 | tf_op jit(solution)/shard_map/ppermute | solution.py:669
  41.8 5.4 %collective-permute-done.7.refs_3_ = f32[3,10,8,128]{3,2,1,0:T(8,128)S(1)} collective-permute-done((f32[3,10,8,128]{3,2,1,0:T(8,128)S(1)}, f32[3,10,8,128]{3,2,1,0:T(8,128)S(1)}, u32[]{:S(2)}, u32[]{:S(2)}) %collective-permute-start.7) | collective-permute-done | bytes 122912 | tf_op jit(solution)/shard_map/ppermute | solution.py:669
  47.2 1.3 %collective-permute-done.8.refs_4_ = f32[3,10,8,128]{3,2,1,0:T(8,128)S(1)} collective-permute-done((f32[3,10,8,128]{3,2,1,0:T(8,128)S(1)}, f32[3,10,8,128]{3,2,1,0:T(8,128)S(1)}, u32[]{:S(2)}, u32[]{:S(2)}) %collective-permute-start.8) | collective-permute-done | bytes 122912 | tf_op jit(solution)/shard_map/ppermute | solution.py:668
  48.6 8.8 %up.1 = (f32[5,256,128]{2,1,0:T(8,128)S(1)}, f32[5,88,128]{2,1,0:T(8,128)S(1)}, f32[5,88,128]{2,1,0:T(8,128)S(1)}) custom-call(s32[2]{0:T(128)S(1)} %pad_add_fusion.where_ref.refs_0_, f32[2,10,8,128]{3,2,1,0:T(8,128)S(1)} %get-tuple-element.54.own.refs_1_, f32[2,10,8,128]{3,2,1,0:T(8,128)S(1)} %collective-permute-done.6.beside.refs_2_, ...), custom_call_target="tpu_custom_call" | custom-call | tf_op jit(solution)/shard_map/up/pallas_call | solution.py:644
  57.4 0.2 collective-permute-start.9
  57.6 1.9 %collective-permute-start.10 = (f32[5,88,128]{2,1,0:T(8,128)S(1)}, f32[5,88,128]{2,1,0:T(8,128)S(1)}, u32[]{:S(2)}, u32[]{:S(2)}) collective-permute-start(f32[5,88,128]{2,1,0:T(8,128)S(1)} %get-tuple-element.67), channel_id=1, source_target_pairs={{1,2},{2,1},{3,4},{4,3},{5,6},{6,5},{7,8},{8,7},{9,10},{10,9},{11,... | collective-permute-start | bytes 675848 | tf_op jit(solution)/shard_map/ppermute | solution.py:669
  59.6 2.8 %interior.3 = (f32[5,720,128]{2,1,0:T(8,128)S(1)}, f32[5,720,128]{2,1,0:T(8,128)S(1)}, f32[5,480,128]{2,1,0:T(8,128)S(1)}, f32[5,32,8,128]{3,2,1,0:T(8,128)S(1)}, f32[5,480,128]{2,1,0:T(8,128)S(1)}) custom-call(s32[2]{0:T(128)S(1)} %pad_add_fusion.where_ref.refs_0_, f32[5,256,128]{2,1,0:T(8,128)S(1)} %get-tuple-element.60.state, ...), custom_call_target="tpu_custom_call" | custom-call | tf_op jit(solution)/shard_map/interior/pallas_call | solution.py:644
  62.4 4.9 %collective-permute-done.10.refs_7_ = f32[5,88,128]{2,1,0:T(8,128)S(1)} collective-permute-done((f32[5,88,128]{2,1,0:T(8,128)S(1)}, f32[5,88,128]{2,1,0:T(8,128)S(1)}, u32[]{:S(2)}, u32[]{:S(2)}) %collective-permute-start.10) | collective-permute-done | bytes 225312 | tf_op jit(solution)/shard_map/ppermute | solution.py:669
  67.3 4.2 %down.1 = (f32[5,720,128]{2,1,0:T(8,128)S(1)}, f32[5,480,128]{2,1,0:T(8,128)S(1)}, f32[5,32,8,128]{3,2,1,0:T(8,128)S(1)}, f32[5,480,128]{2,1,0:T(8,128)S(1)}, f32[2,10,8,128]{3,2,1,0:T(8,128)S(1)}) custom-call(s32[2]{0:T(128)S(1)} %pad_add_fusion.where_ref.refs_0_, f32[5,720,128]{2,1,0:T(8,128)S(1)} %get-tuple-element.61.refs_1_, ...), custom_call_target="tpu_custom_call" | custom-call | tf_op jit(solution)/shard_map/down/pallas_call | solution.py:644
  71.6 1.3 %collective-permute-done.11.beside.refs_2_ = f32[2,10,8,128]{3,2,1,0:T(8,128)S(1)} collective-permute-done((f32[2,10,8,128]{3,2,1,0:T(8,128)S(1)}, f32[2,10,8,128]{3,2,1,0:T(8,128)S(1)}, u32[]{:S(2)}, u32[]{:S(2)}) %collective-permute-start.11) | collective-permute-done | bytes 81952 | tf_op jit(solution)/shard_map/ppermute | solution.py:668
  72.9 0.6 relay.3
  73.4 2.1 %collective-permute-start.12 = (f32[3,10,8,128]{3,2,1,0:T(8,128)S(1)}, f32[3,10,8,128]{3,2,1,0:T(8,128)S(1)}, u32[]{:S(2)}, u32[]{:S(2)}) collective-permute-start(f32[3,10,8,128]{3,2,1,0:T(8,128)S(1)} %relay.3), channel_id=1, source_target_pairs={{1,2},{2,1},{3,4},{4,3},{5,6},{6,5},{7,8},{8,7},{9,10},{10,9},{11,... | collective-permute-start | bytes 368648 | tf_op jit(solution)/shard_map/ppermute | solution.py:669
  75.5 5.4 %collective-permute-done.12.refs_3_ = f32[3,10,8,128]{3,2,1,0:T(8,128)S(1)} collective-permute-done((f32[3,10,8,128]{3,2,1,0:T(8,128)S(1)}, f32[3,10,8,128]{3,2,1,0:T(8,128)S(1)}, u32[]{:S(2)}, u32[]{:S(2)}) %collective-permute-start.12) | collective-permute-done | bytes 122912 | tf_op jit(solution)/shard_map/ppermute | solution.py:669
  80.9 1.3 %collective-permute-done.13.refs_4_ = f32[3,10,8,128]{3,2,1,0:T(8,128)S(1)} collective-permute-done((f32[3,10,8,128]{3,2,1,0:T(8,128)S(1)}, f32[3,10,8,128]{3,2,1,0:T(8,128)S(1)}, u32[]{:S(2)}, u32[]{:S(2)}) %collective-permute-start.13) | collective-permute-done | bytes 122912 | tf_op jit(solution)/shard_map/ppermute | solution.py:668
  82.3 11.3 %up_last.1 = f32[5,32,1024]{2,1,0:T(8,128)} custom-call(s32[2]{0:T(128)S(1)} %pad_add_fusion.where_ref.refs_0_, f32[2,10,8,128]{3,2,1,0:T(8,128)S(1)} %get-tuple-element.68.own.refs_1_, f32[2,10,8,128]{3,2,1,0:T(8,128)S(1)} %collective-permute-done.11.beside.refs_2_, f32[3,10,8,128]{3,2,1,0:T(8,128)S(1)} %collective-permute-done.12.refs_3_, ...), custom_call_target="tpu_custom_call" | custom-call | tf_op jit(solution)/shard_map/up_last/pallas_call | solution.py:644
  (13 shorter events, 0.3 us)
Async XLA Ops:
  1.4 1.6 %collective-permute-start = (f32[96,128]{1,0:T(8,128)S(1)}, f32[96,128]{1,0:T(8,128)S(1)}, u32[]{:S(2)}, u32[]{:S(2)}) collective-permute-start(f32[96,128]{1,0:T(8,128)S(1)} %prep.1), channel_id=1, source_target_pairs={{0,1},{1,0},{2,3},{3,2},{4,5},{5,4},{6,7},{7,6},{8,9},{9,8},{10,11... | collective-permute-start | bytes 147464 | tf_op jit(solution)/shard_map/ppermute | solution.py:689
  3.0 4.8 %collective-permute-start.1 = (f32[96,128]{1,0:T(8,128)S(1)}, f32[96,128]{1,0:T(8,128)S(1)}, u32[]{:S(2)}, u32[]{:S(2)}) collective-permute-start(f32[96,128]{1,0:T(8,128)S(1)} %add.12), channel_id=1, source_target_pairs={{0,2},{1,3},{2,0},{3,1},{4,6},{5,7},{6,4},{7,5},{8,10},{9,11},{10,... | collective-permute-start | bytes 147464 | tf_op jit(solution)/shard_map/ppermute | solution.py:689
  7.8 4.9 %collective-permute-start.2 = (f32[96,128]{1,0:T(8,128)S(1)}, f32[96,128]{1,0:T(8,128)S(1)}, u32[]{:S(2)}, u32[]{:S(2)}) collective-permute-start(f32[96,128]{1,0:T(8,128)S(1)} %add.13), channel_id=1, source_target_pairs={{0,4},{1,5},{2,6},{3,7},{4,0},{5,1},{6,2},{7,3},{8,12},{9,13},{10,... | collective-permute-start | bytes 147464 | tf_op jit(solution)/shard_map/ppermute | solution.py:689
  12.8 3.9 %collective-permute-start.3 = (f32[96,128]{1,0:T(8,128)S(1)}, f32[96,128]{1,0:T(8,128)S(1)}, u32[]{:S(2)}, u32[]{:S(2)}) collective-permute-start(f32[96,128]{1,0:T(8,128)S(1)} %add.14), channel_id=1, source_target_pairs={{0,8},{1,9},{2,10},{3,11},{4,12},{5,13},{6,14},{7,15},{8,0},{9,1},... | collective-permute-start | bytes 147464 | tf_op jit(solution)/shard_map/ppermute | solution.py:689
  16.7 9.1 %collective-permute-start.4 = (f32[10,88,128]{2,1,0:T(8,128)S(1)}, f32[10,88,128]{2,1,0:T(8,128)S(1)}, u32[]{:S(2)}, u32[]{:S(2)}) collective-permute-start(f32[10,88,128]{2,1,0:T(8,128)S(1)} %get-tuple-element.52), channel_id=1, source_target_pairs={{0,1},{1,0},{2,3},{3,2},{4,5},{5,4},{6,7},{7,6},{8,9},{9,8},{10,11... | collective-permute-start | bytes 1351688 | tf_op jit(solution)/shard_map/ppermute | solution.py:668
  18.9 14.5 %collective-permute-start.5 = (f32[10,88,128]{2,1,0:T(8,128)S(1)}, f32[10,88,128]{2,1,0:T(8,128)S(1)}, u32[]{:S(2)}, u32[]{:S(2)}) collective-permute-start(f32[10,88,128]{2,1,0:T(8,128)S(1)} %get-tuple-element.53), channel_id=1, source_target_pairs={{1,2},{2,1},{3,4},{4,3},{5,6},{6,5},{7,8},{8,7},{9,10},{10,9},{11,... | collective-permute-start | bytes 1351688 | tf_op jit(solution)/shard_map/ppermute | solution.py:669
  37.8 1.3 %collective-permute-start.6 = (f32[2,10,8,128]{3,2,1,0:T(8,128)S(1)}, f32[2,10,8,128]{3,2,1,0:T(8,128)S(1)}, u32[]{:S(2)}, u32[]{:S(2)}) collective-permute-start(f32[2,10,8,128]{3,2,1,0:T(8,128)S(1)} %get-tuple-element.54.own.refs_1_), channel_id=1, source_target_pairs={{0,1},{1,0},{2,3},{3,2},{4,5},{5,4},{6,7},{7,6},{8,9},{9,8},{10,11... | collective-permute-start | bytes 245768 | tf_op jit(solution)/shard_map/ppermute | solution.py:668
  39.7 7.5 %collective-permute-start.7 = (f32[3,10,8,128]{3,2,1,0:T(8,128)S(1)}, f32[3,10,8,128]{3,2,1,0:T(8,128)S(1)}, u32[]{:S(2)}, u32[]{:S(2)}) collective-permute-start(f32[3,10,8,128]{3,2,1,0:T(8,128)S(1)} %relay.2), channel_id=1, source_target_pairs={{1,2},{2,1},{3,4},{4,3},{5,6},{6,5},{7,8},{8,7},{9,10},{10,9},{11,... | collective-permute-start | bytes 368648 | tf_op jit(solution)/shard_map/ppermute | solution.py:669
  47.2 1.3 %collective-permute-start.8 = (f32[3,10,8,128]{3,2,1,0:T(8,128)S(1)}, f32[3,10,8,128]{3,2,1,0:T(8,128)S(1)}, u32[]{:S(2)}, u32[]{:S(2)}) collective-permute-start(f32[3,10,8,128]{3,2,1,0:T(8,128)S(1)} %collective-permute-done.7.refs_3_), channel_id=1, source_target_pairs={{0,1},{1,0},{2,3},{3,2},{4,5},{5,4},{6,7},{7,6},{8,9},{9,8},{10,11... | collective-permute-start | bytes 368648 | tf_op jit(solution)/shard_map/ppermute | solution.py:668
  57.4 5.0 %collective-permute-start.9 = (f32[5,88,128]{2,1,0:T(8,128)S(1)}, f32[5,88,128]{2,1,0:T(8,128)S(1)}, u32[]{:S(2)}, u32[]{:S(2)}) collective-permute-start(f32[5,88,128]{2,1,0:T(8,128)S(1)} %get-tuple-element.66), channel_id=1, source_target_pairs={{0,1},{1,0},{2,3},{3,2},{4,5},{5,4},{6,7},{7,6},{8,9},{9,8},{10,11... | collective-permute-start | bytes 675848 | tf_op jit(solution)/shard_map/ppermute | solution.py:668
  57.6 9.7 %collective-permute-start.10 = (f32[5,88,128]{2,1,0:T(8,128)S(1)}, f32[5,88,128]{2,1,0:T(8,128)S(1)}, u32[]{:S(2)}, u32[]{:S(2)}) collective-permute-start(f32[5,88,128]{2,1,0:T(8,128)S(1)} %get-tuple-element.67), channel_id=1, source_target_pairs={{1,2},{2,1},{3,4},{4,3},{5,6},{6,5},{7,8},{8,7},{9,10},{10,9},{11,... | collective-permute-start | bytes 675848 | tf_op jit(solution)/shard_map/ppermute | solution.py:669
  71.5 1.3 %collective-permute-start.11 = (f32[2,10,8,128]{3,2,1,0:T(8,128)S(1)}, f32[2,10,8,128]{3,2,1,0:T(8,128)S(1)}, u32[]{:S(2)}, u32[]{:S(2)}) collective-permute-start(f32[2,10,8,128]{3,2,1,0:T(8,128)S(1)} %get-tuple-element.68.own.refs_1_), channel_id=1, source_target_pairs={{0,1},{1,0},{2,3},{3,2},{4,5},{5,4},{6,7},{7,6},{8,9},{9,8},{10,11... | collective-permute-start | bytes 245768 | tf_op jit(solution)/shard_map/ppermute | solution.py:668
  73.4 7.5 %collective-permute-start.12 = (f32[3,10,8,128]{3,2,1,0:T(8,128)S(1)}, f32[3,10,8,128]{3,2,1,0:T(8,128)S(1)}, u32[]{:S(2)}, u32[]{:S(2)}) collective-permute-start(f32[3,10,8,128]{3,2,1,0:T(8,128)S(1)} %relay.3), channel_id=1, source_target_pairs={{1,2},{2,1},{3,4},{4,3},{5,6},{6,5},{7,8},{8,7},{9,10},{10,9},{11,... | collective-permute-start | bytes 368648 | tf_op jit(solution)/shard_map/ppermute | solution.py:669
  80.9 1.3 %collective-permute-start.13 = (f32[3,10,8,128]{3,2,1,0:T(8,128)S(1)}, f32[3,10,8,128]{3,2,1,0:T(8,128)S(1)}, u32[]{:S(2)}, u32[]{:S(2)}) collective-permute-start(f32[3,10,8,128]{3,2,1,0:T(8,128)S(1)} %collective-permute-done.12.refs_3_), channel_id=1, source_target_pairs={{0,1},{1,0},{2,3},{3,2},{4,5},{5,4},{6,7},{7,6},{8,9},{9,8},{10,11... | collective-permute-start | bytes 368648 | tf_op jit(solution)/shard_map/ppermute | solution.py:668

commit v7 on v5

--- a/solution.py
+++ b/solution.py
@@ -22,12 +22,14 @@
 T1, O1 = 32, 8
 T2, O2 = 40, 16
 T3, O3 = 20, 8
+COARSEST = 3
+EDGE_BATCH = 10
 GROUP = 4
 SPREAD = 16
 
 
 def stride_of(level):
-    return SUB + 2 * 2**level
+    return SUB + (0 if level == COARSEST else 2 * 2**level) + (level == 2)
 
 
 def padded_rows(rows, level):
@@ -35,7 +37,7 @@
 
 
 def at(row, level):
-    return stride_of(level) * row + 2**level
+    return stride_of(level) * row + (0 if level == COARSEST else 2**level)
 
 
 def lane_iota():
@@ -55,13 +57,20 @@
 
 
 def edges(ref, level, first, last):
+    if level == COARSEST:
+        return
     width, stride, lane = 2**level, stride_of(level), lane_iota()
-    for row in range(first, last, SUB):
-        start = at(row, level)
-        for field in range(FIELDS):
-            rows = lambda sub: (field, pl.ds(start + sub, SUB, stride=stride), slice(None))
+    places = [(row, field) for row in range(first, last, SUB) for field in range(FIELDS)]
+    for part in range(0, len(places), EDGE_BATCH):
+        written = []
+        for row, field in places[part : part + EDGE_BATCH]:
+            rows = lambda sub, row=row, field=field: (
+                field, pl.ds(at(row, level) + sub, SUB, stride=stride), slice(None)
+            )
             before = jnp.where(lane == 0, 0.0, pltpu.roll(ref[rows(SUB - 1)], 1, 1))
             after = jnp.where(lane == LANES - 1, 0.0, pltpu.roll(ref[rows(0)], LANES - 1, 1))
+            written.append((rows, before, after))
+        for rows, before, after in written:
             for i in range(width):
                 ref[rows(i - width)] = before
                 ref[rows(SUB + i)] = after
@@ -87,12 +96,19 @@
 
 def neighbours(ref, row, level):
     start, width, stride = at(row, level), 2**level, stride_of(level)
+    lane = lane_iota()
     sums, centres = [], []
     for field in range(FIELDS):
-        load = lambda first: ref[field, pl.ds(first, SUB), :]
-        radial = load(start - width) + load(start + width)
+        load = lambda first, field=field: ref[field, pl.ds(first, SUB), :]
+        centre = load(start)
+        if level == COARSEST:
+            radial = jnp.where(lane == 0, 0.0, pltpu.roll(centre, 1, 1)) + jnp.where(
+                lane == LANES - 1, 0.0, pltpu.roll(centre, LANES - 1, 1)
+            )
+        else:
+            radial = load(start - width) + load(start + width)
         sums.append(radial + (load(start - stride) + load(start + stride)))
-        centres.append(load(start))
+        centres.append(centre)
     return sums, centres
 
 
@@ -431,7 +447,7 @@
     rows_loop(0, FINE_HALO, halo)
 
 
-def interior_kernel(fresh, where_ref, state, force, table, v0, tmp0, c1, q1, tmp1):
+def interior_kernel(where_ref, state, f0, table, v0, tmp0, c1, q1, tmp1):
     def own(row):
         start = pl.multiple_of(row * SUB, SUB)
         for field in range(FIELDS):
@@ -439,47 +455,49 @@
 
     rows_loop(0, OWN, own)
     edges(v0, 0, O0, O0 + OWN)
-    if fresh:
-        source = lambda field, row: force[field, pl.ds(pl.multiple_of((row - O0) * SUB, SUB), SUB), :]
-    else:
-        source = lambda field, row: force[field, row]
+    source = lambda field, row: f0[field, row]
     sweep(source, v0, tmp0, table, 0, O0 + 1, O0 + OWN - 1, batch=5)
     sweep(source, tmp0, v0, table, 0, O0 + 2, O0 + OWN - 2, batch=4)
     descend(source, v0, table, 0, c1, q1, tmp1, O1 + INNER, O1 + OWN // 2 - INNER)
 
 
 def down_kernel(fresh, *refs):
+    half = OWN // 2
+    low, high = O0 - FINE_HALO, O0 + OWN + FINE_HALO
     if fresh:
-        (where_ref, v0_in, tmp0_in, c1_in, q1_in, tmp1_in, force, got_a, got_b, table,
-         v0, v1, s1, c1, send, f0, tmp0, tmp1, q1) = refs
+        where_ref, state, force, got_a, got_b, table, v0, v1, s1, c1, send, f0, tmp0, tmp1, q1 = refs
+        place_halo(where_ref, v0, state, got_a, got_b, 0, True)
+        edges(v0, 0, low, high)
+        place_halo(where_ref, f0, force, got_a, got_b, FIELDS, False)
     else:
         (where_ref, v0_in, tmp0_in, c1_in, q1_in, tmp1_in, got_a, got_b, f0, table,
          v0, v1, s1, c1, send, tmp0, tmp1, q1) = refs
-    half = OWN // 2
-
-    def take(target, source, level, first, last):
-        rows = slice(at(first, level) - 2**level, at(last, level) - 2**level)
-        target[:, rows, :] = source[:, rows, :]
-
-    take(v0, v0_in, 0, O0, O0 + OWN)
-    take(tmp0, tmp0_in, 0, O0 + 1, O0 + 3)
-    take(tmp0, tmp0_in, 0, O0 + OWN - 3, O0 + OWN - 1)
-    inner = slice(O1 + INNER, O1 + half - INNER)
-    take(c1, c1_in, 1, inner.start, inner.stop)
-    take(tmp1, tmp1_in, 1, inner.start, inner.stop)
-    q1[:, inner] = q1_in[:, inner]
-
-    place_halo(where_ref, v0, None, got_a, got_b, 0, True)
-    edges(v0, 0, O0 - FINE_HALO, O0)
-    edges(v0, 0, O0 + OWN, O0 + OWN + FINE_HALO)
+
+        def take(target, source, level, first, last):
+            rows = slice(at(first, level) - 2**level, at(last, level) - 2**level)
+            target[:, rows, :] = source[:, rows, :]
+
+        take(v0, v0_in, 0, O0, O0 + OWN)
+        take(tmp0, tmp0_in, 0, O0 + 1, O0 + 3)
+        take(tmp0, tmp0_in, 0, O0 + OWN - 3, O0 + OWN - 1)
+        inner = slice(O1 + INNER, O1 + half - INNER)
+        take(c1, c1_in, 1, inner.start, inner.stop)
+        take(tmp1, tmp1_in, 1, inner.start, inner.stop)
+        q1[:, inner] = q1_in[:, inner]
+        place_halo(where_ref, v0, None, got_a, got_b, 0, True)
+        edges(v0, 0, low, O0)
+        edges(v0, 0, O0 + OWN, high)
+    fine_source = lambda field, row: f0[field, row]
     if fresh:
-        place_halo(where_ref, f0, force, got_a, got_b, FIELDS, False)
-    fine_source = lambda field, row: f0[field, row]
-    for swept, (old, new) in enumerate(((v0, tmp0), (tmp0, v0))):
-        for first in (O0 - FINE_HALO + swept, O0 + OWN - 1 - swept):
-            sweep(fine_source, old, new, table, 0, first, first + FINE_HALO + 1)
-    for first in (O1 - 4, O1 + half - INNER):
-        descend(fine_source, v0, table, 0, c1, q1, tmp1, first, first + 4 + INNER)
+        sweep(fine_source, v0, tmp0, table, 0, low + 1, high - 1)
+        sweep(fine_source, tmp0, v0, table, 0, low + 2, high - 2)
+        descend(fine_source, v0, table, 0, c1, q1, tmp1, O1 - 4, O1 + half + 4)
+    else:
+        for swept, (old, new) in enumerate(((v0, tmp0), (tmp0, v0))):
+            for first in (low + swept, O0 + OWN - 1 - swept):
+                sweep(fine_source, old, new, table, 0, first, first + FINE_HALO + 1)
+        for first in (O1 - 4, O1 + half - INNER):
+            descend(fine_source, v0, table, 0, c1, q1, tmp1, first, first + 4 + INNER)
     make_source(c1, q1, s1, table, 1, O1 - 3, O1 + half + 3)
     first_source = lambda field, row: s1[field, row]
     sweep(first_source, tmp1, v1, table, 1, O1 - 3, O1 + half + 3)
@@ -604,7 +622,7 @@
 
 VMEM = pl.BlockSpec(memory_space=pltpu.VMEM)
 SMEM = pl.BlockSpec(memory_space=pltpu.SMEM)
-ANY = pl.BlockSpec(memory_space=pltpu.HBM)
+HBM = pl.BlockSpec(memory_space=pltpu.HBM)
 
 
 def f32(*shape):
@@ -623,11 +641,11 @@
     return (FIELDS, rows, SUB, LANES)
 
 
-def call(kernel, name, grant, outs, operands, scratches=(), raw=False):
+def call(kernel, name, grant, outs, operands, scratches=(), raw=()):
     return pl.pallas_call(
         kernel,
         out_shape=outs,
-        in_specs=[SMEM] + [ANY if raw else VMEM] * (len(operands) - 1),
+        in_specs=[SMEM] + [HBM if i in raw else VMEM for i in range(1, len(operands))],
         out_specs=[VMEM] * len(outs),
         scratch_shapes=list(scratches),
         name=name,
@@ -665,7 +683,7 @@
             pltpu.VMEM((SUB, OWN), jnp.int32),
             pltpu.SemaphoreType.DMA((2,)),
         ],
-        True,
+        (1, 2),
     )
 
     def doubled(held, step):
@@ -673,7 +691,8 @@
 
     state, force, send_a, send_b = call(
         split_kernel,
-        "split", 12,
+        "split",
+        12,
         [f32(FIELDS, OWN * SUB, LANES)] * 2 + [f32(2 * FIELDS, FINE_HALO * SUB, LANES)] * 2,
         [where_ref, in_hbm(initial_state), in_hbm(forcing)],
         [
@@ -681,10 +700,10 @@
             scratch(2, FIELDS, OWN, SUB * LANES),
             pltpu.SemaphoreType.DMA((2,)),
         ],
-        True,
+        (1, 2),
     )
     step = 1
-    while step < min(size, 8):
+    while step < min(size, 4):
         gathered = doubled(gathered, step)
         step *= 2
     gathered, send_a, send_b = lax.optimization_barrier((gathered, send_a, send_b))
@@ -702,21 +721,20 @@
 
     f0 = None
     for cycle in range(CYCLES):
-        fresh = cycle == 0
-        inner = call(
-            functools.partial(interior_kernel, fresh), "interior", 4,
-            [f32(*padded(T0, 0))] * 2 + [f32(*padded(T1, 1)), f32(*plain(T1)), f32(*padded(T1, 1))],
-            [where_ref, state, force if fresh else f0, table],
-        )
         outs = [f32(*padded(T0, 0)), f32(*padded(T1, 1)), f32(*plain(T1)), f32(*padded(T1, 1)),
                 f32(2, 2 * FIELDS, SUB, LANES)]
         temps = [scratch(*padded(T0, 0)), scratch(*padded(T1, 1)), scratch(*plain(T1))]
-        if fresh:
+        if cycle == 0:
             v0, v1, s1, c1, own, f0 = call(
                 functools.partial(down_kernel, True), "down_fresh", 14, outs + [f32(*plain(T0))],
-                [where_ref, *inner, force, got_a, got_b, table], temps,
+                [where_ref, state, force, got_a, got_b, table], temps,
             )
         else:
+            inner = call(
+                interior_kernel, "interior", 4,
+                [f32(*padded(T0, 0))] * 2 + [f32(*padded(T1, 1)), f32(*plain(T1)), f32(*padded(T1, 1))],
+                [where_ref, state, f0, table],
+            )
             v0, v1, s1, c1, own = call(
                 functools.partial(down_kernel, False), "down", 14, outs,
                 [where_ref, *inner, got_a, got_b, f0, table], temps,

time: 91.9 us -> 89.3 us (0.972)
  the two profiles are of different devices: /device:TPU:9 before, /device:TPU:17 now
where the time goes in v7:
time: 89.3 us; the launch traced here: 89.1 us
  Pallas kernels  41.5 us (46%)
  waiting for transfers between devices  30.9 us (35%)
  starting transfers between devices  16.5 us (18%)
    pallas_call x10, Pallas kernels, call(): pl.pallas_call(kernel, out_shape=outs, in_specs=[SMEM] + [HBM if i in raw...  41.5 us
    ppermute x4, waiting for transfers between devices, per_device(): swap_b = lambda x: lax.ppermute(x, 'axial', pair_b)  18.9 us
    ppermute x4, starting transfers between devices, per_device(): swap_b = lambda x: lax.ppermute(x, 'axial', pair_b)  7.72 us
    ppermute x4, waiting for transfers between devices, doubled(): lax.ppermute(held, 'axial', [(i, i ^ step) for i in range(size)])  7.18 us
    ppermute x6, starting transfers between devices, per_device(): swap_a = lambda x: lax.ppermute(x, 'axial', pair_a)  5.34 us
    ppermute x6, waiting for transfers between devices, per_device(): swap_a = lambda x: lax.ppermute(x, 'axial', pair_a)  4.83 us
    ppermute x4, starting transfers between devices, doubled(): lax.ppermute(held, 'axial', [(i, i ^ step) for i in range(size)])  3.4 us
  transfers between devices with their start and end apart: 14, of which 11 were waited for; matrix products, arithmetic and copies ran while one was open for 0% of the time, Pallas kernels for 11%

profile of v7, /device:TPU:17, one launch (start us, length us, event | category | flops | bytes accessed | tf_op | source)
XLA Modules:
  0.0 89.1 jit_solution(2795333129307934932)
XLA Ops:
  0.0 0.1 pad_add_fusion.where_ref.refs_0_
  0.1 1.3 %prep.1 = f32[96,128]{1,0:T(8,128)S(1)} custom-call(s32[2]{0:T(128)S(1)} %pad_add_fusion.where_ref.refs_0_, f32[4,25]{1,0:T(4,128)} %bitcast.4, s32[8,32]{1,0:T(8,128)} %bitcast.3), custom_call_target="tpu_custom_call" | custom-call | tf_op jit(solution)/shard_map/prep/pallas_call | solution.py:645
  1.4 0.7 collective-permute-start
  2.1 0.9 collective-permute-done
  3.0 1.3 %collective-permute-start.1 = (f32[96,128]{1,0:T(8,128)S(1)}, f32[96,128]{1,0:T(8,128)S(1)}, u32[]{:S(2)}, u32[]{:S(2)}) collective-permute-start(f32[96,128]{1,0:T(8,128)S(1)} %add.12), channel_id=1, source_target_pairs={{0,2},{1,3},{2,0},{3,1},{4,6},{5,7},{6,4},{7,5},{8,10},{9,11},{10,... | collective-permute-start | bytes 147464 | tf_op jit(solution)/shard_map/ppermute | solution.py:690
  4.3 4.8 %split.1 = (f32[5,256,128]{2,1,0:T(8,128)S(1)}, f32[5,256,128]{2,1,0:T(8,128)S(1)}, f32[10,88,128]{2,1,0:T(8,128)S(1)}, f32[10,88,128]{2,1,0:T(8,128)S(1)}) custom-call(s32[2]{0:T(128)S(1)} %pad_add_fusion.where_ref.refs_0_, f32[5,32,1024]{2,1,0:T(8,128)} %state_ref.1, f32[5,32,1024]{2,1,0:T(8,128)} %forcing_ref.1), custom_call_target="tpu_custom_call" | custom-call | tf_op jit(solution)/shard_map/split/pallas_call | solution.py:645
  9.1 0.8 collective-permute-start.2
  9.8 2.0 %collective-permute-start.3 = (f32[10,88,128]{2,1,0:T(8,128)S(1)}, f32[10,88,128]{2,1,0:T(8,128)S(1)}, u32[]{:S(2)}, u32[]{:S(2)}) collective-permute-start(f32[10,88,128]{2,1,0:T(8,128)S(1)} %get-tuple-element.36), channel_id=1, source_target_pairs={{1,2},{2,1},{3,4},{4,3},{5,6},{6,5},{7,8},{8,7},{9,10},{10,9},{11,... | collective-permute-start | bytes 1351688 | tf_op jit(solution)/shard_map/ppermute | solution.py:670
  11.8 1.4 %collective-permute-start.4 = (f32[96,128]{1,0:T(8,128)S(1)}, f32[96,128]{1,0:T(8,128)S(1)}, u32[]{:S(2)}, u32[]{:S(2)}) collective-permute-start(f32[96,128]{1,0:T(8,128)S(1)} %add.13), channel_id=1, source_target_pairs={{0,4},{1,5},{2,6},{3,7},{4,0},{5,1},{6,2},{7,3},{8,12},{9,13},{10,... | collective-permute-start | bytes 147464 | tf_op jit(solution)/shard_map/ppermute | solution.py:690
  13.2 2.2 %collective-permute-done.4 = f32[96,128]{1,0:T(8,128)S(1)} collective-permute-done((f32[96,128]{1,0:T(8,128)S(1)}, f32[96,128]{1,0:T(8,128)S(1)}, u32[]{:S(2)}, u32[]{:S(2)}) %collective-permute-start.4) | collective-permute-done | bytes 49184 | tf_op jit(solution)/shard_map/ppermute | solution.py:690
  15.4 4.1 %collective-permute-done.5 = f32[96,128]{1,0:T(8,128)S(1)} collective-permute-done((f32[96,128]{1,0:T(8,128)S(1)}, f32[96,128]{1,0:T(8,128)S(1)}, u32[]{:S(2)}, u32[]{:S(2)}) %collective-permute-start.5) | collective-permute-done | bytes 49184 | tf_op jit(solution)/shard_map/ppermute | solution.py:690
  19.6 2.0 %tables.1.refs_5_.refs_10_.table.refs_9_ = f32[50,160,128]{2,1,0:T(8,128)S(1)} custom-call(s32[2]{0:T(128)S(1)} %pad_add_fusion.where_ref.refs_0_, f32[96,128]{1,0:T(8,128)S(1)} %add.15.regions_ref), custom_call_target="tpu_custom_call" | custom-call | tf_op jit(solution)/shard_map/tables/pallas_call | solution.py:645
  21.6 2.8 %collective-permute-done.3.refs_4_ = f32[10,88,128]{2,1,0:T(8,128)S(1)} collective-permute-done((f32[10,88,128]{2,1,0:T(8,128)S(1)}, f32[10,88,128]{2,1,0:T(8,128)S(1)}, u32[]{:S(2)}, u32[]{:S(2)}) %collective-permute-start.3) | collective-permute-done | bytes 450592 | tf_op jit(solution)/shard_map/ppermute | solution.py:670
  24.4 6.1 %down_fresh.1 = (f32[5,720,128]{2,1,0:T(8,128)S(1)}, f32[5,480,128]{2,1,0:T(8,128)S(1)}, f32[5,32,8,128]{3,2,1,0:T(8,128)S(1)}, f32[5,480,128]{2,1,0:T(8,128)S(1...) custom-call(s32[2]{0:T(128)S(1)} %pad_add_fusion.where_ref.refs_0_, ...), custom_call_target="tpu_custom_call" | custom-call | tf_op jit(solution)/shard_map/down_fresh/pallas_call | solution.py:645
  30.4 4.3 %collective-permute-start.6 = (f32[2,10,8,128]{3,2,1,0:T(8,128)S(1)}, f32[2,10,8,128]{3,2,1,0:T(8,128)S(1)}, u32[]{:S(2)}, u32[]{:S(2)}) collective-permute-start(f32[2,10,8,128]{3,2,1,0:T(8,128)S(1)} %get-tuple-element.38.own.refs_1_), channel_id=1, source_target_pairs={{0,1},{1,0},{2,3},{3,2},{4,5},{5,4},{6,7},{7,6},{8,9},{9,8},{10,11... | collective-permute-start | bytes 245768 | tf_op jit(solution)/shard_map/ppermute | solution.py:669
  34.7 0.9 %collective-permute-done.6.beside.refs_2_ = f32[2,10,8,128]{3,2,1,0:T(8,128)S(1)} collective-permute-done((f32[2,10,8,128]{3,2,1,0:T(8,128)S(1)}, f32[2,10,8,128]{3,2,1,0:T(8,128)S(1)}, u32[]{:S(2)}, u32[]{:S(2)}) %collective-permute-start.6) | collective-permute-done | bytes 81952 | tf_op jit(solution)/shard_map/ppermute | solution.py:669
  35.6 0.6 relay.2
  36.2 1.9 %collective-permute-start.7 = (f32[3,10,8,128]{3,2,1,0:T(8,128)S(1)}, f32[3,10,8,128]{3,2,1,0:T(8,128)S(1)}, u32[]{:S(2)}, u32[]{:S(2)}) collective-permute-start(f32[3,10,8,128]{3,2,1,0:T(8,128)S(1)} %relay.2), channel_id=1, source_target_pairs={{1,2},{2,1},{3,4},{4,3},{5,6},{6,5},{7,8},{8,7},{9,10},{10,9},{11,... | collective-permute-start | bytes 368648 | tf_op jit(solution)/shard_map/ppermute | solution.py:670
  38.1 5.6 %collective-permute-done.7.refs_3_ = f32[3,10,8,128]{3,2,1,0:T(8,128)S(1)} collective-permute-done((f32[3,10,8,128]{3,2,1,0:T(8,128)S(1)}, f32[3,10,8,128]{3,2,1,0:T(8,128)S(1)}, u32[]{:S(2)}, u32[]{:S(2)}) %collective-permute-start.7) | collective-permute-done | bytes 122912 | tf_op jit(solution)/shard_map/ppermute | solution.py:670
  43.7 1.3 %collective-permute-done.8.refs_4_ = f32[3,10,8,128]{3,2,1,0:T(8,128)S(1)} collective-permute-done((f32[3,10,8,128]{3,2,1,0:T(8,128)S(1)}, f32[3,10,8,128]{3,2,1,0:T(8,128)S(1)}, u32[]{:S(2)}, u32[]{:S(2)}) %collective-permute-start.8) | collective-permute-done | bytes 122912 | tf_op jit(solution)/shard_map/ppermute | solution.py:669
  45.0 8.3 %up.1 = (f32[5,256,128]{2,1,0:T(8,128)S(1)}, f32[5,88,128]{2,1,0:T(8,128)S(1)}, f32[5,88,128]{2,1,0:T(8,128)S(1)}) custom-call(s32[2]{0:T(128)S(1)} %pad_add_fusion.where_ref.refs_0_, f32[2,10,8,128]{3,2,1,0:T(8,128)S(1)} %get-tuple-element.38.own.refs_1_, f32[2,10,8,128]{3,2,1,0:T(8,128)S(1)} %collective-permute-done.6.beside.refs_2_, ...), custom_call_target="tpu_custom_call" | custom-call | tf_op jit(solution)/shard_map/up/pallas_call | solution.py:645
  53.4 0.2 collective-permute-start.9
  53.6 1.9 %collective-permute-start.10 = (f32[5,88,128]{2,1,0:T(8,128)S(1)}, f32[5,88,128]{2,1,0:T(8,128)S(1)}, u32[]{:S(2)}, u32[]{:S(2)}) collective-permute-start(f32[5,88,128]{2,1,0:T(8,128)S(1)} %get-tuple-element.51), channel_id=1, source_target_pairs={{1,2},{2,1},{3,4},{4,3},{5,6},{6,5},{7,8},{8,7},{9,10},{10,9},{11,... | collective-permute-start | bytes 675848 | tf_op jit(solution)/shard_map/ppermute | solution.py:670
  55.5 2.8 %interior.1 = (f32[5,720,128]{2,1,0:T(8,128)S(1)}, f32[5,720,128]{2,1,0:T(8,128)S(1)}, f32[5,480,128]{2,1,0:T(8,128)S(1)}, f32[5,32,8,128]{3,2,1,0:T(8,128)S(1)}, f32[5,480,128]{2,1,0:T(8,128)S(1)}) custom-call(s32[2]{0:T(128)S(1)} %pad_add_fusion.where_ref.refs_0_, f32[5,256,128]{2,1,0:T(8,128)S(1)} %get-tuple-element.44.state, ...), custom_call_target="tpu_custom_call" | custom-call | tf_op jit(solution)/shard_map/interior/pallas_call | solution.py:645
  58.4 4.9 %collective-permute-done.10.refs_7_ = f32[5,88,128]{2,1,0:T(8,128)S(1)} collective-permute-done((f32[5,88,128]{2,1,0:T(8,128)S(1)}, f32[5,88,128]{2,1,0:T(8,128)S(1)}, u32[]{:S(2)}, u32[]{:S(2)}) %collective-permute-start.10) | collective-permute-done | bytes 225312 | tf_op jit(solution)/shard_map/ppermute | solution.py:670
  63.3 4.2 %down.1 = (f32[5,720,128]{2,1,0:T(8,128)S(1)}, f32[5,480,128]{2,1,0:T(8,128)S(1)}, f32[5,32,8,128]{3,2,1,0:T(8,128)S(1)}, f32[5,480,128]{2,1,0:T(8,128)S(1)}, f32[2,10,8,128]{3,2,1,0:T(8,128)S(1)}) custom-call(s32[2]{0:T(128)S(1)} %pad_add_fusion.where_ref.refs_0_, f32[5,720,128]{2,1,0:T(8,128)S(1)} %get-tuple-element.45.refs_1_, ...), custom_call_target="tpu_custom_call" | custom-call | tf_op jit(solution)/shard_map/down/pallas_call | solution.py:645
  67.6 1.3 %collective-permute-done.11.beside.refs_2_ = f32[2,10,8,128]{3,2,1,0:T(8,128)S(1)} collective-permute-done((f32[2,10,8,128]{3,2,1,0:T(8,128)S(1)}, f32[2,10,8,128]{3,2,1,0:T(8,128)S(1)}, u32[]{:S(2)}, u32[]{:S(2)}) %collective-permute-start.11) | collective-permute-done | bytes 81952 | tf_op jit(solution)/shard_map/ppermute | solution.py:669
  68.8 0.6 relay.3
  69.4 1.9 %collective-permute-start.12 = (f32[3,10,8,128]{3,2,1,0:T(8,128)S(1)}, f32[3,10,8,128]{3,2,1,0:T(8,128)S(1)}, u32[]{:S(2)}, u32[]{:S(2)}) collective-permute-start(f32[3,10,8,128]{3,2,1,0:T(8,128)S(1)} %relay.3), channel_id=1, source_target_pairs={{1,2},{2,1},{3,4},{4,3},{5,6},{6,5},{7,8},{8,7},{9,10},{10,9},{11,... | collective-permute-start | bytes 368648 | tf_op jit(solution)/shard_map/ppermute | solution.py:670
  71.3 5.6 %collective-permute-done.12.refs_3_ = f32[3,10,8,128]{3,2,1,0:T(8,128)S(1)} collective-permute-done((f32[3,10,8,128]{3,2,1,0:T(8,128)S(1)}, f32[3,10,8,128]{3,2,1,0:T(8,128)S(1)}, u32[]{:S(2)}, u32[]{:S(2)}) %collective-permute-start.12) | collective-permute-done | bytes 122912 | tf_op jit(solution)/shard_map/ppermute | solution.py:670
  76.9 1.3 %collective-permute-done.13.refs_4_ = f32[3,10,8,128]{3,2,1,0:T(8,128)S(1)} collective-permute-done((f32[3,10,8,128]{3,2,1,0:T(8,128)S(1)}, f32[3,10,8,128]{3,2,1,0:T(8,128)S(1)}, u32[]{:S(2)}, u32[]{:S(2)}) %collective-permute-start.13) | collective-permute-done | bytes 122912 | tf_op jit(solution)/shard_map/ppermute | solution.py:669
  78.2 10.8 %up_last.1 = f32[5,32,1024]{2,1,0:T(8,128)} custom-call(s32[2]{0:T(128)S(1)} %pad_add_fusion.where_ref.refs_0_, f32[2,10,8,128]{3,2,1,0:T(8,128)S(1)} %get-tuple-element.52.own.refs_1_, f32[2,10,8,128]{3,2,1,0:T(8,128)S(1)} %collective-permute-done.11.beside.refs_2_, f32[3,10,8,128]{3,2,1,0:T(8,128)S(1)} %collective-permute-done.12.refs_3_, ...), custom_call_target="tpu_custom_call" | custom-call | tf_op jit(solution)/shard_map/up_last/pallas_call | solution.py:645
  (11 shorter events, 0.2 us)
Async XLA Ops:
  1.4 1.6 %collective-permute-start = (f32[96,128]{1,0:T(8,128)S(1)}, f32[96,128]{1,0:T(8,128)S(1)}, u32[]{:S(2)}, u32[]{:S(2)}) collective-permute-start(f32[96,128]{1,0:T(8,128)S(1)} %prep.1), channel_id=1, source_target_pairs={{0,1},{1,0},{2,3},{3,2},{4,5},{5,4},{6,7},{7,6},{8,9},{9,8},{10,11... | collective-permute-start | bytes 147464 | tf_op jit(solution)/shard_map/ppermute | solution.py:690
  3.0 6.1 %collective-permute-start.1 = (f32[96,128]{1,0:T(8,128)S(1)}, f32[96,128]{1,0:T(8,128)S(1)}, u32[]{:S(2)}, u32[]{:S(2)}) collective-permute-start(f32[96,128]{1,0:T(8,128)S(1)} %add.12), channel_id=1, source_target_pairs={{0,2},{1,3},{2,0},{3,1},{4,6},{5,7},{6,4},{7,5},{8,10},{9,11},{10,... | collective-permute-start | bytes 147464 | tf_op jit(solution)/shard_map/ppermute | solution.py:690
  9.1 12.5 %collective-permute-start.2 = (f32[10,88,128]{2,1,0:T(8,128)S(1)}, f32[10,88,128]{2,1,0:T(8,128)S(1)}, u32[]{:S(2)}, u32[]{:S(2)}) collective-permute-start(f32[10,88,128]{2,1,0:T(8,128)S(1)} %get-tuple-element.35), channel_id=1, source_target_pairs={{0,1},{1,0},{2,3},{3,2},{4,5},{5,4},{6,7},{7,6},{8,9},{9,8},{10,11... | collective-permute-start | bytes 1351688 | tf_op jit(solution)/shard_map/ppermute | solution.py:669
  9.8 14.5 %collective-permute-start.3 = (f32[10,88,128]{2,1,0:T(8,128)S(1)}, f32[10,88,128]{2,1,0:T(8,128)S(1)}, u32[]{:S(2)}, u32[]{:S(2)}) collective-permute-start(f32[10,88,128]{2,1,0:T(8,128)S(1)} %get-tuple-element.36), channel_id=1, source_target_pairs={{1,2},{2,1},{3,4},{4,3},{5,6},{6,5},{7,8},{8,7},{9,10},{10,9},{11,... | collective-permute-start | bytes 1351688 | tf_op jit(solution)/shard_map/ppermute | solution.py:670
  11.8 3.5 %collective-permute-start.4 = (f32[96,128]{1,0:T(8,128)S(1)}, f32[96,128]{1,0:T(8,128)S(1)}, u32[]{:S(2)}, u32[]{:S(2)}) collective-permute-start(f32[96,128]{1,0:T(8,128)S(1)} %add.13), channel_id=1, source_target_pairs={{0,4},{1,5},{2,6},{3,7},{4,0},{5,1},{6,2},{7,3},{8,12},{9,13},{10,... | collective-permute-start | bytes 147464 | tf_op jit(solution)/shard_map/ppermute | solution.py:690
  15.4 4.2 %collective-permute-start.5 = (f32[96,128]{1,0:T(8,128)S(1)}, f32[96,128]{1,0:T(8,128)S(1)}, u32[]{:S(2)}, u32[]{:S(2)}) collective-permute-start(f32[96,128]{1,0:T(8,128)S(1)} %add.14), channel_id=1, source_target_pairs={{0,8},{1,9},{2,10},{3,11},{4,12},{5,13},{6,14},{7,15},{8,0},{9,1},... | collective-permute-start | bytes 147464 | tf_op jit(solution)/shard_map/ppermute | solution.py:690
  30.4 5.2 %collective-permute-start.6 = (f32[2,10,8,128]{3,2,1,0:T(8,128)S(1)}, f32[2,10,8,128]{3,2,1,0:T(8,128)S(1)}, u32[]{:S(2)}, u32[]{:S(2)}) collective-permute-start(f32[2,10,8,128]{3,2,1,0:T(8,128)S(1)} %get-tuple-element.38.own.refs_1_), channel_id=1, source_target_pairs={{0,1},{1,0},{2,3},{3,2},{4,5},{5,4},{6,7},{7,6},{8,9},{9,8},{10,11... | collective-permute-start | bytes 245768 | tf_op jit(solution)/shard_map/ppermute | solution.py:669
  36.2 7.5 %collective-permute-start.7 = (f32[3,10,8,128]{3,2,1,0:T(8,128)S(1)}, f32[3,10,8,128]{3,2,1,0:T(8,128)S(1)}, u32[]{:S(2)}, u32[]{:S(2)}) collective-permute-start(f32[3,10,8,128]{3,2,1,0:T(8,128)S(1)} %relay.2), channel_id=1, source_target_pairs={{1,2},{2,1},{3,4},{4,3},{5,6},{6,5},{7,8},{8,7},{9,10},{10,9},{11,... | collective-permute-start | bytes 368648 | tf_op jit(solution)/shard_map/ppermute | solution.py:670
  43.7 1.3 %collective-permute-start.8 = (f32[3,10,8,128]{3,2,1,0:T(8,128)S(1)}, f32[3,10,8,128]{3,2,1,0:T(8,128)S(1)}, u32[]{:S(2)}, u32[]{:S(2)}) collective-permute-start(f32[3,10,8,128]{3,2,1,0:T(8,128)S(1)} %collective-permute-done.7.refs_3_), channel_id=1, source_target_pairs={{0,1},{1,0},{2,3},{3,2},{4,5},{5,4},{6,7},{7,6},{8,9},{9,8},{10,11... | collective-permute-start | bytes 368648 | tf_op jit(solution)/shard_map/ppermute | solution.py:669
  53.4 5.0 %collective-permute-start.9 = (f32[5,88,128]{2,1,0:T(8,128)S(1)}, f32[5,88,128]{2,1,0:T(8,128)S(1)}, u32[]{:S(2)}, u32[]{:S(2)}) collective-permute-start(f32[5,88,128]{2,1,0:T(8,128)S(1)} %get-tuple-element.50), channel_id=1, source_target_pairs={{0,1},{1,0},{2,3},{3,2},{4,5},{5,4},{6,7},{7,6},{8,9},{9,8},{10,11... | collective-permute-start | bytes 675848 | tf_op jit(solution)/shard_map/ppermute | solution.py:669
  53.6 9.7 %collective-permute-start.10 = (f32[5,88,128]{2,1,0:T(8,128)S(1)}, f32[5,88,128]{2,1,0:T(8,128)S(1)}, u32[]{:S(2)}, u32[]{:S(2)}) collective-permute-start(f32[5,88,128]{2,1,0:T(8,128)S(1)} %get-tuple-element.51), channel_id=1, source_target_pairs={{1,2},{2,1},{3,4},{4,3},{5,6},{6,5},{7,8},{8,7},{9,10},{10,9},{11,... | collective-permute-start | bytes 675848 | tf_op jit(solution)/shard_map/ppermute | solution.py:670
  67.5 1.3 %collective-permute-start.11 = (f32[2,10,8,128]{3,2,1,0:T(8,128)S(1)}, f32[2,10,8,128]{3,2,1,0:T(8,128)S(1)}, u32[]{:S(2)}, u32[]{:S(2)}) collective-permute-start(f32[2,10,8,128]{3,2,1,0:T(8,128)S(1)} %get-tuple-element.52.own.refs_1_), channel_id=1, source_target_pairs={{0,1},{1,0},{2,3},{3,2},{4,5},{5,4},{6,7},{7,6},{8,9},{9,8},{10,11... | collective-permute-start | bytes 245768 | tf_op jit(solution)/shard_map/ppermute | solution.py:669
  69.4 7.5 %collective-permute-start.12 = (f32[3,10,8,128]{3,2,1,0:T(8,128)S(1)}, f32[3,10,8,128]{3,2,1,0:T(8,128)S(1)}, u32[]{:S(2)}, u32[]{:S(2)}) collective-permute-start(f32[3,10,8,128]{3,2,1,0:T(8,128)S(1)} %relay.3), channel_id=1, source_target_pairs={{1,2},{2,1},{3,4},{4,3},{5,6},{6,5},{7,8},{8,7},{9,10},{10,9},{11,... | collective-permute-start | bytes 368648 | tf_op jit(solution)/shard_map/ppermute | solution.py:670
  76.9 1.3 %collective-permute-start.13 = (f32[3,10,8,128]{3,2,1,0:T(8,128)S(1)}, f32[3,10,8,128]{3,2,1,0:T(8,128)S(1)}, u32[]{:S(2)}, u32[]{:S(2)}) collective-permute-start(f32[3,10,8,128]{3,2,1,0:T(8,128)S(1)} %collective-permute-done.12.refs_3_), channel_id=1, source_target_pairs={{0,1},{1,0},{2,3},{3,2},{4,5},{5,4},{6,7},{7,6},{8,9},{9,8},{10,11... | collective-permute-start | bytes 368648 | tf_op jit(solution)/shard_map/ppermute | solution.py:669

commit v8 on v7

--- a/solution.py
+++ b/solution.py
@@ -708,9 +708,12 @@
         step *= 2
     gathered, send_a, send_b = lax.optimization_barrier((gathered, send_a, send_b))
     got_b, got_a = swap_b(send_b), swap_a(send_a)
-    while step < size:
-        gathered = doubled(gathered, step)
-        step *= 2
+    if size > 4:
+        free = [i for i in range(size) if i % 2 != i // 2 % 2]
+        while step < size:
+            gathered = gathered + lax.ppermute(gathered, "axial", [(i, i ^ step) for i in free])
+            step *= 2
+        gathered = jnp.where(odd != device // 2 % 2, gathered, swap_a(gathered))
     (table,) = call(
         functools.partial(tables_kernel, regions),
         "tables", 12,

time: 89.3 us -> 89.3 us (level)
  waiting for transfers between devices: 30.9 us -> 24.7 us
  starting transfers between devices: 16.5 us -> 22.2 us
    ppermute x4, waiting for transfers between devices: 18.9 us -> 11.2 us  [per_device(): swap_b = lambda x: lax.ppermute(x, 'axial', pair_b)]
    ppermute x0 -> x2, waiting for transfers between devices: none -> 6.35 us  [per_device(): lax.ppermute(gathered, 'axial', [(i, i ^ step) for i in free])]
    ppermute x4 -> x2, waiting for transfers between devices: 7.18 us -> 0.88 us  [doubled(): lax.ppermute(held, 'axial', [(i, i ^ step) for i in range(size)])]
    ppermute x4, starting transfers between devices: 7.72 us -> 13.8 us  [per_device(): swap_b = lambda x: lax.ppermute(x, 'axial', pair_b)]
    ppermute x0 -> x2, starting transfers between devices: none -> 5.11 us  [per_device(): lax.ppermute(gathered, 'axial', [(i, i ^ step) for i in free])]
    ppermute x6 -> x7, starting transfers between devices: 5.34 us -> 1.33 us  [per_device(): swap_a = lambda x: lax.ppermute(x, 'axial', pair_a)]
    ppermute x4 -> x2, starting transfers between devices: 3.4 us -> 1.98 us  [doubled(): lax.ppermute(held, 'axial', [(i, i ^ step) for i in range(size)])]
    ppermute x6 -> x7, waiting for transfers between devices: 4.83 us -> 6.24 us  [per_device(): swap_a = lambda x: lax.ppermute(x, 'axial', pair_a)]
  transfers between devices with their start and end apart: 14 -> 15, of which waited for: 11 -> 11; matrix products, arithmetic and copies ran while one was open for 0% -> 0% of each run, Pallas kernels for 11% -> 11%
where the time goes in v8:
time: 89.3 us; the launch traced here: 88.7 us
  Pallas kernels  41.5 us (46%)
  waiting for transfers between devices  24.7 us (28%)
  starting transfers between devices  22.2 us (25%)
    pallas_call x10, Pallas kernels, call(): pl.pallas_call(kernel, out_shape=outs, in_specs=[SMEM] + [HBM if i in raw...  41.5 us
    ppermute x4, starting transfers between devices, per_device(): swap_b = lambda x: lax.ppermute(x, 'axial', pair_b)  13.8 us
    ppermute x4, waiting for transfers between devices, per_device(): swap_b = lambda x: lax.ppermute(x, 'axial', pair_b)  11.2 us
    ppermute x2, waiting for transfers between devices, per_device(): lax.ppermute(gathered, 'axial', [(i, i ^ step) for i in free])  6.35 us
    ppermute x7, waiting for transfers between devices, per_device(): swap_a = lambda x: lax.ppermute(x, 'axial', pair_a)  6.24 us
    ppermute x2, starting transfers between devices, per_device(): lax.ppermute(gathered, 'axial', [(i, i ^ step) for i in free])  5.11 us
    ppermute x2, starting transfers between devices, doubled(): lax.ppermute(held, 'axial', [(i, i ^ step) for i in range(size)])  1.98 us
  transfers between devices with their start and end apart: 15, of which 11 were waited for; matrix products, arithmetic and copies ran while one was open for 0% of the time, Pallas kernels for 11%

profile of v8, /device:TPU:17, one launch (start us, length us, event | category | flops | bytes accessed | tf_op | source)
XLA Modules:
  0.0 88.7 jit_solution(1272130859811855048)
XLA Ops:
  0.1 1.3 %prep.1 = f32[96,128]{1,0:T(8,128)S(1)} custom-call(s32[2]{0:T(128)S(1)} %pad_add_fusion.where_ref.refs_0_, f32[4,25]{1,0:T(4,128)} %bitcast.4, s32[8,32]{1,0:T(8,128)} %bitcast.3), custom_call_target="tpu_custom_call" | custom-call | tf_op jit(solution)/shard_map/prep/pallas_call | solution.py:645
  1.4 0.7 collective-permute-start
  2.1 0.9 collective-permute-done
  3.0 1.3 %collective-permute-start.1 = (f32[96,128]{1,0:T(8,128)S(1)}, f32[96,128]{1,0:T(8,128)S(1)}, u32[]{:S(2)}, u32[]{:S(2)}) collective-permute-start(f32[96,128]{1,0:T(8,128)S(1)} %add.20), channel_id=1, source_target_pairs={{0,2},{1,3},{2,0},{3,1},{4,6},{5,7},{6,4},{7,5},{8,10},{9,11},{10,... | collective-permute-start | bytes 147464 | tf_op jit(solution)/shard_map/ppermute | solution.py:690
  4.3 4.8 %split.1 = (f32[5,256,128]{2,1,0:T(8,128)S(1)}, f32[5,256,128]{2,1,0:T(8,128)S(1)}, f32[10,88,128]{2,1,0:T(8,128)S(1)}, f32[10,88,128]{2,1,0:T(8,128)S(1)}) custom-call(s32[2]{0:T(128)S(1)} %pad_add_fusion.where_ref.refs_0_, f32[5,32,1024]{2,1,0:T(8,128)} %state_ref.1, f32[5,32,1024]{2,1,0:T(8,128)} %forcing_ref.1), custom_call_target="tpu_custom_call" | custom-call | tf_op jit(solution)/shard_map/split/pallas_call | solution.py:645
  9.1 0.8 collective-permute-start.2
  9.8 2.0 %collective-permute-start.3 = (f32[10,88,128]{2,1,0:T(8,128)S(1)}, f32[10,88,128]{2,1,0:T(8,128)S(1)}, u32[]{:S(2)}, u32[]{:S(2)}) collective-permute-start(f32[10,88,128]{2,1,0:T(8,128)S(1)} %get-tuple-element.36), channel_id=1, source_target_pairs={{1,2},{2,1},{3,4},{4,3},{5,6},{6,5},{7,8},{8,7},{9,10},{10,9},{11,... | collective-permute-start | bytes 1351688 | tf_op jit(solution)/shard_map/ppermute | solution.py:670
  11.8 3.2 %collective-permute-start.4 = (f32[96,128]{1,0:T(8,128)S(1)}, f32[96,128]{1,0:T(8,128)S(1)}, u32[]{:S(2)}, u32[]{:S(2)}) collective-permute-start(f32[96,128]{1,0:T(8,128)S(1)} %add.21), channel_id=1, source_target_pairs={{1,5},{2,6},{5,1},{6,2},{9,13},{10,14},{13,9},{14,10},{17,21},{18,... | collective-permute-start | bytes 147464 | tf_op jit(solution)/shard_map/ppermute | solution.py:714
  15.0 2.4 %collective-permute-done.4 = f32[96,128]{1,0:T(8,128)S(1)} collective-permute-done((f32[96,128]{1,0:T(8,128)S(1)}, f32[96,128]{1,0:T(8,128)S(1)}, u32[]{:S(2)}, u32[]{:S(2)}) %collective-permute-start.4) | collective-permute-done | bytes 49184 | tf_op jit(solution)/shard_map/ppermute | solution.py:714
  17.5 1.9 %collective-permute-start.5 = (f32[96,128]{1,0:T(8,128)S(1)}, f32[96,128]{1,0:T(8,128)S(1)}, u32[]{:S(2)}, u32[]{:S(2)}) collective-permute-start(f32[96,128]{1,0:T(8,128)S(1)} %add.24), channel_id=1, source_target_pairs={{1,9},{2,10},{5,13},{6,14},{9,1},{10,2},{13,5},{14,6},{17,25},{18,... | collective-permute-start | bytes 147464 | tf_op jit(solution)/shard_map/ppermute | solution.py:714
  19.4 3.9 %collective-permute-done.5 = f32[96,128]{1,0:T(8,128)S(1)} collective-permute-done((f32[96,128]{1,0:T(8,128)S(1)}, f32[96,128]{1,0:T(8,128)S(1)}, u32[]{:S(2)}, u32[]{:S(2)}) %collective-permute-start.5) | collective-permute-done | bytes 49184 | tf_op jit(solution)/shard_map/ppermute | solution.py:714
  23.4 1.2 %collective-permute-done.6 = f32[96,128]{1,0:T(8,128)S(1)} collective-permute-done((f32[96,128]{1,0:T(8,128)S(1)}, f32[96,128]{1,0:T(8,128)S(1)}, u32[]{:S(2)}, u32[]{:S(2)}) %collective-permute-start.6) | collective-permute-done | bytes 49184 | tf_op jit(solution)/shard_map/ppermute | solution.py:669
  24.6 2.0 %tables.1.refs_5_.refs_10_.table.refs_9_ = f32[50,160,128]{2,1,0:T(8,128)S(1)} custom-call(s32[2]{0:T(128)S(1)} %pad_add_fusion.where_ref.refs_0_, f32[96,128]{1,0:T(8,128)S(1)} %broadcast_select_fusion.regions_ref), custom_call_target="tpu_custom_call" | custom-call | tf_op jit(solution)/shard_map/tables/pallas_call | solution.py:645
  26.7 6.1 %down_fresh.1 = (f32[5,720,128]{2,1,0:T(8,128)S(1)}, f32[5,480,128]{2,1,0:T(8,128)S(1)}, f32[5,32,8,128]{3,2,1,0:T(8,128)S(1)}, f32[5,480,128]{2,1,0:T(8,128)S(1...) custom-call(s32[2]{0:T(128)S(1)} %pad_add_fusion.where_ref.refs_0_, ...), custom_call_target="tpu_custom_call" | custom-call | tf_op jit(solution)/shard_map/down_fresh/pallas_call | solution.py:645
  32.7 0.2 collective-permute-start.7
  33.0 1.1 %collective-permute-done.7.beside.refs_2_ = f32[2,10,8,128]{3,2,1,0:T(8,128)S(1)} collective-permute-done((f32[2,10,8,128]{3,2,1,0:T(8,128)S(1)}, f32[2,10,8,128]{3,2,1,0:T(8,128)S(1)}, u32[]{:S(2)}, u32[]{:S(2)}) %collective-permute-start.7) | collective-permute-done | bytes 81952 | tf_op jit(solution)/shard_map/ppermute | solution.py:669
  34.1 0.6 relay.2
  34.7 5.0 %collective-permute-start.8 = (f32[3,10,8,128]{3,2,1,0:T(8,128)S(1)}, f32[3,10,8,128]{3,2,1,0:T(8,128)S(1)}, u32[]{:S(2)}, u32[]{:S(2)}) collective-permute-start(f32[3,10,8,128]{3,2,1,0:T(8,128)S(1)} %relay.2), channel_id=1, source_target_pairs={{1,2},{2,1},{3,4},{4,3},{5,6},{6,5},{7,8},{8,7},{9,10},{10,9},{11,... | collective-permute-start | bytes 368648 | tf_op jit(solution)/shard_map/ppermute | solution.py:670
  39.6 3.7 %collective-permute-done.8.refs_3_ = f32[3,10,8,128]{3,2,1,0:T(8,128)S(1)} collective-permute-done((f32[3,10,8,128]{3,2,1,0:T(8,128)S(1)}, f32[3,10,8,128]{3,2,1,0:T(8,128)S(1)}, u32[]{:S(2)}, u32[]{:S(2)}) %collective-permute-start.8) | collective-permute-done | bytes 122912 | tf_op jit(solution)/shard_map/ppermute | solution.py:670
  43.4 1.3 %collective-permute-done.9.refs_4_ = f32[3,10,8,128]{3,2,1,0:T(8,128)S(1)} collective-permute-done((f32[3,10,8,128]{3,2,1,0:T(8,128)S(1)}, f32[3,10,8,128]{3,2,1,0:T(8,128)S(1)}, u32[]{:S(2)}, u32[]{:S(2)}) %collective-permute-start.9) | collective-permute-done | bytes 122912 | tf_op jit(solution)/shard_map/ppermute | solution.py:669
  44.7 8.3 %up.1 = (f32[5,256,128]{2,1,0:T(8,128)S(1)}, f32[5,88,128]{2,1,0:T(8,128)S(1)}, f32[5,88,128]{2,1,0:T(8,128)S(1)}) custom-call(s32[2]{0:T(128)S(1)} %pad_add_fusion.where_ref.refs_0_, f32[2,10,8,128]{3,2,1,0:T(8,128)S(1)} %get-tuple-element.38.own.refs_1_, f32[2,10,8,128]{3,2,1,0:T(8,128)S(1)} %collective-permute-done.7.beside.refs_2_, ...), custom_call_target="tpu_custom_call" | custom-call | tf_op jit(solution)/shard_map/up/pallas_call | solution.py:645
  53.1 0.2 collective-permute-start.10
  53.3 3.4 %collective-permute-start.11 = (f32[5,88,128]{2,1,0:T(8,128)S(1)}, f32[5,88,128]{2,1,0:T(8,128)S(1)}, u32[]{:S(2)}, u32[]{:S(2)}) collective-permute-start(f32[5,88,128]{2,1,0:T(8,128)S(1)} %get-tuple-element.51), channel_id=1, source_target_pairs={{1,2},{2,1},{3,4},{4,3},{5,6},{6,5},{7,8},{8,7},{9,10},{10,9},{11,... | collective-permute-start | bytes 675848 | tf_op jit(solution)/shard_map/ppermute | solution.py:670
  56.7 2.8 %interior.1 = (f32[5,720,128]{2,1,0:T(8,128)S(1)}, f32[5,720,128]{2,1,0:T(8,128)S(1)}, f32[5,480,128]{2,1,0:T(8,128)S(1)}, f32[5,32,8,128]{3,2,1,0:T(8,128)S(1)}, f32[5,480,128]{2,1,0:T(8,128)S(1)}) custom-call(s32[2]{0:T(128)S(1)} %pad_add_fusion.where_ref.refs_0_, f32[5,256,128]{2,1,0:T(8,128)S(1)} %get-tuple-element.44.state, ...), custom_call_target="tpu_custom_call" | custom-call | tf_op jit(solution)/shard_map/interior/pallas_call | solution.py:645
  59.6 3.4 %collective-permute-done.11.refs_7_ = f32[5,88,128]{2,1,0:T(8,128)S(1)} collective-permute-done((f32[5,88,128]{2,1,0:T(8,128)S(1)}, f32[5,88,128]{2,1,0:T(8,128)S(1)}, u32[]{:S(2)}, u32[]{:S(2)}) %collective-permute-start.11) | collective-permute-done | bytes 225312 | tf_op jit(solution)/shard_map/ppermute | solution.py:670
  63.0 4.2 %down.1 = (f32[5,720,128]{2,1,0:T(8,128)S(1)}, f32[5,480,128]{2,1,0:T(8,128)S(1)}, f32[5,32,8,128]{3,2,1,0:T(8,128)S(1)}, f32[5,480,128]{2,1,0:T(8,128)S(1)}, f32[2,10,8,128]{3,2,1,0:T(8,128)S(1)}) custom-call(s32[2]{0:T(128)S(1)} %pad_add_fusion.where_ref.refs_0_, f32[5,720,128]{2,1,0:T(8,128)S(1)} %get-tuple-element.45.refs_1_, ...), custom_call_target="tpu_custom_call" | custom-call | tf_op jit(solution)/shard_map/down/pallas_call | solution.py:645
  67.2 1.3 %collective-permute-done.12.beside.refs_2_ = f32[2,10,8,128]{3,2,1,0:T(8,128)S(1)} collective-permute-done((f32[2,10,8,128]{3,2,1,0:T(8,128)S(1)}, f32[2,10,8,128]{3,2,1,0:T(8,128)S(1)}, u32[]{:S(2)}, u32[]{:S(2)}) %collective-permute-start.12) | collective-permute-done | bytes 81952 | tf_op jit(solution)/shard_map/ppermute | solution.py:669
  68.5 0.6 relay.3
  69.1 3.4 %collective-permute-start.13 = (f32[3,10,8,128]{3,2,1,0:T(8,128)S(1)}, f32[3,10,8,128]{3,2,1,0:T(8,128)S(1)}, u32[]{:S(2)}, u32[]{:S(2)}) collective-permute-start(f32[3,10,8,128]{3,2,1,0:T(8,128)S(1)} %relay.3), channel_id=1, source_target_pairs={{1,2},{2,1},{3,4},{4,3},{5,6},{6,5},{7,8},{8,7},{9,10},{10,9},{11,... | collective-permute-start | bytes 368648 | tf_op jit(solution)/shard_map/ppermute | solution.py:670
  72.5 4.1 %collective-permute-done.13.refs_3_ = f32[3,10,8,128]{3,2,1,0:T(8,128)S(1)} collective-permute-done((f32[3,10,8,128]{3,2,1,0:T(8,128)S(1)}, f32[3,10,8,128]{3,2,1,0:T(8,128)S(1)}, u32[]{:S(2)}, u32[]{:S(2)}) %collective-permute-start.13) | collective-permute-done | bytes 122912 | tf_op jit(solution)/shard_map/ppermute | solution.py:670
  76.6 1.3 %collective-permute-done.14.refs_4_ = f32[3,10,8,128]{3,2,1,0:T(8,128)S(1)} collective-permute-done((f32[3,10,8,128]{3,2,1,0:T(8,128)S(1)}, f32[3,10,8,128]{3,2,1,0:T(8,128)S(1)}, u32[]{:S(2)}, u32[]{:S(2)}) %collective-permute-start.14) | collective-permute-done | bytes 122912 | tf_op jit(solution)/shard_map/ppermute | solution.py:669
  77.9 10.8 %up_last.1 = f32[5,32,1024]{2,1,0:T(8,128)} custom-call(s32[2]{0:T(128)S(1)} %pad_add_fusion.where_ref.refs_0_, f32[2,10,8,128]{3,2,1,0:T(8,128)S(1)} %get-tuple-element.52.own.refs_1_, f32[2,10,8,128]{3,2,1,0:T(8,128)S(1)} %collective-permute-done.12.beside.refs_2_, f32[3,10,8,128]{3,2,1,0:T(8,128)S(1)} %collective-permute-done.13.refs_3_, ...), custom_call_target="tpu_custom_call" | custom-call | tf_op jit(solution)/shard_map/up_last/pallas_call | solution.py:645
  (14 shorter events, 0.3 us)
Async XLA Ops:
  1.4 1.6 %collective-permute-start = (f32[96,128]{1,0:T(8,128)S(1)}, f32[96,128]{1,0:T(8,128)S(1)}, u32[]{:S(2)}, u32[]{:S(2)}) collective-permute-start(f32[96,128]{1,0:T(8,128)S(1)} %prep.1), channel_id=1, source_target_pairs={{0,1},{1,0},{2,3},{3,2},{4,5},{5,4},{6,7},{7,6},{8,9},{9,8},{10,11... | collective-permute-start | bytes 147464 | tf_op jit(solution)/shard_map/ppermute | solution.py:690
  3.0 6.1 %collective-permute-start.1 = (f32[96,128]{1,0:T(8,128)S(1)}, f32[96,128]{1,0:T(8,128)S(1)}, u32[]{:S(2)}, u32[]{:S(2)}) collective-permute-start(f32[96,128]{1,0:T(8,128)S(1)} %add.20), channel_id=1, source_target_pairs={{0,2},{1,3},{2,0},{3,1},{4,6},{5,7},{6,4},{7,5},{8,10},{9,11},{10,... | collective-permute-start | bytes 147464 | tf_op jit(solution)/shard_map/ppermute | solution.py:690
  9.1 17.6 %collective-permute-start.2 = (f32[10,88,128]{2,1,0:T(8,128)S(1)}, f32[10,88,128]{2,1,0:T(8,128)S(1)}, u32[]{:S(2)}, u32[]{:S(2)}) collective-permute-start(f32[10,88,128]{2,1,0:T(8,128)S(1)} %get-tuple-element.35), channel_id=1, source_target_pairs={{0,1},{1,0},{2,3},{3,2},{4,5},{5,4},{6,7},{7,6},{8,9},{9,8},{10,11... | collective-permute-start | bytes 1351688 | tf_op jit(solution)/shard_map/ppermute | solution.py:669
  9.8 16.8 %collective-permute-start.3 = (f32[10,88,128]{2,1,0:T(8,128)S(1)}, f32[10,88,128]{2,1,0:T(8,128)S(1)}, u32[]{:S(2)}, u32[]{:S(2)}) collective-permute-start(f32[10,88,128]{2,1,0:T(8,128)S(1)} %get-tuple-element.36), channel_id=1, source_target_pairs={{1,2},{2,1},{3,4},{4,3},{5,6},{6,5},{7,8},{8,7},{9,10},{10,9},{11,... | collective-permute-start | bytes 1351688 | tf_op jit(solution)/shard_map/ppermute | solution.py:670
  11.8 5.7 %collective-permute-start.4 = (f32[96,128]{1,0:T(8,128)S(1)}, f32[96,128]{1,0:T(8,128)S(1)}, u32[]{:S(2)}, u32[]{:S(2)}) collective-permute-start(f32[96,128]{1,0:T(8,128)S(1)} %add.21), channel_id=1, source_target_pairs={{1,5},{2,6},{5,1},{6,2},{9,13},{10,14},{13,9},{14,10},{17,21},{18,... | collective-permute-start | bytes 147464 | tf_op jit(solution)/shard_map/ppermute | solution.py:714
  17.5 5.8 %collective-permute-start.5 = (f32[96,128]{1,0:T(8,128)S(1)}, f32[96,128]{1,0:T(8,128)S(1)}, u32[]{:S(2)}, u32[]{:S(2)}) collective-permute-start(f32[96,128]{1,0:T(8,128)S(1)} %add.24), channel_id=1, source_target_pairs={{1,9},{2,10},{5,13},{6,14},{9,1},{10,2},{13,5},{14,6},{17,25},{18,... | collective-permute-start | bytes 147464 | tf_op jit(solution)/shard_map/ppermute | solution.py:714
  23.3 1.3 %collective-permute-start.6 = (f32[96,128]{1,0:T(8,128)S(1)}, f32[96,128]{1,0:T(8,128)S(1)}, u32[]{:S(2)}, u32[]{:S(2)}) collective-permute-start(f32[96,128]{1,0:T(8,128)S(1)} %add.25), channel_id=1, source_target_pairs={{0,1},{1,0},{2,3},{3,2},{4,5},{5,4},{6,7},{7,6},{8,9},{9,8},{10,11... | collective-permute-start | bytes 147464 | tf_op jit(solution)/shard_map/ppermute | solution.py:669
  32.7 1.3 %collective-permute-start.7 = (f32[2,10,8,128]{3,2,1,0:T(8,128)S(1)}, f32[2,10,8,128]{3,2,1,0:T(8,128)S(1)}, u32[]{:S(2)}, u32[]{:S(2)}) collective-permute-start(f32[2,10,8,128]{3,2,1,0:T(8,128)S(1)} %get-tuple-element.38.own.refs_1_), channel_id=1, source_target_pairs={{0,1},{1,0},{2,3},{3,2},{4,5},{5,4},{6,7},{7,6},{8,9},{9,8},{10,11... | collective-permute-start | bytes 245768 | tf_op jit(solution)/shard_map/ppermute | solution.py:669
  34.7 8.7 %collective-permute-start.8 = (f32[3,10,8,128]{3,2,1,0:T(8,128)S(1)}, f32[3,10,8,128]{3,2,1,0:T(8,128)S(1)}, u32[]{:S(2)}, u32[]{:S(2)}) collective-permute-start(f32[3,10,8,128]{3,2,1,0:T(8,128)S(1)} %relay.2), channel_id=1, source_target_pairs={{1,2},{2,1},{3,4},{4,3},{5,6},{6,5},{7,8},{8,7},{9,10},{10,9},{11,... | collective-permute-start | bytes 368648 | tf_op jit(solution)/shard_map/ppermute | solution.py:670
  43.4 1.3 %collective-permute-start.9 = (f32[3,10,8,128]{3,2,1,0:T(8,128)S(1)}, f32[3,10,8,128]{3,2,1,0:T(8,128)S(1)}, u32[]{:S(2)}, u32[]{:S(2)}) collective-permute-start(f32[3,10,8,128]{3,2,1,0:T(8,128)S(1)} %collective-permute-done.8.refs_3_), channel_id=1, source_target_pairs={{0,1},{1,0},{2,3},{3,2},{4,5},{5,4},{6,7},{7,6},{8,9},{9,8},{10,11... | collective-permute-start | bytes 368648 | tf_op jit(solution)/shard_map/ppermute | solution.py:669
  53.1 6.5 %collective-permute-start.10 = (f32[5,88,128]{2,1,0:T(8,128)S(1)}, f32[5,88,128]{2,1,0:T(8,128)S(1)}, u32[]{:S(2)}, u32[]{:S(2)}) collective-permute-start(f32[5,88,128]{2,1,0:T(8,128)S(1)} %get-tuple-element.50), channel_id=1, source_target_pairs={{0,1},{1,0},{2,3},{3,2},{4,5},{5,4},{6,7},{7,6},{8,9},{9,8},{10,11... | collective-permute-start | bytes 675848 | tf_op jit(solution)/shard_map/ppermute | solution.py:669
  53.3 9.7 %collective-permute-start.11 = (f32[5,88,128]{2,1,0:T(8,128)S(1)}, f32[5,88,128]{2,1,0:T(8,128)S(1)}, u32[]{:S(2)}, u32[]{:S(2)}) collective-permute-start(f32[5,88,128]{2,1,0:T(8,128)S(1)} %get-tuple-element.51), channel_id=1, source_target_pairs={{1,2},{2,1},{3,4},{4,3},{5,6},{6,5},{7,8},{8,7},{9,10},{10,9},{11,... | collective-permute-start | bytes 675848 | tf_op jit(solution)/shard_map/ppermute | solution.py:670
  67.2 1.3 %collective-permute-start.12 = (f32[2,10,8,128]{3,2,1,0:T(8,128)S(1)}, f32[2,10,8,128]{3,2,1,0:T(8,128)S(1)}, u32[]{:S(2)}, u32[]{:S(2)}) collective-permute-start(f32[2,10,8,128]{3,2,1,0:T(8,128)S(1)} %get-tuple-element.52.own.refs_1_), channel_id=1, source_target_pairs={{0,1},{1,0},{2,3},{3,2},{4,5},{5,4},{6,7},{7,6},{8,9},{9,8},{10,11... | collective-permute-start | bytes 245768 | tf_op jit(solution)/shard_map/ppermute | solution.py:669
  69.1 7.5 %collective-permute-start.13 = (f32[3,10,8,128]{3,2,1,0:T(8,128)S(1)}, f32[3,10,8,128]{3,2,1,0:T(8,128)S(1)}, u32[]{:S(2)}, u32[]{:S(2)}) collective-permute-start(f32[3,10,8,128]{3,2,1,0:T(8,128)S(1)} %relay.3), channel_id=1, source_target_pairs={{1,2},{2,1},{3,4},{4,3},{5,6},{6,5},{7,8},{8,7},{9,10},{10,9},{11,... | collective-permute-start | bytes 368648 | tf_op jit(solution)/shard_map/ppermute | solution.py:670
  76.6 1.3 %collective-permute-start.14 = (f32[3,10,8,128]{3,2,1,0:T(8,128)S(1)}, f32[3,10,8,128]{3,2,1,0:T(8,128)S(1)}, u32[]{:S(2)}, u32[]{:S(2)}) collective-permute-start(f32[3,10,8,128]{3,2,1,0:T(8,128)S(1)} %collective-permute-done.13.refs_3_), channel_id=1, source_target_pairs={{0,1},{1,0},{2,3},{3,2},{4,5},{5,4},{6,7},{7,6},{8,9},{9,8},{10,11... | collective-permute-start | bytes 368648 | tf_op jit(solution)/shard_map/ppermute | solution.py:669

commit v9 on v8

--- a/solution.py
+++ b/solution.py
@@ -25,6 +25,7 @@
 COARSEST = 3
 EDGE_BATCH = 10
 GROUP = 4
+HELD_PARTS = 2
 SPREAD = 16
 
 
@@ -394,13 +395,13 @@
     for which, copy in enumerate(copies):
         copy.wait()
         for field in range(FIELDS):
-            for p, part in enumerate(three_parts(held_in[which, field])):
+            for p, part in enumerate(three_parts(held_in[which, field])[:HELD_PARTS]):
                 start = p * held + (which * FIELDS + field) * OWN
                 parts[start : start + OWN, :] = part
 
     def two_subs(index):
         values = dot(parts[...], turn(2 * index, True))
-        values = (values[:held] + values[held : 2 * held]) + values[2 * held :]
+        values = values[:held] + values[held:]
         for which, target in enumerate((state_rows, forcing_rows)):
             for field in range(FIELDS):
                 start = (which * FIELDS + field) * OWN
@@ -447,7 +448,7 @@
     rows_loop(0, FINE_HALO, halo)
 
 
-def interior_kernel(where_ref, state, f0, table, v0, tmp0, c1, q1, tmp1):
+def interior_kernel(fresh, where_ref, state, force, table, v0, tmp0, c1, q1, tmp1):
     def own(row):
         start = pl.multiple_of(row * SUB, SUB)
         for field in range(FIELDS):
@@ -455,7 +456,10 @@
 
     rows_loop(0, OWN, own)
     edges(v0, 0, O0, O0 + OWN)
-    source = lambda field, row: f0[field, row]
+    if fresh:
+        source = lambda field, row: force[field, pl.ds(pl.multiple_of((row - O0) * SUB, SUB), SUB), :]
+    else:
+        source = lambda field, row: force[field, row]
     sweep(source, v0, tmp0, table, 0, O0 + 1, O0 + OWN - 1, batch=5)
     sweep(source, tmp0, v0, table, 0, O0 + 2, O0 + OWN - 2, batch=4)
     descend(source, v0, table, 0, c1, q1, tmp1, O1 + INNER, O1 + OWN // 2 - INNER)
@@ -465,39 +469,33 @@
     half = OWN // 2
     low, high = O0 - FINE_HALO, O0 + OWN + FINE_HALO
     if fresh:
-        where_ref, state, force, got_a, got_b, table, v0, v1, s1, c1, send, f0, tmp0, tmp1, q1 = refs
-        place_halo(where_ref, v0, state, got_a, got_b, 0, True)
-        edges(v0, 0, low, high)
+        (where_ref, v0_in, tmp0_in, c1_in, q1_in, tmp1_in, force, got_a, got_b, table,
+         v0, v1, s1, c1, send, f0, tmp0, tmp1, q1) = refs
         place_halo(where_ref, f0, force, got_a, got_b, FIELDS, False)
     else:
         (where_ref, v0_in, tmp0_in, c1_in, q1_in, tmp1_in, got_a, got_b, f0, table,
          v0, v1, s1, c1, send, tmp0, tmp1, q1) = refs
 
-        def take(target, source, level, first, last):
-            rows = slice(at(first, level) - 2**level, at(last, level) - 2**level)
-            target[:, rows, :] = source[:, rows, :]
-
-        take(v0, v0_in, 0, O0, O0 + OWN)
-        take(tmp0, tmp0_in, 0, O0 + 1, O0 + 3)
-        take(tmp0, tmp0_in, 0, O0 + OWN - 3, O0 + OWN - 1)
-        inner = slice(O1 + INNER, O1 + half - INNER)
-        take(c1, c1_in, 1, inner.start, inner.stop)
-        take(tmp1, tmp1_in, 1, inner.start, inner.stop)
-        q1[:, inner] = q1_in[:, inner]
-        place_halo(where_ref, v0, None, got_a, got_b, 0, True)
-        edges(v0, 0, low, O0)
-        edges(v0, 0, O0 + OWN, high)
+    def take(target, source, level, first, last):
+        rows = slice(at(first, level) - 2**level, at(last, level) - 2**level)
+        target[:, rows, :] = source[:, rows, :]
+
+    take(v0, v0_in, 0, O0, O0 + OWN)
+    take(tmp0, tmp0_in, 0, O0 + 1, O0 + 3)
+    take(tmp0, tmp0_in, 0, O0 + OWN - 3, O0 + OWN - 1)
+    inner = slice(O1 + INNER, O1 + half - INNER)
+    take(c1, c1_in, 1, inner.start, inner.stop)
+    take(tmp1, tmp1_in, 1, inner.start, inner.stop)
+    q1[:, inner] = q1_in[:, inner]
+    place_halo(where_ref, v0, None, got_a, got_b, 0, True)
+    edges(v0, 0, low, O0)
+    edges(v0, 0, O0 + OWN, high)
     fine_source = lambda field, row: f0[field, row]
-    if fresh:
-        sweep(fine_source, v0, tmp0, table, 0, low + 1, high - 1)
-        sweep(fine_source, tmp0, v0, table, 0, low + 2, high - 2)
-        descend(fine_source, v0, table, 0, c1, q1, tmp1, O1 - 4, O1 + half + 4)
-    else:
-        for swept, (old, new) in enumerate(((v0, tmp0), (tmp0, v0))):
-            for first in (low + swept, O0 + OWN - 1 - swept):
-                sweep(fine_source, old, new, table, 0, first, first + FINE_HALO + 1)
-        for first in (O1 - 4, O1 + half - INNER):
-            descend(fine_source, v0, table, 0, c1, q1, tmp1, first, first + 4 + INNER)
+    for swept, (old, new) in enumerate(((v0, tmp0), (tmp0, v0))):
+        for first in (low + swept, O0 + OWN - 1 - swept):
+            sweep(fine_source, old, new, table, 0, first, first + FINE_HALO + 1)
+    for first in (O1 - 4, O1 + half - INNER):
+        descend(fine_source, v0, table, 0, c1, q1, tmp1, first, first + 4 + INNER)
     make_source(c1, q1, s1, table, 1, O1 - 3, O1 + half + 3)
     first_source = lambda field, row: s1[field, row]
     sweep(first_source, tmp1, v1, table, 1, O1 - 3, O1 + half + 3)
@@ -582,13 +580,13 @@
         for field in range(FIELDS):
             for sub in range(SUB):
                 value = work0[field, pl.ds(at(O0, 0) + sub, OWN, stride=stride_of(0)), :]
-                for p, part in enumerate(three_parts(value)):
+                for p, part in enumerate(three_parts(value)[:HELD_PARTS]):
                     start = p * held + field * OWN
                     parts[start : start + OWN, sub * LANES : (sub + 1) * LANES] = part
 
         def columns_out(index):
             values = dot(parts[...], turn(2 * index, False))
-            values = (values[:held] + values[held : 2 * held]) + values[2 * held :]
+            values = values[:held] + values[held:]
             cells = pl.ds(pl.multiple_of(index * 2 * LANES, 2 * LANES), 2 * LANES)
             for field in range(FIELDS):
                 out[field, :, cells] = values[field * OWN : (field + 1) * OWN]
@@ -696,19 +694,19 @@
         [f32(FIELDS, OWN * SUB, LANES)] * 2 + [f32(2 * FIELDS, FINE_HALO * SUB, LANES)] * 2,
         [where_ref, in_hbm(initial_state), in_hbm(forcing)],
         [
-            pltpu.VMEM((3 * 2 * FIELDS * OWN, SUB * LANES), jnp.bfloat16),
+            pltpu.VMEM((HELD_PARTS * 2 * FIELDS * OWN, SUB * LANES), jnp.bfloat16),
             scratch(2, FIELDS, OWN, SUB * LANES),
             pltpu.SemaphoreType.DMA((2,)),
         ],
         (1, 2),
     )
     step = 1
-    while step < min(size, 4):
+    while step < min(size, 8):
         gathered = doubled(gathered, step)
         step *= 2
     gathered, send_a, send_b = lax.optimization_barrier((gathered, send_a, send_b))
     got_b, got_a = swap_b(send_b), swap_a(send_a)
-    if size > 4:
+    if step < size:
         free = [i for i in range(size) if i % 2 != i // 2 % 2]
         while step < size:
             gathered = gathered + lax.ppermute(gathered, "axial", [(i, i ^ step) for i in free])
@@ -727,17 +725,18 @@
         outs = [f32(*padded(T0, 0)), f32(*padded(T1, 1)), f32(*plain(T1)), f32(*padded(T1, 1)),
                 f32(2, 2 * FIELDS, SUB, LANES)]
         temps = [scratch(*padded(T0, 0)), scratch(*padded(T1, 1)), scratch(*plain(T1))]
-        if cycle == 0:
+        fresh = cycle == 0
+        inner = call(
+            functools.partial(interior_kernel, fresh), "interior", 4,
+            [f32(*padded(T0, 0))] * 2 + [f32(*padded(T1, 1)), f32(*plain(T1)), f32(*padded(T1, 1))],
+            [where_ref, state, force if fresh else f0, table],
+        )
+        if fresh:
             v0, v1, s1, c1, own, f0 = call(
                 functools.partial(down_kernel, True), "down_fresh", 14, outs + [f32(*plain(T0))],
-                [where_ref, state, force, got_a, got_b, table], temps,
+                [where_ref, *inner, force, got_a, got_b, table], temps,
             )
         else:
-            inner = call(
-                interior_kernel, "interior", 4,
-                [f32(*padded(T0, 0))] * 2 + [f32(*padded(T1, 1)), f32(*plain(T1)), f32(*padded(T1, 1))],
-                [where_ref, state, f0, table],
-            )
             v0, v1, s1, c1, own = call(
                 functools.partial(down_kernel, False), "down", 14, outs,
                 [where_ref, *inner, got_a, got_b, f0, table], temps,
@@ -756,7 +755,7 @@
             return call(
                 functools.partial(up_kernel, True), "up_last", 26,
                 [f32(FIELDS, OWN, SUB * LANES)], operands,
-                [pltpu.VMEM((3 * FIELDS * OWN, SUB * LANES), jnp.bfloat16)] + temps,
+                [pltpu.VMEM((HELD_PARTS * FIELDS * OWN, SUB * LANES), jnp.bfloat16)] + temps,
             )[0]
         state, send_a, send_b = call(
             functools.partial(up_kernel, False), "up", 26,

time: 89.3 us -> 87.7 us (0.982)
  starting transfers between devices: 22.2 us -> 20.4 us
    ppermute x2 -> x1, starting transfers between devices: 5.11 us -> 1.96 us  [per_device(): lax.ppermute(gathered, 'axial', [(i, i ^ step) for i in free])]
    ppermute x2 -> x1, waiting for transfers between devices: 6.35 us -> 4.06 us  [per_device(): lax.ppermute(gathered, 'axial', [(i, i ^ step) for i in free])]
    ppermute x2 -> x3, waiting for transfers between devices: 0.88 us -> 2.52 us  [doubled(): lax.ppermute(held, 'axial', [(i, i ^ step) for i in range(size)])]
    ppermute x2 -> x3, starting transfers between devices: 1.98 us -> 3.34 us  [doubled(): lax.ppermute(held, 'axial', [(i, i ^ step) for i in range(size)])]
    ppermute x4, starting transfers between devices: 13.8 us -> 12.6 us  [per_device(): swap_b = lambda x: lax.ppermute(x, 'axial', pair_b)]
    ppermute x7, starting transfers between devices: 1.33 us -> 2.49 us  [per_device(): swap_a = lambda x: lax.ppermute(x, 'axial', pair_a)]
    ppermute x4, waiting for transfers between devices: 11.2 us -> 12.4 us  [per_device(): swap_b = lambda x: lax.ppermute(x, 'axial', pair_b)]
    pallas_call x10 -> x11, Pallas kernels: 41.5 us -> 41.5 us  [call(): pl.pallas_call(kernel, out_shape=outs, in_specs=[SMEM] + [HBM if i in raw...]
  transfers between devices with their start and end apart: 15 -> 15, of which waited for: 11 -> 11; matrix products, arithmetic and copies ran while one was open for 0% -> 0% of each run, Pallas kernels for 11% -> 13%
where the time goes in v9:
time: 87.7 us; the launch traced here: 87.4 us
  Pallas kernels  41.5 us (47%)
  waiting for transfers between devices  25.2 us (29%)
  starting transfers between devices  20.4 us (23%)
    pallas_call x11, Pallas kernels, call(): pl.pallas_call(kernel, out_shape=outs, in_specs=[SMEM] + [HBM if i in raw...  41.5 us
    ppermute x4, starting transfers between devices, per_device(): swap_b = lambda x: lax.ppermute(x, 'axial', pair_b)  12.6 us
    ppermute x4, waiting for transfers between devices, per_device(): swap_b = lambda x: lax.ppermute(x, 'axial', pair_b)  12.4 us
    ppermute x7, waiting for transfers between devices, per_device(): swap_a = lambda x: lax.ppermute(x, 'axial', pair_a)  6.24 us
    ppermute x1, waiting for transfers between devices, per_device(): lax.ppermute(gathered, 'axial', [(i, i ^ step) for i in free])  4.06 us
    ppermute x3, starting transfers between devices, doubled(): lax.ppermute(held, 'axial', [(i, i ^ step) for i in range(size)])  3.34 us
    ppermute x3, waiting for transfers between devices, doubled(): lax.ppermute(held, 'axial', [(i, i ^ step) for i in range(size)])  2.52 us
    ppermute x7, starting transfers between devices, per_device(): swap_a = lambda x: lax.ppermute(x, 'axial', pair_a)  2.49 us
  transfers between devices with their start and end apart: 15, of which 11 were waited for; matrix products, arithmetic and copies ran while one was open for 0% of the time, Pallas kernels for 13%

profile of v9, /device:TPU:17, one launch (start us, length us, event | category | flops | bytes accessed | tf_op | source)
XLA Modules:
  0.0 87.4 jit_solution(1090665050515236208)
XLA Ops:
  0.1 1.3 %prep.1 = f32[96,128]{1,0:T(8,128)S(1)} custom-call(s32[2]{0:T(128)S(1)} %pad_add_fusion.where_ref.refs_0_, f32[4,25]{1,0:T(4,128)} %bitcast.4, s32[8,32]{1,0:T(8,128)} %bitcast.3), custom_call_target="tpu_custom_call" | custom-call | tf_op jit(solution)/shard_map/prep/pallas_call | solution.py:643
  1.4 0.7 collective-permute-start
  2.1 0.9 %collective-permute-done = f32[96,128]{1,0:T(8,128)S(1)} collective-permute-done((f32[96,128]{1,0:T(8,128)S(1)}, f32[96,128]{1,0:T(8,128)S(1)}, u32[]{:S(2)}, u32[]{:S(2)}) %collective-permute-start) | collective-permute-done | bytes 49184 | tf_op jit(solution)/shard_map/ppermute | solution.py:688
  3.0 1.3 %collective-permute-start.1 = (f32[96,128]{1,0:T(8,128)S(1)}, f32[96,128]{1,0:T(8,128)S(1)}, u32[]{:S(2)}, u32[]{:S(2)}) collective-permute-start(f32[96,128]{1,0:T(8,128)S(1)} %add.22), channel_id=1, source_target_pairs={{0,2},{1,3},{2,0},{3,1},{4,6},{5,7},{6,4},{7,5},{8,10},{9,11},{10,... | collective-permute-start | bytes 147464 | tf_op jit(solution)/shard_map/ppermute | solution.py:688
  4.3 1.6 %collective-permute-done.1 = f32[96,128]{1,0:T(8,128)S(1)} collective-permute-done((f32[96,128]{1,0:T(8,128)S(1)}, f32[96,128]{1,0:T(8,128)S(1)}, u32[]{:S(2)}, u32[]{:S(2)}) %collective-permute-start.1) | collective-permute-done | bytes 49184 | tf_op jit(solution)/shard_map/ppermute | solution.py:688
  5.9 1.4 %collective-permute-start.2 = (f32[96,128]{1,0:T(8,128)S(1)}, f32[96,128]{1,0:T(8,128)S(1)}, u32[]{:S(2)}, u32[]{:S(2)}) collective-permute-start(f32[96,128]{1,0:T(8,128)S(1)} %add.23), channel_id=1, source_target_pairs={{0,4},{1,5},{2,6},{3,7},{4,0},{5,1},{6,2},{7,3},{8,12},{9,13},{10,... | collective-permute-start | bytes 147464 | tf_op jit(solution)/shard_map/ppermute | solution.py:688
  7.3 4.0 %split.1 = (f32[5,256,128]{2,1,0:T(8,128)S(1)}, f32[5,256,128]{2,1,0:T(8,128)S(1)}, f32[10,88,128]{2,1,0:T(8,128)S(1)}, f32[10,88,128]{2,1,0:T(8,128)S(1)}) custom-call(s32[2]{0:T(128)S(1)} %pad_add_fusion.where_ref.refs_0_, f32[5,32,1024]{2,1,0:T(8,128)} %state_ref.1, f32[5,32,1024]{2,1,0:T(8,128)} %forcing_ref.1), custom_call_target="tpu_custom_call" | custom-call | tf_op jit(solution)/shard_map/split/pallas_call | solution.py:643
  11.3 1.9 %collective-permute-start.5 = (f32[10,88,128]{2,1,0:T(8,128)S(1)}, f32[10,88,128]{2,1,0:T(8,128)S(1)}, u32[]{:S(2)}, u32[]{:S(2)}) collective-permute-start(f32[10,88,128]{2,1,0:T(8,128)S(1)} %get-tuple-element.46), channel_id=1, source_target_pairs={{0,1},{1,0},{2,3},{3,2},{4,5},{5,4},{6,7},{7,6},{8,9},{9,8},{10,11... | collective-permute-start | bytes 1351688 | tf_op jit(solution)/shard_map/ppermute | solution.py:667
  13.3 3.1 %collective-permute-start.6 = (f32[10,88,128]{2,1,0:T(8,128)S(1)}, f32[10,88,128]{2,1,0:T(8,128)S(1)}, u32[]{:S(2)}, u32[]{:S(2)}) collective-permute-start(f32[10,88,128]{2,1,0:T(8,128)S(1)} %get-tuple-element.47), channel_id=1, source_target_pairs={{1,2},{2,1},{3,4},{4,3},{5,6},{6,5},{7,8},{8,7},{9,10},{10,9},{11,... | collective-permute-start | bytes 1351688 | tf_op jit(solution)/shard_map/ppermute | solution.py:668
  16.4 2.0 %collective-permute-start.3 = (f32[96,128]{1,0:T(8,128)S(1)}, f32[96,128]{1,0:T(8,128)S(1)}, u32[]{:S(2)}, u32[]{:S(2)}) collective-permute-start(f32[96,128]{1,0:T(8,128)S(1)} %add.24), channel_id=1, source_target_pairs={{1,9},{2,10},{5,13},{6,14},{9,1},{10,2},{13,5},{14,6},{17,25},{18,... | collective-permute-start | bytes 147464 | tf_op jit(solution)/shard_map/ppermute | solution.py:712
  18.3 4.1 %collective-permute-done.3 = f32[96,128]{1,0:T(8,128)S(1)} collective-permute-done((f32[96,128]{1,0:T(8,128)S(1)}, f32[96,128]{1,0:T(8,128)S(1)}, u32[]{:S(2)}, u32[]{:S(2)}) %collective-permute-start.3) | collective-permute-done | bytes 49184 | tf_op jit(solution)/shard_map/ppermute | solution.py:712
  22.5 1.2 %collective-permute-done.4 = f32[96,128]{1,0:T(8,128)S(1)} collective-permute-done((f32[96,128]{1,0:T(8,128)S(1)}, f32[96,128]{1,0:T(8,128)S(1)}, u32[]{:S(2)}, u32[]{:S(2)}) %collective-permute-start.4) | collective-permute-done | bytes 49184 | tf_op jit(solution)/shard_map/ppermute | solution.py:667
  23.7 2.0 %tables.1.table.refs_9_.refs_10_ = f32[50,160,128]{2,1,0:T(8,128)S(1)} custom-call(s32[2]{0:T(128)S(1)} %pad_add_fusion.where_ref.refs_0_, f32[96,128]{1,0:T(8,128)S(1)} %broadcast_select_fusion.regions_ref), custom_call_target="tpu_custom_call" | custom-call | tf_op jit(solution)/shard_map/tables/pallas_call | solution.py:643
  25.7 2.8 %interior.2 = (f32[5,720,128]{2,1,0:T(8,128)S(1)}, f32[5,720,128]{2,1,0:T(8,128)S(1)}, f32[5,480,128]{2,1,0:T(8,128)S(1)}, f32[5,32,8,128]{3,2,1,0:T(8,128)S(1)}, f32[5,480,128]{2,1,0:T(8,128)S(1)}) custom-call(s32[2]{0:T(128)S(1)} %pad_add_fusion.where_ref.refs_0_, f32[5,256,128]{2,1,0:T(8,128)S(1)} %get-tuple-element.36.state, ...), custom_call_target="tpu_custom_call" | custom-call | tf_op jit(solution)/shard_map/interior/pallas_call | solution.py:643
  28.6 4.5 %down_fresh.1 = (f32[5,720,128]{2,1,0:T(8,128)S(1)}, f32[5,480,128]{2,1,0:T(8,128)S(1)}, f32[5,32,8,128]{3,2,1,0:T(8,128)S(1)}, f32[5,480,128]{2,1,0:T(8,128)S(1...) custom-call(s32[2]{0:T(128)S(1)} %pad_add_fusion.where_ref.refs_0_, ...), custom_call_target="tpu_custom_call" | custom-call | tf_op jit(solution)/shard_map/down_fresh/pallas_call | solution.py:643
  33.1 0.2 collective-permute-start.7
  33.3 1.1 %collective-permute-done.7.beside.refs_2_ = f32[2,10,8,128]{3,2,1,0:T(8,128)S(1)} collective-permute-done((f32[2,10,8,128]{3,2,1,0:T(8,128)S(1)}, f32[2,10,8,128]{3,2,1,0:T(8,128)S(1)}, u32[]{:S(2)}, u32[]{:S(2)}) %collective-permute-start.7) | collective-permute-done | bytes 81952 | tf_op jit(solution)/shard_map/ppermute | solution.py:667
  34.4 0.6 relay.2
  35.0 3.4 %collective-permute-start.8 = (f32[3,10,8,128]{3,2,1,0:T(8,128)S(1)}, f32[3,10,8,128]{3,2,1,0:T(8,128)S(1)}, u32[]{:S(2)}, u32[]{:S(2)}) collective-permute-start(f32[3,10,8,128]{3,2,1,0:T(8,128)S(1)} %relay.2), channel_id=1, source_target_pairs={{1,2},{2,1},{3,4},{4,3},{5,6},{6,5},{7,8},{8,7},{9,10},{10,9},{11,... | collective-permute-start | bytes 368648 | tf_op jit(solution)/shard_map/ppermute | solution.py:668
  38.4 4.1 %collective-permute-done.8.refs_3_ = f32[3,10,8,128]{3,2,1,0:T(8,128)S(1)} collective-permute-done((f32[3,10,8,128]{3,2,1,0:T(8,128)S(1)}, f32[3,10,8,128]{3,2,1,0:T(8,128)S(1)}, u32[]{:S(2)}, u32[]{:S(2)}) %collective-permute-start.8) | collective-permute-done | bytes 122912 | tf_op jit(solution)/shard_map/ppermute | solution.py:668
  42.5 1.3 %collective-permute-done.9.refs_4_ = f32[3,10,8,128]{3,2,1,0:T(8,128)S(1)} collective-permute-done((f32[3,10,8,128]{3,2,1,0:T(8,128)S(1)}, f32[3,10,8,128]{3,2,1,0:T(8,128)S(1)}, u32[]{:S(2)}, u32[]{:S(2)}) %collective-permute-start.9) | collective-permute-done | bytes 122912 | tf_op jit(solution)/shard_map/ppermute | solution.py:667
  43.8 8.3 %up.1 = (f32[5,256,128]{2,1,0:T(8,128)S(1)}, f32[5,88,128]{2,1,0:T(8,128)S(1)}, f32[5,88,128]{2,1,0:T(8,128)S(1)}) custom-call(s32[2]{0:T(128)S(1)} %pad_add_fusion.where_ref.refs_0_, f32[2,10,8,128]{3,2,1,0:T(8,128)S(1)} %get-tuple-element.48.own.refs_1_, f32[2,10,8,128]{3,2,1,0:T(8,128)S(1)} %collective-permute-done.7.beside.refs_2_, ...), custom_call_target="tpu_custom_call" | custom-call | tf_op jit(solution)/shard_map/up/pallas_call | solution.py:643
  52.4 3.1 %collective-permute-start.11 = (f32[5,88,128]{2,1,0:T(8,128)S(1)}, f32[5,88,128]{2,1,0:T(8,128)S(1)}, u32[]{:S(2)}, u32[]{:S(2)}) collective-permute-start(f32[5,88,128]{2,1,0:T(8,128)S(1)} %get-tuple-element.61), channel_id=1, source_target_pairs={{1,2},{2,1},{3,4},{4,3},{5,6},{6,5},{7,8},{8,7},{9,10},{10,9},{11,... | collective-permute-start | bytes 675848 | tf_op jit(solution)/shard_map/ppermute | solution.py:668
  55.5 2.8 %interior.3 = (f32[5,720,128]{2,1,0:T(8,128)S(1)}, f32[5,720,128]{2,1,0:T(8,128)S(1)}, f32[5,480,128]{2,1,0:T(8,128)S(1)}, f32[5,32,8,128]{3,2,1,0:T(8,128)S(1)}, f32[5,480,128]{2,1,0:T(8,128)S(1)}) custom-call(s32[2]{0:T(128)S(1)} %pad_add_fusion.where_ref.refs_0_, f32[5,256,128]{2,1,0:T(8,128)S(1)} %get-tuple-element.54.state, ...), custom_call_target="tpu_custom_call" | custom-call | tf_op jit(solution)/shard_map/interior/pallas_call | solution.py:643
  58.3 3.8 %collective-permute-done.11.refs_7_ = f32[5,88,128]{2,1,0:T(8,128)S(1)} collective-permute-done((f32[5,88,128]{2,1,0:T(8,128)S(1)}, f32[5,88,128]{2,1,0:T(8,128)S(1)}, u32[]{:S(2)}, u32[]{:S(2)}) %collective-permute-start.11) | collective-permute-done | bytes 225312 | tf_op jit(solution)/shard_map/ppermute | solution.py:668
  62.1 4.2 %down.1 = (f32[5,720,128]{2,1,0:T(8,128)S(1)}, f32[5,480,128]{2,1,0:T(8,128)S(1)}, f32[5,32,8,128]{3,2,1,0:T(8,128)S(1)}, f32[5,480,128]{2,1,0:T(8,128)S(1)}, f32[2,10,8,128]{3,2,1,0:T(8,128)S(1)}) custom-call(s32[2]{0:T(128)S(1)} %pad_add_fusion.where_ref.refs_0_, f32[5,720,128]{2,1,0:T(8,128)S(1)} %get-tuple-element.55.refs_1_, ...), custom_call_target="tpu_custom_call" | custom-call | tf_op jit(solution)/shard_map/down/pallas_call | solution.py:643
  66.3 1.3 %collective-permute-done.12.beside.refs_2_ = f32[2,10,8,128]{3,2,1,0:T(8,128)S(1)} collective-permute-done((f32[2,10,8,128]{3,2,1,0:T(8,128)S(1)}, f32[2,10,8,128]{3,2,1,0:T(8,128)S(1)}, u32[]{:S(2)}, u32[]{:S(2)}) %collective-permute-start.12) | collective-permute-done | bytes 81952 | tf_op jit(solution)/shard_map/ppermute | solution.py:667
  67.6 0.6 relay.3
  68.2 3.1 %collective-permute-start.13 = (f32[3,10,8,128]{3,2,1,0:T(8,128)S(1)}, f32[3,10,8,128]{3,2,1,0:T(8,128)S(1)}, u32[]{:S(2)}, u32[]{:S(2)}) collective-permute-start(f32[3,10,8,128]{3,2,1,0:T(8,128)S(1)} %relay.3), channel_id=1, source_target_pairs={{1,2},{2,1},{3,4},{4,3},{5,6},{6,5},{7,8},{8,7},{9,10},{10,9},{11,... | collective-permute-start | bytes 368648 | tf_op jit(solution)/shard_map/ppermute | solution.py:668
  71.3 4.4 %collective-permute-done.13.refs_3_ = f32[3,10,8,128]{3,2,1,0:T(8,128)S(1)} collective-permute-done((f32[3,10,8,128]{3,2,1,0:T(8,128)S(1)}, f32[3,10,8,128]{3,2,1,0:T(8,128)S(1)}, u32[]{:S(2)}, u32[]{:S(2)}) %collective-permute-start.13) | collective-permute-done | bytes 122912 | tf_op jit(solution)/shard_map/ppermute | solution.py:668
  75.7 1.3 %collective-permute-done.14.refs_4_ = f32[3,10,8,128]{3,2,1,0:T(8,128)S(1)} collective-permute-done((f32[3,10,8,128]{3,2,1,0:T(8,128)S(1)}, f32[3,10,8,128]{3,2,1,0:T(8,128)S(1)}, u32[]{:S(2)}, u32[]{:S(2)}) %collective-permute-start.14) | collective-permute-done | bytes 122912 | tf_op jit(solution)/shard_map/ppermute | solution.py:667
  77.0 10.4 %up_last.1 = f32[5,32,1024]{2,1,0:T(8,128)} custom-call(s32[2]{0:T(128)S(1)} %pad_add_fusion.where_ref.refs_0_, f32[2,10,8,128]{3,2,1,0:T(8,128)S(1)} %get-tuple-element.62.own.refs_1_, f32[2,10,8,128]{3,2,1,0:T(8,128)S(1)} %collective-permute-done.12.beside.refs_2_, f32[3,10,8,128]{3,2,1,0:T(8,128)S(1)} %collective-permute-done.13.refs_3_, ...), custom_call_target="tpu_custom_call" | custom-call | tf_op jit(solution)/shard_map/up_last/pallas_call | solution.py:643
  (15 shorter events, 0.5 us)
Async XLA Ops:
  1.4 1.6 %collective-permute-start = (f32[96,128]{1,0:T(8,128)S(1)}, f32[96,128]{1,0:T(8,128)S(1)}, u32[]{:S(2)}, u32[]{:S(2)}) collective-permute-start(f32[96,128]{1,0:T(8,128)S(1)} %prep.1), channel_id=1, source_target_pairs={{0,1},{1,0},{2,3},{3,2},{4,5},{5,4},{6,7},{7,6},{8,9},{9,8},{10,11... | collective-permute-start | bytes 147464 | tf_op jit(solution)/shard_map/ppermute | solution.py:688
  3.0 2.9 %collective-permute-start.1 = (f32[96,128]{1,0:T(8,128)S(1)}, f32[96,128]{1,0:T(8,128)S(1)}, u32[]{:S(2)}, u32[]{:S(2)}) collective-permute-start(f32[96,128]{1,0:T(8,128)S(1)} %add.22), channel_id=1, source_target_pairs={{0,2},{1,3},{2,0},{3,1},{4,6},{5,7},{6,4},{7,5},{8,10},{9,11},{10,... | collective-permute-start | bytes 147464 | tf_op jit(solution)/shard_map/ppermute | solution.py:688
  5.9 5.4 %collective-permute-start.2 = (f32[96,128]{1,0:T(8,128)S(1)}, f32[96,128]{1,0:T(8,128)S(1)}, u32[]{:S(2)}, u32[]{:S(2)}) collective-permute-start(f32[96,128]{1,0:T(8,128)S(1)} %add.23), channel_id=1, source_target_pairs={{0,4},{1,5},{2,6},{3,7},{4,0},{5,1},{6,2},{7,3},{8,12},{9,13},{10,... | collective-permute-start | bytes 147464 | tf_op jit(solution)/shard_map/ppermute | solution.py:688
  11.3 17.2 %collective-permute-start.5 = (f32[10,88,128]{2,1,0:T(8,128)S(1)}, f32[10,88,128]{2,1,0:T(8,128)S(1)}, u32[]{:S(2)}, u32[]{:S(2)}) collective-permute-start(f32[10,88,128]{2,1,0:T(8,128)S(1)} %get-tuple-element.46), channel_id=1, source_target_pairs={{0,1},{1,0},{2,3},{3,2},{4,5},{5,4},{6,7},{7,6},{8,9},{9,8},{10,11... | collective-permute-start | bytes 1351688 | tf_op jit(solution)/shard_map/ppermute | solution.py:667
  13.3 15.3 %collective-permute-start.6 = (f32[10,88,128]{2,1,0:T(8,128)S(1)}, f32[10,88,128]{2,1,0:T(8,128)S(1)}, u32[]{:S(2)}, u32[]{:S(2)}) collective-permute-start(f32[10,88,128]{2,1,0:T(8,128)S(1)} %get-tuple-element.47), channel_id=1, source_target_pairs={{1,2},{2,1},{3,4},{4,3},{5,6},{6,5},{7,8},{8,7},{9,10},{10,9},{11,... | collective-permute-start | bytes 1351688 | tf_op jit(solution)/shard_map/ppermute | solution.py:668
  16.4 6.0 %collective-permute-start.3 = (f32[96,128]{1,0:T(8,128)S(1)}, f32[96,128]{1,0:T(8,128)S(1)}, u32[]{:S(2)}, u32[]{:S(2)}) collective-permute-start(f32[96,128]{1,0:T(8,128)S(1)} %add.24), channel_id=1, source_target_pairs={{1,9},{2,10},{5,13},{6,14},{9,1},{10,2},{13,5},{14,6},{17,25},{18,... | collective-permute-start | bytes 147464 | tf_op jit(solution)/shard_map/ppermute | solution.py:712
  22.4 1.3 %collective-permute-start.4 = (f32[96,128]{1,0:T(8,128)S(1)}, f32[96,128]{1,0:T(8,128)S(1)}, u32[]{:S(2)}, u32[]{:S(2)}) collective-permute-start(f32[96,128]{1,0:T(8,128)S(1)} %add.25), channel_id=1, source_target_pairs={{0,1},{1,0},{2,3},{3,2},{4,5},{5,4},{6,7},{7,6},{8,9},{9,8},{10,11... | collective-permute-start | bytes 147464 | tf_op jit(solution)/shard_map/ppermute | solution.py:667
  33.1 1.3 %collective-permute-start.7 = (f32[2,10,8,128]{3,2,1,0:T(8,128)S(1)}, f32[2,10,8,128]{3,2,1,0:T(8,128)S(1)}, u32[]{:S(2)}, u32[]{:S(2)}) collective-permute-start(f32[2,10,8,128]{3,2,1,0:T(8,128)S(1)} %get-tuple-element.48.own.refs_1_), channel_id=1, source_target_pairs={{0,1},{1,0},{2,3},{3,2},{4,5},{5,4},{6,7},{7,6},{8,9},{9,8},{10,11... | collective-permute-start | bytes 245768 | tf_op jit(solution)/shard_map/ppermute | solution.py:667
  35.0 7.5 %collective-permute-start.8 = (f32[3,10,8,128]{3,2,1,0:T(8,128)S(1)}, f32[3,10,8,128]{3,2,1,0:T(8,128)S(1)}, u32[]{:S(2)}, u32[]{:S(2)}) collective-permute-start(f32[3,10,8,128]{3,2,1,0:T(8,128)S(1)} %relay.2), channel_id=1, source_target_pairs={{1,2},{2,1},{3,4},{4,3},{5,6},{6,5},{7,8},{8,7},{9,10},{10,9},{11,... | collective-permute-start | bytes 368648 | tf_op jit(solution)/shard_map/ppermute | solution.py:668
  42.5 1.3 %collective-permute-start.9 = (f32[3,10,8,128]{3,2,1,0:T(8,128)S(1)}, f32[3,10,8,128]{3,2,1,0:T(8,128)S(1)}, u32[]{:S(2)}, u32[]{:S(2)}) collective-permute-start(f32[3,10,8,128]{3,2,1,0:T(8,128)S(1)} %collective-permute-done.8.refs_3_), channel_id=1, source_target_pairs={{0,1},{1,0},{2,3},{3,2},{4,5},{5,4},{6,7},{7,6},{8,9},{9,8},{10,11... | collective-permute-start | bytes 368648 | tf_op jit(solution)/shard_map/ppermute | solution.py:667
  52.2 6.1 %collective-permute-start.10 = (f32[5,88,128]{2,1,0:T(8,128)S(1)}, f32[5,88,128]{2,1,0:T(8,128)S(1)}, u32[]{:S(2)}, u32[]{:S(2)}) collective-permute-start(f32[5,88,128]{2,1,0:T(8,128)S(1)} %get-tuple-element.60), channel_id=1, source_target_pairs={{0,1},{1,0},{2,3},{3,2},{4,5},{5,4},{6,7},{7,6},{8,9},{9,8},{10,11... | collective-permute-start | bytes 675848 | tf_op jit(solution)/shard_map/ppermute | solution.py:667
  52.4 9.7 %collective-permute-start.11 = (f32[5,88,128]{2,1,0:T(8,128)S(1)}, f32[5,88,128]{2,1,0:T(8,128)S(1)}, u32[]{:S(2)}, u32[]{:S(2)}) collective-permute-start(f32[5,88,128]{2,1,0:T(8,128)S(1)} %get-tuple-element.61), channel_id=1, source_target_pairs={{1,2},{2,1},{3,4},{4,3},{5,6},{6,5},{7,8},{8,7},{9,10},{10,9},{11,... | collective-permute-start | bytes 675848 | tf_op jit(solution)/shard_map/ppermute | solution.py:668
  66.3 1.3 %collective-permute-start.12 = (f32[2,10,8,128]{3,2,1,0:T(8,128)S(1)}, f32[2,10,8,128]{3,2,1,0:T(8,128)S(1)}, u32[]{:S(2)}, u32[]{:S(2)}) collective-permute-start(f32[2,10,8,128]{3,2,1,0:T(8,128)S(1)} %get-tuple-element.62.own.refs_1_), channel_id=1, source_target_pairs={{0,1},{1,0},{2,3},{3,2},{4,5},{5,4},{6,7},{7,6},{8,9},{9,8},{10,11... | collective-permute-start | bytes 245768 | tf_op jit(solution)/shard_map/ppermute | solution.py:667
  68.2 7.5 %collective-permute-start.13 = (f32[3,10,8,128]{3,2,1,0:T(8,128)S(1)}, f32[3,10,8,128]{3,2,1,0:T(8,128)S(1)}, u32[]{:S(2)}, u32[]{:S(2)}) collective-permute-start(f32[3,10,8,128]{3,2,1,0:T(8,128)S(1)} %relay.3), channel_id=1, source_target_pairs={{1,2},{2,1},{3,4},{4,3},{5,6},{6,5},{7,8},{8,7},{9,10},{10,9},{11,... | collective-permute-start | bytes 368648 | tf_op jit(solution)/shard_map/ppermute | solution.py:668
  75.7 1.3 %collective-permute-start.14 = (f32[3,10,8,128]{3,2,1,0:T(8,128)S(1)}, f32[3,10,8,128]{3,2,1,0:T(8,128)S(1)}, u32[]{:S(2)}, u32[]{:S(2)}) collective-permute-start(f32[3,10,8,128]{3,2,1,0:T(8,128)S(1)} %collective-permute-done.13.refs_3_), channel_id=1, source_target_pairs={{0,1},{1,0},{2,3},{3,2},{4,5},{5,4},{6,7},{7,6},{8,9},{9,8},{10,11... | collective-permute-start | bytes 368648 | tf_op jit(solution)/shard_map/ppermute | solution.py:667

commit v10 on v9

--- a/solution.py
+++ b/solution.py
@@ -6,6 +6,7 @@
 from jax.experimental import pallas as pl
 from jax.experimental.pallas import tpu as pltpu
 from jax.sharding import PartitionSpec as P
+
 
 DIFFUSION = 1.0
 RELAXATION = 0.8
@@ -639,14 +640,13 @@
     return (FIELDS, rows, SUB, LANES)
 
 
-def call(kernel, name, grant, outs, operands, scratches=(), raw=()):
+def call(kernel, grant, outs, operands, scratches=(), raw=()):
     return pl.pallas_call(
         kernel,
         out_shape=outs,
         in_specs=[SMEM] + [HBM if i in raw else VMEM for i in range(1, len(operands))],
         out_specs=[VMEM] * len(outs),
         scratch_shapes=list(scratches),
-        name=name,
         compiler_params=pltpu.CompilerParams(vmem_limit_bytes=grant * 1024 * 1024),
     )(*operands)
 
@@ -661,7 +661,6 @@
     assert initial_state.shape == (FIELDS, OWN, SUB * LANES)
     assert region_ids.shape == (OWN, SUB)
     where_ref = jnp.stack([device, jnp.int32(size)]).astype(jnp.int32)
-    odd = device % 2
     pair_a = [(i, i ^ 1) for i in range(size)]
     pair_b = [(i, i + 1 if i % 2 else i - 1) for i in range(1, size - 1)]
     swap_a = lambda x: lax.ppermute(x, "axial", pair_a)
@@ -672,7 +671,6 @@
     per_tile = LANES // OWN
     (gathered,) = call(
         functools.partial(prep_kernel, share),
-        "prep",
         4,
         [f32(regions + SUB * -(-size // per_tile), LANES)],
         [where_ref, in_hbm(coefficients.T), in_hbm(region_ids.T)],
@@ -689,7 +687,6 @@
 
     state, force, send_a, send_b = call(
         split_kernel,
-        "split",
         12,
         [f32(FIELDS, OWN * SUB, LANES)] * 2 + [f32(2 * FIELDS, FINE_HALO * SUB, LANES)] * 2,
         [where_ref, in_hbm(initial_state), in_hbm(forcing)],
@@ -706,15 +703,12 @@
         step *= 2
     gathered, send_a, send_b = lax.optimization_barrier((gathered, send_a, send_b))
     got_b, got_a = swap_b(send_b), swap_a(send_a)
-    if step < size:
-        free = [i for i in range(size) if i % 2 != i // 2 % 2]
-        while step < size:
-            gathered = gathered + lax.ppermute(gathered, "axial", [(i, i ^ step) for i in free])
-            step *= 2
-        gathered = jnp.where(odd != device // 2 % 2, gathered, swap_a(gathered))
+    while step < size:
+        gathered = doubled(gathered, step)
+        step *= 2
     (table,) = call(
         functools.partial(tables_kernel, regions),
-        "tables", 12,
+        12,
         [f32(2 * ENTRIES, TABLE_ROWS, LANES)],
         [where_ref, gathered],
         [scratch(2, 32 * SUB, LANES), scratch(LANES, 2 * LANES)],
@@ -727,24 +721,22 @@
         temps = [scratch(*padded(T0, 0)), scratch(*padded(T1, 1)), scratch(*plain(T1))]
         fresh = cycle == 0
         inner = call(
-            functools.partial(interior_kernel, fresh), "interior", 4,
+            functools.partial(interior_kernel, fresh), 4,
             [f32(*padded(T0, 0))] * 2 + [f32(*padded(T1, 1)), f32(*plain(T1)), f32(*padded(T1, 1))],
             [where_ref, state, force if fresh else f0, table],
         )
         if fresh:
             v0, v1, s1, c1, own, f0 = call(
-                functools.partial(down_kernel, True), "down_fresh", 14, outs + [f32(*plain(T0))],
+                functools.partial(down_kernel, True), 14, outs + [f32(*plain(T0))],
                 [where_ref, *inner, force, got_a, got_b, table], temps,
             )
         else:
             v0, v1, s1, c1, own = call(
-                functools.partial(down_kernel, False), "down", 14, outs,
+                functools.partial(down_kernel, False), 14, outs,
                 [where_ref, *inner, got_a, got_b, f0, table], temps,
             )
         beside = swap_a(own)
-        (row,) = call(
-            relay_kernel, "relay", 2, [f32(3, 2 * FIELDS, SUB, LANES)], [where_ref, own, beside]
-        )
+        (row,) = call(relay_kernel, 2, [f32(3, 2 * FIELDS, SUB, LANES)], [where_ref, own, beside])
         far = swap_b(row)
         beyond = swap_a(far)
         operands = [where_ref, own, beside, far, beyond, v0, f0, v1, s1, c1, table]
@@ -753,12 +745,12 @@
         temps += [scratch(*padded(T3, 3)), scratch(*plain(T3)), scratch(*plain(T3)), scratch(*padded(T3, 3)), scratch(*padded(T3, 3))]
         if cycle == CYCLES - 1:
             return call(
-                functools.partial(up_kernel, True), "up_last", 26,
+                functools.partial(up_kernel, True), 26,
                 [f32(FIELDS, OWN, SUB * LANES)], operands,
                 [pltpu.VMEM((HELD_PARTS * FIELDS * OWN, SUB * LANES), jnp.bfloat16)] + temps,
             )[0]
         state, send_a, send_b = call(
-            functools.partial(up_kernel, False), "up", 26,
+            functools.partial(up_kernel, False), 26,
             [f32(FIELDS, OWN * SUB, LANES)] + [f32(FIELDS, FINE_HALO * SUB, LANES)] * 2,
             operands, temps,
         )

time: 87.7 us -> 89.9 us (1.025)
  the two profiles are of different devices: /device:TPU:17 before, /device:TPU:9 now
where the time goes in v10:
time: 89.9 us; the launch traced here: 89.6 us
  Pallas kernels  41.5 us (46%)
  waiting for transfers between devices  27.2 us (30%)
  starting transfers between devices  20.7 us (23%)
    pallas_call x11, Pallas kernels, call(): pl.pallas_call(kernel, out_shape=outs, in_specs=[SMEM] + [HBM if i in raw...  41.5 us
    ppermute x4, waiting for transfers between devices, per_device(): swap_b = lambda x: lax.ppermute(x, 'axial', pair_b)  18 us
    ppermute x4, starting transfers between devices, per_device(): swap_b = lambda x: lax.ppermute(x, 'axial', pair_b)  9.29 us
    ppermute x6, starting transfers between devices, per_device(): swap_a = lambda x: lax.ppermute(x, 'axial', pair_a)  6.94 us
    ppermute x6, waiting for transfers between devices, per_device(): swap_a = lambda x: lax.ppermute(x, 'axial', pair_a)  4.83 us
    ppermute x4, starting transfers between devices, doubled(): lax.ppermute(held, 'axial', [(i, i ^ step) for i in range(size)])  4.43 us
    ppermute x4, waiting for transfers between devices, doubled(): lax.ppermute(held, 'axial', [(i, i ^ step) for i in range(size)])  4.34 us
  transfers between devices with their start and end apart: 14, of which 11 were waited for; matrix products, arithmetic and copies ran while one was open for 0% of the time, Pallas kernels for 13%

profile of v10, /device:TPU:9, one launch (start us, length us, event | category | flops | bytes accessed | tf_op | source)
XLA Modules:
  0.0 89.6 jit_solution(663638449808473836)
XLA Ops:
  0.1 1.3 %shard_map.47 = f32[96,128]{1,0:T(8,128)S(1)} custom-call(s32[2]{0:T(128)S(1)} %pad_add_fusion.where_ref.refs_0_, f32[4,25]{1,0:T(4,128)} %bitcast.4, s32[8,32]{1,0:T(8,128)} %bitcast.3), custom_call_target="tpu_custom_call" | custom-call | tf_op jit(solution)/shard_map/pallas_call | solution.py:644
  1.4 0.7 collective-permute-start
  2.1 0.9 collective-permute-done
  3.0 1.3 %collective-permute-start.1 = (f32[96,128]{1,0:T(8,128)S(1)}, f32[96,128]{1,0:T(8,128)S(1)}, u32[]{:S(2)}, u32[]{:S(2)}) collective-permute-start(f32[96,128]{1,0:T(8,128)S(1)} %add.12), channel_id=1, source_target_pairs={{0,2},{1,3},{2,0},{3,1},{4,6},{5,7},{6,4},{7,5},{8,10},{9,11},{10,... | collective-permute-start | bytes 147464 | tf_op jit(solution)/shard_map/ppermute | solution.py:686
  4.3 1.6 %collective-permute-done.1 = f32[96,128]{1,0:T(8,128)S(1)} collective-permute-done((f32[96,128]{1,0:T(8,128)S(1)}, f32[96,128]{1,0:T(8,128)S(1)}, u32[]{:S(2)}, u32[]{:S(2)}) %collective-permute-start.1) | collective-permute-done | bytes 49184 | tf_op jit(solution)/shard_map/ppermute | solution.py:686
  6.0 4.0 %shard_map.46 = (f32[5,256,128]{2,1,0:T(8,128)S(1)}, f32[5,256,128]{2,1,0:T(8,128)S(1)}, f32[10,88,128]{2,1,0:T(8,128)S(1)}, f32[10,88,128]{2,1,0:T(8,128)S(1)}) custom-call(s32[2]{0:T(128)S(1)} %pad_add_fusion.where_ref.refs_0_, f32[5,32,1024]{2,1,0:T(8,128)} %state_ref.1, f32[5,32,1024]{2,1,0:T(8,128)} %forcing_ref.1), custom_call_target="tpu_custom_call" | custom-call | tf_op jit(solution)/shard_map/pallas_call | solution.py:644
  10.1 1.6 %collective-permute-start.4 = (f32[10,88,128]{2,1,0:T(8,128)S(1)}, f32[10,88,128]{2,1,0:T(8,128)S(1)}, u32[]{:S(2)}, u32[]{:S(2)}) collective-permute-start(f32[10,88,128]{2,1,0:T(8,128)S(1)} %get-tuple-element.46), channel_id=1, source_target_pairs={{0,1},{1,0},{2,3},{3,2},{4,5},{5,4},{6,7},{7,6},{8,9},{9,8},{10,11... | collective-permute-start | bytes 1351688 | tf_op jit(solution)/shard_map/ppermute | solution.py:666
  11.7 3.5 %collective-permute-start.5 = (f32[10,88,128]{2,1,0:T(8,128)S(1)}, f32[10,88,128]{2,1,0:T(8,128)S(1)}, u32[]{:S(2)}, u32[]{:S(2)}) collective-permute-start(f32[10,88,128]{2,1,0:T(8,128)S(1)} %get-tuple-element.47), channel_id=1, source_target_pairs={{1,2},{2,1},{3,4},{4,3},{5,6},{6,5},{7,8},{8,7},{9,10},{10,9},{11,... | collective-permute-start | bytes 1351688 | tf_op jit(solution)/shard_map/ppermute | solution.py:667
  15.2 2.4 %collective-permute-start.3 = (f32[96,128]{1,0:T(8,128)S(1)}, f32[96,128]{1,0:T(8,128)S(1)}, u32[]{:S(2)}, u32[]{:S(2)}) collective-permute-start(f32[96,128]{1,0:T(8,128)S(1)} %add.14), channel_id=1, source_target_pairs={{0,8},{1,9},{2,10},{3,11},{4,12},{5,13},{6,14},{7,15},{8,0},{9,1},... | collective-permute-start | bytes 147464 | tf_op jit(solution)/shard_map/ppermute | solution.py:686
  17.6 1.8 %collective-permute-done.3 = f32[96,128]{1,0:T(8,128)S(1)} collective-permute-done((f32[96,128]{1,0:T(8,128)S(1)}, f32[96,128]{1,0:T(8,128)S(1)}, u32[]{:S(2)}, u32[]{:S(2)}) %collective-permute-start.3) | collective-permute-done | bytes 49184 | tf_op jit(solution)/shard_map/ppermute | solution.py:686
  19.5 2.0 %shard_map.48.table.refs_9_.refs_10_ = f32[50,160,128]{2,1,0:T(8,128)S(1)} custom-call(s32[2]{0:T(128)S(1)} %pad_add_fusion.where_ref.refs_0_, f32[96,128]{1,0:T(8,128)S(1)} %add.15.regions_ref), custom_call_target="tpu_custom_call" | custom-call | tf_op jit(solution)/shard_map/pallas_call | solution.py:644
  21.5 2.8 %shard_map.49 = (f32[5,720,128]{2,1,0:T(8,128)S(1)}, f32[5,720,128]{2,1,0:T(8,128)S(1)}, f32[5,480,128]{2,1,0:T(8,128)S(1)}, f32[5,32,8,128]{3,2,1,0:T(8,128)S(1)}, f32[5,480,128]{2,1,0:T(8,128)S(1)}) custom-call(s32[2]{0:T(128)S(1)} %pad_add_fusion.where_ref.refs_0_, f32[5,256,128]{2,1,0:T(8,128)S(1)} %get-tuple-element.36.state, ...), custom_call_target="tpu_custom_call" | custom-call | tf_op jit(solution)/shard_map/pallas_call | solution.py:644
  24.3 1.9 %collective-permute-done.5.refs_8_ = f32[10,88,128]{2,1,0:T(8,128)S(1)} collective-permute-done((f32[10,88,128]{2,1,0:T(8,128)S(1)}, f32[10,88,128]{2,1,0:T(8,128)S(1)}, u32[]{:S(2)}, u32[]{:S(2)}) %collective-permute-start.5) | collective-permute-done | bytes 450592 | tf_op jit(solution)/shard_map/ppermute | solution.py:667
  26.2 4.5 %shard_map.50 = (f32[5,720,128]{2,1,0:T(8,128)S(1)}, f32[5,480,128]{2,1,0:T(8,128)S(1)}, f32[5,32,8,128]{3,2,1,0:T(8,128)S(1)}, f32[5,480,128]{2,1,0:T(8,128)S(1...) custom-call(s32[2]{0:T(128)S(1)} %pad_add_fusion.where_ref.refs_0_, ...), custom_call_target="tpu_custom_call" | custom-call | tf_op jit(solution)/shard_map/pallas_call | solution.py:644
  30.7 5.0 %collective-permute-start.6 = (f32[2,10,8,128]{3,2,1,0:T(8,128)S(1)}, f32[2,10,8,128]{3,2,1,0:T(8,128)S(1)}, u32[]{:S(2)}, u32[]{:S(2)}) collective-permute-start(f32[2,10,8,128]{3,2,1,0:T(8,128)S(1)} %get-tuple-element.48.own.refs_1_), channel_id=1, source_target_pairs={{0,1},{1,0},{2,3},{3,2},{4,5},{5,4},{6,7},{7,6},{8,9},{9,8},{10,11... | collective-permute-start | bytes 245768 | tf_op jit(solution)/shard_map/ppermute | solution.py:666
  35.7 0.9 %collective-permute-done.6.beside.refs_2_ = f32[2,10,8,128]{3,2,1,0:T(8,128)S(1)} collective-permute-done((f32[2,10,8,128]{3,2,1,0:T(8,128)S(1)}, f32[2,10,8,128]{3,2,1,0:T(8,128)S(1)}, u32[]{:S(2)}, u32[]{:S(2)}) %collective-permute-start.6) | collective-permute-done | bytes 81952 | tf_op jit(solution)/shard_map/ppermute | solution.py:666
  36.6 0.6 shard_map.51
  37.2 1.9 %collective-permute-start.7 = (f32[3,10,8,128]{3,2,1,0:T(8,128)S(1)}, f32[3,10,8,128]{3,2,1,0:T(8,128)S(1)}, u32[]{:S(2)}, u32[]{:S(2)}) collective-permute-start(f32[3,10,8,128]{3,2,1,0:T(8,128)S(1)} %shard_map.51), channel_id=1, source_target_pairs={{1,2},{2,1},{3,4},{4,3},{5,6},{6,5},{7,8},{8,7},{9,10},{10,9},{11,... | collective-permute-start | bytes 368648 | tf_op jit(solution)/shard_map/ppermute | solution.py:667
  39.1 5.6 %collective-permute-done.7.refs_3_ = f32[3,10,8,128]{3,2,1,0:T(8,128)S(1)} collective-permute-done((f32[3,10,8,128]{3,2,1,0:T(8,128)S(1)}, f32[3,10,8,128]{3,2,1,0:T(8,128)S(1)}, u32[]{:S(2)}, u32[]{:S(2)}) %collective-permute-start.7) | collective-permute-done | bytes 122912 | tf_op jit(solution)/shard_map/ppermute | solution.py:667
  44.7 1.3 %collective-permute-done.8.refs_4_ = f32[3,10,8,128]{3,2,1,0:T(8,128)S(1)} collective-permute-done((f32[3,10,8,128]{3,2,1,0:T(8,128)S(1)}, f32[3,10,8,128]{3,2,1,0:T(8,128)S(1)}, u32[]{:S(2)}, u32[]{:S(2)}) %collective-permute-start.8) | collective-permute-done | bytes 122912 | tf_op jit(solution)/shard_map/ppermute | solution.py:666
  46.0 8.3 %shard_map.52 = (f32[5,256,128]{2,1,0:T(8,128)S(1)}, f32[5,88,128]{2,1,0:T(8,128)S(1)}, f32[5,88,128]{2,1,0:T(8,128)S(1)}) custom-call(s32[2]{0:T(128)S(1)} %pad_add_fusion.where_ref.refs_0_, f32[2,10,8,128]{3,2,1,0:T(8,128)S(1)} %get-tuple-element.48.own.refs_1_, f32[2,10,8,128]{3,2,1,0:T(8,128)S(1)} %collective-permute-done.6.beside.refs_2_, ...), custom_call_target="tpu_custom_call" | custom-call | tf_op jit(solution)/shard_map/pallas_call | solution.py:644
  54.4 0.2 collective-permute-start.9
  54.6 1.9 %collective-permute-start.10 = (f32[5,88,128]{2,1,0:T(8,128)S(1)}, f32[5,88,128]{2,1,0:T(8,128)S(1)}, u32[]{:S(2)}, u32[]{:S(2)}) collective-permute-start(f32[5,88,128]{2,1,0:T(8,128)S(1)} %get-tuple-element.61), channel_id=1, source_target_pairs={{1,2},{2,1},{3,4},{4,3},{5,6},{6,5},{7,8},{8,7},{9,10},{10,9},{11,... | collective-permute-start | bytes 675848 | tf_op jit(solution)/shard_map/ppermute | solution.py:667
  56.5 2.8 %shard_map.53 = (f32[5,720,128]{2,1,0:T(8,128)S(1)}, f32[5,720,128]{2,1,0:T(8,128)S(1)}, f32[5,480,128]{2,1,0:T(8,128)S(1)}, f32[5,32,8,128]{3,2,1,0:T(8,128)S(1)}, f32[5,480,128]{2,1,0:T(8,128)S(1)}) custom-call(s32[2]{0:T(128)S(1)} %pad_add_fusion.where_ref.refs_0_, f32[5,256,128]{2,1,0:T(8,128)S(1)} %get-tuple-element.54.state, ...), custom_call_target="tpu_custom_call" | custom-call | tf_op jit(solution)/shard_map/pallas_call | solution.py:644
  59.3 4.9 %collective-permute-done.10.refs_7_ = f32[5,88,128]{2,1,0:T(8,128)S(1)} collective-permute-done((f32[5,88,128]{2,1,0:T(8,128)S(1)}, f32[5,88,128]{2,1,0:T(8,128)S(1)}, u32[]{:S(2)}, u32[]{:S(2)}) %collective-permute-start.10) | collective-permute-done | bytes 225312 | tf_op jit(solution)/shard_map/ppermute | solution.py:667
  64.3 4.2 %shard_map.54 = (f32[5,720,128]{2,1,0:T(8,128)S(1)}, f32[5,480,128]{2,1,0:T(8,128)S(1)}, f32[5,32,8,128]{3,2,1,0:T(8,128)S(1)}, f32[5,480,128]{2,1,0:T(8,128)S(1)}, f32[2,10,8,128]{3,2,1,0:T(8,128)S(1)}) custom-call(s32[2]{0:T(128)S(1)} %pad_add_fusion.where_ref.refs_0_, f32[5,720,128]{2,1,0:T(8,128)S(1)} %get-tuple-element.55.refs_1_, ...), custom_call_target="tpu_custom_call" | custom-call | tf_op jit(solution)/shard_map/pallas_call | solution.py:644
  68.5 1.3 %collective-permute-done.11.beside.refs_2_ = f32[2,10,8,128]{3,2,1,0:T(8,128)S(1)} collective-permute-done((f32[2,10,8,128]{3,2,1,0:T(8,128)S(1)}, f32[2,10,8,128]{3,2,1,0:T(8,128)S(1)}, u32[]{:S(2)}, u32[]{:S(2)}) %collective-permute-start.11) | collective-permute-done | bytes 81952 | tf_op jit(solution)/shard_map/ppermute | solution.py:666
  69.8 0.6 shard_map.55
  70.4 1.9 %collective-permute-start.12 = (f32[3,10,8,128]{3,2,1,0:T(8,128)S(1)}, f32[3,10,8,128]{3,2,1,0:T(8,128)S(1)}, u32[]{:S(2)}, u32[]{:S(2)}) collective-permute-start(f32[3,10,8,128]{3,2,1,0:T(8,128)S(1)} %shard_map.55), channel_id=1, source_target_pairs={{1,2},{2,1},{3,4},{4,3},{5,6},{6,5},{7,8},{8,7},{9,10},{10,9},{11,... | collective-permute-start | bytes 368648 | tf_op jit(solution)/shard_map/ppermute | solution.py:667
  72.3 5.6 %collective-permute-done.12.refs_3_ = f32[3,10,8,128]{3,2,1,0:T(8,128)S(1)} collective-permute-done((f32[3,10,8,128]{3,2,1,0:T(8,128)S(1)}, f32[3,10,8,128]{3,2,1,0:T(8,128)S(1)}, u32[]{:S(2)}, u32[]{:S(2)}) %collective-permute-start.12) | collective-permute-done | bytes 122912 | tf_op jit(solution)/shard_map/ppermute | solution.py:667
  77.9 1.3 %collective-permute-done.13.refs_4_ = f32[3,10,8,128]{3,2,1,0:T(8,128)S(1)} collective-permute-done((f32[3,10,8,128]{3,2,1,0:T(8,128)S(1)}, f32[3,10,8,128]{3,2,1,0:T(8,128)S(1)}, u32[]{:S(2)}, u32[]{:S(2)}) %collective-permute-start.13) | collective-permute-done | bytes 122912 | tf_op jit(solution)/shard_map/ppermute | solution.py:666
  79.2 10.4 %shard_map.56 = f32[5,32,1024]{2,1,0:T(8,128)} custom-call(s32[2]{0:T(128)S(1)} %pad_add_fusion.where_ref.refs_0_, f32[2,10,8,128]{3,2,1,0:T(8,128)S(1)} %get-tuple-element.62.own.refs_1_, f32[2,10,8,128]{3,2,1,0:T(8,128)S(1)} %collective-permute-done.11.beside.refs_2_, f32[3,10,8,128]{3,2,1,0:T(8,128)S(1)} %collective-permute-done.12.refs_3_, ...), custom_call_target="tpu_custom_call" | custom-call | tf_op jit(solution)/shard_map/pallas_call | solution.py:644
  (12 shorter events, 0.3 us)
Async XLA Ops:
  1.4 1.6 %collective-permute-start = (f32[96,128]{1,0:T(8,128)S(1)}, f32[96,128]{1,0:T(8,128)S(1)}, u32[]{:S(2)}, u32[]{:S(2)}) collective-permute-start(f32[96,128]{1,0:T(8,128)S(1)} %shard_map.47), channel_id=1, source_target_pairs={{0,1},{1,0},{2,3},{3,2},{4,5},{5,4},{6,7},{7,6},{8,9},{9,8},{10,11... | collective-permute-start | bytes 147464 | tf_op jit(solution)/shard_map/ppermute | solution.py:686
  3.0 2.9 %collective-permute-start.1 = (f32[96,128]{1,0:T(8,128)S(1)}, f32[96,128]{1,0:T(8,128)S(1)}, u32[]{:S(2)}, u32[]{:S(2)}) collective-permute-start(f32[96,128]{1,0:T(8,128)S(1)} %add.12), channel_id=1, source_target_pairs={{0,2},{1,3},{2,0},{3,1},{4,6},{5,7},{6,4},{7,5},{8,10},{9,11},{10,... | collective-permute-start | bytes 147464 | tf_op jit(solution)/shard_map/ppermute | solution.py:686
  5.9 4.1 %collective-permute-start.2 = (f32[96,128]{1,0:T(8,128)S(1)}, f32[96,128]{1,0:T(8,128)S(1)}, u32[]{:S(2)}, u32[]{:S(2)}) collective-permute-start(f32[96,128]{1,0:T(8,128)S(1)} %add.13), channel_id=1, source_target_pairs={{0,4},{1,5},{2,6},{3,7},{4,0},{5,1},{6,2},{7,3},{8,12},{9,13},{10,... | collective-permute-start | bytes 147464 | tf_op jit(solution)/shard_map/ppermute | solution.py:686
  10.1 14.3 %collective-permute-start.4 = (f32[10,88,128]{2,1,0:T(8,128)S(1)}, f32[10,88,128]{2,1,0:T(8,128)S(1)}, u32[]{:S(2)}, u32[]{:S(2)}) collective-permute-start(f32[10,88,128]{2,1,0:T(8,128)S(1)} %get-tuple-element.46), channel_id=1, source_target_pairs={{0,1},{1,0},{2,3},{3,2},{4,5},{5,4},{6,7},{7,6},{8,9},{9,8},{10,11... | collective-permute-start | bytes 1351688 | tf_op jit(solution)/shard_map/ppermute | solution.py:666
  11.7 14.5 %collective-permute-start.5 = (f32[10,88,128]{2,1,0:T(8,128)S(1)}, f32[10,88,128]{2,1,0:T(8,128)S(1)}, u32[]{:S(2)}, u32[]{:S(2)}) collective-permute-start(f32[10,88,128]{2,1,0:T(8,128)S(1)} %get-tuple-element.47), channel_id=1, source_target_pairs={{1,2},{2,1},{3,4},{4,3},{5,6},{6,5},{7,8},{8,7},{9,10},{10,9},{11,... | collective-permute-start | bytes 1351688 | tf_op jit(solution)/shard_map/ppermute | solution.py:667
  15.2 4.2 %collective-permute-start.3 = (f32[96,128]{1,0:T(8,128)S(1)}, f32[96,128]{1,0:T(8,128)S(1)}, u32[]{:S(2)}, u32[]{:S(2)}) collective-permute-start(f32[96,128]{1,0:T(8,128)S(1)} %add.14), channel_id=1, source_target_pairs={{0,8},{1,9},{2,10},{3,11},{4,12},{5,13},{6,14},{7,15},{8,0},{9,1},... | collective-permute-start | bytes 147464 | tf_op jit(solution)/shard_map/ppermute | solution.py:686
  30.7 5.9 %collective-permute-start.6 = (f32[2,10,8,128]{3,2,1,0:T(8,128)S(1)}, f32[2,10,8,128]{3,2,1,0:T(8,128)S(1)}, u32[]{:S(2)}, u32[]{:S(2)}) collective-permute-start(f32[2,10,8,128]{3,2,1,0:T(8,128)S(1)} %get-tuple-element.48.own.refs_1_), channel_id=1, source_target_pairs={{0,1},{1,0},{2,3},{3,2},{4,5},{5,4},{6,7},{7,6},{8,9},{9,8},{10,11... | collective-permute-start | bytes 245768 | tf_op jit(solution)/shard_map/ppermute | solution.py:666
  37.2 7.5 %collective-permute-start.7 = (f32[3,10,8,128]{3,2,1,0:T(8,128)S(1)}, f32[3,10,8,128]{3,2,1,0:T(8,128)S(1)}, u32[]{:S(2)}, u32[]{:S(2)}) collective-permute-start(f32[3,10,8,128]{3,2,1,0:T(8,128)S(1)} %shard_map.51), channel_id=1, source_target_pairs={{1,2},{2,1},{3,4},{4,3},{5,6},{6,5},{7,8},{8,7},{9,10},{10,9},{11,... | collective-permute-start | bytes 368648 | tf_op jit(solution)/shard_map/ppermute | solution.py:667
  44.7 1.3 %collective-permute-start.8 = (f32[3,10,8,128]{3,2,1,0:T(8,128)S(1)}, f32[3,10,8,128]{3,2,1,0:T(8,128)S(1)}, u32[]{:S(2)}, u32[]{:S(2)}) collective-permute-start(f32[3,10,8,128]{3,2,1,0:T(8,128)S(1)} %collective-permute-done.7.refs_3_), channel_id=1, source_target_pairs={{0,1},{1,0},{2,3},{3,2},{4,5},{5,4},{6,7},{7,6},{8,9},{9,8},{10,11... | collective-permute-start | bytes 368648 | tf_op jit(solution)/shard_map/ppermute | solution.py:666
  54.4 5.0 %collective-permute-start.9 = (f32[5,88,128]{2,1,0:T(8,128)S(1)}, f32[5,88,128]{2,1,0:T(8,128)S(1)}, u32[]{:S(2)}, u32[]{:S(2)}) collective-permute-start(f32[5,88,128]{2,1,0:T(8,128)S(1)} %get-tuple-element.60), channel_id=1, source_target_pairs={{0,1},{1,0},{2,3},{3,2},{4,5},{5,4},{6,7},{7,6},{8,9},{9,8},{10,11... | collective-permute-start | bytes 675848 | tf_op jit(solution)/shard_map/ppermute | solution.py:666
  54.6 9.7 %collective-permute-start.10 = (f32[5,88,128]{2,1,0:T(8,128)S(1)}, f32[5,88,128]{2,1,0:T(8,128)S(1)}, u32[]{:S(2)}, u32[]{:S(2)}) collective-permute-start(f32[5,88,128]{2,1,0:T(8,128)S(1)} %get-tuple-element.61), channel_id=1, source_target_pairs={{1,2},{2,1},{3,4},{4,3},{5,6},{6,5},{7,8},{8,7},{9,10},{10,9},{11,... | collective-permute-start | bytes 675848 | tf_op jit(solution)/shard_map/ppermute | solution.py:667
  68.5 1.3 %collective-permute-start.11 = (f32[2,10,8,128]{3,2,1,0:T(8,128)S(1)}, f32[2,10,8,128]{3,2,1,0:T(8,128)S(1)}, u32[]{:S(2)}, u32[]{:S(2)}) collective-permute-start(f32[2,10,8,128]{3,2,1,0:T(8,128)S(1)} %get-tuple-element.62.own.refs_1_), channel_id=1, source_target_pairs={{0,1},{1,0},{2,3},{3,2},{4,5},{5,4},{6,7},{7,6},{8,9},{9,8},{10,11... | collective-permute-start | bytes 245768 | tf_op jit(solution)/shard_map/ppermute | solution.py:666
  70.4 7.5 %collective-permute-start.12 = (f32[3,10,8,128]{3,2,1,0:T(8,128)S(1)}, f32[3,10,8,128]{3,2,1,0:T(8,128)S(1)}, u32[]{:S(2)}, u32[]{:S(2)}) collective-permute-start(f32[3,10,8,128]{3,2,1,0:T(8,128)S(1)} %shard_map.55), channel_id=1, source_target_pairs={{1,2},{2,1},{3,4},{4,3},{5,6},{6,5},{7,8},{8,7},{9,10},{10,9},{11,... | collective-permute-start | bytes 368648 | tf_op jit(solution)/shard_map/ppermute | solution.py:667
  77.9 1.3 %collective-permute-start.13 = (f32[3,10,8,128]{3,2,1,0:T(8,128)S(1)}, f32[3,10,8,128]{3,2,1,0:T(8,128)S(1)}, u32[]{:S(2)}, u32[]{:S(2)}) collective-permute-start(f32[3,10,8,128]{3,2,1,0:T(8,128)S(1)} %collective-permute-done.12.refs_3_), channel_id=1, source_target_pairs={{0,1},{1,0},{2,3},{3,2},{4,5},{5,4},{6,7},{7,6},{8,9},{9,8},{10,11... | collective-permute-start | bytes 368648 | tf_op jit(solution)/shard_map/ppermute | solution.py:666

commit v11 on v8

--- a/solution.py
+++ b/solution.py
@@ -25,6 +25,7 @@
 COARSEST = 3
 EDGE_BATCH = 10
 GROUP = 4
+HELD_PARTS = 2
 SPREAD = 16
 
 
@@ -394,13 +395,13 @@
     for which, copy in enumerate(copies):
         copy.wait()
         for field in range(FIELDS):
-            for p, part in enumerate(three_parts(held_in[which, field])):
+            for p, part in enumerate(three_parts(held_in[which, field])[:HELD_PARTS]):
                 start = p * held + (which * FIELDS + field) * OWN
                 parts[start : start + OWN, :] = part
 
     def two_subs(index):
         values = dot(parts[...], turn(2 * index, True))
-        values = (values[:held] + values[held : 2 * held]) + values[2 * held :]
+        values = values[:held] + values[held:]
         for which, target in enumerate((state_rows, forcing_rows)):
             for field in range(FIELDS):
                 start = (which * FIELDS + field) * OWN
@@ -582,13 +583,13 @@
         for field in range(FIELDS):
             for sub in range(SUB):
                 value = work0[field, pl.ds(at(O0, 0) + sub, OWN, stride=stride_of(0)), :]
-                for p, part in enumerate(three_parts(value)):
+                for p, part in enumerate(three_parts(value)[:HELD_PARTS]):
                     start = p * held + field * OWN
                     parts[start : start + OWN, sub * LANES : (sub + 1) * LANES] = part
 
         def columns_out(index):
             values = dot(parts[...], turn(2 * index, False))
-            values = (values[:held] + values[held : 2 * held]) + values[2 * held :]
+            values = values[:held] + values[held:]
             cells = pl.ds(pl.multiple_of(index * 2 * LANES, 2 * LANES), 2 * LANES)
             for field in range(FIELDS):
                 out[field, :, cells] = values[field * OWN : (field + 1) * OWN]
@@ -696,19 +697,19 @@
         [f32(FIELDS, OWN * SUB, LANES)] * 2 + [f32(2 * FIELDS, FINE_HALO * SUB, LANES)] * 2,
         [where_ref, in_hbm(initial_state), in_hbm(forcing)],
         [
-            pltpu.VMEM((3 * 2 * FIELDS * OWN, SUB * LANES), jnp.bfloat16),
+            pltpu.VMEM((HELD_PARTS * 2 * FIELDS * OWN, SUB * LANES), jnp.bfloat16),
             scratch(2, FIELDS, OWN, SUB * LANES),
             pltpu.SemaphoreType.DMA((2,)),
         ],
         (1, 2),
     )
     step = 1
-    while step < min(size, 4):
+    while step < min(size, 8):
         gathered = doubled(gathered, step)
         step *= 2
     gathered, send_a, send_b = lax.optimization_barrier((gathered, send_a, send_b))
     got_b, got_a = swap_b(send_b), swap_a(send_a)
-    if size > 4:
+    if step < size:
         free = [i for i in range(size) if i % 2 != i // 2 % 2]
         while step < size:
             gathered = gathered + lax.ppermute(gathered, "axial", [(i, i ^ step) for i in free])
@@ -756,7 +757,7 @@
             return call(
                 functools.partial(up_kernel, True), "up_last", 26,
                 [f32(FIELDS, OWN, SUB * LANES)], operands,
-                [pltpu.VMEM((3 * FIELDS * OWN, SUB * LANES), jnp.bfloat16)] + temps,
+                [pltpu.VMEM((HELD_PARTS * FIELDS * OWN, SUB * LANES), jnp.bfloat16)] + temps,
             )[0]
         state, send_a, send_b = call(
             functools.partial(up_kernel, False), "up", 26,

time: 89.3 us -> 88.5 us (level)
  waiting for transfers between devices: 24.7 us -> 28.1 us
  starting transfers between devices: 22.2 us -> 19.5 us
  Pallas kernels: 41.5 us -> 40.3 us
    ppermute x4, waiting for transfers between devices: 11.2 us -> 15.2 us  [per_device(): swap_b = lambda x: lax.ppermute(x, 'axial', pair_b)]
    ppermute x2 -> x1, starting transfers between devices: 5.11 us -> 1.96 us  [per_device(): lax.ppermute(gathered, 'axial', [(i, i ^ step) for i in free])]
    ppermute x2 -> x1, waiting for transfers between devices: 6.35 us -> 4.06 us  [per_device(): lax.ppermute(gathered, 'axial', [(i, i ^ step) for i in free])]
    ppermute x4, starting transfers between devices: 13.8 us -> 11.8 us  [per_device(): swap_b = lambda x: lax.ppermute(x, 'axial', pair_b)]
    ppermute x2 -> x3, waiting for transfers between devices: 0.88 us -> 2.52 us  [doubled(): lax.ppermute(held, 'axial', [(i, i ^ step) for i in range(size)])]
    ppermute x2 -> x3, starting transfers between devices: 1.98 us -> 3.34 us  [doubled(): lax.ppermute(held, 'axial', [(i, i ^ step) for i in range(size)])]
    pallas_call x10, Pallas kernels: 41.5 us -> 40.3 us  [call(): pl.pallas_call(kernel, out_shape=outs, in_specs=[SMEM] + [HBM if i in raw...]
    ppermute x7, starting transfers between devices: 1.33 us -> 2.33 us  [per_device(): swap_a = lambda x: lax.ppermute(x, 'axial', pair_a)]
  transfers between devices with their start and end apart: 15 -> 15, of which waited for: 11 -> 12; matrix products, arithmetic and copies ran while one was open for 0% -> 0% of each run, Pallas kernels for 11% -> 10%
where the time goes in v11:
time: 88.5 us; the launch traced here: 88.2 us
  Pallas kernels  40.3 us (46%)
  waiting for transfers between devices  28.1 us (32%)
  starting transfers between devices  19.5 us (22%)
    pallas_call x10, Pallas kernels, call(): pl.pallas_call(kernel, out_shape=outs, in_specs=[SMEM] + [HBM if i in raw...  40.3 us
    ppermute x4, waiting for transfers between devices, per_device(): swap_b = lambda x: lax.ppermute(x, 'axial', pair_b)  15.2 us
    ppermute x4, starting transfers between devices, per_device(): swap_b = lambda x: lax.ppermute(x, 'axial', pair_b)  11.8 us
    ppermute x7, waiting for transfers between devices, per_device(): swap_a = lambda x: lax.ppermute(x, 'axial', pair_a)  6.38 us
    ppermute x1, waiting for transfers between devices, per_device(): lax.ppermute(gathered, 'axial', [(i, i ^ step) for i in free])  4.06 us
    ppermute x3, starting transfers between devices, doubled(): lax.ppermute(held, 'axial', [(i, i ^ step) for i in range(size)])  3.34 us
    ppermute x3, waiting for transfers between devices, doubled(): lax.ppermute(held, 'axial', [(i, i ^ step) for i in range(size)])  2.52 us
    ppermute x7, starting transfers between devices, per_device(): swap_a = lambda x: lax.ppermute(x, 'axial', pair_a)  2.33 us
  transfers between devices with their start and end apart: 15, of which 12 were waited for; matrix products, arithmetic and copies ran while one was open for 0% of the time, Pallas kernels for 10%

profile of v11, /device:TPU:17, one launch (start us, length us, event | category | flops | bytes accessed | tf_op | source)
XLA Modules:
  0.0 88.2 jit_solution(2960015525334942849)
XLA Ops:
  0.1 1.3 %prep.1 = f32[96,128]{1,0:T(8,128)S(1)} custom-call(s32[2]{0:T(128)S(1)} %pad_add_fusion.where_ref.refs_0_, f32[4,25]{1,0:T(4,128)} %bitcast.4, s32[8,32]{1,0:T(8,128)} %bitcast.3), custom_call_target="tpu_custom_call" | custom-call | tf_op jit(solution)/shard_map/prep/pallas_call | solution.py:646
  1.4 0.7 collective-permute-start
  2.1 0.9 collective-permute-done
  3.0 1.3 %collective-permute-start.1 = (f32[96,128]{1,0:T(8,128)S(1)}, f32[96,128]{1,0:T(8,128)S(1)}, u32[]{:S(2)}, u32[]{:S(2)}) collective-permute-start(f32[96,128]{1,0:T(8,128)S(1)} %add.20), channel_id=1, source_target_pairs={{0,2},{1,3},{2,0},{3,1},{4,6},{5,7},{6,4},{7,5},{8,10},{9,11},{10,... | collective-permute-start | bytes 147464 | tf_op jit(solution)/shard_map/ppermute | solution.py:691
  4.3 1.6 %collective-permute-done.1 = f32[96,128]{1,0:T(8,128)S(1)} collective-permute-done((f32[96,128]{1,0:T(8,128)S(1)}, f32[96,128]{1,0:T(8,128)S(1)}, u32[]{:S(2)}, u32[]{:S(2)}) %collective-permute-start.1) | collective-permute-done | bytes 49184 | tf_op jit(solution)/shard_map/ppermute | solution.py:691
  5.9 1.4 %collective-permute-start.2 = (f32[96,128]{1,0:T(8,128)S(1)}, f32[96,128]{1,0:T(8,128)S(1)}, u32[]{:S(2)}, u32[]{:S(2)}) collective-permute-start(f32[96,128]{1,0:T(8,128)S(1)} %add.21), channel_id=1, source_target_pairs={{0,4},{1,5},{2,6},{3,7},{4,0},{5,1},{6,2},{7,3},{8,12},{9,13},{10,... | collective-permute-start | bytes 147464 | tf_op jit(solution)/shard_map/ppermute | solution.py:691
  7.3 4.0 %split.1 = (f32[5,256,128]{2,1,0:T(8,128)S(1)}, f32[5,256,128]{2,1,0:T(8,128)S(1)}, f32[10,88,128]{2,1,0:T(8,128)S(1)}, f32[10,88,128]{2,1,0:T(8,128)S(1)}) custom-call(s32[2]{0:T(128)S(1)} %pad_add_fusion.where_ref.refs_0_, f32[5,32,1024]{2,1,0:T(8,128)} %state_ref.1, f32[5,32,1024]{2,1,0:T(8,128)} %forcing_ref.1), custom_call_target="tpu_custom_call" | custom-call | tf_op jit(solution)/shard_map/split/pallas_call | solution.py:646
  11.3 1.9 %collective-permute-start.3 = (f32[10,88,128]{2,1,0:T(8,128)S(1)}, f32[10,88,128]{2,1,0:T(8,128)S(1)}, u32[]{:S(2)}, u32[]{:S(2)}) collective-permute-start(f32[10,88,128]{2,1,0:T(8,128)S(1)} %get-tuple-element.35), channel_id=1, source_target_pairs={{0,1},{1,0},{2,3},{3,2},{4,5},{5,4},{6,7},{7,6},{8,9},{9,8},{10,11... | collective-permute-start | bytes 1351688 | tf_op jit(solution)/shard_map/ppermute | solution.py:670
  13.3 3.1 %collective-permute-start.4 = (f32[10,88,128]{2,1,0:T(8,128)S(1)}, f32[10,88,128]{2,1,0:T(8,128)S(1)}, u32[]{:S(2)}, u32[]{:S(2)}) collective-permute-start(f32[10,88,128]{2,1,0:T(8,128)S(1)} %get-tuple-element.36), channel_id=1, source_target_pairs={{1,2},{2,1},{3,4},{4,3},{5,6},{6,5},{7,8},{8,7},{9,10},{10,9},{11,... | collective-permute-start | bytes 1351688 | tf_op jit(solution)/shard_map/ppermute | solution.py:671
  16.4 2.0 %collective-permute-start.5 = (f32[96,128]{1,0:T(8,128)S(1)}, f32[96,128]{1,0:T(8,128)S(1)}, u32[]{:S(2)}, u32[]{:S(2)}) collective-permute-start(f32[96,128]{1,0:T(8,128)S(1)} %add.22), channel_id=1, source_target_pairs={{1,9},{2,10},{5,13},{6,14},{9,1},{10,2},{13,5},{14,6},{17,25},{18,... | collective-permute-start | bytes 147464 | tf_op jit(solution)/shard_map/ppermute | solution.py:715
  18.3 4.1 %collective-permute-done.5 = f32[96,128]{1,0:T(8,128)S(1)} collective-permute-done((f32[96,128]{1,0:T(8,128)S(1)}, f32[96,128]{1,0:T(8,128)S(1)}, u32[]{:S(2)}, u32[]{:S(2)}) %collective-permute-start.5) | collective-permute-done | bytes 49184 | tf_op jit(solution)/shard_map/ppermute | solution.py:715
  22.5 1.2 %collective-permute-done.6 = f32[96,128]{1,0:T(8,128)S(1)} collective-permute-done((f32[96,128]{1,0:T(8,128)S(1)}, f32[96,128]{1,0:T(8,128)S(1)}, u32[]{:S(2)}, u32[]{:S(2)}) %collective-permute-start.6) | collective-permute-done | bytes 49184 | tf_op jit(solution)/shard_map/ppermute | solution.py:670
  23.7 2.0 %tables.1.refs_5_.refs_10_.table.refs_9_ = f32[50,160,128]{2,1,0:T(8,128)S(1)} custom-call(s32[2]{0:T(128)S(1)} %pad_add_fusion.where_ref.refs_0_, f32[96,128]{1,0:T(8,128)S(1)} %broadcast_select_fusion.regions_ref), custom_call_target="tpu_custom_call" | custom-call | tf_op jit(solution)/shard_map/tables/pallas_call | solution.py:646
  25.8 2.0 %collective-permute-done.4.refs_4_ = f32[10,88,128]{2,1,0:T(8,128)S(1)} collective-permute-done((f32[10,88,128]{2,1,0:T(8,128)S(1)}, f32[10,88,128]{2,1,0:T(8,128)S(1)}, u32[]{:S(2)}, u32[]{:S(2)}) %collective-permute-start.4) | collective-permute-done | bytes 450592 | tf_op jit(solution)/shard_map/ppermute | solution.py:671
  27.8 6.1 %down_fresh.1 = (f32[5,720,128]{2,1,0:T(8,128)S(1)}, f32[5,480,128]{2,1,0:T(8,128)S(1)}, f32[5,32,8,128]{3,2,1,0:T(8,128)S(1)}, f32[5,480,128]{2,1,0:T(8,128)S(1...) custom-call(s32[2]{0:T(128)S(1)} %pad_add_fusion.where_ref.refs_0_, ...), custom_call_target="tpu_custom_call" | custom-call | tf_op jit(solution)/shard_map/down_fresh/pallas_call | solution.py:646
  33.9 1.3 %collective-permute-done.7.beside.refs_2_ = f32[2,10,8,128]{3,2,1,0:T(8,128)S(1)} collective-permute-done((f32[2,10,8,128]{3,2,1,0:T(8,128)S(1)}, f32[2,10,8,128]{3,2,1,0:T(8,128)S(1)}, u32[]{:S(2)}, u32[]{:S(2)}) %collective-permute-start.7) | collective-permute-done | bytes 81952 | tf_op jit(solution)/shard_map/ppermute | solution.py:670
  35.2 0.6 relay.2
  35.8 3.1 %collective-permute-start.8 = (f32[3,10,8,128]{3,2,1,0:T(8,128)S(1)}, f32[3,10,8,128]{3,2,1,0:T(8,128)S(1)}, u32[]{:S(2)}, u32[]{:S(2)}) collective-permute-start(f32[3,10,8,128]{3,2,1,0:T(8,128)S(1)} %relay.2), channel_id=1, source_target_pairs={{1,2},{2,1},{3,4},{4,3},{5,6},{6,5},{7,8},{8,7},{9,10},{10,9},{11,... | collective-permute-start | bytes 368648 | tf_op jit(solution)/shard_map/ppermute | solution.py:671
  38.9 4.4 %collective-permute-done.8.refs_3_ = f32[3,10,8,128]{3,2,1,0:T(8,128)S(1)} collective-permute-done((f32[3,10,8,128]{3,2,1,0:T(8,128)S(1)}, f32[3,10,8,128]{3,2,1,0:T(8,128)S(1)}, u32[]{:S(2)}, u32[]{:S(2)}) %collective-permute-start.8) | collective-permute-done | bytes 122912 | tf_op jit(solution)/shard_map/ppermute | solution.py:671
  43.3 1.3 %collective-permute-done.9.refs_4_ = f32[3,10,8,128]{3,2,1,0:T(8,128)S(1)} collective-permute-done((f32[3,10,8,128]{3,2,1,0:T(8,128)S(1)}, f32[3,10,8,128]{3,2,1,0:T(8,128)S(1)}, u32[]{:S(2)}, u32[]{:S(2)}) %collective-permute-start.9) | collective-permute-done | bytes 122912 | tf_op jit(solution)/shard_map/ppermute | solution.py:670
  44.6 8.3 %up.1 = (f32[5,256,128]{2,1,0:T(8,128)S(1)}, f32[5,88,128]{2,1,0:T(8,128)S(1)}, f32[5,88,128]{2,1,0:T(8,128)S(1)}) custom-call(s32[2]{0:T(128)S(1)} %pad_add_fusion.where_ref.refs_0_, f32[2,10,8,128]{3,2,1,0:T(8,128)S(1)} %get-tuple-element.38.own.refs_1_, f32[2,10,8,128]{3,2,1,0:T(8,128)S(1)} %collective-permute-done.7.beside.refs_2_, ...), custom_call_target="tpu_custom_call" | custom-call | tf_op jit(solution)/shard_map/up/pallas_call | solution.py:646
  53.0 0.2 collective-permute-start.10
  53.2 2.8 %collective-permute-start.11 = (f32[5,88,128]{2,1,0:T(8,128)S(1)}, f32[5,88,128]{2,1,0:T(8,128)S(1)}, u32[]{:S(2)}, u32[]{:S(2)}) collective-permute-start(f32[5,88,128]{2,1,0:T(8,128)S(1)} %get-tuple-element.51), channel_id=1, source_target_pairs={{1,2},{2,1},{3,4},{4,3},{5,6},{6,5},{7,8},{8,7},{9,10},{10,9},{11,... | collective-permute-start | bytes 675848 | tf_op jit(solution)/shard_map/ppermute | solution.py:671
  56.0 2.8 %interior.1 = (f32[5,720,128]{2,1,0:T(8,128)S(1)}, f32[5,720,128]{2,1,0:T(8,128)S(1)}, f32[5,480,128]{2,1,0:T(8,128)S(1)}, f32[5,32,8,128]{3,2,1,0:T(8,128)S(1)}, f32[5,480,128]{2,1,0:T(8,128)S(1)}) custom-call(s32[2]{0:T(128)S(1)} %pad_add_fusion.where_ref.refs_0_, f32[5,256,128]{2,1,0:T(8,128)S(1)} %get-tuple-element.44.state, ...), custom_call_target="tpu_custom_call" | custom-call | tf_op jit(solution)/shard_map/interior/pallas_call | solution.py:646
  58.8 4.1 %collective-permute-done.11.refs_7_ = f32[5,88,128]{2,1,0:T(8,128)S(1)} collective-permute-done((f32[5,88,128]{2,1,0:T(8,128)S(1)}, f32[5,88,128]{2,1,0:T(8,128)S(1)}, u32[]{:S(2)}, u32[]{:S(2)}) %collective-permute-start.11) | collective-permute-done | bytes 225312 | tf_op jit(solution)/shard_map/ppermute | solution.py:671
  62.9 4.2 %down.1 = (f32[5,720,128]{2,1,0:T(8,128)S(1)}, f32[5,480,128]{2,1,0:T(8,128)S(1)}, f32[5,32,8,128]{3,2,1,0:T(8,128)S(1)}, f32[5,480,128]{2,1,0:T(8,128)S(1)}, f32[2,10,8,128]{3,2,1,0:T(8,128)S(1)}) custom-call(s32[2]{0:T(128)S(1)} %pad_add_fusion.where_ref.refs_0_, f32[5,720,128]{2,1,0:T(8,128)S(1)} %get-tuple-element.45.refs_1_, ...), custom_call_target="tpu_custom_call" | custom-call | tf_op jit(solution)/shard_map/down/pallas_call | solution.py:646
  67.1 1.3 %collective-permute-done.12.beside.refs_2_ = f32[2,10,8,128]{3,2,1,0:T(8,128)S(1)} collective-permute-done((f32[2,10,8,128]{3,2,1,0:T(8,128)S(1)}, f32[2,10,8,128]{3,2,1,0:T(8,128)S(1)}, u32[]{:S(2)}, u32[]{:S(2)}) %collective-permute-start.12) | collective-permute-done | bytes 81952 | tf_op jit(solution)/shard_map/ppermute | solution.py:670
  68.4 0.6 relay.3
  69.0 2.8 %collective-permute-start.13 = (f32[3,10,8,128]{3,2,1,0:T(8,128)S(1)}, f32[3,10,8,128]{3,2,1,0:T(8,128)S(1)}, u32[]{:S(2)}, u32[]{:S(2)}) collective-permute-start(f32[3,10,8,128]{3,2,1,0:T(8,128)S(1)} %relay.3), channel_id=1, source_target_pairs={{1,2},{2,1},{3,4},{4,3},{5,6},{6,5},{7,8},{8,7},{9,10},{10,9},{11,... | collective-permute-start | bytes 368648 | tf_op jit(solution)/shard_map/ppermute | solution.py:671
  71.8 4.7 %collective-permute-done.13.refs_3_ = f32[3,10,8,128]{3,2,1,0:T(8,128)S(1)} collective-permute-done((f32[3,10,8,128]{3,2,1,0:T(8,128)S(1)}, f32[3,10,8,128]{3,2,1,0:T(8,128)S(1)}, u32[]{:S(2)}, u32[]{:S(2)}) %collective-permute-start.13) | collective-permute-done | bytes 122912 | tf_op jit(solution)/shard_map/ppermute | solution.py:671
  76.5 1.3 %collective-permute-done.14.refs_4_ = f32[3,10,8,128]{3,2,1,0:T(8,128)S(1)} collective-permute-done((f32[3,10,8,128]{3,2,1,0:T(8,128)S(1)}, f32[3,10,8,128]{3,2,1,0:T(8,128)S(1)}, u32[]{:S(2)}, u32[]{:S(2)}) %collective-permute-start.14) | collective-permute-done | bytes 122912 | tf_op jit(solution)/shard_map/ppermute | solution.py:670
  77.8 10.4 %up_last.1 = f32[5,32,1024]{2,1,0:T(8,128)} custom-call(s32[2]{0:T(128)S(1)} %pad_add_fusion.where_ref.refs_0_, f32[2,10,8,128]{3,2,1,0:T(8,128)S(1)} %get-tuple-element.52.own.refs_1_, f32[2,10,8,128]{3,2,1,0:T(8,128)S(1)} %collective-permute-done.12.beside.refs_2_, f32[3,10,8,128]{3,2,1,0:T(8,128)S(1)} %collective-permute-done.13.refs_3_, ...), custom_call_target="tpu_custom_call" | custom-call | tf_op jit(solution)/shard_map/up_last/pallas_call | solution.py:646
  (14 shorter events, 0.3 us)
Async XLA Ops:
  1.4 1.6 %collective-permute-start = (f32[96,128]{1,0:T(8,128)S(1)}, f32[96,128]{1,0:T(8,128)S(1)}, u32[]{:S(2)}, u32[]{:S(2)}) collective-permute-start(f32[96,128]{1,0:T(8,128)S(1)} %prep.1), channel_id=1, source_target_pairs={{0,1},{1,0},{2,3},{3,2},{4,5},{5,4},{6,7},{7,6},{8,9},{9,8},{10,11... | collective-permute-start | bytes 147464 | tf_op jit(solution)/shard_map/ppermute | solution.py:691
  3.0 2.9 %collective-permute-start.1 = (f32[96,128]{1,0:T(8,128)S(1)}, f32[96,128]{1,0:T(8,128)S(1)}, u32[]{:S(2)}, u32[]{:S(2)}) collective-permute-start(f32[96,128]{1,0:T(8,128)S(1)} %add.20), channel_id=1, source_target_pairs={{0,2},{1,3},{2,0},{3,1},{4,6},{5,7},{6,4},{7,5},{8,10},{9,11},{10,... | collective-permute-start | bytes 147464 | tf_op jit(solution)/shard_map/ppermute | solution.py:691
  5.9 5.4 %collective-permute-start.2 = (f32[96,128]{1,0:T(8,128)S(1)}, f32[96,128]{1,0:T(8,128)S(1)}, u32[]{:S(2)}, u32[]{:S(2)}) collective-permute-start(f32[96,128]{1,0:T(8,128)S(1)} %add.21), channel_id=1, source_target_pairs={{0,4},{1,5},{2,6},{3,7},{4,0},{5,1},{6,2},{7,3},{8,12},{9,13},{10,... | collective-permute-start | bytes 147464 | tf_op jit(solution)/shard_map/ppermute | solution.py:691
  11.3 14.4 %collective-permute-start.3 = (f32[10,88,128]{2,1,0:T(8,128)S(1)}, f32[10,88,128]{2,1,0:T(8,128)S(1)}, u32[]{:S(2)}, u32[]{:S(2)}) collective-permute-start(f32[10,88,128]{2,1,0:T(8,128)S(1)} %get-tuple-element.35), channel_id=1, source_target_pairs={{0,1},{1,0},{2,3},{3,2},{4,5},{5,4},{6,7},{7,6},{8,9},{9,8},{10,11... | collective-permute-start | bytes 1351688 | tf_op jit(solution)/shard_map/ppermute | solution.py:670
  13.3 14.5 %collective-permute-start.4 = (f32[10,88,128]{2,1,0:T(8,128)S(1)}, f32[10,88,128]{2,1,0:T(8,128)S(1)}, u32[]{:S(2)}, u32[]{:S(2)}) collective-permute-start(f32[10,88,128]{2,1,0:T(8,128)S(1)} %get-tuple-element.36), channel_id=1, source_target_pairs={{1,2},{2,1},{3,4},{4,3},{5,6},{6,5},{7,8},{8,7},{9,10},{10,9},{11,... | collective-permute-start | bytes 1351688 | tf_op jit(solution)/shard_map/ppermute | solution.py:671
  16.4 6.0 %collective-permute-start.5 = (f32[96,128]{1,0:T(8,128)S(1)}, f32[96,128]{1,0:T(8,128)S(1)}, u32[]{:S(2)}, u32[]{:S(2)}) collective-permute-start(f32[96,128]{1,0:T(8,128)S(1)} %add.22), channel_id=1, source_target_pairs={{1,9},{2,10},{5,13},{6,14},{9,1},{10,2},{13,5},{14,6},{17,25},{18,... | collective-permute-start | bytes 147464 | tf_op jit(solution)/shard_map/ppermute | solution.py:715
  22.4 1.3 %collective-permute-start.6 = (f32[96,128]{1,0:T(8,128)S(1)}, f32[96,128]{1,0:T(8,128)S(1)}, u32[]{:S(2)}, u32[]{:S(2)}) collective-permute-start(f32[96,128]{1,0:T(8,128)S(1)} %add.25), channel_id=1, source_target_pairs={{0,1},{1,0},{2,3},{3,2},{4,5},{5,4},{6,7},{7,6},{8,9},{9,8},{10,11... | collective-permute-start | bytes 147464 | tf_op jit(solution)/shard_map/ppermute | solution.py:670
  33.9 1.3 %collective-permute-start.7 = (f32[2,10,8,128]{3,2,1,0:T(8,128)S(1)}, f32[2,10,8,128]{3,2,1,0:T(8,128)S(1)}, u32[]{:S(2)}, u32[]{:S(2)}) collective-permute-start(f32[2,10,8,128]{3,2,1,0:T(8,128)S(1)} %get-tuple-element.38.own.refs_1_), channel_id=1, source_target_pairs={{0,1},{1,0},{2,3},{3,2},{4,5},{5,4},{6,7},{7,6},{8,9},{9,8},{10,11... | collective-permute-start | bytes 245768 | tf_op jit(solution)/shard_map/ppermute | solution.py:670
  35.8 7.5 %collective-permute-start.8 = (f32[3,10,8,128]{3,2,1,0:T(8,128)S(1)}, f32[3,10,8,128]{3,2,1,0:T(8,128)S(1)}, u32[]{:S(2)}, u32[]{:S(2)}) collective-permute-start(f32[3,10,8,128]{3,2,1,0:T(8,128)S(1)} %relay.2), channel_id=1, source_target_pairs={{1,2},{2,1},{3,4},{4,3},{5,6},{6,5},{7,8},{8,7},{9,10},{10,9},{11,... | collective-permute-start | bytes 368648 | tf_op jit(solution)/shard_map/ppermute | solution.py:671
  43.3 1.3 %collective-permute-start.9 = (f32[3,10,8,128]{3,2,1,0:T(8,128)S(1)}, f32[3,10,8,128]{3,2,1,0:T(8,128)S(1)}, u32[]{:S(2)}, u32[]{:S(2)}) collective-permute-start(f32[3,10,8,128]{3,2,1,0:T(8,128)S(1)} %collective-permute-done.8.refs_3_), channel_id=1, source_target_pairs={{0,1},{1,0},{2,3},{3,2},{4,5},{5,4},{6,7},{7,6},{8,9},{9,8},{10,11... | collective-permute-start | bytes 368648 | tf_op jit(solution)/shard_map/ppermute | solution.py:670
  53.0 5.8 %collective-permute-start.10 = (f32[5,88,128]{2,1,0:T(8,128)S(1)}, f32[5,88,128]{2,1,0:T(8,128)S(1)}, u32[]{:S(2)}, u32[]{:S(2)}) collective-permute-start(f32[5,88,128]{2,1,0:T(8,128)S(1)} %get-tuple-element.50), channel_id=1, source_target_pairs={{0,1},{1,0},{2,3},{3,2},{4,5},{5,4},{6,7},{7,6},{8,9},{9,8},{10,11... | collective-permute-start | bytes 675848 | tf_op jit(solution)/shard_map/ppermute | solution.py:670
  53.2 9.7 %collective-permute-start.11 = (f32[5,88,128]{2,1,0:T(8,128)S(1)}, f32[5,88,128]{2,1,0:T(8,128)S(1)}, u32[]{:S(2)}, u32[]{:S(2)}) collective-permute-start(f32[5,88,128]{2,1,0:T(8,128)S(1)} %get-tuple-element.51), channel_id=1, source_target_pairs={{1,2},{2,1},{3,4},{4,3},{5,6},{6,5},{7,8},{8,7},{9,10},{10,9},{11,... | collective-permute-start | bytes 675848 | tf_op jit(solution)/shard_map/ppermute | solution.py:671
  67.1 1.3 %collective-permute-start.12 = (f32[2,10,8,128]{3,2,1,0:T(8,128)S(1)}, f32[2,10,8,128]{3,2,1,0:T(8,128)S(1)}, u32[]{:S(2)}, u32[]{:S(2)}) collective-permute-start(f32[2,10,8,128]{3,2,1,0:T(8,128)S(1)} %get-tuple-element.52.own.refs_1_), channel_id=1, source_target_pairs={{0,1},{1,0},{2,3},{3,2},{4,5},{5,4},{6,7},{7,6},{8,9},{9,8},{10,11... | collective-permute-start | bytes 245768 | tf_op jit(solution)/shard_map/ppermute | solution.py:670
  69.0 7.5 %collective-permute-start.13 = (f32[3,10,8,128]{3,2,1,0:T(8,128)S(1)}, f32[3,10,8,128]{3,2,1,0:T(8,128)S(1)}, u32[]{:S(2)}, u32[]{:S(2)}) collective-permute-start(f32[3,10,8,128]{3,2,1,0:T(8,128)S(1)} %relay.3), channel_id=1, source_target_pairs={{1,2},{2,1},{3,4},{4,3},{5,6},{6,5},{7,8},{8,7},{9,10},{10,9},{11,... | collective-permute-start | bytes 368648 | tf_op jit(solution)/shard_map/ppermute | solution.py:671
  76.5 1.3 %collective-permute-start.14 = (f32[3,10,8,128]{3,2,1,0:T(8,128)S(1)}, f32[3,10,8,128]{3,2,1,0:T(8,128)S(1)}, u32[]{:S(2)}, u32[]{:S(2)}) collective-permute-start(f32[3,10,8,128]{3,2,1,0:T(8,128)S(1)} %collective-permute-done.13.refs_3_), channel_id=1, source_target_pairs={{0,1},{1,0},{2,3},{3,2},{4,5},{5,4},{6,7},{7,6},{8,9},{9,8},{10,11... | collective-permute-start | bytes 368648 | tf_op jit(solution)/shard_map/ppermute | solution.py:670
